TPU v7x, 32 devices: a whole 2x2x4 slice. The times are simulated.
32 devices in a mesh: ctx: 8 (over z, x), head: 4 (over y, core).
Axes of the slice: x: 2, y: 2, z: 4, core: 2. Of those that a mesh axis runs over, the one named last changes fastest.
Arguments:
- queries: bfloat16 [3072, 8192], P(('ctx', 'head')), may hold values from -6 to 6
- keys: bfloat16 [3072, 1024], P(('ctx', 'head')), may hold values from -6 to 6
- values: bfloat16 [3072, 1024], P(('ctx', 'head')), may hold values from -6 to 6
- attn_out: bfloat16 [3072, 8192], P('ctx', 'head'), may hold values from -6 to 6
- out_grad: bfloat16 [3072, 8192], P('ctx', 'head'), may hold values from -12 to 12
- log_sum: float32 [64, 3072], P('head', 'ctx'), as said below
- file_ids: int32 [3072], P('ctx'), may hold values from 0 to 7, as said below
Outputs:
- q_grad: bfloat16 [3072, 8192], P(('ctx', 'head'))
- k_grad: bfloat16 [3072, 1024], P(('ctx', 'head'))
- v_grad: bfloat16 [3072, 1024], P(('ctx', 'head'))
Inputs may be any that keep to these rules, and one draw needn't show every extreme that they name: file_ids never fall along the tokens, so each file's tokens are consecutive; each of the 8 files holds 1 to 1536 tokens, and the first file holds exactly 1536. log_sum is positive.
All inputs are finite; a program needn't handle non-finite values.
Results may differ from a plain program's by a relative error of at most 0.0053.
Values may be sent and summed in bfloat16 or wider, within the bound.
No kernel may reach another device: no remote copies, remote signals or barrier semaphores. Data moves between devices by JAX's collectives and lax.ppermute only.
A program may use at most 64 MiB of HBM per device.

v0:
```python
import math

import jax
import jax.numpy as jnp
from jax import lax
from jax.sharding import PartitionSpec as P

DH = 128


def passed_along(block, axis, distance):
    devices = range(lax.axis_size(axis))
    route = [(i - distance, i) for i in devices if i - distance in devices]
    return lax.ppermute(block, axis, route)


def shifted(block, axis, distance):
    devices = range(lax.axis_size(axis))
    route = [((i - distance) % len(devices), i) for i in devices]
    return lax.ppermute(block, axis, route)


def tile_grads(q_four, g_four, lse_three, delta_three, key_part, value_part, allowed):
    score_scale = 1.0 / math.sqrt(q_four.shape[-1])
    scores = (
        jnp.einsum("rkgd,ckd->kgrc", q_four, key_part, preferred_element_type=jnp.float32)
        * score_scale
    )
    attn_probs = jnp.exp(jnp.where(allowed[None, None], scores - lse_three[..., None], -1e30))
    probs_low = attn_probs.astype(jnp.bfloat16)
    dprobs = jnp.einsum("rkgd,ckd->kgrc", g_four, value_part, preferred_element_type=jnp.float32)
    dscores_low = (attn_probs * (dprobs - delta_three[..., None])).astype(jnp.bfloat16)
    q_part = jnp.einsum("kgrc,ckd->rkgd", dscores_low, key_part, preferred_element_type=jnp.float32)
    k_part = jnp.einsum("kgrc,rkgd->ckd", dscores_low, q_four, preferred_element_type=jnp.float32)
    v_part = jnp.einsum("kgrc,rkgd->ckd", probs_low, g_four, preferred_element_type=jnp.float32)
    return (q_part, k_part, v_part)


def per_device(queries, keys, values, attn_out, out_grad, log_sum, file_ids):
    q_rows, key_rows, value_rows = (
        lax.all_to_all(queries, "head", split_axis=1, concat_axis=0, tiled=True),
        lax.all_to_all(keys, "head", split_axis=1, concat_axis=0, tiled=True),
        lax.all_to_all(values, "head", split_axis=1, concat_axis=0, tiled=True),
    )
    block_rows = q_rows.shape[0]
    kv_local = key_rows.shape[1] // DH
    group_size = q_rows.shape[1] // (DH * kv_local)
    score_scale = 1.0 / math.sqrt(DH)
    q_four = q_rows.reshape(block_rows, kv_local, group_size, DH)
    g_four = out_grad.reshape(block_rows, kv_local, group_size, DH)
    o_four = attn_out.reshape(block_rows, kv_local, group_size, DH)
    key_three = key_rows.reshape(block_rows, kv_local, DH)
    value_three = value_rows.reshape(block_rows, kv_local, DH)
    lse_three = log_sum.reshape(kv_local, group_size, block_rows)
    delta_three = jnp.einsum("rkgd,rkgd->kgr", g_four, o_four, preferred_element_type=jnp.float32)
    ctx_count = lax.axis_size("ctx")
    reach_back = ctx_count // 2
    own_index = lax.axis_index("ctx")
    offsets = jnp.arange(block_rows, dtype=jnp.int32)
    query_pos = own_index * block_rows + offsets
    own_tags = file_ids.astype(jnp.bfloat16)
    grad_shape = (block_rows, kv_local, DH)

    def block_grads(key_part, value_part, tag_part, anchor):
        key_pos = anchor * block_rows + offsets
        allowed = (own_tags[:, None] == tag_part[None, :]) & (
            key_pos[None, :] <= query_pos[:, None]
        )

        def compute():
            return tile_grads(q_four, g_four, lse_three, delta_three, key_part, value_part, allowed)

        def skipped():
            return (
                jnp.zeros(q_four.shape, jnp.float32),
                jnp.zeros(grad_shape, jnp.float32),
                jnp.zeros(grad_shape, jnp.float32),
            )

        return lax.cond(jnp.any(allowed), compute, skipped)

    dq_first, dk_first, dv_first = block_grads(key_three, value_three, own_tags, own_index)
    k_store, v_store = (dk_first, dv_first)

    def visit_block(step_index, loop_state):
        dq_acc, key_part, value_part, tag_part, k_store, v_store = loop_state
        anchor = (own_index - step_index) % ctx_count
        key_part, value_part, tag_part = passed_along((key_part, value_part, tag_part), "ctx", 1)
        q_part, k_part, v_part = block_grads(key_part, value_part, tag_part, anchor)
        k_store, v_store = shifted((k_store, v_store), "ctx", 1)
        k_store = k_store + k_part
        v_store = v_store + v_part
        return (dq_acc + q_part, key_part, value_part, tag_part, k_store, v_store)

    loop_state = lax.fori_loop(
        1,
        reach_back + 1,
        visit_block,
        (dq_first, key_three, value_three, own_tags, k_store, v_store),
    )
    dq_sum = loop_state[0]
    k_total, v_total = shifted((loop_state[4], loop_state[5]), "ctx", -reach_back)
    q_done = (
        (dq_sum * score_scale).astype(jnp.bfloat16).reshape(block_rows, kv_local * group_size * DH)
    )
    k_done = (k_total * score_scale).astype(jnp.bfloat16).reshape(block_rows, kv_local * DH)
    v_done = v_total.astype(jnp.bfloat16).reshape(block_rows, kv_local * DH)
    q_grad, k_grad, v_grad = (
        lax.all_to_all(q_done, "head", split_axis=0, concat_axis=1, tiled=True),
        lax.all_to_all(k_done, "head", split_axis=0, concat_axis=1, tiled=True),
        lax.all_to_all(v_done, "head", split_axis=0, concat_axis=1, tiled=True),
    )
    return (q_grad, k_grad, v_grad)


def solution(mesh):
    return jax.shard_map(
        per_device,
        mesh=mesh,
        in_specs=(
            P(("ctx", "head"), None),
            P(("ctx", "head"), None),
            P(("ctx", "head"), None),
            P("ctx", "head"),
            P("ctx", "head"),
            P("head", "ctx"),
            P("ctx"),
        ),
        out_specs=(P(("ctx", "head"), None), P(("ctx", "head"), None), P(("ctx", "head"), None)),
        check_vma=False,
    )
```

profile of v0, /device:TPU:0, one launch (start us, length us, event | category | flops | bytes accessed | tf_op | source)
XLA Modules:
  0.0 267.3 jit_solution(12738604949703533861)
XLA Ops:
  0.7 1.7 copy.97
  2.4 4.2 %all-to-all-start = ((bf16[96,4,256]{2,0,1:T(8,128)(2,1)}), bf16[96,4,256]{2,0,1:T(8,128)(2,1)S(1)}, u32[]{:S(2)}, u32[]{:S(2)}) async-start(bf16[96,4,256]{2,0,1:T(8,128)(2,1)} %bitcast.126), calls=%async_computation | async-start | bytes 393216 | tf_op jit(solution)/shard_map/all_to_all | solution.py:42
  6.6 1.6 copy.96
  8.2 3.7 %all-to-all-done = bf16[96,4,256]{2,0,1:T(8,128)(2,1)S(1)} async-done(((bf16[96,4,256]{2,0,1:T(8,128)(2,1)}), bf16[96,4,256]{2,0,1:T(8,128)(2,1)S(1)}, u32[]{:S(2)}, u32[]{:S(2)}) %all-to-all-start) | async-done | bytes 196640 | tf_op jit(solution)/shard_map/all_to_all | solution.py:42
  12.0 3.4 %all-to-all-start.2 = ((bf16[96,4,256]{2,0,1:T(8,128)(2,1)}), bf16[96,4,256]{2,0,1:T(8,128)(2,1)S(1)}, u32[]{:S(2)}, u32[]{:S(2)}) async-start(bf16[96,4,256]{2,0,1:T(8,128)(2,1)} %bitcast.125), calls=%async_computation.2 | async-start | bytes 393216 | tf_op jit(solution)/shard_map/all_to_all | solution.py:43
  15.3 2.7 %copy.95 = bf16[12,4,8,2048]{3,2,0,1:T(8,128)(2,1)} copy(bf16[12,4,8,2048]{3,2,1,0:T(8,128)(2,1)} %bitcast.136) | data formatting | bytes 3145728 | tf_op jit(solution)/shard_map/all_to_all | solution.py:41
  18.1 2.6 all-to-all-done.2
  20.6 4.4 %all-to-all-start.1 = ((bf16[96,4,2048]{2,0,1:T(8,128)(2,1)}), bf16[96,4,2048]{2,0,1:T(8,128)(2,1)}, u32[]{:S(2)}, u32[]{:S(2)}) async-start(bf16[96,4,2048]{2,0,1:T(8,128)(2,1)} %bitcast.124), calls=%async_computation.1 | async-start | bytes 3145728 | tf_op jit(solution)/shard_map/all_to_all | solution.py:41
  28.1 1.6 copy.42
  29.8 1.8 copy.79
  31.6 2.2 copy.65
  33.8 3.0 %multiply_reduce_fusion = f32[2,8,384]{1,0,2:T(2,128)S(1)} fusion(f32[2,8,384,128]{3,1,0,2:T(8,128)} %copy.65, bf16[384,2,8,128]{3,2,1,0:T(8,128)(2,1)S(1)} %bitcast.133), kind=kLoop, calls=%fused_computation.44 | loop fusion | flops 2353152 | bytes 4743168
  41.0 4.2 %all-to-all-done.1 = bf16[96,4,2048]{2,0,1:T(8,128)(2,1)} async-done(((bf16[96,4,2048]{2,0,1:T(8,128)(2,1)}), bf16[96,4,2048]{2,0,1:T(8,128)(2,1)}, u32[]{:S(2)}, u32[]{:S(2)}) %all-to-all-start.1) | async-done | bytes 1572896 | tf_op jit(solution)/shard_map/all_to_all | solution.py:41
  45.1 1.8 copy.78
  48.5 10.1 %conditional.2 = (f32[384,2,8,128]{3,0,2,1:T(8,128)S(1)}, f32[384,2,128]{2,0,1:T(8,128)S(1)}, f32[384,2,128]{2,0,1:T(8,128)S(1)}) conditional(s32[]{:T(128)} %convert_element_type.38, () %tuple.46, (pred[384,384]{0,1:T(8,128)(4,1)}, bf16[384,2,128]{2,1,0:T(2,128)(2,1)S(1)}, bf16[384,2,8,128]{3,2,1,0:T(8,128)(2,1)S(1)}, f32[16,384]{1,0:T(8,128)}, ...), branch_computations={%region_1.0_spmd, %region_2.3_spmd} | conditional | flops 3043491840 | bytes 54337616 | solution.py:80
  50.0 2.0 fusion.19
  52.0 3.2 %fusion.5 = bf16[2,8,384,384]{2,3,1,0:T(8,128)(2,1)S(1)} fusion(f32[2,384,384,8]{2,1,3,0:T(8,128)S(1)} %fusion.12, f32[2,8,384]{2,1,0:T(8,128)S(1)} %get-tuple-element.370, f32[2,8,384]{2,1,0:T(8,128)S(1)} %bitcast.149, pred[384,384]{0,1:T(8,128)(4,1)S(1)} %copy-done.10, bf16[384,2,8,128]{0,3,2,1:T(8,128)(2,1)S(1)} %get-tuple-element.473, ...), kind=kOutput, calls=%fused_computation.4 | convolution fusion | flops 618135552 | bytes 16121856 | tf_op jit(solution)/shard_map/cond/branch_1_fun/rkgd,ckd->kgrc/dot_general | solution.py:31
  56.6 1.8 convolution_bitcast_fusion
  58.7 1.6 copy-done.1
  60.5 145.0 %while.26 = (s32[]{:T(128)}, f32[384,2,8,128]{3,0,2,1:T(8,128)}, bf16[384,2,128]{2,0,1:T(8,128)(2,1)}, bf16[384,2,128]{2,0,1:T(8,128)(2,1)}, bf16[384]{0:T(512)(...) while((s32[]{:T(128)}, f32[384,2,8,128]{3,0,2,1:T(8,128)}, ...), condition=%wide.region_7.8_spmd.clone, body=%wide.region_3.7_spmd.clone.sunk | while | flops 3045360384 | bytes 84480736 | solution.py:95
  60.5 3.9 %collective-permute-start = (bf16[384]{0:T(512)(128)(2,1)S(1)}, bf16[384]{0:T(512)(128)(2,1)S(1)}, u32[]{:S(2)}, u32[]{:S(2)}) collective-permute-start(bf16[384]{0:T(512)(128)(2,1)S(1)} %get-tuple-element.651), channel_id=1, source_target_pairs={{0,4},{4,8},{8,12},{12,16},{16,20},{20,24},{24,28},{1,5},{5,9},{9,... | collective-permute-start | bytes 2312 | tf_op jit(solution)/shard_map/while/body/eval_jaxpr/ppermute | solution.py:14
  64.5 3.5 %collective-permute-start.2 = (bf16[384,2,128]{2,0,1:T(8,128)(2,1)}, bf16[384,2,128]{2,0,1:T(8,128)(2,1)S(1)}, u32[]{:S(2)}, u32[]{:S(2)}) collective-permute-start(bf16[384,2,128]{2,0,1:T(8,128)(2,1)} %get-tuple-element.650), channel_id=1, source_target_pairs={{0,4},{4,8},{8,12},{12,16},{16,20},{20,24},{24,28},{1,5},{5,9},{9,... | collective-permute-start | bytes 589832 | tf_op jit(solution)/shard_map/while/body/eval_jaxpr/ppermute | solution.py:14
  68.0 3.4 %collective-permute-start.1 = (bf16[384,2,128]{2,0,1:T(8,128)(2,1)}, bf16[384,2,128]{2,0,1:T(8,128)(2,1)S(1)}, u32[]{:S(2)}, u32[]{:S(2)}) collective-permute-start(bf16[384,2,128]{2,0,1:T(8,128)(2,1)} %get-tuple-element.649), channel_id=1, source_target_pairs={{0,4},{4,8},{8,12},{12,16},{16,20},{20,24},{24,28},{1,5},{5,9},{9,... | collective-permute-start | bytes 589832 | tf_op jit(solution)/shard_map/while/body/eval_jaxpr/ppermute | solution.py:14
  77.5 3.8 %add.135 = f32[384,2,8,128]{3,0,2,1:T(8,128)} add(f32[384,2,8,128]{3,0,2,1:T(8,128)} %get-tuple-element.648, f32[384,2,8,128]{3,0,2,1:T(8,128)S(1)} %get-tuple-element.613) | non-fusion elementwise | flops 786432 | bytes 9437184 | tf_op jit(solution)/shard_map/while/body/eval_jaxpr/add | solution.py:93
  82.7 3.8 %collective-permute-done.4 = f32[384,2,128]{2,0,1:T(8,128)} collective-permute-done((f32[384,2,128]{2,0,1:T(8,128)}, f32[384,2,128]{2,0,1:T(8,128)}, u32[]{:S(2)}, u32[]{:S(2)}) %collective-permute-start.4) | collective-permute-done | bytes 393248 | tf_op jit(solution)/shard_map/while/body/eval_jaxpr/ppermute | solution.py:20
  86.5 1.8 add.137
  88.3 4.7 %collective-permute-done.3 = f32[384,2,128]{2,0,1:T(8,128)} collective-permute-done((f32[384,2,128]{2,0,1:T(8,128)}, f32[384,2,128]{2,0,1:T(8,128)}, u32[]{:S(2)}, u32[]{:S(2)}) %collective-permute-start.3) | collective-permute-done | bytes 393248 | tf_op jit(solution)/shard_map/while/body/eval_jaxpr/ppermute | solution.py:20
  93.0 1.8 add.136
  94.8 6.9 %collective-permute-start = (bf16[384]{0:T(512)(128)(2,1)S(1)}, bf16[384]{0:T(512)(128)(2,1)S(1)}, u32[]{:S(2)}, u32[]{:S(2)}) collective-permute-start(bf16[384]{0:T(512)(128)(2,1)S(1)} %get-tuple-element.651), channel_id=1, source_target_pairs={{0,4},{4,8},{8,12},{12,16},{16,20},{20,24},{24,28},{1,5},{5,9},{9,... | collective-permute-start | bytes 2312 | tf_op jit(solution)/shard_map/while/body/eval_jaxpr/ppermute | solution.py:14
  101.7 4.3 %collective-permute-start.2 = (bf16[384,2,128]{2,0,1:T(8,128)(2,1)}, bf16[384,2,128]{2,0,1:T(8,128)(2,1)S(1)}, u32[]{:S(2)}, u32[]{:S(2)}) collective-permute-start(bf16[384,2,128]{2,0,1:T(8,128)(2,1)} %get-tuple-element.650), channel_id=1, source_target_pairs={{0,4},{4,8},{8,12},{12,16},{16,20},{20,24},{24,28},{1,5},{5,9},{9,... | collective-permute-start | bytes 589832 | tf_op jit(solution)/shard_map/while/body/eval_jaxpr/ppermute | solution.py:14
  105.9 2.6 collective-permute-start.1
  108.7 3.0 %collective-permute-start.3 = (f32[384,2,128]{2,0,1:T(8,128)}, f32[384,2,128]{2,0,1:T(8,128)}, u32[]{:S(2)}, u32[]{:S(2)}) collective-permute-start(f32[384,2,128]{2,0,1:T(8,128)} %get-tuple-element.652), channel_id=1, source_target_pairs={{28,0},{0,4},{4,8},{8,12},{12,16},{16,20},{20,24},{24,28},{29,1},{... | collective-permute-start | bytes 1179656 | tf_op jit(solution)/shard_map/while/body/eval_jaxpr/ppermute | solution.py:20
  113.9 1.8 collective-permute-done.1
  116.1 3.8 %add.135 = f32[384,2,8,128]{3,0,2,1:T(8,128)} add(f32[384,2,8,128]{3,0,2,1:T(8,128)} %get-tuple-element.648, f32[384,2,8,128]{3,0,2,1:T(8,128)S(1)} %get-tuple-element.613) | non-fusion elementwise | flops 786432 | bytes 9437184 | tf_op jit(solution)/shard_map/while/body/eval_jaxpr/add | solution.py:93
  121.3 2.8 %collective-permute-done.4 = f32[384,2,128]{2,0,1:T(8,128)} collective-permute-done((f32[384,2,128]{2,0,1:T(8,128)}, f32[384,2,128]{2,0,1:T(8,128)}, u32[]{:S(2)}, u32[]{:S(2)}) %collective-permute-start.4) | collective-permute-done | bytes 393248 | tf_op jit(solution)/shard_map/while/body/eval_jaxpr/ppermute | solution.py:20
  124.1 1.8 add.137
  125.9 3.7 %collective-permute-done.3 = f32[384,2,128]{2,0,1:T(8,128)} collective-permute-done((f32[384,2,128]{2,0,1:T(8,128)}, f32[384,2,128]{2,0,1:T(8,128)}, u32[]{:S(2)}, u32[]{:S(2)}) %collective-permute-start.3) | collective-permute-done | bytes 393248 | tf_op jit(solution)/shard_map/while/body/eval_jaxpr/ppermute | solution.py:20
  129.7 1.8 add.136
  131.4 4.4 %collective-permute-start = (bf16[384]{0:T(512)(128)(2,1)S(1)}, bf16[384]{0:T(512)(128)(2,1)S(1)}, u32[]{:S(2)}, u32[]{:S(2)}) collective-permute-start(bf16[384]{0:T(512)(128)(2,1)S(1)} %get-tuple-element.651), channel_id=1, source_target_pairs={{0,4},{4,8},{8,12},{12,16},{16,20},{20,24},{24,28},{1,5},{5,9},{9,... | collective-permute-start | bytes 2312 | tf_op jit(solution)/shard_map/while/body/eval_jaxpr/ppermute | solution.py:14
  135.8 7.9 %collective-permute-start.2 = (bf16[384,2,128]{2,0,1:T(8,128)(2,1)}, bf16[384,2,128]{2,0,1:T(8,128)(2,1)S(1)}, u32[]{:S(2)}, u32[]{:S(2)}) collective-permute-start(bf16[384,2,128]{2,0,1:T(8,128)(2,1)} %get-tuple-element.650), channel_id=1, source_target_pairs={{0,4},{4,8},{8,12},{12,16},{16,20},{20,24},{24,28},{1,5},{5,9},{9,... | collective-permute-start | bytes 589832 | tf_op jit(solution)/shard_map/while/body/eval_jaxpr/ppermute | solution.py:14
  143.7 2.5 collective-permute-start.1
  149.4 4.2 %collective-permute-done.1 = bf16[384,2,128]{2,0,1:T(8,128)(2,1)S(1)} collective-permute-done((bf16[384,2,128]{2,0,1:T(8,128)(2,1)}, bf16[384,2,128]{2,0,1:T(8,128)(2,1)S(1)}, u32[]{:S(2)}, u32[]{:S(2)}) %collective-permute-start.1) | collective-permute-done | bytes 196640 | tf_op jit(solution)/shard_map/while/body/eval_jaxpr/ppermute | solution.py:14
  154.0 3.8 %add.135 = f32[384,2,8,128]{3,0,2,1:T(8,128)} add(f32[384,2,8,128]{3,0,2,1:T(8,128)} %get-tuple-element.648, f32[384,2,8,128]{3,0,2,1:T(8,128)S(1)} %get-tuple-element.613) | non-fusion elementwise | flops 786432 | bytes 9437184 | tf_op jit(solution)/shard_map/while/body/eval_jaxpr/add | solution.py:93
  160.2 1.8 add.137
  162.0 2.4 collective-permute-done.3
  164.4 1.8 add.136
  166.2 4.4 %collective-permute-start = (bf16[384]{0:T(512)(128)(2,1)S(1)}, bf16[384]{0:T(512)(128)(2,1)S(1)}, u32[]{:S(2)}, u32[]{:S(2)}) collective-permute-start(bf16[384]{0:T(512)(128)(2,1)S(1)} %get-tuple-element.651), channel_id=1, source_target_pairs={{0,4},{4,8},{8,12},{12,16},{16,20},{20,24},{24,28},{1,5},{5,9},{9,... | collective-permute-start | bytes 2312 | tf_op jit(solution)/shard_map/while/body/eval_jaxpr/ppermute | solution.py:14
  170.6 3.8 %collective-permute-start.2 = (bf16[384,2,128]{2,0,1:T(8,128)(2,1)}, bf16[384,2,128]{2,0,1:T(8,128)(2,1)S(1)}, u32[]{:S(2)}, u32[]{:S(2)}) collective-permute-start(bf16[384,2,128]{2,0,1:T(8,128)(2,1)} %get-tuple-element.650), channel_id=1, source_target_pairs={{0,4},{4,8},{8,12},{12,16},{16,20},{20,24},{24,28},{1,5},{5,9},{9,... | collective-permute-start | bytes 589832 | tf_op jit(solution)/shard_map/while/body/eval_jaxpr/ppermute | solution.py:14
  174.4 8.2 %collective-permute-start.1 = (bf16[384,2,128]{2,0,1:T(8,128)(2,1)}, bf16[384,2,128]{2,0,1:T(8,128)(2,1)S(1)}, u32[]{:S(2)}, u32[]{:S(2)}) collective-permute-start(bf16[384,2,128]{2,0,1:T(8,128)(2,1)} %get-tuple-element.649), channel_id=1, source_target_pairs={{0,4},{4,8},{8,12},{12,16},{16,20},{20,24},{24,28},{1,5},{5,9},{9,... | collective-permute-start | bytes 589832 | tf_op jit(solution)/shard_map/while/body/eval_jaxpr/ppermute | solution.py:14
  185.0 2.6 collective-permute-done.1
  187.9 3.8 %add.135 = f32[384,2,8,128]{3,0,2,1:T(8,128)} add(f32[384,2,8,128]{3,0,2,1:T(8,128)} %get-tuple-element.648, f32[384,2,8,128]{3,0,2,1:T(8,128)S(1)} %get-tuple-element.613) | non-fusion elementwise | flops 786432 | bytes 9437184 | tf_op jit(solution)/shard_map/while/body/eval_jaxpr/add | solution.py:93
  193.1 2.2 collective-permute-done.4
  195.3 1.8 add.137
  197.1 6.6 %collective-permute-done.3 = f32[384,2,128]{2,0,1:T(8,128)} collective-permute-done((f32[384,2,128]{2,0,1:T(8,128)}, f32[384,2,128]{2,0,1:T(8,128)}, u32[]{:S(2)}, u32[]{:S(2)}) %collective-permute-start.3) | collective-permute-done | bytes 393248 | tf_op jit(solution)/shard_map/while/body/eval_jaxpr/ppermute | solution.py:20
  203.7 1.8 add.136
  205.5 10.5 %collective-permute-start.5 = (f32[384,2,128]{2,0,1:T(8,128)}, f32[384,2,128]{2,0,1:T(8,128)}, u32[]{:S(2)}, u32[]{:S(2)}) collective-permute-start(f32[384,2,128]{2,0,1:T(8,128)} %get-tuple-element.410), channel_id=1, source_target_pairs={{16,0},{20,4},{24,8},{28,12},{0,16},{4,20},{8,24},{12,28},{17,1},{... | collective-permute-start | bytes 1179656 | tf_op jit(solution)/shard_map/ppermute | solution.py:20
  217.2 6.8 %collective-permute-done.6 = bf16[384,2,128]{2,0,1:T(8,128)(2,1)S(1)} collective-permute-done((bf16[384,2,128]{2,0,1:T(8,128)(2,1)S(1)}, bf16[384,2,128]{2,0,1:T(8,128)(2,1)S(1)}, u32[]{:S(2)}, u32[]{:S(2)}) %collective-permute-start.6) | collective-permute-done | bytes 196640 | tf_op jit(solution)/shard_map/ppermute | solution.py:20
  225.1 3.4 %all-to-all-start.5 = ((bf16[4,96,256]{2,1,0:T(8,128)(2,1)}), bf16[4,96,256]{2,1,0:T(8,128)(2,1)S(1)}, u32[]{:S(2)}, u32[]{:S(2)}) async-start(bf16[4,96,256]{2,1,0:T(8,128)(2,1)} %all_to_all.95), calls=%async_computation.5 | async-start | bytes 393216 | tf_op jit(solution)/shard_map/all_to_all | solution.py:111
  230.5 3.2 %all-to-all-done.5 = bf16[4,96,256]{2,1,0:T(8,128)(2,1)S(1)} async-done(((bf16[4,96,256]{2,1,0:T(8,128)(2,1)}), bf16[4,96,256]{2,1,0:T(8,128)(2,1)S(1)}, u32[]{:S(2)}, u32[]{:S(2)}) %all-to-all-start.5) | async-done | bytes 196640 | tf_op jit(solution)/shard_map/all_to_all | solution.py:111
  233.8 3.4 %all-to-all-start.4 = ((bf16[4,96,256]{2,1,0:T(8,128)(2,1)}), bf16[4,96,256]{2,1,0:T(8,128)(2,1)S(1)}, u32[]{:S(2)}, u32[]{:S(2)}) async-start(bf16[4,96,256]{2,1,0:T(8,128)(2,1)} %all_to_all.91), calls=%async_computation.4 | async-start | bytes 393216 | tf_op jit(solution)/shard_map/all_to_all | solution.py:110
  238.6 2.1 all_to_all.87
  240.6 1.8 all-to-all-done.4
  242.4 3.6 %all-to-all-start.3 = ((bf16[4,96,2048]{2,1,0:T(8,128)(2,1)}), bf16[4,96,2048]{2,1,0:T(8,128)(2,1)S(1)}, u32[]{:S(2)}, u32[]{:S(2)}) async-start(bf16[4,96,2048]{2,1,0:T(8,128)(2,1)} %all_to_all.87), calls=%async_computation.3 | async-start | bytes 3145728 | tf_op jit(solution)/shard_map/all_to_all | solution.py:109
  247.4 18.7 %all-to-all-done.3 = bf16[4,96,2048]{2,1,0:T(8,128)(2,1)S(1)} async-done(((bf16[4,96,2048]{2,1,0:T(8,128)(2,1)}), bf16[4,96,2048]{2,1,0:T(8,128)(2,1)S(1)}, u32[]{:S(2)}, u32[]{:S(2)}) %all-to-all-start.3) | async-done | bytes 1572896 | tf_op jit(solution)/shard_map/all_to_all | solution.py:109
  (104 shorter events, 39.7 us)
Async XLA Ops:
  0.6 24.4 %copy-start.13 = (s32[384]{0:T(512)S(1)}, s32[384]{0:T(512)}, u32[]{:S(2)}) copy-start(s32[384]{0:T(512)} %param.19) | copy-start | bytes 4612
  0.6 26.6 %copy-start.4 = (bf16[384,2048]{1,0:T(8,128)(2,1)S(1)}, bf16[384,2048]{1,0:T(8,128)(2,1)}, u32[]{:S(2)}) copy-start(bf16[384,2048]{1,0:T(8,128)(2,1)} %param.17) | copy-start | bytes 4718596
  2.4 9.6 %all-to-all-start = ((bf16[96,4,256]{2,0,1:T(8,128)(2,1)}), bf16[96,4,256]{2,0,1:T(8,128)(2,1)S(1)}, u32[]{:S(2)}, u32[]{:S(2)}) async-start(bf16[96,4,256]{2,0,1:T(8,128)(2,1)} %bitcast.126), calls=%async_computation | async-start | bytes 393216 | tf_op jit(solution)/shard_map/all_to_all | solution.py:42
  12.0 14.7 %copy-start.7 = (bf16[96,4,256]{2,0,1:T(8,128)(2,1)}, bf16[96,4,256]{2,0,1:T(8,128)(2,1)S(1)}, u32[]{:S(2)}) copy-start(bf16[96,4,256]{2,0,1:T(8,128)(2,1)S(1)} %all-to-all-done) | copy-start | bytes 589828
  12.0 8.7 %all-to-all-start.2 = ((bf16[96,4,256]{2,0,1:T(8,128)(2,1)}), bf16[96,4,256]{2,0,1:T(8,128)(2,1)S(1)}, u32[]{:S(2)}, u32[]{:S(2)}) async-start(bf16[96,4,256]{2,0,1:T(8,128)(2,1)} %bitcast.125), calls=%async_computation.2 | async-start | bytes 393216 | tf_op jit(solution)/shard_map/all_to_all | solution.py:43
  20.6 6.0 %copy-start.8 = (bf16[96,4,256]{2,0,1:T(8,128)(2,1)}, bf16[96,4,256]{2,0,1:T(8,128)(2,1)S(1)}, u32[]{:S(2)}) copy-start(bf16[96,4,256]{2,0,1:T(8,128)(2,1)S(1)} %all-to-all-done.2) | copy-start | bytes 589828
  20.6 24.5 %all-to-all-start.1 = ((bf16[96,4,2048]{2,0,1:T(8,128)(2,1)}), bf16[96,4,2048]{2,0,1:T(8,128)(2,1)}, u32[]{:S(2)}, u32[]{:S(2)}) async-start(bf16[96,4,2048]{2,0,1:T(8,128)(2,1)} %bitcast.124), calls=%async_computation.1 | async-start | bytes 3145728 | tf_op jit(solution)/shard_map/all_to_all | solution.py:41
  45.1 3.4 %copy-start.11 = (f32[2,8,384]{2,1,0:T(8,128)S(1)}, f32[2,8,384]{2,1,0:T(8,128)}, u32[]{:S(2)}) copy-start(f32[2,8,384]{2,1,0:T(8,128)} %copy.66) | copy-start | bytes 73732
  48.5 1.4 copy-start.10
  48.5 1.4 copy-start.14
  58.6 1.6 copy-start.1
  58.7 1.8 copy-start.6
  58.7 1.9 copy-start.9
  60.5 13.9 %collective-permute-start = (bf16[384]{0:T(512)(128)(2,1)S(1)}, bf16[384]{0:T(512)(128)(2,1)S(1)}, u32[]{:S(2)}, u32[]{:S(2)}) collective-permute-start(bf16[384]{0:T(512)(128)(2,1)S(1)} %get-tuple-element.651), channel_id=1, source_target_pairs={{0,4},{4,8},{8,12},{12,16},{16,20},{20,24},{24,28},{1,5},{5,9},{9,... | collective-permute-start | bytes 2312 | tf_op jit(solution)/shard_map/while/body/eval_jaxpr/ppermute | solution.py:14
  64.5 12.2 %collective-permute-start.2 = (bf16[384,2,128]{2,0,1:T(8,128)(2,1)}, bf16[384,2,128]{2,0,1:T(8,128)(2,1)S(1)}, u32[]{:S(2)}, u32[]{:S(2)}) collective-permute-start(bf16[384,2,128]{2,0,1:T(8,128)(2,1)} %get-tuple-element.650), channel_id=1, source_target_pairs={{0,4},{4,8},{8,12},{12,16},{16,20},{20,24},{24,28},{1,5},{5,9},{9,... | collective-permute-start | bytes 589832 | tf_op jit(solution)/shard_map/while/body/eval_jaxpr/ppermute | solution.py:14
  68.0 9.2 %collective-permute-start.1 = (bf16[384,2,128]{2,0,1:T(8,128)(2,1)}, bf16[384,2,128]{2,0,1:T(8,128)(2,1)S(1)}, u32[]{:S(2)}, u32[]{:S(2)}) collective-permute-start(bf16[384,2,128]{2,0,1:T(8,128)(2,1)} %get-tuple-element.649), channel_id=1, source_target_pairs={{0,4},{4,8},{8,12},{12,16},{16,20},{20,24},{24,28},{1,5},{5,9},{9,... | collective-permute-start | bytes 589832 | tf_op jit(solution)/shard_map/while/body/eval_jaxpr/ppermute | solution.py:14
  71.4 15.1 %collective-permute-start.4 = (f32[384,2,128]{2,0,1:T(8,128)}, f32[384,2,128]{2,0,1:T(8,128)}, u32[]{:S(2)}, u32[]{:S(2)}) collective-permute-start(f32[384,2,128]{2,0,1:T(8,128)} %get-tuple-element.653), channel_id=1, source_target_pairs={{28,0},{0,4},{4,8},{8,12},{12,16},{16,20},{20,24},{24,28},{29,1},{... | collective-permute-start | bytes 1179656 | tf_op jit(solution)/shard_map/while/body/eval_jaxpr/ppermute | solution.py:20
  73.0 20.0 %collective-permute-start.3 = (f32[384,2,128]{2,0,1:T(8,128)}, f32[384,2,128]{2,0,1:T(8,128)}, u32[]{:S(2)}, u32[]{:S(2)}) collective-permute-start(f32[384,2,128]{2,0,1:T(8,128)} %get-tuple-element.652), channel_id=1, source_target_pairs={{28,0},{0,4},{4,8},{8,12},{12,16},{16,20},{20,24},{24,28},{29,1},{... | collective-permute-start | bytes 1179656 | tf_op jit(solution)/shard_map/while/body/eval_jaxpr/ppermute | solution.py:20
  94.8 16.9 %collective-permute-start = (bf16[384]{0:T(512)(128)(2,1)S(1)}, bf16[384]{0:T(512)(128)(2,1)S(1)}, u32[]{:S(2)}, u32[]{:S(2)}) collective-permute-start(bf16[384]{0:T(512)(128)(2,1)S(1)} %get-tuple-element.651), channel_id=1, source_target_pairs={{0,4},{4,8},{8,12},{12,16},{16,20},{20,24},{24,28},{1,5},{5,9},{9,... | collective-permute-start | bytes 2312 | tf_op jit(solution)/shard_map/while/body/eval_jaxpr/ppermute | solution.py:14
  101.7 12.2 %collective-permute-start.2 = (bf16[384,2,128]{2,0,1:T(8,128)(2,1)}, bf16[384,2,128]{2,0,1:T(8,128)(2,1)S(1)}, u32[]{:S(2)}, u32[]{:S(2)}) collective-permute-start(bf16[384,2,128]{2,0,1:T(8,128)(2,1)} %get-tuple-element.650), channel_id=1, source_target_pairs={{0,4},{4,8},{8,12},{12,16},{16,20},{20,24},{24,28},{1,5},{5,9},{9,... | collective-permute-start | bytes 589832 | tf_op jit(solution)/shard_map/while/body/eval_jaxpr/ppermute | solution.py:14
  105.9 9.8 %collective-permute-start.1 = (bf16[384,2,128]{2,0,1:T(8,128)(2,1)}, bf16[384,2,128]{2,0,1:T(8,128)(2,1)S(1)}, u32[]{:S(2)}, u32[]{:S(2)}) collective-permute-start(bf16[384,2,128]{2,0,1:T(8,128)(2,1)} %get-tuple-element.649), channel_id=1, source_target_pairs={{0,4},{4,8},{8,12},{12,16},{16,20},{20,24},{24,28},{1,5},{5,9},{9,... | collective-permute-start | bytes 589832 | tf_op jit(solution)/shard_map/while/body/eval_jaxpr/ppermute | solution.py:14
  108.6 15.5 %collective-permute-start.4 = (f32[384,2,128]{2,0,1:T(8,128)}, f32[384,2,128]{2,0,1:T(8,128)}, u32[]{:S(2)}, u32[]{:S(2)}) collective-permute-start(f32[384,2,128]{2,0,1:T(8,128)} %get-tuple-element.653), channel_id=1, source_target_pairs={{28,0},{0,4},{4,8},{8,12},{12,16},{16,20},{20,24},{24,28},{29,1},{... | collective-permute-start | bytes 1179656 | tf_op jit(solution)/shard_map/while/body/eval_jaxpr/ppermute | solution.py:20
  108.7 21.0 %collective-permute-start.3 = (f32[384,2,128]{2,0,1:T(8,128)}, f32[384,2,128]{2,0,1:T(8,128)}, u32[]{:S(2)}, u32[]{:S(2)}) collective-permute-start(f32[384,2,128]{2,0,1:T(8,128)} %get-tuple-element.652), channel_id=1, source_target_pairs={{28,0},{0,4},{4,8},{8,12},{12,16},{16,20},{20,24},{24,28},{29,1},{... | collective-permute-start | bytes 1179656 | tf_op jit(solution)/shard_map/while/body/eval_jaxpr/ppermute | solution.py:20
  131.4 15.0 %collective-permute-start = (bf16[384]{0:T(512)(128)(2,1)S(1)}, bf16[384]{0:T(512)(128)(2,1)S(1)}, u32[]{:S(2)}, u32[]{:S(2)}) collective-permute-start(bf16[384]{0:T(512)(128)(2,1)S(1)} %get-tuple-element.651), channel_id=1, source_target_pairs={{0,4},{4,8},{8,12},{12,16},{16,20},{20,24},{24,28},{1,5},{5,9},{9,... | collective-permute-start | bytes 2312 | tf_op jit(solution)/shard_map/while/body/eval_jaxpr/ppermute | solution.py:14
  135.8 13.6 %collective-permute-start.2 = (bf16[384,2,128]{2,0,1:T(8,128)(2,1)}, bf16[384,2,128]{2,0,1:T(8,128)(2,1)S(1)}, u32[]{:S(2)}, u32[]{:S(2)}) collective-permute-start(bf16[384,2,128]{2,0,1:T(8,128)(2,1)} %get-tuple-element.650), channel_id=1, source_target_pairs={{0,4},{4,8},{8,12},{12,16},{16,20},{20,24},{24,28},{1,5},{5,9},{9,... | collective-permute-start | bytes 589832 | tf_op jit(solution)/shard_map/while/body/eval_jaxpr/ppermute | solution.py:14
  143.7 9.9 %collective-permute-start.1 = (bf16[384,2,128]{2,0,1:T(8,128)(2,1)}, bf16[384,2,128]{2,0,1:T(8,128)(2,1)S(1)}, u32[]{:S(2)}, u32[]{:S(2)}) collective-permute-start(bf16[384,2,128]{2,0,1:T(8,128)(2,1)} %get-tuple-element.649), channel_id=1, source_target_pairs={{0,4},{4,8},{8,12},{12,16},{16,20},{20,24},{24,28},{1,5},{5,9},{9,... | collective-permute-start | bytes 589832 | tf_op jit(solution)/shard_map/while/body/eval_jaxpr/ppermute | solution.py:14
  146.3 13.9 %collective-permute-start.4 = (f32[384,2,128]{2,0,1:T(8,128)}, f32[384,2,128]{2,0,1:T(8,128)}, u32[]{:S(2)}, u32[]{:S(2)}) collective-permute-start(f32[384,2,128]{2,0,1:T(8,128)} %get-tuple-element.653), channel_id=1, source_target_pairs={{28,0},{0,4},{4,8},{8,12},{12,16},{16,20},{20,24},{24,28},{29,1},{... | collective-permute-start | bytes 1179656 | tf_op jit(solution)/shard_map/while/body/eval_jaxpr/ppermute | solution.py:20
  146.3 18.0 %collective-permute-start.3 = (f32[384,2,128]{2,0,1:T(8,128)}, f32[384,2,128]{2,0,1:T(8,128)}, u32[]{:S(2)}, u32[]{:S(2)}) collective-permute-start(f32[384,2,128]{2,0,1:T(8,128)} %get-tuple-element.652), channel_id=1, source_target_pairs={{28,0},{0,4},{4,8},{8,12},{12,16},{16,20},{20,24},{24,28},{29,1},{... | collective-permute-start | bytes 1179656 | tf_op jit(solution)/shard_map/while/body/eval_jaxpr/ppermute | solution.py:20
  166.2 16.6 %collective-permute-start = (bf16[384]{0:T(512)(128)(2,1)S(1)}, bf16[384]{0:T(512)(128)(2,1)S(1)}, u32[]{:S(2)}, u32[]{:S(2)}) collective-permute-start(bf16[384]{0:T(512)(128)(2,1)S(1)} %get-tuple-element.651), channel_id=1, source_target_pairs={{0,4},{4,8},{8,12},{12,16},{16,20},{20,24},{24,28},{1,5},{5,9},{9,... | collective-permute-start | bytes 2312 | tf_op jit(solution)/shard_map/while/body/eval_jaxpr/ppermute | solution.py:14
  170.6 14.4 %collective-permute-start.2 = (bf16[384,2,128]{2,0,1:T(8,128)(2,1)}, bf16[384,2,128]{2,0,1:T(8,128)(2,1)S(1)}, u32[]{:S(2)}, u32[]{:S(2)}) collective-permute-start(bf16[384,2,128]{2,0,1:T(8,128)(2,1)} %get-tuple-element.650), channel_id=1, source_target_pairs={{0,4},{4,8},{8,12},{12,16},{16,20},{20,24},{24,28},{1,5},{5,9},{9,... | collective-permute-start | bytes 589832 | tf_op jit(solution)/shard_map/while/body/eval_jaxpr/ppermute | solution.py:14
  174.4 13.2 %collective-permute-start.1 = (bf16[384,2,128]{2,0,1:T(8,128)(2,1)}, bf16[384,2,128]{2,0,1:T(8,128)(2,1)S(1)}, u32[]{:S(2)}, u32[]{:S(2)}) collective-permute-start(bf16[384,2,128]{2,0,1:T(8,128)(2,1)} %get-tuple-element.649), channel_id=1, source_target_pairs={{0,4},{4,8},{8,12},{12,16},{16,20},{20,24},{24,28},{1,5},{5,9},{9,... | collective-permute-start | bytes 589832 | tf_op jit(solution)/shard_map/while/body/eval_jaxpr/ppermute | solution.py:14
  182.6 12.7 %collective-permute-start.4 = (f32[384,2,128]{2,0,1:T(8,128)}, f32[384,2,128]{2,0,1:T(8,128)}, u32[]{:S(2)}, u32[]{:S(2)}) collective-permute-start(f32[384,2,128]{2,0,1:T(8,128)} %get-tuple-element.653), channel_id=1, source_target_pairs={{28,0},{0,4},{4,8},{8,12},{12,16},{16,20},{20,24},{24,28},{29,1},{... | collective-permute-start | bytes 1179656 | tf_op jit(solution)/shard_map/while/body/eval_jaxpr/ppermute | solution.py:20
  182.6 21.1 %collective-permute-start.3 = (f32[384,2,128]{2,0,1:T(8,128)}, f32[384,2,128]{2,0,1:T(8,128)}, u32[]{:S(2)}, u32[]{:S(2)}) collective-permute-start(f32[384,2,128]{2,0,1:T(8,128)} %get-tuple-element.652), channel_id=1, source_target_pairs={{28,0},{0,4},{4,8},{8,12},{12,16},{16,20},{20,24},{24,28},{29,1},{... | collective-permute-start | bytes 1179656 | tf_op jit(solution)/shard_map/while/body/eval_jaxpr/ppermute | solution.py:20
  205.5 31.6 %copy-start.2 = (f32[384,2,8,128]{3,0,2,1:T(8,128)S(1)}, f32[384,2,8,128]{3,0,2,1:T(8,128)}, u32[]{:S(2)}) copy-start(f32[384,2,8,128]{3,0,2,1:T(8,128)} %get-tuple-element.409) | copy-start | bytes 9437188
  205.5 22.9 %collective-permute-start.5 = (f32[384,2,128]{2,0,1:T(8,128)}, f32[384,2,128]{2,0,1:T(8,128)}, u32[]{:S(2)}, u32[]{:S(2)}) collective-permute-start(f32[384,2,128]{2,0,1:T(8,128)} %get-tuple-element.410), channel_id=1, source_target_pairs={{16,0},{20,4},{24,8},{28,12},{0,16},{4,20},{8,24},{12,28},{17,1},{... | collective-permute-start | bytes 1179656 | tf_op jit(solution)/shard_map/ppermute | solution.py:20
  217.0 7.0 %collective-permute-start.6 = (bf16[384,2,128]{2,0,1:T(8,128)(2,1)S(1)}, bf16[384,2,128]{2,0,1:T(8,128)(2,1)S(1)}, u32[]{:S(2)}, u32[]{:S(2)}) collective-permute-start(bf16[384,2,128]{2,0,1:T(8,128)(2,1)S(1)} %convert.8), channel_id=1, source_target_pairs={{16,0},{20,4},{24,8},{28,12},{0,16},{4,20},{8,24},{12,28},{17,1},{... | collective-permute-start | bytes 589832 | tf_op jit(solution)/shard_map/ppermute | solution.py:20
  225.1 8.7 %all-to-all-start.5 = ((bf16[4,96,256]{2,1,0:T(8,128)(2,1)}), bf16[4,96,256]{2,1,0:T(8,128)(2,1)S(1)}, u32[]{:S(2)}, u32[]{:S(2)}) async-start(bf16[4,96,256]{2,1,0:T(8,128)(2,1)} %all_to_all.95), calls=%async_computation.5 | async-start | bytes 393216 | tf_op jit(solution)/shard_map/all_to_all | solution.py:111
  233.8 8.7 %all-to-all-start.4 = ((bf16[4,96,256]{2,1,0:T(8,128)(2,1)}), bf16[4,96,256]{2,1,0:T(8,128)(2,1)S(1)}, u32[]{:S(2)}, u32[]{:S(2)}) async-start(bf16[4,96,256]{2,1,0:T(8,128)(2,1)} %all_to_all.91), calls=%async_computation.4 | async-start | bytes 393216 | tf_op jit(solution)/shard_map/all_to_all | solution.py:110
  242.4 23.6 %all-to-all-start.3 = ((bf16[4,96,2048]{2,1,0:T(8,128)(2,1)}), bf16[4,96,2048]{2,1,0:T(8,128)(2,1)S(1)}, u32[]{:S(2)}, u32[]{:S(2)}) async-start(bf16[4,96,2048]{2,1,0:T(8,128)(2,1)} %all_to_all.87), calls=%async_computation.3 | async-start | bytes 3145728 | tf_op jit(solution)/shard_map/all_to_all | solution.py:109
where the time goes:
time: 269 us; the launch traced here: 267 us
  starting transfers between devices  95.2 us (35%)
  waiting for transfers between devices  78.2 us (29%)
  other arithmetic  42.8 us (16%)
  local copies, waits for them, and re-layouts  36.6 us (14%)
  matrix products  9.83 us (4%)
  loops' own time  3.25 us (1%)
    ppermute x12, starting transfers between devices, passed_along(): return lax.ppermute(block, axis, route)  55.8 us
    ppermute x10, waiting for transfers between devices, shifted(): return lax.ppermute(block, axis, route)  34.2 us
    all_to_all x1, waiting for transfers between devices, per_device(): lax.all_to_all(q_done, 'head', split_axis=0, concat_axis=1, tiled=True)  18.7 us
    ppermute x10, starting transfers between devices, shifted(): return lax.ppermute(block, axis, route)  17.1 us
    add x4, other arithmetic, visit_block(): return (dq_acc + q_part, key_part, value_part, tag_part, k_store, v_store)  15.4 us
    unnamed x27, local copies, waits for them, and re-layouts  13.2 us
    ppermute x12, waiting for transfers between devices, passed_along(): return lax.ppermute(block, axis, route)  9.85 us
    add x4, other arithmetic, visit_block(): v_store = v_store + v_part  7.14 us
  transfers between devices with their start and end apart: 28, of which 20 were waited for; matrix products, arithmetic and copies ran while one was open for 23% of the time, Pallas kernels for 0%

commit v1 on v0

v1 whole, which is shorter than its diff:
```python
import math

import jax
import jax.numpy as jnp
from jax import lax
from jax.experimental import pallas as pl
from jax.experimental.pallas import tpu as pltpu
from jax.sharding import PartitionSpec as P

DH = 128
SCORE_SCALE = 1.0 / math.sqrt(DH)
LOG2E = math.log2(math.e)
NT = (((1,), (1,)), ((), ()))
NN = (((1,), (0,)), ((), ()))
TN = (((0,), (0,)), ((), ()))


def dot(a, b, dims):
    return lax.dot_general(a, b, dims, preferred_element_type=jnp.float32)


def delta_kernel(grad_ref, out_ref, delta_ref):
    heads = delta_ref.shape[0]
    for head in range(heads):
        cols = slice(head * DH, (head + 1) * DH)
        prod = grad_ref[:, cols].astype(jnp.float32) * out_ref[:, cols].astype(jnp.float32)
        delta_ref[head : head + 1, :] = jnp.sum(jnp.transpose(prod), axis=0, keepdims=True)


def row_deltas(out_grad, attn_out, heads):
    rows = out_grad.shape[0]
    return pl.pallas_call(
        delta_kernel,
        out_shape=jax.ShapeDtypeStruct((heads, rows), jnp.float32),
        compiler_params=pltpu.CompilerParams(vmem_limit_bytes=32 << 20),
        cost_estimate=pl.CostEstimate(
            flops=4 * rows * heads * DH, bytes_accessed=4 * rows * heads * DH, transcendentals=0
        ),
        name="row_deltas",
    )(out_grad, attn_out)


def grads_kernel(half, kv_heads, group, info_ref, *refs):
    start_ref, q_ref, g_ref, lse_ref, delta_ref, kv_own = refs[:6]
    kv_in = refs[6 : 6 + half - 1]
    dq_ref, dkv_own = refs[5 + half : 7 + half]
    dkv_out = refs[7 + half : 6 + 2 * half]
    kv_buf, dkv_buf, dq_acc, dk_acc, dv_acc, bias, in_sem, out_sem = refs[6 + 2 * half :]
    rows = q_ref.shape[0]
    own = info_ref[0]
    first_start = info_ref[1]
    last_start = info_ref[2]
    base = info_ref[3]

    for step in range(1, half):
        @pl.when((own ^ step) < own)
        def _():
            pltpu.make_async_copy(kv_in[step - 1], kv_buf.at[step - 1], in_sem.at[step - 1]).start()

    def tile(load_kv, masked, first, store):
        def per_kv_head(kv_head, _):
            k_cols = pl.ds(pl.multiple_of(kv_head * DH, DH), DH)
            v_cols = pl.ds(pl.multiple_of((kv_heads + kv_head) * DH, DH), DH)
            key = load_kv(k_cols)
            value = load_kv(v_cols)
            for member in range(group):
                head = kv_head * group + member
                cols = pl.ds(pl.multiple_of(head * DH, DH), DH)
                query = q_ref[:, cols]
                grad = g_ref[:, cols]
                scores = dot(key, query, NT) * (SCORE_SCALE * LOG2E) - lse_ref[pl.ds(head, 1), :]
                if masked:
                    scores = scores + bias[...]
                probs = jnp.exp2(scores)
                dprobs = dot(value, grad, NT)
                dscores = (probs * (dprobs - delta_ref[pl.ds(head, 1), :])).astype(jnp.bfloat16)
                dv_part = dot(probs.astype(jnp.bfloat16), grad, NN)
                dk_part = dot(dscores, query, NN)
                dq_part = dot(dscores, key, TN)
                if member == 0:
                    dv_acc[...] = dv_part
                    dk_acc[...] = dk_part
                else:
                    dv_acc[...] += dv_part
                    dk_acc[...] += dk_part
                if first:
                    dq_acc[:, cols] = dq_part
                else:
                    dq_acc[:, cols] += dq_part
            store(k_cols, dk_acc[...] * SCORE_SCALE)
            store(v_cols, dv_acc[...])
            return 0

        lax.fori_loop(0, kv_heads, per_kv_head, 0)

    def set_bias(block):
        key_pos = (base + block) * rows + lax.broadcasted_iota(jnp.int32, (rows, rows), 0)
        query_pos = (base + own) * rows + lax.broadcasted_iota(jnp.int32, (rows, rows), 1)
        allowed = (key_pos >= start_ref[...]) & (key_pos <= query_pos)
        bias[...] = jnp.where(allowed, 0.0, -1e30)

    def store_own(cols, value):
        dkv_own[:, cols] = value

    set_bias(own)
    tile(lambda cols: kv_own[:, cols], True, True, store_own)

    def visit(step, _):
        block = own ^ step

        @pl.when(block < own)
        def _():
            slot = step - 1
            pltpu.make_async_copy(kv_buf.at[slot], kv_buf.at[slot], in_sem.at[slot]).wait()
            end = (base + block + 1) * rows
            needed = first_start < end
            full = last_start <= (base + block) * rows

            def store(cols, value):
                dkv_buf[slot, :, cols] = value.astype(dkv_buf.dtype)

            def load(cols):
                return kv_buf[slot, :, cols]

            @pl.when(full)
            def _():
                tile(load, False, False, store)

            @pl.when(needed & jnp.logical_not(full))
            def _():
                set_bias(block)
                tile(load, True, False, store)

            @pl.when(jnp.logical_not(needed))
            def _():
                dkv_buf[slot] = jnp.zeros(dkv_buf.shape[1:], dkv_buf.dtype)

        return 0

    lax.fori_loop(1, half, visit, 0)
    for step in range(1, half):
        @pl.when((own ^ step) < own)
        def _():
            pltpu.make_async_copy(dkv_buf.at[step - 1], dkv_out[step - 1], out_sem.at[step - 1]).start()
    dq_ref[...] = (dq_acc[...] * SCORE_SCALE).astype(dq_ref.dtype)
    for step in range(1, half):
        @pl.when((own ^ step) < own)
        def _():
            pltpu.make_async_copy(dkv_buf.at[step - 1], dkv_out[step - 1], out_sem.at[step - 1]).wait()


def attention_grads(info, start, q_rows, out_grad, lse2, delta, kv_own, kv_in, kv_heads):
    half = len(kv_in) + 1
    rows, width = q_rows.shape
    group = width // (DH * kv_heads)
    any_spec = pl.BlockSpec(memory_space=pl.ANY)
    vmem_spec = pl.BlockSpec(memory_space=pltpu.VMEM)
    kv_shape = kv_own.shape

    def kernel(info_ref, *refs):
        grads_kernel(half, kv_heads, group, info_ref, *refs)

    tiles = half
    return pl.pallas_call(
        kernel,
        out_shape=[
            jax.ShapeDtypeStruct((rows, width), jnp.bfloat16),
            jax.ShapeDtypeStruct(kv_shape, jnp.float32),
        ]
        + [jax.ShapeDtypeStruct(kv_shape, jnp.bfloat16)] * (half - 1),
        in_specs=[pl.BlockSpec(memory_space=pltpu.SMEM)] + [vmem_spec] * 6 + [any_spec] * (half - 1),
        out_specs=[vmem_spec] * 2 + [any_spec] * (half - 1),
        scratch_shapes=[
            pltpu.VMEM((half - 1,) + kv_shape, jnp.bfloat16),
            pltpu.VMEM((half - 1,) + kv_shape, jnp.bfloat16),
            pltpu.VMEM((rows, width), jnp.float32),
            pltpu.VMEM((rows, DH), jnp.float32),
            pltpu.VMEM((rows, DH), jnp.float32),
            pltpu.VMEM((rows, rows), jnp.float32),
            pltpu.SemaphoreType.DMA((half - 1,)),
            pltpu.SemaphoreType.DMA((half - 1,)),
        ],
        compiler_params=pltpu.CompilerParams(vmem_limit_bytes=56 << 20),
        cost_estimate=pl.CostEstimate(
            flops=10 * rows * rows * width * tiles,
            bytes_accessed=8 * rows * width + 8 * tiles * rows * kv_shape[1],
            transcendentals=rows * rows * (width // DH) * tiles,
        ),
        name="attention_grads",
    )(info, start, q_rows, out_grad, lse2, delta, kv_own, *kv_in)


def per_device(queries, keys, values, attn_out, out_grad, log_sum, file_ids):
    ctx_count = lax.axis_size("ctx")
    head_count = lax.axis_size("head")
    half = ctx_count // 2
    index = lax.axis_index("ctx")
    own = index % half
    base = index - own
    part_rows = queries.shape[0]
    rows = out_grad.shape[0]
    heads = log_sum.shape[0]
    kv_width = keys.shape[1] // head_count
    kv_heads = kv_width // DH

    def to_heads(x):
        return lax.all_to_all(x, "head", split_axis=0, concat_axis=0, tiled=True)

    def by_head(x):
        return x.reshape(part_rows, head_count, -1).transpose(1, 0, 2)

    all_ids = lax.all_gather(file_ids, "ctx", axis=0, tiled=True)
    kv_send = jnp.concatenate([by_head(keys), by_head(values)], axis=2)
    kv_own = to_heads(kv_send.reshape(rows, 2 * kv_width))
    q_rows = to_heads(by_head(queries).reshape(rows, heads * DH))
    delta = row_deltas(out_grad, attn_out, heads)

    def forward_route(step):
        pairs = []
        for i in range(ctx_count):
            j = (i // half) * half + ((i % half) ^ step)
            if i < j:
                pairs.append((i, j))
        return pairs

    kv_in = [lax.ppermute(kv_own, "ctx", forward_route(step)) for step in range(1, half)]
    start = jnp.sum(
        (all_ids[None, :] < file_ids[:, None]).astype(jnp.int32), axis=1, dtype=jnp.int32
    )
    info = jnp.stack([own, start[0], start[-1], base]).astype(jnp.int32)
    dq, dkv_own, *dkv_parts = attention_grads(
        info, start[None, :], q_rows, out_grad, log_sum * LOG2E, delta, kv_own, kv_in, kv_heads
    )
    q_back = lax.all_to_all(dq, "head", split_axis=0, concat_axis=0, tiled=True)
    dkv = dkv_own
    for step in range(1, half):
        back = [(j, i) for i, j in forward_route(step)]
        dkv = dkv + lax.ppermute(dkv_parts[step - 1], "ctx", back).astype(jnp.float32)
    kv_back = to_heads(dkv.astype(jnp.bfloat16)).reshape(head_count, part_rows, 2, kv_width)

    def joined(x):
        return x.transpose(1, 0, 2).reshape(part_rows, -1)

    q_grad = joined(q_back.reshape(head_count, part_rows, -1))
    return (q_grad, joined(kv_back[:, :, 0]), joined(kv_back[:, :, 1]))


def solution(mesh):
    return jax.shard_map(
        per_device,
        mesh=mesh,
        in_specs=(
            P(("ctx", "head"), None),
            P(("ctx", "head"), None),
            P(("ctx", "head"), None),
            P("ctx", "head"),
            P("ctx", "head"),
            P("head", "ctx"),
            P("ctx"),
        ),
        out_specs=(P(("ctx", "head"), None), P(("ctx", "head"), None), P(("ctx", "head"), None)),
        check_vma=False,
    )
```

time: 269 us -> 152 us (0.57)
  starting transfers between devices: 95.2 us -> 25.4 us
  other arithmetic: 42.8 us -> 5.12 us
  blocking collectives: 0 us -> 36.8 us
  local copies, waits for them, and re-layouts: 36.6 us -> 8.01 us
  waiting for transfers between devices: 78.2 us -> 64.1 us
  Pallas kernels: 0 us -> 11.4 us
  matrix products: 9.83 us -> 0 us
  loops' own time: 3.25 us -> 0 us
    ppermute x22 -> x6, starting transfers between devices: 72.9 us -> 12.9 us  [the longest x3 9.07 us: per_device(): lax.ppermute(kv_own, 'ctx', forward_route(step))]
    add x21 -> x0, other arithmetic: 29.7 us -> none  [the longest x4 15.4 us: visit_block(): return (dq_acc + q_part, key_part, value_part, tag_part, k_store, v_store)]
    all_gather x0 -> x1, blocking collectives: none -> 26.9 us  [per_device(): all_ids = lax.all_gather(file_ids, 'ctx', axis=0, tiled=True)]
    all_to_all x9 -> x0, local copies, waits for them, and re-layouts: 12.4 us -> none  [the longest x2 3.3 us: per_device(): lax.all_to_all(q_done, 'head', split_axis=0, concat_axis=1, tiled=True)]
    pallas_call x0 -> x2, Pallas kernels: none -> 11.4 us  [the longest x1 10.5 us: attention_grads(): pl.pallas_call(kernel, out_shape=[jax.ShapeDtypeStruct((rows, width), jnp...]
    unnamed x27 -> x19, local copies, waits for them, and re-layouts: 13.2 us -> 2.55 us
    all_to_all x6 -> x3, waiting for transfers between devices: 34.1 us -> 23.7 us  [the longest x1 17.5 us: per_device(): q_back = lax.all_to_all(dq, 'head', split_axis=0, concat_axis=0, tiled=True)]
    all_to_all x0 -> x1, blocking collectives: none -> 9.86 us  [to_heads(): return lax.all_to_all(x, 'head', split_axis=0, concat_axis=0, tiled=True)]
  transfers between devices with their start and end apart: 28 -> 9, of which waited for: 20 -> 6; matrix products, arithmetic and copies ran while one was open for 23% -> 5% of each run, Pallas kernels for 0% -> 1%
where the time goes in v1:
time: 152 us
  waiting for transfers between devices  64.1 us (42%)
  blocking collectives  36.8 us (24%)
  starting transfers between devices  25.4 us (17%)
  Pallas kernels  11.4 us (8%)
  local copies, waits for them, and re-layouts  8.01 us (5%)
  other arithmetic  5.12 us (3%)
    ppermute x3, waiting for transfers between devices, per_device(): lax.ppermute(dkv_parts[step - 1], 'ctx', back).astype(jnp.float32)  38.8 us
    all_gather x1, blocking collectives, per_device(): all_ids = lax.all_gather(file_ids, 'ctx', axis=0, tiled=True)  26.9 us
    all_to_all x1, waiting for transfers between devices, per_device(): q_back = lax.all_to_all(dq, 'head', split_axis=0, concat_axis=0, tiled=True)  17.5 us
    pallas_call x1, Pallas kernels, attention_grads(): pl.pallas_call(kernel, out_shape=[jax.ShapeDtypeStruct((rows, width), jnp...  10.5 us
    all_to_all x1, blocking collectives, to_heads(): return lax.all_to_all(x, 'head', split_axis=0, concat_axis=0, tiled=True)  9.86 us
    ppermute x3, starting transfers between devices, per_device(): lax.ppermute(kv_own, 'ctx', forward_route(step))  9.07 us
    all_to_all x2, starting transfers between devices, to_heads(): return lax.all_to_all(x, 'head', split_axis=0, concat_axis=0, tiled=True)  8.85 us
    all_to_all x2, waiting for transfers between devices, to_heads(): return lax.all_to_all(x, 'head', split_axis=0, concat_axis=0, tiled=True)  6.2 us
  transfers between devices with their start and end apart: 9, of which 6 were waited for; matrix products, arithmetic and copies ran while one was open for 5% of the time, Pallas kernels for 1%

profile of v1, /device:TPU:0, one launch (start us, length us, event | category | flops | bytes accessed | tf_op | source)
XLA Modules:
  0.0 151.6 jit_solution(15251310382524716272)
XLA Ops:
  0.6 0.0 copy-start.3
  0.6 1.2 bitcast_bitcast_fusion.1
  1.8 0.8 pad_maximum_fusion
  2.6 4.2 %all-to-all-start.1 = ((bf16[4,96,512]{2,1,0:T(8,128)(2,1)}), bf16[4,96,512]{2,1,0:T(8,128)(2,1)S(1)}, u32[]{:S(2)}, u32[]{:S(2)}) async-start(bf16[4,96,512]{2,1,0:T(8,128)(2,1)} %pad_maximum_fusion), calls=%async_computation.1 | async-start | bytes 786432 | tf_op jit(solution)/shard_map/all_to_all | solution.py:207
  6.8 0.0 copy-done.3
  6.8 0.0 copy-start.6
  6.8 1.2 copy.39
  8.1 6.2 %all-to-all-done.1 = bf16[4,96,512]{2,1,0:T(8,128)(2,1)S(1)} async-done(((bf16[4,96,512]{2,1,0:T(8,128)(2,1)}), bf16[4,96,512]{2,1,0:T(8,128)(2,1)S(1)}, u32[]{:S(2)}, u32[]{:S(2)}) %all-to-all-start.1) | async-done | bytes 393248 | tf_op jit(solution)/shard_map/all_to_all | solution.py:207
  14.3 0.0 copy-start.4
  14.3 0.0 copy-start
  14.3 0.0 copy-start.1
  14.3 4.6 %all-to-all-start = ((bf16[4,96,2048]{2,1,0:T(8,128)(2,1)}), bf16[4,96,2048]{2,1,0:T(8,128)(2,1)}, u32[]{:S(2)}, u32[]{:S(2)}) async-start(bf16[4,96,2048]{2,1,0:T(8,128)(2,1)} %bitcast.37), calls=%async_computation | async-start | bytes 3145728 | tf_op jit(solution)/shard_map/all_to_all | solution.py:207
  18.9 0.0 copy-done.6
  18.9 26.9 %all-gather = s32[8,1,384]{2,1,0:T(1,128)S(1)} all-gather(s32[1,1,384]{2,1,0:T(1,128)S(1)} %reshape.51), channel_id=1, replica_groups=mesh['ctx'=8,'head'=4] {'ctx'}, dimensions={0}, use_global_device_ids=true | all-gather | bytes 13824 | tf_op jit(solution)/shard_map/all_gather | solution.py:212
  45.8 0.6 convert_reduce_fusion
  46.4 3.8 %collective-permute-start.2 = (bf16[384,512]{1,0:T(8,128)(2,1)S(1)}, bf16[384,512]{1,0:T(8,128)(2,1)}, u32[]{:S(2)}, u32[]{:S(2)}) collective-permute-start(bf16[384,512]{1,0:T(8,128)(2,1)S(1)} %bitcast.44), channel_id=1, source_target_pairs={{0,12},{4,8},{16,28},{20,24},{1,13},{5,9},{17,29},{21,25},{2,14},{... | collective-permute-start | bytes 1179656 | tf_op jit(solution)/shard_map/ppermute | solution.py:226
  50.3 2.1 %collective-permute-start.1 = (bf16[384,512]{1,0:T(8,128)(2,1)S(1)}, bf16[384,512]{1,0:T(8,128)(2,1)}, u32[]{:S(2)}, u32[]{:S(2)}) collective-permute-start(bf16[384,512]{1,0:T(8,128)(2,1)S(1)} %bitcast.45), channel_id=1, source_target_pairs={{0,8},{4,12},{16,24},{20,28},{1,9},{5,13},{17,25},{21,29},{2,10},{... | collective-permute-start | bytes 1179656 | tf_op jit(solution)/shard_map/ppermute | solution.py:226
  52.3 0.0 copy-done.4
  52.3 3.2 %collective-permute-start = (bf16[384,512]{1,0:T(8,128)(2,1)S(1)}, bf16[384,512]{1,0:T(8,128)(2,1)}, u32[]{:S(2)}, u32[]{:S(2)}) collective-permute-start(bf16[384,512]{1,0:T(8,128)(2,1)S(1)} %bitcast.46), channel_id=1, source_target_pairs={{0,4},{8,12},{16,20},{24,28},{1,5},{9,13},{17,21},{25,29},{2,6},{1... | collective-permute-start | bytes 1179656 | tf_op jit(solution)/shard_map/ppermute | solution.py:226
  55.5 0.6 fusion.1
  56.1 0.6 broadcast_in_dim.2.refs_0_
  56.7 0.0 copy-done
  56.7 0.0 copy-done.1
  56.7 0.0 copy-start.5
  56.7 0.9 row_deltas.1.refs_4_
  57.6 0.0 copy-start.2
  57.6 0.6 copy-done.2
  58.2 1.8 %pad_add_fusion.info_ref = s32[4]{0:T(128)} fusion(s32[1]{0:T(128)} %bitcast.2, s32[1]{0:T(128)} %get-tuple-element.16, s32[1]{0:T(128)} %get-tuple-element.15, s32[1]{0:T(128)} %bitcast), kind=kLoop, calls=%fused_computation.7 | loop fusion | flops 12 | bytes 32 | tf_op jit(solution)/shard_map/stack | solution.py:230
  59.9 0.0 copy-done.5
  60.0 0.6 broadcast_multiply_fusion.refs_3_
  60.6 0.0 collective-permute-done.2.refs_8_
  60.6 1.6 %collective-permute-done.1.refs_7_ = bf16[384,512]{1,0:T(8,128)(2,1)} collective-permute-done((bf16[384,512]{1,0:T(8,128)(2,1)S(1)}, bf16[384,512]{1,0:T(8,128)(2,1)}, u32[]{:S(2)}, u32[]{:S(2)}) %collective-permute-start.1) | collective-permute-done | bytes 393248 | tf_op jit(solution)/shard_map/ppermute | solution.py:226
  62.2 0.0 collective-permute-done.refs_6_
  62.2 0.0 all-to-all-done
  62.2 10.5 %attention_grads.1 = (bf16[384,2048]{1,0:T(8,128)(2,1)}, f32[384,512]{1,0:T(8,128)}, bf16[384,512]{1,0:T(8,128)(2,1)}, bf16[384,512]{1,0:T(8,128)(2,1)}, bf16[384,512]{1,0:T(8,128)(2,1)}) custom-call(s32[4]{0:T(128)} %pad_add_fusion.info_ref, s32[1,384]{1,0:T(1,128)} %broadcast_in_dim.2.refs_0_, bf16[384,2048]{1,0:T(8,128)(2,1)} %bitcast.4.refs_1_, ...), custom_call_target="tpu_custom_call" | custom-call | flops 12079595520 | bytes 12582912 | tf_op jit(solution)/shard_map/attention_grads/pallas_call | solution.py:164
  72.8 1.3 collective-permute-start.3
  74.1 1.3 collective-permute-start.4
  75.4 1.3 collective-permute-start.5
  76.7 11.0 %collective-permute-done.3 = bf16[384,512]{1,0:T(8,128)(2,1)S(1)} collective-permute-done((bf16[384,512]{1,0:T(8,128)(2,1)}, bf16[384,512]{1,0:T(8,128)(2,1)S(1)}, u32[]{:S(2)}, u32[]{:S(2)}) %collective-permute-start.3) | collective-permute-done | bytes 393248 | tf_op jit(solution)/shard_map/ppermute | solution.py:238
  87.6 14.5 %collective-permute-done.4 = bf16[384,512]{1,0:T(8,128)(2,1)S(1)} collective-permute-done((bf16[384,512]{1,0:T(8,128)(2,1)}, bf16[384,512]{1,0:T(8,128)(2,1)S(1)}, u32[]{:S(2)}, u32[]{:S(2)}) %collective-permute-start.4) | collective-permute-done | bytes 393248 | tf_op jit(solution)/shard_map/ppermute | solution.py:238
  102.1 13.3 %collective-permute-done.5 = bf16[384,512]{1,0:T(8,128)(2,1)S(1)} collective-permute-done((bf16[384,512]{1,0:T(8,128)(2,1)}, bf16[384,512]{1,0:T(8,128)(2,1)S(1)}, u32[]{:S(2)}, u32[]{:S(2)}) %collective-permute-start.5) | collective-permute-done | bytes 393248 | tf_op jit(solution)/shard_map/ppermute | solution.py:238
  115.5 1.3 add_convert_fusion
  116.8 9.9 %all_to_all.34 = bf16[4,96,512]{2,1,0:T(8,128)(2,1)S(1)} all-to-all(bf16[4,96,512]{2,1,0:T(8,128)(2,1)S(1)} %bitcast.41), channel_id=1, replica_groups=mesh['ctx'=8,'head'=4] {'head'}, dimensions={0} | all-to-all | bytes 786432 | tf_op jit(solution)/shard_map/all_to_all | solution.py:207
  126.7 3.6 %all-to-all-start.2 = ((bf16[4,96,2048]{2,1,0:T(8,128)(2,1)}), bf16[4,96,2048]{2,1,0:T(8,128)(2,1)S(1)}, u32[]{:S(2)}, u32[]{:S(2)}) async-start(bf16[4,96,2048]{2,1,0:T(8,128)(2,1)} %bitcast.8), calls=%async_computation.2 | async-start | bytes 3145728 | tf_op jit(solution)/shard_map/all_to_all | solution.py:234
  130.3 0.1 reshape.48
  130.4 0.5 fusion
  130.9 0.3 copy.29
  131.2 0.7 copy.35
  131.9 0.3 copy.28
  132.1 0.7 copy.34
  132.9 17.5 %all-to-all-done.2 = bf16[4,96,2048]{2,1,0:T(8,128)(2,1)S(1)} async-done(((bf16[4,96,2048]{2,1,0:T(8,128)(2,1)}), bf16[4,96,2048]{2,1,0:T(8,128)(2,1)S(1)}, u32[]{:S(2)}, u32[]{:S(2)}) %all-to-all-start.2) | async-done | bytes 1572896 | tf_op jit(solution)/shard_map/all_to_all | solution.py:234
  150.3 1.2 copy.33
  (1 shorter events, 0.0 us)
Async XLA Ops:
  0.6 6.2 %copy-start.3 = (bf16[96,8192]{1,0:T(8,128)(2,1)S(1)}, bf16[96,8192]{1,0:T(8,128)(2,1)}, u32[]{:S(2)}) copy-start(bf16[96,8192]{1,0:T(8,128)(2,1)} %param.7) | copy-start | bytes 4718596
  2.6 11.7 %all-to-all-start.1 = ((bf16[4,96,512]{2,1,0:T(8,128)(2,1)}), bf16[4,96,512]{2,1,0:T(8,128)(2,1)S(1)}, u32[]{:S(2)}, u32[]{:S(2)}) async-start(bf16[4,96,512]{2,1,0:T(8,128)(2,1)} %pad_maximum_fusion), calls=%async_computation.1 | async-start | bytes 786432 | tf_op jit(solution)/shard_map/all_to_all | solution.py:207
  6.8 12.1 %copy-start.6 = (s32[384]{0:T(512)S(1)}, s32[384]{0:T(512)}, u32[]{:S(2)}) copy-start(s32[384]{0:T(512)} %param.13) | copy-start | bytes 4612
  14.3 38.0 %copy-start.4 = (bf16[4,96,512]{2,1,0:T(8,128)(2,1)}, bf16[4,96,512]{2,1,0:T(8,128)(2,1)S(1)}, u32[]{:S(2)}) copy-start(bf16[4,96,512]{2,1,0:T(8,128)(2,1)S(1)} %all-to-all-done.1) | copy-start | bytes 1179652
  14.3 42.4 %copy-start = (bf16[384,2048]{1,0:T(8,128)(2,1)S(1)}, bf16[384,2048]{1,0:T(8,128)(2,1)}, u32[]{:S(2)}) copy-start(bf16[384,2048]{1,0:T(8,128)(2,1)} %out_ref.1) | copy-start | bytes 4718596
  14.3 42.4 %copy-start.1 = (bf16[384,2048]{1,0:T(8,128)(2,1)S(1)}, bf16[384,2048]{1,0:T(8,128)(2,1)}, u32[]{:S(2)}) copy-start(bf16[384,2048]{1,0:T(8,128)(2,1)} %refs_2_.1) | copy-start | bytes 4718596
  14.3 47.9 %all-to-all-start = ((bf16[4,96,2048]{2,1,0:T(8,128)(2,1)}), bf16[4,96,2048]{2,1,0:T(8,128)(2,1)}, u32[]{:S(2)}, u32[]{:S(2)}) async-start(bf16[4,96,2048]{2,1,0:T(8,128)(2,1)} %bitcast.37), calls=%async_computation | async-start | bytes 3145728 | tf_op jit(solution)/shard_map/all_to_all | solution.py:207
  46.4 14.1 %collective-permute-start.2 = (bf16[384,512]{1,0:T(8,128)(2,1)S(1)}, bf16[384,512]{1,0:T(8,128)(2,1)}, u32[]{:S(2)}, u32[]{:S(2)}) collective-permute-start(bf16[384,512]{1,0:T(8,128)(2,1)S(1)} %bitcast.44), channel_id=1, source_target_pairs={{0,12},{4,8},{16,28},{20,24},{1,13},{5,9},{17,29},{21,25},{2,14},{... | collective-permute-start | bytes 1179656 | tf_op jit(solution)/shard_map/ppermute | solution.py:226
  50.3 11.9 %collective-permute-start.1 = (bf16[384,512]{1,0:T(8,128)(2,1)S(1)}, bf16[384,512]{1,0:T(8,128)(2,1)}, u32[]{:S(2)}, u32[]{:S(2)}) collective-permute-start(bf16[384,512]{1,0:T(8,128)(2,1)S(1)} %bitcast.45), channel_id=1, source_target_pairs={{0,8},{4,12},{16,24},{20,28},{1,9},{5,13},{17,25},{21,29},{2,10},{... | collective-permute-start | bytes 1179656 | tf_op jit(solution)/shard_map/ppermute | solution.py:226
  52.3 9.9 %collective-permute-start = (bf16[384,512]{1,0:T(8,128)(2,1)S(1)}, bf16[384,512]{1,0:T(8,128)(2,1)}, u32[]{:S(2)}, u32[]{:S(2)}) collective-permute-start(bf16[384,512]{1,0:T(8,128)(2,1)S(1)} %bitcast.46), channel_id=1, source_target_pairs={{0,4},{8,12},{16,20},{24,28},{1,5},{9,13},{17,21},{25,29},{2,6},{1... | collective-permute-start | bytes 1179656 | tf_op jit(solution)/shard_map/ppermute | solution.py:226
  56.7 3.3 %copy-start.5 = (f32[16,384]{1,0:T(8,128)S(1)}, f32[16,384]{1,0:T(8,128)}, u32[]{:S(2)}) copy-start(f32[16,384]{1,0:T(8,128)} %param.12) | copy-start | bytes 73732
  57.6 0.6 copy-start.2
  72.8 14.9 %collective-permute-start.3 = (bf16[384,512]{1,0:T(8,128)(2,1)}, bf16[384,512]{1,0:T(8,128)(2,1)S(1)}, u32[]{:S(2)}, u32[]{:S(2)}) collective-permute-start(bf16[384,512]{1,0:T(8,128)(2,1)} %get-tuple-element.10), channel_id=1, source_target_pairs={{4,0},{12,8},{20,16},{28,24},{5,1},{13,9},{21,17},{29,25},{6,2},{1... | collective-permute-start | bytes 1179656 | tf_op jit(solution)/shard_map/ppermute | solution.py:238
  74.1 28.1 %collective-permute-start.4 = (bf16[384,512]{1,0:T(8,128)(2,1)}, bf16[384,512]{1,0:T(8,128)(2,1)S(1)}, u32[]{:S(2)}, u32[]{:S(2)}) collective-permute-start(bf16[384,512]{1,0:T(8,128)(2,1)} %get-tuple-element.11), channel_id=1, source_target_pairs={{8,0},{12,4},{24,16},{28,20},{9,1},{13,5},{25,17},{29,21},{10,2},{... | collective-permute-start | bytes 1179656 | tf_op jit(solution)/shard_map/ppermute | solution.py:238
  75.4 40.1 %collective-permute-start.5 = (bf16[384,512]{1,0:T(8,128)(2,1)}, bf16[384,512]{1,0:T(8,128)(2,1)S(1)}, u32[]{:S(2)}, u32[]{:S(2)}) collective-permute-start(bf16[384,512]{1,0:T(8,128)(2,1)} %get-tuple-element.12), channel_id=1, source_target_pairs={{12,0},{8,4},{28,16},{24,20},{13,1},{9,5},{29,17},{25,21},{14,2},{... | collective-permute-start | bytes 1179656 | tf_op jit(solution)/shard_map/ppermute | solution.py:238
  126.7 23.6 %all-to-all-start.2 = ((bf16[4,96,2048]{2,1,0:T(8,128)(2,1)}), bf16[4,96,2048]{2,1,0:T(8,128)(2,1)S(1)}, u32[]{:S(2)}, u32[]{:S(2)}) async-start(bf16[4,96,2048]{2,1,0:T(8,128)(2,1)} %bitcast.8), calls=%async_computation.2 | async-start | bytes 3145728 | tf_op jit(solution)/shard_map/all_to_all | solution.py:234

commit v2 on v0

v2 whole, which is shorter than its diff:
```python
import math

import jax
import jax.numpy as jnp
from jax import lax
from jax.experimental import pallas as pl
from jax.experimental.pallas import tpu as pltpu
from jax.sharding import PartitionSpec as P

DH = 128
TAG_ROWS = 16
SCORE_SCALE = 1.0 / math.sqrt(DH)
LOG2E = math.log2(math.e)
NT = (((1,), (1,)), ((), ()))
NN = (((1,), (0,)), ((), ()))
TN = (((0,), (0,)), ((), ()))
ANY = pl.BlockSpec(memory_space=pl.ANY)
VMEM = pl.BlockSpec(memory_space=pltpu.VMEM)


def dot(a, b, dims):
    return lax.dot_general(a, b, dims, preferred_element_type=jnp.float32)


def aligned(index, size):
    return pl.ds(pl.multiple_of(index * size, size), size)


def run_copies(pairs, sems):
    copies = [pltpu.make_async_copy(src, dst, sems.at[i]) for i, (src, dst) in enumerate(pairs)]
    for copy in copies:
        copy.start()
    for copy in copies:
        copy.wait()


def cost(flops, moved):
    return pl.CostEstimate(flops=flops, bytes_accessed=moved, transcendentals=0)


def row_deltas(out_grad, attn_out, heads):
    rows = out_grad.shape[0]

    def kernel(grad_ref, out_ref, delta_ref):
        for head in range(heads):
            cols = slice(head * DH, (head + 1) * DH)
            prod = grad_ref[:, cols].astype(jnp.float32) * out_ref[:, cols].astype(jnp.float32)
            delta_ref[head : head + 1, :] = jnp.sum(jnp.transpose(prod), axis=0, keepdims=True)

    return pl.pallas_call(
        kernel,
        out_shape=jax.ShapeDtypeStruct((heads, rows), jnp.float32),
        compiler_params=pltpu.CompilerParams(vmem_limit_bytes=32 << 20),
        cost_estimate=cost(4 * rows * heads * DH, 4 * rows * heads * DH),
        name="row_deltas",
    )(out_grad, attn_out)


def pack_kv(keys, values, head_count):
    part, width = keys.shape[0], keys.shape[1] // head_count

    def kernel(k_ref, v_ref, *refs):
        outs, sems = refs[:-1], refs[-1]
        own = lax.axis_index("head")
        pairs = []
        for step in range(1, head_count):
            cols = aligned(own ^ step, width)
            pairs.append((k_ref.at[:, cols], outs[step - 1].at[:, :width]))
            pairs.append((v_ref.at[:, cols], outs[step - 1].at[:, width:]))
        run_copies(pairs, sems)

    return pl.pallas_call(
        kernel,
        out_shape=[jax.ShapeDtypeStruct((part, 2 * width), keys.dtype)] * (head_count - 1),
        in_specs=[ANY] * 2,
        out_specs=[ANY] * (head_count - 1),
        scratch_shapes=[pltpu.SemaphoreType.DMA((2 * (head_count - 1),))],
        cost_estimate=cost(0, 4 * part * keys.shape[1]),
        name="pack_kv",
    )(keys, values)


def pack_q(queries, head_count, chunks):
    part, width = queries.shape[0], queries.shape[1] // (head_count * chunks)

    def kernel(q_ref, *refs):
        outs, sems = refs[:-1], refs[-1]
        own = lax.axis_index("head")
        pairs = []
        for chunk in range(chunks):
            for step in range(1, head_count):
                cols = aligned((own ^ step) * chunks + chunk, width)
                pairs.append((q_ref.at[:, cols], outs[chunk * (head_count - 1) + step - 1]))
        run_copies(pairs, sems)

    count = chunks * (head_count - 1)
    return pl.pallas_call(
        kernel,
        out_shape=[jax.ShapeDtypeStruct((part, width), queries.dtype)] * count,
        in_specs=[ANY],
        out_specs=[ANY] * count,
        scratch_shapes=[pltpu.SemaphoreType.DMA((count,))],
        cost_estimate=cost(0, 4 * part * queries.shape[1]),
        name="pack_q",
    )(queries)


def join_kv(keys, values, parts, tags):
    head_count = len(parts) + 1
    part, width = keys.shape[0], keys.shape[1] // head_count
    rows = part * head_count

    def kernel(k_ref, v_ref, tag_ref, *refs):
        ins, out, sems = refs[: head_count - 1], refs[-2], refs[-1]
        own = lax.axis_index("head")
        pairs = [
            (k_ref.at[:, aligned(own, width)], out.at[aligned(own, part), :width]),
            (v_ref.at[:, aligned(own, width)], out.at[aligned(own, part), width:]),
            (tag_ref, out.at[rows:]),
        ]
        for step in range(1, head_count):
            pairs.append((ins[step - 1], out.at[aligned(own ^ step, part)]))
        run_copies(pairs, sems)

    return pl.pallas_call(
        kernel,
        out_shape=jax.ShapeDtypeStruct((rows + tags.shape[0], 2 * width), keys.dtype),
        in_specs=[ANY] * (2 + head_count),
        out_specs=ANY,
        scratch_shapes=[pltpu.SemaphoreType.DMA((head_count + 2,))],
        cost_estimate=cost(0, 8 * rows * width),
        name="join_kv",
    )(keys, values, tags, *parts)


def chunk_grads(chunk, chunks, half, queries, q_parts, out_grad, log_sum, delta, kv_own, kv_in):
    head_count = len(q_parts) + 1
    part, width = q_parts[0].shape
    rows = part * head_count
    group = width // DH
    slots = half

    def kernel(*refs):
        lse_ref, delta_ref, q_own, g_in = refs[:4]
        q_in = refs[4 : 3 + head_count]
        kv_refs = refs[3 + head_count : 3 + head_count + slots]
        outs = refs[3 + head_count + slots :]
        dq_out = outs[:head_count]
        own_out = outs[head_count]
        dkv_out = outs[head_count + 1 : head_count + slots]
        (q_buf, g_buf, kv_buf, tag_buf, dkv_buf, dq_acc, dq_low, dk_acc, dv_acc, bias) = outs[
            head_count + slots : -3
        ]
        in_sem, kv_sem, out_sem = outs[-3:]
        head_index = lax.axis_index("head")
        own = lax.rem(lax.axis_index("ctx"), half)
        loads = [
            (q_own.at[:, aligned(head_index * chunks + chunk, width)], q_buf.at[aligned(head_index, part)])
        ]
        for step in range(1, head_count):
            loads.append((q_in[step - 1], q_buf.at[aligned(head_index ^ step, part)]))
        loads.append((g_in.at[:, chunk * width : (chunk + 1) * width], g_buf))
        loads = [pltpu.make_async_copy(s, d, in_sem.at[i]) for i, (s, d) in enumerate(loads)]

        def kv_copies(slot):
            src = kv_refs[slot]
            k_cols = slice(chunk * DH, (chunk + 1) * DH)
            v_cols = slice((chunks + chunk) * DH, (chunks + chunk + 1) * DH)
            return [
                pltpu.make_async_copy(src.at[:rows, k_cols], kv_buf.at[slot, :, :DH], kv_sem.at[slot, 0]),
                pltpu.make_async_copy(src.at[:rows, v_cols], kv_buf.at[slot, :, DH:], kv_sem.at[slot, 1]),
                pltpu.make_async_copy(src.at[rows:], tag_buf.at[slot], kv_sem.at[slot, 2]),
            ]

        for slot in range(slots):
            if slot == 0:
                for copy in kv_copies(slot) + loads:
                    copy.start()
            else:
                @pl.when((own ^ slot) < own)
                def _():
                    for copy in kv_copies(slot):
                        copy.start()

        dq_acc[...] = jnp.zeros_like(dq_acc)
        for copy in kv_copies(0) + loads:
            copy.wait()

        def load_tags(slot):
            pieces = []
            for first in range(0, rows, tag_buf.shape[2]):
                row = first // tag_buf.shape[2] * TAG_ROWS
                size = min(rows - first, tag_buf.shape[2])
                pieces.append(tag_buf[slot, row : row + TAG_ROWS, :size].astype(jnp.float32)[:8])
            return pieces[0] if len(pieces) == 1 else jnp.concatenate(pieces, axis=1)

        own_tags = load_tags(0)
        own_low, own_high = jnp.min(own_tags), jnp.max(own_tags)

        def tile(slot, masked):
            key = kv_buf[slot, :, :DH]
            value = kv_buf[slot, :, DH:]
            for member in range(group):
                head = chunk * group + member
                cols = slice(member * DH, (member + 1) * DH)
                query = q_buf[:, cols]
                grad = g_buf[:, cols]
                lse = lse_ref[head : head + 1, :] * LOG2E
                scores = dot(key, query, NT) * (SCORE_SCALE * LOG2E) - lse
                if masked:
                    scores = scores + bias[...]
                probs = jnp.exp2(scores)
                dprobs = dot(value, grad, NT)
                dscores = (probs * (dprobs - delta_ref[head : head + 1, :])).astype(jnp.bfloat16)
                dv_part = dot(probs.astype(jnp.bfloat16), grad, NN)
                dk_part = dot(dscores, query, NN)
                dq_part = dot(dscores, key, TN)
                if member == 0:
                    dv_acc[...] = dv_part
                    dk_acc[...] = dk_part
                else:
                    dv_acc[...] += dv_part
                    dk_acc[...] += dk_part
                dq_acc[:, cols] += dq_part

        def store(slot):
            dk = dk_acc[...] * SCORE_SCALE
            dv = dv_acc[...]

            @pl.when(slot == 0)
            def _():
                own_out[:, :DH] = dk
                own_out[:, DH:] = dv

            @pl.when(slot > 0)
            def _():
                dkv_buf[slot, :, :DH] = dk.astype(jnp.bfloat16)
                dkv_buf[slot, :, DH:] = dv.astype(jnp.bfloat16)

        def visit(slot, _):
            block = own ^ slot

            @pl.when(block <= own)
            def _():
                @pl.when(slot > 0)
                def _():
                    pltpu.make_async_copy(
                        kv_buf.at[slot, :, :DH], kv_buf.at[slot, :, :DH], kv_sem.at[slot, 0]
                    ).wait()
                    pltpu.make_async_copy(
                        kv_buf.at[slot, :, DH:], kv_buf.at[slot, :, DH:], kv_sem.at[slot, 1]
                    ).wait()
                    pltpu.make_async_copy(tag_buf.at[slot], tag_buf.at[slot], kv_sem.at[slot, 2]).wait()

                tags = load_tags(slot)
                needed = jnp.max(tags) == own_low
                full = (jnp.min(tags) == own_high) & (slot > 0)

                @pl.when(full)
                def _():
                    tile(slot, False)
                    store(slot)

                @pl.when(jnp.logical_not(full) & (needed | (slot == 0)))
                def _():
                    key_tags = jnp.transpose(tags)[:, :1]
                    key_pos = block * rows + lax.broadcasted_iota(jnp.int32, (rows, rows), 0)
                    query_pos = own * rows + lax.broadcasted_iota(jnp.int32, (rows, rows), 1)
                    allowed = (key_tags == own_tags[:1, :]) & (key_pos <= query_pos)
                    bias[...] = jnp.where(allowed, 0.0, -1e30)
                    tile(slot, True)
                    store(slot)

                @pl.when(jnp.logical_not(full | needed | (slot == 0)))
                def _():
                    dkv_buf[slot] = jnp.zeros(dkv_buf.shape[1:], dkv_buf.dtype)

            return 0

        lax.fori_loop(0, slots, visit, 0)

        def dkv_copy(slot):
            return pltpu.make_async_copy(dkv_buf.at[slot], dkv_out[slot - 1], out_sem.at[slot])

        for slot in range(1, slots):
            @pl.when((own ^ slot) < own)
            def _():
                dkv_copy(slot).start()
        dq_low[...] = (dq_acc[...] * SCORE_SCALE).astype(dq_low.dtype)
        sends = [
            pltpu.make_async_copy(
                dq_low.at[aligned(head_index ^ step, part)], dq_out[step], in_sem.at[step]
            )
            for step in range(head_count)
        ]
        for copy in sends:
            copy.start()
        for copy in sends:
            copy.wait()
        for slot in range(1, slots):
            @pl.when((own ^ slot) < own)
            def _():
                dkv_copy(slot).wait()

    bf16, f32 = jnp.bfloat16, jnp.float32
    heads = log_sum.shape[0]
    return pl.pallas_call(
        kernel,
        out_shape=[jax.ShapeDtypeStruct((part, width), bf16)] * head_count
        + [jax.ShapeDtypeStruct((rows, 2 * DH), f32)]
        + [jax.ShapeDtypeStruct((rows, 2 * DH), bf16)] * (slots - 1),
        in_specs=[VMEM] * 2 + [ANY] * (1 + head_count + slots),
        out_specs=[ANY] * head_count + [VMEM] + [ANY] * (slots - 1),
        scratch_shapes=[
            pltpu.VMEM((rows, width), bf16),
            pltpu.VMEM((rows, width), bf16),
            pltpu.VMEM((slots, rows, 2 * DH), bf16),
            pltpu.VMEM((slots, kv_own.shape[0] - rows, kv_own.shape[1]), bf16),
            pltpu.VMEM((slots, rows, 2 * DH), bf16),
            pltpu.VMEM((rows, width), f32),
            pltpu.VMEM((rows, width), bf16),
            pltpu.VMEM((rows, DH), f32),
            pltpu.VMEM((rows, DH), f32),
            pltpu.VMEM((rows, rows), f32),
            pltpu.SemaphoreType.DMA((head_count + 1,)),
            pltpu.SemaphoreType.DMA((slots, 3)),
            pltpu.SemaphoreType.DMA((slots,)),
        ],
        compiler_params=pltpu.CompilerParams(vmem_limit_bytes=48 << 20),
        cost_estimate=pl.CostEstimate(
            flops=10 * rows * rows * width * slots,
            bytes_accessed=8 * rows * width + 8 * slots * rows * 2 * DH,
            transcendentals=rows * rows * group * slots,
        ),
        name="chunk_grads",
    )(log_sum, delta, queries, out_grad, *q_parts, kv_own, *kv_in)


def sum_kv(own_part, parts, head_count):
    rows, width = own_part.shape
    part = rows // head_count

    def kernel(own_ref, *refs):
        ins, outs, total = refs[: len(parts)], refs[len(parts) : -1], refs[-1]
        value = own_ref[...]
        for ref in ins:
            value = value + ref[...].astype(jnp.float32)
        total[...] = value.astype(jnp.bfloat16)
        index = lax.axis_index("head")
        for step in range(head_count):
            outs[step][...] = total[aligned(index ^ step, part), :]

    return pl.pallas_call(
        kernel,
        out_shape=[jax.ShapeDtypeStruct((part, width), jnp.bfloat16)] * head_count,
        scratch_shapes=[pltpu.VMEM((rows, width), jnp.bfloat16)],
        compiler_params=pltpu.CompilerParams(vmem_limit_bytes=32 << 20),
        cost_estimate=cost(4 * rows * width, 12 * rows * width),
        name="sum_kv",
    )(own_part, *parts)


def join_grads(dq_parts, dkv_parts):
    chunks, head_count = len(dq_parts), len(dq_parts[0])
    part, width = dq_parts[0][0].shape
    count = chunks * head_count

    def kernel(*refs):
        q_ins, kv_ins = refs[:count], refs[count : 2 * count]
        q_out, k_out, v_out, sems = refs[2 * count :]
        own = lax.axis_index("head")
        pairs = []
        for chunk in range(chunks):
            for step in range(head_count):
                slot = (own ^ step) * chunks + chunk
                q_ref = q_ins[chunk * head_count + step]
                kv_ref = kv_ins[chunk * head_count + step]
                pairs.append((q_ref, q_out.at[:, aligned(slot, width)]))
                pairs.append((kv_ref.at[:, :DH], k_out.at[:, aligned(slot, DH)]))
                pairs.append((kv_ref.at[:, DH:], v_out.at[:, aligned(slot, DH)]))
        run_copies(pairs, sems)

    kv_shape = jax.ShapeDtypeStruct((part, count * DH), jnp.bfloat16)
    return pl.pallas_call(
        kernel,
        out_shape=[jax.ShapeDtypeStruct((part, count * width), jnp.bfloat16), kv_shape, kv_shape],
        in_specs=[ANY] * (2 * count),
        out_specs=[ANY] * 3,
        scratch_shapes=[pltpu.SemaphoreType.DMA((3 * count,))],
        cost_estimate=cost(0, 5 * part * count * width),
        name="join_grads",
    )(*[x for group in dq_parts for x in group], *[x for group in dkv_parts for x in group])


def per_device(queries, keys, values, attn_out, out_grad, log_sum, file_ids):
    ctx_count = lax.axis_size("ctx")
    head_count = lax.axis_size("head")
    half = ctx_count // 2
    rows = out_grad.shape[0]
    heads = log_sum.shape[0]
    kv_width = keys.shape[1] // head_count
    chunks = kv_width // DH

    def over_head(blocks):
        return [
            lax.ppermute(x, "head", [(i, i ^ step) for i in range(head_count)])
            for step, x in enumerate(blocks, 1)
        ]

    def route(step):
        pairs = [(i, i - i % half + (i % half ^ step)) for i in range(ctx_count)]
        return [(i, j) for i, j in pairs if i < j]

    tag_groups = pl.cdiv(rows, 2 * kv_width)
    tags = jnp.pad(file_ids.astype(jnp.bfloat16), (0, tag_groups * 2 * kv_width - rows))
    tags = jnp.repeat(tags.reshape(tag_groups, 2 * kv_width), TAG_ROWS, axis=0)
    kv_parts = over_head(pack_kv(keys, values, head_count))
    q_packed = pack_q(queries, head_count, chunks)
    steps = head_count - 1
    q_parts = [over_head(q_packed[i * steps : (i + 1) * steps]) for i in range(chunks)]
    kv_own = join_kv(keys, values, kv_parts, tags)
    delta = row_deltas(out_grad, attn_out, heads)
    kv_in = [lax.ppermute(kv_own, "ctx", route(step)) for step in range(1, half)]

    dq_parts, dkv_parts = [], []
    for chunk in range(chunks):
        outs = chunk_grads(
            chunk, chunks, half, queries, q_parts[chunk], out_grad, log_sum, delta, kv_own, kv_in
        )
        dq_parts.append([outs[0]] + over_head(outs[1:head_count]))
        back = [
            lax.ppermute(x, "ctx", [(j, i) for i, j in route(step)])
            for step, x in enumerate(outs[head_count + 1 :], 1)
        ]
        pieces = sum_kv(outs[head_count], back, head_count)
        dkv_parts.append([pieces[0]] + over_head(pieces[1:]))
    return tuple(join_grads(dq_parts, dkv_parts))


def solution(mesh):
    return jax.shard_map(
        per_device,
        mesh=mesh,
        in_specs=(
            P(("ctx", "head"), None),
            P(("ctx", "head"), None),
            P(("ctx", "head"), None),
            P("ctx", "head"),
            P("ctx", "head"),
            P("head", "ctx"),
            P("ctx"),
        ),
        out_specs=(P(("ctx", "head"), None), P(("ctx", "head"), None), P(("ctx", "head"), None)),
        check_vma=False,
    )
```

time: 269 us -> 220 us (0.82)
  Pallas kernels: 0 us -> 137 us
  starting transfers between devices: 95.2 us -> 33.9 us
  other arithmetic: 42.8 us -> 0.68 us
  waiting for transfers between devices: 78.2 us -> 40.8 us
  local copies, waits for them, and re-layouts: 36.6 us -> 3.95 us
  matrix products: 9.83 us -> 0 us
  loops' own time: 3.25 us -> 0 us
    pallas_call x0 -> x9, Pallas kernels: none -> 137 us  [the longest x1 60.9 us: join_grads(): pl.pallas_call(kernel, out_shape=[jax.ShapeDtypeStruct((part, count * wid...]
    ppermute x22 -> x30, starting transfers between devices: 72.9 us -> 33.9 us  [the longest x21 17.9 us: over_head(): lax.ppermute(x, 'head', [(i, i ^ step) for i in range(head_count)])]
    all_to_all x6 -> x0, waiting for transfers between devices: 34.1 us -> none  [the longest x1 18.7 us: per_device(): lax.all_to_all(q_done, 'head', split_axis=0, concat_axis=1, tiled=True)]
    add x21 -> x0, other arithmetic: 29.7 us -> none  [the longest x4 15.4 us: visit_block(): return (dq_acc + q_part, key_part, value_part, tag_part, k_store, v_store)]
    all_to_all x6 -> x0, starting transfers between devices: 22.3 us -> none  [the longest x1 4.36 us: per_device(): lax.all_to_all(queries, 'head', split_axis=1, concat_axis=0, tiled=True)]
    all_to_all x9 -> x0, local copies, waits for them, and re-layouts: 12.4 us -> none  [the longest x2 3.3 us: per_device(): lax.all_to_all(q_done, 'head', split_axis=0, concat_axis=1, tiled=True)]
    unnamed x27 -> x54, local copies, waits for them, and re-layouts: 13.2 us -> 3.3 us
    dot_general x5 -> x0, matrix products: 9.83 us -> none  [the longest x1 3.17 us: tile_grads(): jnp.einsum('rkgd,ckd->kgrc', g_four, value_part, preferred_element_type=j...]
  transfers between devices with their start and end apart: 28 -> 30, of which waited for: 20 -> 13; matrix products, arithmetic and copies ran while one was open for 23% -> 0% of each run, Pallas kernels for 0% -> 24%
where the time goes in v2:
time: 220 us; the launch traced here: 218 us
  Pallas kernels  137 us (62%)
  waiting for transfers between devices  40.8 us (19%)
  starting transfers between devices  33.9 us (15%)
  local copies, waits for them, and re-layouts  3.95 us (2%)
    pallas_call x1, Pallas kernels, join_grads(): pl.pallas_call(kernel, out_shape=[jax.ShapeDtypeStruct((part, count * wid...  60.9 us
    pallas_call x1, Pallas kernels, pack_q(): pl.pallas_call(kernel, out_shape=[jax.ShapeDtypeStruct((part, width), que...  36.9 us
    ppermute x6, waiting for transfers between devices, per_device(): lax.ppermute(x, 'ctx', [(j, i) for i, j in route(step)])  23.9 us
    ppermute x21, starting transfers between devices, over_head(): lax.ppermute(x, 'head', [(i, i ^ step) for i in range(head_count)])  17.9 us
    ppermute x21, waiting for transfers between devices, over_head(): lax.ppermute(x, 'head', [(i, i ^ step) for i in range(head_count)])  16.9 us
    pallas_call x2, Pallas kernels, chunk_grads(): pl.pallas_call(kernel, out_shape=[jax.ShapeDtypeStruct((part, width), bf1...  14.6 us
    pallas_call x1, Pallas kernels, join_kv(): pl.pallas_call(kernel, out_shape=jax.ShapeDtypeStruct((rows + tags.shape[...  13.6 us
    pallas_call x1, Pallas kernels, pack_kv(): pl.pallas_call(kernel, out_shape=[jax.ShapeDtypeStruct((part, 2 * width),...  10.1 us
  transfers between devices with their start and end apart: 30, of which 13 were waited for; matrix products, arithmetic and copies ran while one was open for 0% of the time, Pallas kernels for 24%

profile of v2, /device:TPU:0, one launch (start us, length us, event | category | flops | bytes accessed | tf_op | source)
XLA Modules:
  0.0 217.8 jit_solution(13416101625613841330)
XLA Ops:
  0.6 10.1 %pack_kv.1 = (bf16[96,512]{1,0:T(8,128)(2,1)}, bf16[96,512]{1,0:T(8,128)(2,1)}, bf16[96,512]{1,0:T(8,128)(2,1)}) custom-call(bf16[96,1024]{1,0:T(8,128)(2,1)} %k_ref.3, bf16[96,1024]{1,0:T(8,128)(2,1)} %v_ref.3), custom_call_target="tpu_custom_call" | custom-call | bytes 393216 | tf_op jit(solution)/shard_map/pack_kv/pallas_call | solution.py:72
  10.7 0.5 collective-permute-start.3
  11.3 2.6 %collective-permute-start.4 = (bf16[96,512]{1,0:T(8,128)(2,1)}, bf16[96,512]{1,0:T(8,128)(2,1)S(1)}, u32[]{:S(2)}, u32[]{:S(2)}) collective-permute-start(bf16[96,512]{1,0:T(8,128)(2,1)} %get-tuple-element.40), channel_id=1, source_target_pairs={{0,2},{1,3},{2,0},{3,1},{4,6},{5,7},{6,4},{7,5},{8,10},{9,11},{10,... | collective-permute-start | bytes 294920 | tf_op jit(solution)/shard_map/ppermute | solution.py:406
  13.9 0.1 collective-permute-start.5
  13.9 0.7 convert_element_type.5
  14.6 0.0 collective-permute-done.3.refs_0_
  14.6 3.1 %collective-permute-done.4.refs_1_ = bf16[96,512]{1,0:T(8,128)(2,1)S(1)} collective-permute-done((bf16[96,512]{1,0:T(8,128)(2,1)}, bf16[96,512]{1,0:T(8,128)(2,1)S(1)}, u32[]{:S(2)}, u32[]{:S(2)}) %collective-permute-start.4) | collective-permute-done | bytes 98336 | tf_op jit(solution)/shard_map/ppermute | solution.py:406
  17.7 1.6 collective-permute-done.5.refs_2_
  19.3 0.6 reshape.10.tag_ref
  19.9 13.6 %join_kv.1.refs_7_ = bf16[400,512]{1,0:T(8,128)(2,1)} custom-call(bf16[96,1024]{1,0:T(8,128)(2,1)} %k_ref.3, bf16[96,1024]{1,0:T(8,128)(2,1)} %v_ref.3, bf16[16,512]{1,0:T(8,128)(2,1)} %reshape.10.tag_ref, bf16[96,512]{1,0:T(8,128)(2,1)} %copy-done.15, bf16[96,512]{1,0:T(8,128)(2,1)} %copy-done.16, bf16[96,512]{1,0:T(8,128)(2,1)} %copy-done.17), custom_call_target="tpu_custom_call" | custom-call | bytes 786432 | tf_op jit(solution)/shard_map/join_kv/pallas_call | solution.py:125
  33.5 3.5 %collective-permute-start.6 = (bf16[400,512]{1,0:T(8,128)(2,1)}, bf16[400,512]{1,0:T(8,128)(2,1)S(1)}, u32[]{:S(2)}, u32[]{:S(2)}) collective-permute-start(bf16[400,512]{1,0:T(8,128)(2,1)} %join_kv.1.refs_7_), channel_id=1, source_target_pairs={{0,4},{8,12},{16,20},{24,28},{1,5},{9,13},{17,21},{25,29},{2,6},{1... | collective-permute-start | bytes 1228808 | tf_op jit(solution)/shard_map/ppermute | solution.py:423
  37.0 3.5 %collective-permute-start.7 = (bf16[400,512]{1,0:T(8,128)(2,1)}, bf16[400,512]{1,0:T(8,128)(2,1)S(1)}, u32[]{:S(2)}, u32[]{:S(2)}) collective-permute-start(bf16[400,512]{1,0:T(8,128)(2,1)} %join_kv.1.refs_7_), channel_id=1, source_target_pairs={{0,8},{4,12},{16,24},{20,28},{1,9},{5,13},{17,25},{21,29},{2,10},{... | collective-permute-start | bytes 1228808 | tf_op jit(solution)/shard_map/ppermute | solution.py:423
  40.5 1.3 collective-permute-start.8
  41.8 36.9 %pack_q.1 = (bf16[96,1024]{1,0:T(8,128)(2,1)}, bf16[96,1024]{1,0:T(8,128)(2,1)}, bf16[96,1024]{1,0:T(8,128)(2,1)}, bf16[96,1024]{1,0:T(8,128)(2,1)}, bf16[96,1024]{1,0:T(8,128)(2,1)}, /*index=5*/bf16[96,1024]{1,0:T(8,128)(2,1)}) custom-call(bf16[96,8192]{1,0:T(8,128)(2,1)} %refs_2_.3), custom_call_target="tpu_custom_call" | custom-call | bytes 3145728 | tf_op jit(solution)/shard_map/pack_q/pallas_call | solution.py:97
  78.7 0.1 collective-permute-start.12
  78.8 1.6 collective-permute-start.13
  80.4 0.1 collective-permute-done.12.refs_4_
  80.5 1.3 collective-permute-start.14
  81.7 1.4 copy-done.1
  83.1 0.0 copy-start.3
  83.2 0.0 copy-start.8
  83.2 0.9 row_deltas.1.refs_1_
  84.1 2.7 %collective-permute-done.13.refs_5_ = bf16[96,1024]{1,0:T(8,128)(2,1)S(1)} collective-permute-done((bf16[96,1024]{1,0:T(8,128)(2,1)}, bf16[96,1024]{1,0:T(8,128)(2,1)S(1)}, u32[]{:S(2)}, u32[]{:S(2)}) %collective-permute-start.13) | collective-permute-done | bytes 196640 | tf_op jit(solution)/shard_map/ppermute | solution.py:406
  86.8 0.0 collective-permute-start
  86.8 3.3 %collective-permute-done.14.refs_6_ = bf16[96,1024]{1,0:T(8,128)(2,1)S(1)} collective-permute-done((bf16[96,1024]{1,0:T(8,128)(2,1)}, bf16[96,1024]{1,0:T(8,128)(2,1)S(1)}, u32[]{:S(2)}, u32[]{:S(2)}) %collective-permute-start.14) | collective-permute-done | bytes 196640 | tf_op jit(solution)/shard_map/ppermute | solution.py:406
  90.1 1.5 collective-permute-start.1
  91.6 0.1 collective-permute-start.2
  91.7 0.0 collective-permute-done.7.refs_9_
  91.7 0.0 collective-permute-done.8.refs_10_
  91.8 7.3 %chunk_grads.3 = (bf16[96,1024]{1,0:T(8,128)(2,1)S(1)}, bf16[96,1024]{1,0:T(8,128)(2,1)S(1)}, bf16[96,1024]{1,0:T(8,128)(2,1)S(1)}, bf16[96,1024]{1,0:T(8,128)(2...) custom-call(f32[16,384]{1,0:T(8,128)S(1)} %copy-done.8, ...), custom_call_target="tpu_custom_call" | custom-call | flops 6039797760 | bytes 6291456 | tf_op jit(solution)/shard_map/chunk_grads/pallas_call | solution.py:307
  99.1 0.7 copy-done.4
  99.8 1.3 collective-permute-start.24
  101.1 1.3 collective-permute-start.25
  102.4 0.0 collective-permute-done.refs_4_
  102.4 1.3 collective-permute-start.26
  103.7 7.3 %chunk_grads.2 = (bf16[96,1024]{1,0:T(8,128)(2,1)S(1)}, bf16[96,1024]{1,0:T(8,128)(2,1)S(1)}, bf16[96,1024]{1,0:T(8,128)(2,1)S(1)}, bf16[96,1024]{1,0:T(8,128)(2...) custom-call(f32[16,384]{1,0:T(8,128)S(1)} %copy-done.8, ...), custom_call_target="tpu_custom_call" | custom-call | flops 6039797760 | bytes 6291456 | tf_op jit(solution)/shard_map/chunk_grads/pallas_call | solution.py:307
  111.0 1.3 collective-permute-start.18
  112.3 1.3 collective-permute-start.19
  113.6 1.3 collective-permute-start.20
  115.0 0.6 collective-permute-start.15
  115.5 5.6 %collective-permute-done.26.refs_2_ = bf16[384,256]{1,0:T(8,128)(2,1)S(1)} collective-permute-done((bf16[384,256]{1,0:T(8,128)(2,1)S(1)}, bf16[384,256]{1,0:T(8,128)(2,1)S(1)}, u32[]{:S(2)}, u32[]{:S(2)}) %collective-permute-start.26) | collective-permute-done | bytes 196640 | tf_op jit(solution)/shard_map/ppermute | solution.py:432
  121.1 1.5 collective-permute-start.16
  122.7 4.1 %collective-permute-done.18.refs_0_ = bf16[384,256]{1,0:T(8,128)(2,1)S(1)} collective-permute-done((bf16[384,256]{1,0:T(8,128)(2,1)S(1)}, bf16[384,256]{1,0:T(8,128)(2,1)S(1)}, u32[]{:S(2)}, u32[]{:S(2)}) %collective-permute-start.18) | collective-permute-done | bytes 196640 | tf_op jit(solution)/shard_map/ppermute | solution.py:432
  126.7 1.1 collective-permute-start.17
  127.8 6.1 %collective-permute-done.19.refs_1_ = bf16[384,256]{1,0:T(8,128)(2,1)S(1)} collective-permute-done((bf16[384,256]{1,0:T(8,128)(2,1)S(1)}, bf16[384,256]{1,0:T(8,128)(2,1)S(1)}, u32[]{:S(2)}, u32[]{:S(2)}) %collective-permute-start.19) | collective-permute-done | bytes 196640 | tf_op jit(solution)/shard_map/ppermute | solution.py:432
  133.9 1.5 collective-permute-start.10
  135.4 8.1 %collective-permute-done.20.refs_2_ = bf16[384,256]{1,0:T(8,128)(2,1)S(1)} collective-permute-done((bf16[384,256]{1,0:T(8,128)(2,1)S(1)}, bf16[384,256]{1,0:T(8,128)(2,1)S(1)}, u32[]{:S(2)}, u32[]{:S(2)}) %collective-permute-start.20) | collective-permute-done | bytes 196640 | tf_op jit(solution)/shard_map/ppermute | solution.py:432
  143.5 0.9 collective-permute-start.11
  144.4 0.7 collective-permute-start.9
  145.2 0.1 sum_kv.3
  145.4 0.1 collective-permute-start.27
  145.4 0.1 sum_kv.2
  145.6 0.6 copy-done.7
  146.2 0.6 collective-permute-start.28
  146.8 1.3 collective-permute-start.29
  148.1 2.5 %collective-permute-done.11.refs_3_ = bf16[96,1024]{1,0:T(8,128)(2,1)S(1)} collective-permute-done((bf16[96,1024]{1,0:T(8,128)(2,1)S(1)}, bf16[96,1024]{1,0:T(8,128)(2,1)S(1)}, u32[]{:S(2)}, u32[]{:S(2)}) %collective-permute-start.11) | collective-permute-done | bytes 196640 | tf_op jit(solution)/shard_map/ppermute | solution.py:406
  150.7 0.1 collective-permute-start.21
  150.8 1.6 collective-permute-start.22
  152.4 0.2 collective-permute-start.23
  152.6 0.2 collective-permute-done.29.refs_15_
  152.8 2.1 collective-permute-done.22.refs_10_
  154.9 1.2 collective-permute-done.23.refs_11_
  156.2 0.5 copy-done.23
  156.8 60.9 %join_grads.1 = (bf16[96,8192]{1,0:T(8,128)(2,1)}, bf16[96,1024]{1,0:T(8,128)(2,1)}, bf16[96,1024]{1,0:T(8,128)(2,1)}) custom-call(bf16[96,1024]{1,0:T(8,128)(2,1)} %copy-done.5, bf16[96,1024]{1,0:T(8,128)(2,1)} %copy-done.14, bf16[96,1024]{1,0:T(8,128)(2,1)} %copy-done.12, bf16[96,1024]{1,0:T(8,128)(2,1)} %copy-done.13, bf16[96,1024]{1,0:T(8,128)(2,1)} %copy-done.4, ...), custom_call_target="tpu_custom_call" | custom-call | bytes 3932160 | tf_op jit(solution)/shard_map/join_grads/pallas_call | solution.py:384
  (62 shorter events, 0.1 us)
Async XLA Ops:
  0.6 81.1 %copy-start = (bf16[384,2048]{1,0:T(8,128)(2,1)S(1)}, bf16[384,2048]{1,0:T(8,128)(2,1)}, u32[]{:S(2)}) copy-start(bf16[384,2048]{1,0:T(8,128)(2,1)} %out_ref.1) | copy-start | bytes 4718596
  10.7 3.9 %collective-permute-start.3 = (bf16[96,512]{1,0:T(8,128)(2,1)}, bf16[96,512]{1,0:T(8,128)(2,1)S(1)}, u32[]{:S(2)}, u32[]{:S(2)}) collective-permute-start(bf16[96,512]{1,0:T(8,128)(2,1)} %get-tuple-element.39), channel_id=1, source_target_pairs={{0,1},{1,0},{2,3},{3,2},{4,5},{5,4},{6,7},{7,6},{8,9},{9,8},{10,11... | collective-permute-start | bytes 294920 | tf_op jit(solution)/shard_map/ppermute | solution.py:406
  11.3 6.4 %collective-permute-start.4 = (bf16[96,512]{1,0:T(8,128)(2,1)}, bf16[96,512]{1,0:T(8,128)(2,1)S(1)}, u32[]{:S(2)}, u32[]{:S(2)}) collective-permute-start(bf16[96,512]{1,0:T(8,128)(2,1)} %get-tuple-element.40), channel_id=1, source_target_pairs={{0,2},{1,3},{2,0},{3,1},{4,6},{5,7},{6,4},{7,5},{8,10},{9,11},{10,... | collective-permute-start | bytes 294920 | tf_op jit(solution)/shard_map/ppermute | solution.py:406
  13.9 5.4 %collective-permute-start.5 = (bf16[96,512]{1,0:T(8,128)(2,1)}, bf16[96,512]{1,0:T(8,128)(2,1)S(1)}, u32[]{:S(2)}, u32[]{:S(2)}) collective-permute-start(bf16[96,512]{1,0:T(8,128)(2,1)} %get-tuple-element.41), channel_id=1, source_target_pairs={{0,3},{1,2},{2,1},{3,0},{4,7},{5,6},{6,5},{7,4},{8,11},{9,10},{10,... | collective-permute-start | bytes 294920 | tf_op jit(solution)/shard_map/ppermute | solution.py:406
  14.6 5.3 %copy-start.15 = (bf16[96,512]{1,0:T(8,128)(2,1)}, bf16[96,512]{1,0:T(8,128)(2,1)S(1)}, u32[]{:S(2)}) copy-start(bf16[96,512]{1,0:T(8,128)(2,1)S(1)} %collective-permute-done.3.refs_0_) | copy-start | bytes 294916
  17.7 2.2 %copy-start.16 = (bf16[96,512]{1,0:T(8,128)(2,1)}, bf16[96,512]{1,0:T(8,128)(2,1)S(1)}, u32[]{:S(2)}) copy-start(bf16[96,512]{1,0:T(8,128)(2,1)S(1)} %collective-permute-done.4.refs_1_) | copy-start | bytes 294916
  19.3 0.6 copy-start.17
  33.5 58.1 %collective-permute-start.6 = (bf16[400,512]{1,0:T(8,128)(2,1)}, bf16[400,512]{1,0:T(8,128)(2,1)S(1)}, u32[]{:S(2)}, u32[]{:S(2)}) collective-permute-start(bf16[400,512]{1,0:T(8,128)(2,1)} %join_kv.1.refs_7_), channel_id=1, source_target_pairs={{0,4},{8,12},{16,20},{24,28},{1,5},{9,13},{17,21},{25,29},{2,6},{1... | collective-permute-start | bytes 1228808 | tf_op jit(solution)/shard_map/ppermute | solution.py:423
  37.0 54.7 %collective-permute-start.7 = (bf16[400,512]{1,0:T(8,128)(2,1)}, bf16[400,512]{1,0:T(8,128)(2,1)S(1)}, u32[]{:S(2)}, u32[]{:S(2)}) collective-permute-start(bf16[400,512]{1,0:T(8,128)(2,1)} %join_kv.1.refs_7_), channel_id=1, source_target_pairs={{0,8},{4,12},{16,24},{20,28},{1,9},{5,13},{17,25},{21,29},{2,10},{... | collective-permute-start | bytes 1228808 | tf_op jit(solution)/shard_map/ppermute | solution.py:423
  40.5 51.2 %collective-permute-start.8 = (bf16[400,512]{1,0:T(8,128)(2,1)}, bf16[400,512]{1,0:T(8,128)(2,1)S(1)}, u32[]{:S(2)}, u32[]{:S(2)}) collective-permute-start(bf16[400,512]{1,0:T(8,128)(2,1)} %join_kv.1.refs_7_), channel_id=1, source_target_pairs={{0,12},{4,8},{16,28},{20,24},{1,13},{5,9},{17,29},{21,25},{2,14},{... | collective-permute-start | bytes 1228808 | tf_op jit(solution)/shard_map/ppermute | solution.py:423
  78.7 1.7 collective-permute-start.12
  78.8 8.0 %collective-permute-start.13 = (bf16[96,1024]{1,0:T(8,128)(2,1)}, bf16[96,1024]{1,0:T(8,128)(2,1)S(1)}, u32[]{:S(2)}, u32[]{:S(2)}) collective-permute-start(bf16[96,1024]{1,0:T(8,128)(2,1)} %get-tuple-element.47), channel_id=1, source_target_pairs={{0,2},{1,3},{2,0},{3,1},{4,6},{5,7},{6,4},{7,5},{8,10},{9,11},{10,... | collective-permute-start | bytes 589832 | tf_op jit(solution)/shard_map/ppermute | solution.py:406
  80.5 9.6 %collective-permute-start.14 = (bf16[96,1024]{1,0:T(8,128)(2,1)}, bf16[96,1024]{1,0:T(8,128)(2,1)S(1)}, u32[]{:S(2)}, u32[]{:S(2)}) collective-permute-start(bf16[96,1024]{1,0:T(8,128)(2,1)} %get-tuple-element.48), channel_id=1, source_target_pairs={{0,3},{1,2},{2,1},{3,0},{4,7},{5,6},{6,5},{7,4},{8,11},{9,10},{10,... | collective-permute-start | bytes 589832 | tf_op jit(solution)/shard_map/ppermute | solution.py:406
  81.7 1.4 copy-start.1
  83.1 3.7 %copy-start.26 = (bf16[96,1024]{1,0:T(8,128)(2,1)S(1)}, bf16[96,1024]{1,0:T(8,128)(2,1)}, u32[]{:S(2)}) copy-start(bf16[96,1024]{1,0:T(8,128)(2,1)} %get-tuple-element.36) | copy-start | bytes 589828
  83.1 7.0 %copy-start.25 = (bf16[96,1024]{1,0:T(8,128)(2,1)S(1)}, bf16[96,1024]{1,0:T(8,128)(2,1)}, u32[]{:S(2)}) copy-start(bf16[96,1024]{1,0:T(8,128)(2,1)} %get-tuple-element.37) | copy-start | bytes 589828
  83.1 8.5 %copy-start.24 = (bf16[96,1024]{1,0:T(8,128)(2,1)S(1)}, bf16[96,1024]{1,0:T(8,128)(2,1)}, u32[]{:S(2)}) copy-start(bf16[96,1024]{1,0:T(8,128)(2,1)} %get-tuple-element.38) | copy-start | bytes 589828
  83.1 8.6 %copy-start.2 = (bf16[96,8192]{1,0:T(8,128)(2,1)S(1)}, bf16[96,8192]{1,0:T(8,128)(2,1)}, u32[]{:S(2)}) copy-start(bf16[96,8192]{1,0:T(8,128)(2,1)} %refs_2_.3) | copy-start | bytes 4718596
  83.1 8.6 %copy-start.3 = (bf16[400,512]{1,0:T(8,128)(2,1)S(1)}, bf16[400,512]{1,0:T(8,128)(2,1)}, u32[]{:S(2)}) copy-start(bf16[400,512]{1,0:T(8,128)(2,1)} %join_kv.1.refs_7_) | copy-start | bytes 1228804
  83.2 8.6 %copy-start.8 = (f32[16,384]{1,0:T(8,128)S(1)}, f32[16,384]{1,0:T(8,128)}, u32[]{:S(2)}) copy-start(f32[16,384]{1,0:T(8,128)} %refs_0_.3) | copy-start | bytes 73732
  86.8 15.6 %collective-permute-start = (bf16[96,1024]{1,0:T(8,128)(2,1)S(1)}, bf16[96,1024]{1,0:T(8,128)(2,1)S(1)}, u32[]{:S(2)}, u32[]{:S(2)}) collective-permute-start(bf16[96,1024]{1,0:T(8,128)(2,1)S(1)} %copy-done.26), channel_id=1, source_target_pairs={{0,1},{1,0},{2,3},{3,2},{4,5},{5,4},{6,7},{7,6},{8,9},{9,8},{10,11... | collective-permute-start | bytes 589832 | tf_op jit(solution)/shard_map/ppermute | solution.py:406
  90.1 13.6 %collective-permute-start.1 = (bf16[96,1024]{1,0:T(8,128)(2,1)S(1)}, bf16[96,1024]{1,0:T(8,128)(2,1)S(1)}, u32[]{:S(2)}, u32[]{:S(2)}) collective-permute-start(bf16[96,1024]{1,0:T(8,128)(2,1)S(1)} %copy-done.25), channel_id=1, source_target_pairs={{0,2},{1,3},{2,0},{3,1},{4,6},{5,7},{6,4},{7,5},{8,10},{9,11},{10,... | collective-permute-start | bytes 589832 | tf_op jit(solution)/shard_map/ppermute | solution.py:406
  91.6 12.1 %collective-permute-start.2 = (bf16[96,1024]{1,0:T(8,128)(2,1)S(1)}, bf16[96,1024]{1,0:T(8,128)(2,1)S(1)}, u32[]{:S(2)}, u32[]{:S(2)}) collective-permute-start(bf16[96,1024]{1,0:T(8,128)(2,1)S(1)} %copy-done.24), channel_id=1, source_target_pairs={{0,3},{1,2},{2,1},{3,0},{4,7},{5,6},{6,5},{7,4},{8,11},{9,10},{10,... | collective-permute-start | bytes 589832 | tf_op jit(solution)/shard_map/ppermute | solution.py:406
  99.1 0.7 copy-start.4
  99.8 13.9 %collective-permute-start.24 = (bf16[384,256]{1,0:T(8,128)(2,1)S(1)}, bf16[384,256]{1,0:T(8,128)(2,1)S(1)}, u32[]{:S(2)}, u32[]{:S(2)}) collective-permute-start(bf16[384,256]{1,0:T(8,128)(2,1)S(1)} %get-tuple-element.62), channel_id=1, source_target_pairs={{4,0},{12,8},{20,16},{28,24},{5,1},{13,9},{21,17},{29,25},{6,2},{1... | collective-permute-start | bytes 589832 | tf_op jit(solution)/shard_map/ppermute | solution.py:432
  101.1 13.9 %collective-permute-start.25 = (bf16[384,256]{1,0:T(8,128)(2,1)S(1)}, bf16[384,256]{1,0:T(8,128)(2,1)S(1)}, u32[]{:S(2)}, u32[]{:S(2)}) collective-permute-start(bf16[384,256]{1,0:T(8,128)(2,1)S(1)} %get-tuple-element.63), channel_id=1, source_target_pairs={{8,0},{12,4},{24,16},{28,20},{9,1},{13,5},{25,17},{29,21},{10,2},{... | collective-permute-start | bytes 589832 | tf_op jit(solution)/shard_map/ppermute | solution.py:432
  102.4 18.8 %collective-permute-start.26 = (bf16[384,256]{1,0:T(8,128)(2,1)S(1)}, bf16[384,256]{1,0:T(8,128)(2,1)S(1)}, u32[]{:S(2)}, u32[]{:S(2)}) collective-permute-start(bf16[384,256]{1,0:T(8,128)(2,1)S(1)} %get-tuple-element.64), channel_id=1, source_target_pairs={{12,0},{8,4},{28,16},{24,20},{13,1},{9,5},{29,17},{25,21},{14,2},{... | collective-permute-start | bytes 589832 | tf_op jit(solution)/shard_map/ppermute | solution.py:432
  111.0 34.6 %copy-start.5 = (bf16[96,1024]{1,0:T(8,128)(2,1)}, bf16[96,1024]{1,0:T(8,128)(2,1)S(1)}, u32[]{:S(2)}) copy-start(bf16[96,1024]{1,0:T(8,128)(2,1)S(1)} %get-tuple-element.42.refs_0_) | copy-start | bytes 589828
  111.0 15.7 %collective-permute-start.18 = (bf16[384,256]{1,0:T(8,128)(2,1)S(1)}, bf16[384,256]{1,0:T(8,128)(2,1)S(1)}, u32[]{:S(2)}, u32[]{:S(2)}) collective-permute-start(bf16[384,256]{1,0:T(8,128)(2,1)S(1)} %get-tuple-element.54), channel_id=1, source_target_pairs={{4,0},{12,8},{20,16},{28,24},{5,1},{13,9},{21,17},{29,25},{6,2},{1... | collective-permute-start | bytes 589832 | tf_op jit(solution)/shard_map/ppermute | solution.py:432
  112.3 21.6 %collective-permute-start.19 = (bf16[384,256]{1,0:T(8,128)(2,1)S(1)}, bf16[384,256]{1,0:T(8,128)(2,1)S(1)}, u32[]{:S(2)}, u32[]{:S(2)}) collective-permute-start(bf16[384,256]{1,0:T(8,128)(2,1)S(1)} %get-tuple-element.55), channel_id=1, source_target_pairs={{8,0},{12,4},{24,16},{28,20},{9,1},{13,5},{25,17},{29,21},{10,2},{... | collective-permute-start | bytes 589832 | tf_op jit(solution)/shard_map/ppermute | solution.py:432
  113.6 29.9 %collective-permute-start.20 = (bf16[384,256]{1,0:T(8,128)(2,1)S(1)}, bf16[384,256]{1,0:T(8,128)(2,1)S(1)}, u32[]{:S(2)}, u32[]{:S(2)}) collective-permute-start(bf16[384,256]{1,0:T(8,128)(2,1)S(1)} %get-tuple-element.56), channel_id=1, source_target_pairs={{12,0},{8,4},{28,16},{24,20},{13,1},{9,5},{29,17},{25,21},{14,2},{... | collective-permute-start | bytes 589832 | tf_op jit(solution)/shard_map/ppermute | solution.py:432
  115.0 29.5 %collective-permute-start.15 = (bf16[96,1024]{1,0:T(8,128)(2,1)S(1)}, bf16[96,1024]{1,0:T(8,128)(2,1)S(1)}, u32[]{:S(2)}, u32[]{:S(2)}) collective-permute-start(bf16[96,1024]{1,0:T(8,128)(2,1)S(1)} %get-tuple-element.50), channel_id=1, source_target_pairs={{0,1},{1,0},{2,3},{3,2},{4,5},{5,4},{6,7},{7,6},{8,9},{9,8},{10,11... | collective-permute-start | bytes 589832 | tf_op jit(solution)/shard_map/ppermute | solution.py:406
  121.1 24.2 %collective-permute-start.16 = (bf16[96,1024]{1,0:T(8,128)(2,1)S(1)}, bf16[96,1024]{1,0:T(8,128)(2,1)S(1)}, u32[]{:S(2)}, u32[]{:S(2)}) collective-permute-start(bf16[96,1024]{1,0:T(8,128)(2,1)S(1)} %get-tuple-element.51), channel_id=1, source_target_pairs={{0,2},{1,3},{2,0},{3,1},{4,6},{5,7},{6,4},{7,5},{8,10},{9,11},{10,... | collective-permute-start | bytes 589832 | tf_op jit(solution)/shard_map/ppermute | solution.py:406
  126.7 19.5 %collective-permute-start.17 = (bf16[96,1024]{1,0:T(8,128)(2,1)S(1)}, bf16[96,1024]{1,0:T(8,128)(2,1)S(1)}, u32[]{:S(2)}, u32[]{:S(2)}) collective-permute-start(bf16[96,1024]{1,0:T(8,128)(2,1)S(1)} %get-tuple-element.52), channel_id=1, source_target_pairs={{0,3},{1,2},{2,1},{3,0},{4,7},{5,6},{6,5},{7,4},{8,11},{9,10},{10,... | collective-permute-start | bytes 589832 | tf_op jit(solution)/shard_map/ppermute | solution.py:406
  133.9 12.9 %collective-permute-start.10 = (bf16[96,1024]{1,0:T(8,128)(2,1)S(1)}, bf16[96,1024]{1,0:T(8,128)(2,1)S(1)}, u32[]{:S(2)}, u32[]{:S(2)}) collective-permute-start(bf16[96,1024]{1,0:T(8,128)(2,1)S(1)} %get-tuple-element.44), channel_id=1, source_target_pairs={{0,2},{1,3},{2,0},{3,1},{4,6},{5,7},{6,4},{7,5},{8,10},{9,11},{10,... | collective-permute-start | bytes 589832 | tf_op jit(solution)/shard_map/ppermute | solution.py:406
  143.5 7.1 %collective-permute-start.11 = (bf16[96,1024]{1,0:T(8,128)(2,1)S(1)}, bf16[96,1024]{1,0:T(8,128)(2,1)S(1)}, u32[]{:S(2)}, u32[]{:S(2)}) collective-permute-start(bf16[96,1024]{1,0:T(8,128)(2,1)S(1)} %get-tuple-element.45), channel_id=1, source_target_pairs={{0,3},{1,2},{2,1},{3,0},{4,7},{5,6},{6,5},{7,4},{8,11},{9,10},{10,... | collective-permute-start | bytes 589832 | tf_op jit(solution)/shard_map/ppermute | solution.py:406
  144.4 11.7 %copy-start.9 = (bf16[96,1024]{1,0:T(8,128)(2,1)}, bf16[96,1024]{1,0:T(8,128)(2,1)S(1)}, u32[]{:S(2)}) copy-start(bf16[96,1024]{1,0:T(8,128)(2,1)S(1)} %collective-permute-done.15.refs_5_) | copy-start | bytes 589828
  144.4 6.4 %collective-permute-start.9 = (bf16[96,1024]{1,0:T(8,128)(2,1)S(1)}, bf16[96,1024]{1,0:T(8,128)(2,1)S(1)}, u32[]{:S(2)}, u32[]{:S(2)}) collective-permute-start(bf16[96,1024]{1,0:T(8,128)(2,1)S(1)} %get-tuple-element.43), channel_id=1, source_target_pairs={{0,1},{1,0},{2,3},{3,2},{4,5},{5,4},{6,7},{7,6},{8,9},{9,8},{10,11... | collective-permute-start | bytes 589832 | tf_op jit(solution)/shard_map/ppermute | solution.py:406
  145.3 0.9 copy-start.6
  145.3 10.8 %copy-start.10 = (bf16[96,1024]{1,0:T(8,128)(2,1)}, bf16[96,1024]{1,0:T(8,128)(2,1)S(1)}, u32[]{:S(2)}) copy-start(bf16[96,1024]{1,0:T(8,128)(2,1)S(1)} %collective-permute-done.16.refs_6_) | copy-start | bytes 589828
  145.4 7.0 %collective-permute-start.27 = (bf16[96,256]{1,0:T(8,128)(2,1)S(1)}, bf16[96,256]{1,0:T(8,128)(2,1)S(1)}, u32[]{:S(2)}, u32[]{:S(2)}) collective-permute-start(bf16[96,256]{1,0:T(8,128)(2,1)S(1)} %get-tuple-element.66), channel_id=1, source_target_pairs={{0,1},{1,0},{2,3},{3,2},{4,5},{5,4},{6,7},{7,6},{8,9},{9,8},{10,11... | collective-permute-start | bytes 147464 | tf_op jit(solution)/shard_map/ppermute | solution.py:406
  145.6 0.6 copy-start.7
  146.2 9.9 %copy-start.11 = (bf16[96,1024]{1,0:T(8,128)(2,1)}, bf16[96,1024]{1,0:T(8,128)(2,1)S(1)}, u32[]{:S(2)}) copy-start(bf16[96,1024]{1,0:T(8,128)(2,1)S(1)} %collective-permute-done.17.refs_7_) | copy-start | bytes 589828
  146.2 6.3 %collective-permute-start.28 = (bf16[96,256]{1,0:T(8,128)(2,1)S(1)}, bf16[96,256]{1,0:T(8,128)(2,1)S(1)}, u32[]{:S(2)}, u32[]{:S(2)}) collective-permute-start(bf16[96,256]{1,0:T(8,128)(2,1)S(1)} %get-tuple-element.67), channel_id=1, source_target_pairs={{0,2},{1,3},{2,0},{3,1},{4,6},{5,7},{6,4},{7,5},{8,10},{9,11},{10,... | collective-permute-start | bytes 147464 | tf_op jit(solution)/shard_map/ppermute | solution.py:406
  146.8 9.4 %copy-start.12 = (bf16[96,1024]{1,0:T(8,128)(2,1)}, bf16[96,1024]{1,0:T(8,128)(2,1)S(1)}, u32[]{:S(2)}) copy-start(bf16[96,1024]{1,0:T(8,128)(2,1)S(1)} %collective-permute-done.10.refs_2_) | copy-start | bytes 589828
  146.8 6.0 %collective-permute-start.29 = (bf16[96,256]{1,0:T(8,128)(2,1)S(1)}, bf16[96,256]{1,0:T(8,128)(2,1)S(1)}, u32[]{:S(2)}, u32[]{:S(2)}) collective-permute-start(bf16[96,256]{1,0:T(8,128)(2,1)S(1)} %get-tuple-element.68), channel_id=1, source_target_pairs={{0,3},{1,2},{2,1},{3,0},{4,7},{5,6},{6,5},{7,4},{8,11},{9,10},{10,... | collective-permute-start | bytes 147464 | tf_op jit(solution)/shard_map/ppermute | solution.py:406
  150.7 5.5 %copy-start.13 = (bf16[96,1024]{1,0:T(8,128)(2,1)}, bf16[96,1024]{1,0:T(8,128)(2,1)S(1)}, u32[]{:S(2)}) copy-start(bf16[96,1024]{1,0:T(8,128)(2,1)S(1)} %collective-permute-done.11.refs_3_) | copy-start | bytes 589828
  150.7 2.1 collective-permute-start.21
  150.8 5.4 %copy-start.14 = (bf16[96,1024]{1,0:T(8,128)(2,1)}, bf16[96,1024]{1,0:T(8,128)(2,1)S(1)}, u32[]{:S(2)}) copy-start(bf16[96,1024]{1,0:T(8,128)(2,1)S(1)} %collective-permute-done.9.refs_1_) | copy-start | bytes 589828
  150.8 4.1 %collective-permute-start.22 = (bf16[96,256]{1,0:T(8,128)(2,1)S(1)}, bf16[96,256]{1,0:T(8,128)(2,1)S(1)}, u32[]{:S(2)}, u32[]{:S(2)}) collective-permute-start(bf16[96,256]{1,0:T(8,128)(2,1)S(1)} %get-tuple-element.59), channel_id=1, source_target_pairs={{0,2},{1,3},{2,0},{3,1},{4,6},{5,7},{6,4},{7,5},{8,10},{9,11},{10,... | collective-permute-start | bytes 147464 | tf_op jit(solution)/shard_map/ppermute | solution.py:406
  152.4 3.8 %copy-start.18 = (bf16[96,256]{1,0:T(8,128)(2,1)}, bf16[96,256]{1,0:T(8,128)(2,1)S(1)}, u32[]{:S(2)}) copy-start(bf16[96,256]{1,0:T(8,128)(2,1)S(1)} %collective-permute-done.27.refs_13_) | copy-start | bytes 147460
  152.4 3.8 %collective-permute-start.23 = (bf16[96,256]{1,0:T(8,128)(2,1)S(1)}, bf16[96,256]{1,0:T(8,128)(2,1)S(1)}, u32[]{:S(2)}, u32[]{:S(2)}) collective-permute-start(bf16[96,256]{1,0:T(8,128)(2,1)S(1)} %get-tuple-element.60), channel_id=1, source_target_pairs={{0,3},{1,2},{2,1},{3,0},{4,7},{5,6},{6,5},{7,4},{8,11},{9,10},{10,... | collective-permute-start | bytes 147464 | tf_op jit(solution)/shard_map/ppermute | solution.py:406
  152.6 3.6 %copy-start.19 = (bf16[96,256]{1,0:T(8,128)(2,1)}, bf16[96,256]{1,0:T(8,128)(2,1)S(1)}, u32[]{:S(2)}) copy-start(bf16[96,256]{1,0:T(8,128)(2,1)S(1)} %collective-permute-done.28.refs_14_) | copy-start | bytes 147460
  152.8 3.4 %copy-start.20 = (bf16[96,256]{1,0:T(8,128)(2,1)}, bf16[96,256]{1,0:T(8,128)(2,1)S(1)}, u32[]{:S(2)}) copy-start(bf16[96,256]{1,0:T(8,128)(2,1)S(1)} %collective-permute-done.29.refs_15_) | copy-start | bytes 147460
  152.8 3.4 %copy-start.21 = (bf16[96,256]{1,0:T(8,128)(2,1)}, bf16[96,256]{1,0:T(8,128)(2,1)S(1)}, u32[]{:S(2)}) copy-start(bf16[96,256]{1,0:T(8,128)(2,1)S(1)} %collective-permute-done.21.refs_9_) | copy-start | bytes 147460
  154.9 1.3 copy-start.22
  156.1 0.6 copy-start.23

commit v3 on v2

v3 whole, which is shorter than its diff:
```python
import math

import jax
import jax.numpy as jnp
from jax import lax
from jax.experimental import pallas as pl
from jax.experimental.pallas import tpu as pltpu
from jax.sharding import PartitionSpec as P

DH = 128
TAG_ROWS = 16
SCORE_SCALE = 1.0 / math.sqrt(DH)
LOG2E = math.log2(math.e)
NT = (((1,), (1,)), ((), ()))
NN = (((1,), (0,)), ((), ()))
TN = (((0,), (0,)), ((), ()))
ANY = pl.BlockSpec(memory_space=pl.ANY)
VMEM = pl.BlockSpec(memory_space=pltpu.VMEM)


def dot(a, b, dims):
    return lax.dot_general(a, b, dims, preferred_element_type=jnp.float32)


def aligned(index, size):
    return pl.ds(pl.multiple_of(index * size, size), size)


def cost(flops, moved):
    return pl.CostEstimate(flops=flops, bytes_accessed=moved, transcendentals=0)


def row_deltas(out_grad, attn_out, heads):
    rows = out_grad.shape[0]

    def kernel(grad_ref, out_ref, delta_ref):
        for head in range(heads):
            cols = slice(head * DH, (head + 1) * DH)
            prod = grad_ref[:, cols].astype(jnp.float32) * out_ref[:, cols].astype(jnp.float32)
            delta_ref[head : head + 1, :] = jnp.sum(jnp.transpose(prod), axis=0, keepdims=True)

    return pl.pallas_call(
        kernel,
        out_shape=jax.ShapeDtypeStruct((heads, rows), jnp.float32),
        compiler_params=pltpu.CompilerParams(vmem_limit_bytes=32 << 20),
        cost_estimate=cost(4 * rows * heads * DH, 4 * rows * heads * DH),
        name="row_deltas",
    )(out_grad, attn_out)


def pack_kv(keys, values, head_count, chunks):
    part = keys.shape[0]

    def kernel(k_ref, v_ref, *outs):
        own = lax.axis_index("head")
        for step in range(head_count):
            for chunk in range(chunks):
                cols = aligned((own ^ step) * chunks + chunk, DH)
                at = 2 * DH * chunk
                outs[step][:, at : at + DH] = k_ref[:, cols]
                outs[step][:, at + DH : at + 2 * DH] = v_ref[:, cols]

    return pl.pallas_call(
        kernel,
        out_shape=[jax.ShapeDtypeStruct((part, 2 * chunks * DH), keys.dtype)] * head_count,
        cost_estimate=cost(0, 8 * keys.size),
        name="pack_kv",
    )(keys, values)


def pack_q(queries, head_count, chunks, whole):
    part, width = queries.shape[0], queries.shape[1] // (head_count * chunks)
    layout = []
    for step in range(head_count):
        layout += [(step, 0, chunks)] if step in whole else [(step, c, 1) for c in range(chunks)]

    def kernel(q_ref, *outs):
        own = lax.axis_index("head")
        for out, (step, chunk, count) in zip(outs, layout):
            first = pl.multiple_of(((own ^ step) * chunks + chunk) * width, width)
            out[...] = q_ref[:, pl.ds(first, count * width)]

    outs = pl.pallas_call(
        kernel,
        out_shape=[
            jax.ShapeDtypeStruct((part, count * width), queries.dtype) for _, _, count in layout
        ],
        compiler_params=pltpu.CompilerParams(vmem_limit_bytes=32 << 20),
        cost_estimate=cost(0, 4 * queries.size),
        name="pack_q",
    )(queries)
    return {(step, chunk): out for out, (step, chunk, _) in zip(outs, layout)}


def join_kv(parts, file_ids, chunks):
    head_count = len(parts)
    part, width = parts[0].shape[0], 2 * DH
    rows = part * head_count
    tag_lines = pl.cdiv(rows, width)

    def kernel(tag_ref, *refs):
        ins, outs = refs[:head_count], refs[head_count:]
        own = lax.axis_index("head")
        line = lax.broadcasted_iota(jnp.int32, (TAG_ROWS, DH), 0)
        tags = tag_ref[...].astype(jnp.float32)
        for chunk, out in enumerate(outs):
            for step in range(head_count):
                out[aligned(own ^ step, part), :] = ins[step][:, chunk * width : (chunk + 1) * width]
            for column in range(0, width, DH):
                value = jnp.zeros((TAG_ROWS, DH), jnp.float32)
                for index in range(tag_lines):
                    first = index * width + column
                    if first < rows:
                        value = jnp.where(line == index, tags[:, first : first + DH], value)
                out[rows:, column : column + DH] = value.astype(out.dtype)

    shape = jax.ShapeDtypeStruct((rows + TAG_ROWS, width), parts[0].dtype)
    return pl.pallas_call(
        kernel,
        out_shape=[shape] * chunks,
        cost_estimate=cost(0, 4 * rows * width * chunks),
        name="join_kv",
    )(file_ids[None, :], *parts)


def chunk_grads(chunk, half, q_parts, out_grad, log_sum, delta, kv_blocks):
    head_count = len(q_parts)
    part, rows = q_parts[0].shape[0], out_grad.shape[0]
    width = min(x.shape[1] for x in q_parts)
    group = width // DH
    pair = 2 if group % 2 == 0 else 1
    slots = half

    def kernel(*refs):
        lse_ref, delta_ref, g_in = refs[:3]
        q_in = refs[3 : 3 + head_count]
        kv_refs = refs[3 + head_count : 3 + head_count + slots]
        outs = refs[3 + head_count + slots :]
        dq_out = outs[:head_count]
        own_out = outs[head_count]
        dkv_out = outs[head_count + 1 : head_count + slots]
        (q_buf, g_buf, kv_buf, dkv_buf, dq_acc, dq_low, dk_acc, dv_acc, bias) = outs[
            head_count + slots : -3
        ]
        in_sem, kv_sem, out_sem = outs[-3:]
        head_index = lax.axis_index("head")
        own = lax.rem(lax.axis_index("ctx"), half)
        loads = [
            (
                ref if ref.shape[1] == width else ref.at[:, chunk * width : (chunk + 1) * width],
                q_buf.at[aligned(head_index ^ step, part)],
            )
            for step, ref in enumerate(q_in)
        ]
        loads.append((g_in.at[:, chunk * width : (chunk + 1) * width], g_buf))
        loads = [pltpu.make_async_copy(s, d, in_sem.at[i]) for i, (s, d) in enumerate(loads)]

        def kv_copy(slot):
            return pltpu.make_async_copy(kv_refs[slot], kv_buf.at[slot], kv_sem.at[slot])

        for slot in range(slots):
            if slot == 0:
                for copy in [kv_copy(slot)] + loads:
                    copy.start()
            else:
                @pl.when((own ^ slot) < own)
                def _():
                    kv_copy(slot).start()

        dq_acc[...] = jnp.zeros_like(dq_acc)
        for copy in [kv_copy(0)] + loads:
            copy.wait()

        def load_tags(slot):
            lines = kv_buf[slot, rows:, :].astype(jnp.float32)
            pieces = [
                lines[first // (2 * DH) : first // (2 * DH) + 1, : min(rows - first, 2 * DH)]
                for first in range(0, rows, 2 * DH)
            ]
            return jnp.concatenate(pieces, axis=1)

        own_tags = load_tags(0)
        own_low, own_high = jnp.min(own_tags), jnp.max(own_tags)

        def tile(slot, masked):
            key = kv_buf[slot, :rows, :DH]
            value = kv_buf[slot, :rows, DH:]
            for first in range(0, group, pair):
                heads_here = [chunk * group + first + i for i in range(pair)]
                columns = [slice((first + i) * DH, (first + i + 1) * DH) for i in range(pair)]
                query = jnp.concatenate([q_buf[:, cols] for cols in columns], axis=0)
                grad = jnp.concatenate([g_buf[:, cols] for cols in columns], axis=0)
                lse = jnp.concatenate([lse_ref[h : h + 1, :] for h in heads_here], axis=1) * LOG2E
                shift = jnp.concatenate([delta_ref[h : h + 1, :] for h in heads_here], axis=1)
                scores = dot(key, query, NT) * (SCORE_SCALE * LOG2E) - lse
                if masked:
                    scores = scores + jnp.concatenate([bias[...]] * pair, axis=1)
                probs = jnp.exp2(scores)
                dprobs = dot(value, grad, NT)
                dscores = (probs * (dprobs - shift)).astype(jnp.bfloat16)
                dv_part = dot(probs.astype(jnp.bfloat16), grad, NN)
                dk_part = dot(dscores, query, NN)
                dq_part = dot(key, dscores, TN)
                if first == 0:
                    dv_acc[...] = dv_part
                    dk_acc[...] = dk_part
                else:
                    dv_acc[...] += dv_part
                    dk_acc[...] += dk_part
                for i in range(pair):
                    dq_acc[columns[i], :] += dq_part[:, i * rows : (i + 1) * rows]

        def store(slot):
            dk = dk_acc[...] * SCORE_SCALE
            dv = dv_acc[...]

            @pl.when(slot == 0)
            def _():
                own_out[:, :DH] = dk
                own_out[:, DH:] = dv

            @pl.when(slot > 0)
            def _():
                dkv_buf[slot, :, :DH] = dk.astype(jnp.bfloat16)
                dkv_buf[slot, :, DH:] = dv.astype(jnp.bfloat16)

        def visit(slot, _):
            block = own ^ slot

            @pl.when(block <= own)
            def _():
                @pl.when(slot > 0)
                def _():
                    pltpu.make_async_copy(kv_buf.at[slot], kv_buf.at[slot], kv_sem.at[slot]).wait()

                tags = load_tags(slot)
                needed = jnp.max(tags) == own_low
                full = (jnp.min(tags) == own_high) & (slot > 0)

                @pl.when(full)
                def _():
                    tile(slot, False)
                    store(slot)

                @pl.when(jnp.logical_not(full) & (needed | (slot == 0)))
                def _():
                    key_tags = jnp.transpose(jnp.broadcast_to(tags, (8, rows)))[:, :1]
                    key_pos = block * rows + lax.broadcasted_iota(jnp.int32, (rows, rows), 0)
                    query_pos = own * rows + lax.broadcasted_iota(jnp.int32, (rows, rows), 1)
                    allowed = (key_tags == own_tags) & (key_pos <= query_pos)
                    bias[...] = jnp.where(allowed, 0.0, -1e30)
                    tile(slot, True)
                    store(slot)

                @pl.when(jnp.logical_not(full | needed | (slot == 0)))
                def _():
                    dkv_buf[slot] = jnp.zeros(dkv_buf.shape[1:], dkv_buf.dtype)

            return 0

        lax.fori_loop(0, slots, visit, 0)

        def dkv_copy(slot):
            return pltpu.make_async_copy(dkv_buf.at[slot], dkv_out[slot - 1], out_sem.at[slot])

        for slot in range(1, slots):
            @pl.when((own ^ slot) < own)
            def _():
                dkv_copy(slot).start()
        for member in range(group):
            cols = slice(member * DH, (member + 1) * DH)
            dq_low[:, cols] = jnp.transpose((dq_acc[cols, :] * SCORE_SCALE).astype(dq_low.dtype))
        sends = [
            pltpu.make_async_copy(
                dq_low.at[aligned(head_index ^ step, part)], dq_out[step], in_sem.at[step]
            )
            for step in range(head_count)
        ]
        for copy in sends:
            copy.start()
        for copy in sends:
            copy.wait()
        for slot in range(1, slots):
            @pl.when((own ^ slot) < own)
            def _():
                dkv_copy(slot).wait()

    bf16, f32 = jnp.bfloat16, jnp.float32
    heads = log_sum.shape[0]
    return pl.pallas_call(
        kernel,
        out_shape=[jax.ShapeDtypeStruct((part, width), bf16)] * head_count
        + [jax.ShapeDtypeStruct((rows, 2 * DH), f32)]
        + [jax.ShapeDtypeStruct((rows, 2 * DH), bf16)] * (slots - 1),
        in_specs=[VMEM] * 2 + [ANY] * (1 + head_count + slots),
        out_specs=[ANY] * head_count + [VMEM] + [ANY] * (slots - 1),
        scratch_shapes=[
            pltpu.VMEM((rows, width), bf16),
            pltpu.VMEM((rows, width), bf16),
            pltpu.VMEM((slots,) + kv_blocks[0].shape, bf16),
            pltpu.VMEM((slots, rows, 2 * DH), bf16),
            pltpu.VMEM((width, rows), f32),
            pltpu.VMEM((rows, width), bf16),
            pltpu.VMEM((rows, DH), f32),
            pltpu.VMEM((rows, DH), f32),
            pltpu.VMEM((rows, rows), f32),
            pltpu.SemaphoreType.DMA((head_count + 1,)),
            pltpu.SemaphoreType.DMA((slots,)),
            pltpu.SemaphoreType.DMA((slots,)),
        ],
        compiler_params=pltpu.CompilerParams(vmem_limit_bytes=48 << 20),
        cost_estimate=pl.CostEstimate(
            flops=10 * rows * rows * width * slots,
            bytes_accessed=8 * rows * width + 8 * slots * rows * 2 * DH,
            transcendentals=rows * rows * group * slots,
        ),
        name="chunk_grads",
    )(log_sum, delta, out_grad, *q_parts, *kv_blocks)


def sum_kv(parts, head_count, half):
    chunks, count = len(parts), len(parts[0])
    rows, width = parts[0][0].shape
    part = rows // head_count

    def kernel(*refs):
        ins, outs, total = refs[: chunks * count], refs[chunks * count : -1], refs[-1]
        block = lax.rem(lax.axis_index("ctx"), half)
        for chunk in range(chunks):
            value = ins[chunk * count][...]
            for step in range(1, count):
                later = jnp.full((1, width), block ^ step, jnp.int32) > block
                sent = ins[chunk * count + step][...].astype(jnp.float32)
                value = value + jnp.where(later, sent, 0.0)
            total[:, chunk * width : (chunk + 1) * width] = value.astype(jnp.bfloat16)
        index = lax.axis_index("head")
        for step in range(head_count):
            outs[step][...] = total[aligned(index ^ step, part), :]

    return pl.pallas_call(
        kernel,
        out_shape=[jax.ShapeDtypeStruct((part, chunks * width), jnp.bfloat16)] * head_count,
        scratch_shapes=[pltpu.VMEM((rows, chunks * width), jnp.bfloat16)],
        compiler_params=pltpu.CompilerParams(vmem_limit_bytes=32 << 20),
        cost_estimate=cost(4 * chunks * rows * width, 12 * chunks * rows * width),
        name="sum_kv",
    )(*[x for group in parts for x in group])


def join_grads(dq_parts, dkv_parts):
    chunks, head_count = len(dq_parts), len(dkv_parts)
    part, width = dq_parts[0][0].shape
    count = chunks * head_count

    def kernel(*refs):
        q_ins, kv_ins = refs[:count], refs[count : count + head_count]
        q_out, k_out, v_out = refs[count + head_count :]
        own = lax.axis_index("head")
        for chunk in range(chunks):
            for step in range(head_count):
                slot = (own ^ step) * chunks + chunk
                q_out[:, aligned(slot, width)] = q_ins[chunk * head_count + step][...]
                at = 2 * DH * chunk
                k_out[:, aligned(slot, DH)] = kv_ins[step][:, at : at + DH]
                v_out[:, aligned(slot, DH)] = kv_ins[step][:, at + DH : at + 2 * DH]

    kv_shape = jax.ShapeDtypeStruct((part, count * DH), jnp.bfloat16)
    return pl.pallas_call(
        kernel,
        out_shape=[jax.ShapeDtypeStruct((part, count * width), jnp.bfloat16), kv_shape, kv_shape],
        compiler_params=pltpu.CompilerParams(vmem_limit_bytes=32 << 20),
        cost_estimate=cost(0, 5 * part * count * width),
        name="join_grads",
    )(*[x for group in dq_parts for x in group], *dkv_parts)


def per_device(queries, keys, values, attn_out, out_grad, log_sum, file_ids):
    ctx_count = lax.axis_size("ctx")
    head_count = lax.axis_size("head")
    half = ctx_count // 2
    heads = log_sum.shape[0]
    chunks = keys.shape[1] // head_count // DH
    whole = (0, 1)

    def over_head(block, step):
        if step == 0:
            return block
        return lax.ppermute(block, "head", [(i, i ^ step) for i in range(head_count)])

    def over_ctx(block, step):
        pairs = [(i, i - i % half + (i % half ^ step)) for i in range(ctx_count)]
        return lax.ppermute(block, "ctx", pairs)

    steps = range(head_count)
    kv_packed = pack_kv(keys, values, head_count, chunks)
    queries, kv_packed = lax.optimization_barrier((queries, kv_packed))
    kv_parts = [over_head(kv_packed[step], step) for step in steps]
    packed = pack_q(queries, head_count, chunks, whole)
    packed, kv_parts = lax.optimization_barrier((packed, kv_parts))
    kv_joined = join_kv(kv_parts, file_ids, chunks)
    q_sent = {key: over_head(packed[key], key[0]) for key in packed}
    delta = row_deltas(out_grad, attn_out, heads)
    inputs = []
    for chunk in range(chunks):
        q_parts = [q_sent[step, 0 if step in whole else chunk] for step in steps]
        own = kv_joined[chunk]
        inputs.append((q_parts, [own] + [over_ctx(own, step) for step in range(1, half)]))

    dq_parts, dq_kept, dkv_parts = [], [], []
    for chunk in range(chunks):
        q_parts, kv_blocks = inputs[chunk]
        outs = chunk_grads(chunk, half, q_parts, out_grad, log_sum, delta, kv_blocks)
        if chunk + 1 < chunks:
            outs, inputs[chunk + 1] = lax.optimization_barrier((outs, inputs[chunk + 1]))
        if chunk:
            outs, dkv_parts, dq_parts = lax.optimization_barrier((outs, dkv_parts, dq_parts))
        back = [over_ctx(x, step) for step, x in enumerate(outs[head_count + 1 :], 1)]
        dkv_parts.append([outs[head_count]] + back)
        dq_sent = {step: over_head(outs[step], step) for step in steps if step not in whole}
        dq_kept.append([outs[step] for step in steps if step in whole])
        dq_parts.append(dq_sent)
    dq_parts = [
        [over_head(kept[step], step) if step in whole else sent[step] for step in steps]
        for kept, sent in zip(dq_kept, dq_parts)
    ]
    pieces = sum_kv(dkv_parts, head_count, half)
    return tuple(join_grads(dq_parts, [over_head(pieces[step], step) for step in steps]))


def solution(mesh):
    return jax.shard_map(
        per_device,
        mesh=mesh,
        in_specs=(
            P(("ctx", "head"), None),
            P(("ctx", "head"), None),
            P(("ctx", "head"), None),
            P("ctx", "head"),
            P("ctx", "head"),
            P("head", "ctx"),
            P("ctx"),
        ),
        out_specs=(P(("ctx", "head"), None), P(("ctx", "head"), None), P(("ctx", "head"), None)),
        check_vma=False,
    )
```

time: 220 us -> 93.5 us (0.42)
  Pallas kernels: 137 us -> 19.6 us
  waiting for transfers between devices: 40.8 us -> 25.2 us
  starting transfers between devices: 33.9 us -> 42.6 us
    pallas_call x1, Pallas kernels: 60.9 us -> 1.44 us  [join_grads(): pl.pallas_call(kernel, out_shape=[jax.ShapeDtypeStruct((part, count * wid...]
    pallas_call x5 -> x4, Pallas kernels: 60.9 us -> 4.87 us  [the longest x1 1.86 us: pack_kv(): pl.pallas_call(kernel, out_shape=[jax.ShapeDtypeStruct((part, 2 * chunks...]
    ppermute x30 -> x29, waiting for transfers between devices: 40.8 us -> 25.2 us  [the longest x17 15.8 us: over_head(): lax.ppermute(block, 'head', [(i, i ^ step) for i in range(head_count)])]
    ppermute x30 -> x29, starting transfers between devices: 33.9 us -> 42.6 us  [the longest x12 31.2 us: over_ctx(): return lax.ppermute(block, 'ctx', pairs)]
    pallas_call x2, Pallas kernels: 14.6 us -> 12.4 us  [chunk_grads(): pl.pallas_call(kernel, out_shape=[jax.ShapeDtypeStruct((part, width), bf1...]
  transfers between devices with their start and end apart: 30 -> 29, of which waited for: 13 -> 13; matrix products, arithmetic and copies ran while one was open for 0% -> 1% of each run, Pallas kernels for 24% -> 18%
where the time goes in v3:
time: 93.5 us; the launch traced here: 92.1 us
  starting transfers between devices  42.6 us (46%)
  waiting for transfers between devices  25.2 us (27%)
  Pallas kernels  19.6 us (21%)
  local copies, waits for them, and re-layouts  4.07 us (4%)
    ppermute x12, starting transfers between devices, over_ctx(): return lax.ppermute(block, 'ctx', pairs)  31.2 us
    ppermute x17, waiting for transfers between devices, over_head(): lax.ppermute(block, 'head', [(i, i ^ step) for i in range(head_count)])  15.8 us
    pallas_call x2, Pallas kernels, chunk_grads(): pl.pallas_call(kernel, out_shape=[jax.ShapeDtypeStruct((part, width), bf1...  12.4 us
    ppermute x17, starting transfers between devices, over_head(): lax.ppermute(block, 'head', [(i, i ^ step) for i in range(head_count)])  11.3 us
    ppermute x12, waiting for transfers between devices, over_ctx(): return lax.ppermute(block, 'ctx', pairs)  9.32 us
    unnamed x22, local copies, waits for them, and re-layouts  3.48 us
  transfers between devices with their start and end apart: 29, of which 13 were waited for; matrix products, arithmetic and copies ran while one was open for 1% of the time, Pallas kernels for 18%

profile of v3, /device:TPU:0, one launch (start us, length us, event | category | flops | bytes accessed | tf_op | source)
XLA Modules:
  0.0 92.1 jit_solution(7142584007300261682)
XLA Ops:
  0.6 1.9 %pack_kv.1 = (bf16[96,512]{1,0:T(8,128)(2,1)}, bf16[96,512]{1,0:T(8,128)(2,1)}, bf16[96,512]{1,0:T(8,128)(2,1)}, bf16[96,512]{1,0:T(8,128)(2,1)}) custom-call(bf16[96,1024]{1,0:T(8,128)(2,1)} %k_ref.1, bf16[96,1024]{1,0:T(8,128)(2,1)} %v_ref.1), custom_call_target="tpu_custom_call" | custom-call | bytes 786432 | tf_op jit(solution)/shard_map/pack_kv/pallas_call | solution.py:63
  2.5 0.5 collective-permute-start
  3.0 2.5 %collective-permute-start.1 = (bf16[96,512]{1,0:T(8,128)(2,1)}, bf16[96,512]{1,0:T(8,128)(2,1)S(1)}, u32[]{:S(2)}, u32[]{:S(2)}) collective-permute-start(bf16[96,512]{1,0:T(8,128)(2,1)} %get-tuple-element.93), channel_id=1, source_target_pairs={{0,2},{1,3},{2,0},{3,1},{4,6},{5,7},{6,4},{7,5},{8,10},{9,11},{10,... | collective-permute-start | bytes 294920 | tf_op jit(solution)/shard_map/ppermute | solution.py:388
  5.5 0.1 collective-permute-start.2
  5.6 1.4 %copy-done = bf16[96,8192]{1,0:T(8,128)(2,1)S(1)} copy-done((bf16[96,8192]{1,0:T(8,128)(2,1)S(1)}, bf16[96,8192]{1,0:T(8,128)(2,1)}, u32[]{:S(2)}) %copy-start) | copy-done | bytes 1572888
  7.0 0.8 pack_q.1
  7.8 0.0 collective-permute-done.refs_1_
  7.8 1.5 %collective-permute-done.1.refs_2_ = bf16[96,512]{1,0:T(8,128)(2,1)S(1)} collective-permute-done((bf16[96,512]{1,0:T(8,128)(2,1)}, bf16[96,512]{1,0:T(8,128)(2,1)S(1)}, u32[]{:S(2)}, u32[]{:S(2)}) %collective-permute-start.1) | collective-permute-done | bytes 98336 | tf_op jit(solution)/shard_map/ppermute | solution.py:388
  9.3 1.7 %collective-permute-done.2.refs_3_ = bf16[96,512]{1,0:T(8,128)(2,1)S(1)} collective-permute-done((bf16[96,512]{1,0:T(8,128)(2,1)}, bf16[96,512]{1,0:T(8,128)(2,1)S(1)}, u32[]{:S(2)}, u32[]{:S(2)}) %collective-permute-start.2) | collective-permute-done | bytes 98336 | tf_op jit(solution)/shard_map/ppermute | solution.py:388
  11.1 0.6 copy-done.9
  11.7 1.5 %collective-permute-start.4 = (bf16[96,1024]{1,0:T(8,128)(2,1)}, bf16[96,1024]{1,0:T(8,128)(2,1)S(1)}, u32[]{:S(2)}, u32[]{:S(2)}) collective-permute-start(bf16[96,1024]{1,0:T(8,128)(2,1)} %get-tuple-element.97), channel_id=1, source_target_pairs={{0,2},{1,3},{2,0},{3,1},{4,6},{5,7},{6,4},{7,5},{8,10},{9,11},{10,... | collective-permute-start | bytes 589832 | tf_op jit(solution)/shard_map/ppermute | solution.py:388
  13.2 0.0 collective-permute-start.3
  13.2 0.6 broadcast_in_dim.3.tag_ref
  13.8 1.8 %join_kv.1 = (bf16[400,256]{1,0:T(8,128)(2,1)}, bf16[400,256]{1,0:T(8,128)(2,1)}) custom-call(s32[1,384]{1,0:T(1,128)} %broadcast_in_dim.3.tag_ref, bf16[96,512]{1,0:T(8,128)(2,1)} %get-tuple-element.99.refs_0_, bf16[96,512]{1,0:T(8,128)(2,1)} %copy-done.7, bf16[96,512]{1,0:T(8,128)(2,1)} %copy-done.8, bf16[96,512]{1,0:T(8,128)(2,1)} %copy-done.9), custom_call_target="tpu_custom_call" | custom-call | bytes 786432 | tf_op jit(solution)/shard_map/join_kv/pallas_call | solution.py:118
  15.7 2.5 %collective-permute-start.8 = (bf16[400,256]{1,0:T(8,128)(2,1)}, bf16[400,256]{1,0:T(8,128)(2,1)S(1)}, u32[]{:S(2)}, u32[]{:S(2)}) collective-permute-start(bf16[400,256]{1,0:T(8,128)(2,1)} %get-tuple-element.103.refs_7_), channel_id=1, source_target_pairs={{0,12},{4,8},{8,4},{12,0},{16,28},{20,24},{24,20},{28,16},{1,13},{... | collective-permute-start | bytes 614408 | tf_op jit(solution)/shard_map/ppermute | solution.py:392
  18.2 0.4 collective-permute-start.7
  18.6 0.5 collective-permute-start.6
  19.1 0.0 collective-permute-done.4.refs_5_
  19.2 0.3 collective-permute-start.5
  19.5 1.4 %copy-done.2 = bf16[384,2048]{1,0:T(8,128)(2,1)S(1)} copy-done((bf16[384,2048]{1,0:T(8,128)(2,1)S(1)}, bf16[384,2048]{1,0:T(8,128)(2,1)}, u32[]{:S(2)}) %copy-start.2) | copy-done | bytes 1572888
  20.9 0.9 row_deltas.1.refs_1_
  21.8 4.4 %collective-permute-done.5.refs_6_ = bf16[96,1024]{1,0:T(8,128)(2,1)S(1)} collective-permute-done((bf16[96,1024]{1,0:T(8,128)(2,1)S(1)}, bf16[96,1024]{1,0:T(8,128)(2,1)S(1)}, u32[]{:S(2)}, u32[]{:S(2)}) %collective-permute-start.5) | collective-permute-done | bytes 196640 | tf_op jit(solution)/shard_map/ppermute | solution.py:388
  26.2 2.5 %collective-permute-start.13 = (bf16[400,256]{1,0:T(8,128)(2,1)S(1)}, bf16[400,256]{1,0:T(8,128)(2,1)S(1)}, u32[]{:S(2)}, u32[]{:S(2)}) collective-permute-start(bf16[400,256]{1,0:T(8,128)(2,1)S(1)} %copy-done.4), channel_id=1, source_target_pairs={{0,12},{4,8},{8,4},{12,0},{16,28},{20,24},{24,20},{28,16},{1,13},{... | collective-permute-start | bytes 614408 | tf_op jit(solution)/shard_map/ppermute | solution.py:392
  28.7 0.0 collective-permute-done.8.refs_10_
  28.7 0.5 collective-permute-start.12
  29.2 0.0 collective-permute-done.7.refs_9_
  29.2 0.5 collective-permute-start.11
  29.7 0.0 collective-permute-done.6.refs_8_
  29.7 1.0 %collective-permute-start.9 = (bf16[96,1024]{1,0:T(8,128)(2,1)S(1)}, bf16[96,1024]{1,0:T(8,128)(2,1)S(1)}, u32[]{:S(2)}, u32[]{:S(2)}) collective-permute-start(bf16[96,1024]{1,0:T(8,128)(2,1)S(1)} %get-tuple-element.112), channel_id=1, source_target_pairs={{0,2},{1,3},{2,0},{3,1},{4,6},{5,7},{6,4},{7,5},{8,10},{9,11},{10,... | collective-permute-start | bytes 589832 | tf_op jit(solution)/shard_map/ppermute | solution.py:388
  30.8 0.0 collective-permute-start.10
  30.8 6.1 %chunk_grads.2 = (bf16[96,1024]{1,0:T(8,128)(2,1)S(1)}, bf16[96,1024]{1,0:T(8,128)(2,1)S(1)}, bf16[96,1024]{1,0:T(8,128)(2,1)S(1)}, bf16[96,1024]{1,0:T(8,128)(2...) custom-call(f32[16,384]{1,0:T(8,128)S(1)} %copy-done.6, ...), custom_call_target="tpu_custom_call" | custom-call | flops 6039797760 | bytes 6291456 | tf_op jit(solution)/shard_map/chunk_grads/pallas_call | solution.py:290
  36.9 0.7 collective-permute-done.9.refs_5_
  37.6 0.6 collective-permute-done.10.refs_6_
  38.2 0.0 collective-permute-done.13.refs_10_
  38.2 0.3 collective-permute-done.12.refs_9_
  38.6 0.0 collective-permute-done.11.refs_8_
  38.6 3.7 %collective-permute-start.15 = (bf16[384,256]{1,0:T(8,128)(2,1)S(1)}, bf16[384,256]{1,0:T(8,128)(2,1)S(1)}, u32[]{:S(2)}, u32[]{:S(2)}) collective-permute-start(bf16[384,256]{1,0:T(8,128)(2,1)S(1)} %get-tuple-element.134), channel_id=1, source_target_pairs={{0,4},{4,0},{8,12},{12,8},{16,20},{20,16},{24,28},{28,24},{1,5},{5... | collective-permute-start | bytes 589832 | tf_op jit(solution)/shard_map/ppermute | solution.py:392
  42.3 9.0 %collective-permute-start.16 = (bf16[384,256]{1,0:T(8,128)(2,1)S(1)}, bf16[384,256]{1,0:T(8,128)(2,1)S(1)}, u32[]{:S(2)}, u32[]{:S(2)}) collective-permute-start(bf16[384,256]{1,0:T(8,128)(2,1)S(1)} %get-tuple-element.135), channel_id=1, source_target_pairs={{0,8},{4,12},{8,0},{12,4},{16,24},{20,28},{24,16},{28,20},{1,9},{5... | collective-permute-start | bytes 589832 | tf_op jit(solution)/shard_map/ppermute | solution.py:392
  51.3 1.0 %collective-permute-start.18 = (bf16[96,1024]{1,0:T(8,128)(2,1)S(1)}, bf16[96,1024]{1,0:T(8,128)(2,1)S(1)}, u32[]{:S(2)}, u32[]{:S(2)}) collective-permute-start(bf16[96,1024]{1,0:T(8,128)(2,1)S(1)} %get-tuple-element.137), channel_id=1, source_target_pairs={{0,2},{1,3},{2,0},{3,1},{4,6},{5,7},{6,4},{7,5},{8,10},{9,11},{10,... | collective-permute-start | bytes 589832 | tf_op jit(solution)/shard_map/ppermute | solution.py:388
  52.3 0.9 collective-permute-start.19
  53.2 6.3 %chunk_grads.3 = (bf16[96,1024]{1,0:T(8,128)(2,1)S(1)}, bf16[96,1024]{1,0:T(8,128)(2,1)S(1)}, bf16[96,1024]{1,0:T(8,128)(2,1)S(1)}, bf16[96,1024]{1,0:T(8,128)(2...) custom-call(f32[16,384]{1,0:T(8,128)S(1)} %copy-done.6, ...), custom_call_target="tpu_custom_call" | custom-call | flops 6039797760 | bytes 6291456 | tf_op jit(solution)/shard_map/chunk_grads/pallas_call | solution.py:290
  59.5 0.0 collective-permute-done.16.refs_2_
  59.5 1.2 %collective-permute-done.17.refs_3_ = bf16[384,256]{1,0:T(8,128)(2,1)S(1)} collective-permute-done((bf16[384,256]{1,0:T(8,128)(2,1)S(1)}, bf16[384,256]{1,0:T(8,128)(2,1)S(1)}, u32[]{:S(2)}, u32[]{:S(2)}) %collective-permute-start.17) | collective-permute-done | bytes 196640 | tf_op jit(solution)/shard_map/ppermute | solution.py:392
  60.7 1.9 %collective-permute-done.19.refs_3_ = bf16[96,1024]{1,0:T(8,128)(2,1)S(1)} collective-permute-done((bf16[96,1024]{1,0:T(8,128)(2,1)S(1)}, bf16[96,1024]{1,0:T(8,128)(2,1)S(1)}, u32[]{:S(2)}, u32[]{:S(2)}) %collective-permute-start.19) | collective-permute-done | bytes 196640 | tf_op jit(solution)/shard_map/ppermute | solution.py:388
  62.5 2.3 %collective-permute-start.23 = (bf16[384,256]{1,0:T(8,128)(2,1)S(1)}, bf16[384,256]{1,0:T(8,128)(2,1)S(1)}, u32[]{:S(2)}, u32[]{:S(2)}) collective-permute-start(bf16[384,256]{1,0:T(8,128)(2,1)S(1)} %get-tuple-element.150), channel_id=1, source_target_pairs={{0,4},{4,0},{8,12},{12,8},{16,20},{20,16},{24,28},{28,24},{1,5},{5... | collective-permute-start | bytes 589832 | tf_op jit(solution)/shard_map/ppermute | solution.py:392
  64.8 9.2 %collective-permute-start.24 = (bf16[384,256]{1,0:T(8,128)(2,1)S(1)}, bf16[384,256]{1,0:T(8,128)(2,1)S(1)}, u32[]{:S(2)}, u32[]{:S(2)}) collective-permute-start(bf16[384,256]{1,0:T(8,128)(2,1)S(1)} %get-tuple-element.151), channel_id=1, source_target_pairs={{0,8},{4,12},{8,0},{12,4},{16,24},{20,28},{24,16},{28,20},{1,9},{5... | collective-permute-start | bytes 589832 | tf_op jit(solution)/shard_map/ppermute | solution.py:392
  74.0 0.0 collective-permute-start.25
  74.0 0.5 collective-permute-start.20
  74.5 0.0 collective-permute-done.23.refs_5_
  74.5 1.0 %collective-permute-start.21 = (bf16[96,1024]{1,0:T(8,128)(2,1)S(1)}, bf16[96,1024]{1,0:T(8,128)(2,1)S(1)}, u32[]{:S(2)}, u32[]{:S(2)}) collective-permute-start(bf16[96,1024]{1,0:T(8,128)(2,1)S(1)} %get-tuple-element.143), channel_id=1, source_target_pairs={{0,2},{1,3},{2,0},{3,1},{4,6},{5,7},{6,4},{7,5},{8,10},{9,11},{10,... | collective-permute-start | bytes 589832 | tf_op jit(solution)/shard_map/ppermute | solution.py:388
  75.5 4.1 %collective-permute-done.24.refs_6_ = bf16[384,256]{1,0:T(8,128)(2,1)S(1)} collective-permute-done((bf16[384,256]{1,0:T(8,128)(2,1)S(1)}, bf16[384,256]{1,0:T(8,128)(2,1)S(1)}, u32[]{:S(2)}, u32[]{:S(2)}) %collective-permute-start.24) | collective-permute-done | bytes 196640 | tf_op jit(solution)/shard_map/ppermute | solution.py:392
  79.7 3.7 %collective-permute-done.25.refs_7_ = bf16[384,256]{1,0:T(8,128)(2,1)S(1)} collective-permute-done((bf16[384,256]{1,0:T(8,128)(2,1)S(1)}, bf16[384,256]{1,0:T(8,128)(2,1)S(1)}, u32[]{:S(2)}, u32[]{:S(2)}) %collective-permute-start.25) | collective-permute-done | bytes 196640 | tf_op jit(solution)/shard_map/ppermute | solution.py:392
  83.3 0.4 sum_kv.1
  83.8 0.1 collective-permute-start.26
  83.8 0.0 collective-permute-done.14.refs_1_
  83.8 1.1 %collective-permute-start.27 = (bf16[96,512]{1,0:T(8,128)(2,1)S(1)}, bf16[96,512]{1,0:T(8,128)(2,1)S(1)}, u32[]{:S(2)}, u32[]{:S(2)}) collective-permute-start(bf16[96,512]{1,0:T(8,128)(2,1)S(1)} %get-tuple-element.155), channel_id=1, source_target_pairs={{0,2},{1,3},{2,0},{3,1},{4,6},{5,7},{6,4},{7,5},{8,10},{9,11},{10,... | collective-permute-start | bytes 294920 | tf_op jit(solution)/shard_map/ppermute | solution.py:388
  84.9 0.0 collective-permute-done.20.refs_5_
  84.9 0.8 collective-permute-start.28
  85.7 0.0 collective-permute-done.21.refs_6_
  85.7 0.8 collective-permute-done.22.refs_7_
  86.5 0.0 collective-permute-done.26.refs_9_
  86.5 3.0 %collective-permute-done.27.refs_10_ = bf16[96,512]{1,0:T(8,128)(2,1)S(1)} collective-permute-done((bf16[96,512]{1,0:T(8,128)(2,1)S(1)}, bf16[96,512]{1,0:T(8,128)(2,1)S(1)}, u32[]{:S(2)}, u32[]{:S(2)}) %collective-permute-start.27) | collective-permute-done | bytes 98336 | tf_op jit(solution)/shard_map/ppermute | solution.py:388
  89.5 1.2 %collective-permute-done.28.refs_11_ = bf16[96,512]{1,0:T(8,128)(2,1)S(1)} collective-permute-done((bf16[96,512]{1,0:T(8,128)(2,1)S(1)}, bf16[96,512]{1,0:T(8,128)(2,1)S(1)}, u32[]{:S(2)}, u32[]{:S(2)}) %collective-permute-start.28) | collective-permute-done | bytes 98336 | tf_op jit(solution)/shard_map/ppermute | solution.py:388
  90.7 1.4 %join_grads.1 = (bf16[96,8192]{1,0:T(8,128)(2,1)}, bf16[96,1024]{1,0:T(8,128)(2,1)}, bf16[96,1024]{1,0:T(8,128)(2,1)}) custom-call(bf16[96,1024]{1,0:T(8,128)(2,1)S(1)} %get-tuple-element.115.refs_0_, bf16[96,1024]{1,0:T(8,128)(2,1)S(1)} %collective-permute-done.14.refs_1_, bf16[96,1024]{1,0:T(8,128)(2,1)S(1)} %collective-permute-done.18.refs_2_, ...), custom_call_target="tpu_custom_call" | custom-call | bytes 3932160 | tf_op jit(solution)/shard_map/join_grads/pallas_call | solution.py:368
  (25 shorter events, 0.1 us)
Async XLA Ops:
  0.6 12.6 %copy-start.10 = (s32[384]{0:T(512)S(1)}, s32[384]{0:T(512)}, u32[]{:S(2)}) copy-start(s32[384]{0:T(512)} %param.13) | copy-start | bytes 4612
  2.5 5.3 %collective-permute-start = (bf16[96,512]{1,0:T(8,128)(2,1)}, bf16[96,512]{1,0:T(8,128)(2,1)S(1)}, u32[]{:S(2)}, u32[]{:S(2)}) collective-permute-start(bf16[96,512]{1,0:T(8,128)(2,1)} %get-tuple-element.92), channel_id=1, source_target_pairs={{0,1},{1,0},{2,3},{3,2},{4,5},{5,4},{6,7},{7,6},{8,9},{9,8},{10,11... | collective-permute-start | bytes 294920 | tf_op jit(solution)/shard_map/ppermute | solution.py:388
  3.0 6.4 %collective-permute-start.1 = (bf16[96,512]{1,0:T(8,128)(2,1)}, bf16[96,512]{1,0:T(8,128)(2,1)S(1)}, u32[]{:S(2)}, u32[]{:S(2)}) collective-permute-start(bf16[96,512]{1,0:T(8,128)(2,1)} %get-tuple-element.93), channel_id=1, source_target_pairs={{0,2},{1,3},{2,0},{3,1},{4,6},{5,7},{6,4},{7,5},{8,10},{9,11},{10,... | collective-permute-start | bytes 294920 | tf_op jit(solution)/shard_map/ppermute | solution.py:388
  5.5 5.6 %collective-permute-start.2 = (bf16[96,512]{1,0:T(8,128)(2,1)}, bf16[96,512]{1,0:T(8,128)(2,1)S(1)}, u32[]{:S(2)}, u32[]{:S(2)}) collective-permute-start(bf16[96,512]{1,0:T(8,128)(2,1)} %get-tuple-element.94), channel_id=1, source_target_pairs={{0,3},{1,2},{2,1},{3,0},{4,7},{5,6},{6,5},{7,4},{8,11},{9,10},{10,... | collective-permute-start | bytes 294920 | tf_op jit(solution)/shard_map/ppermute | solution.py:388
  5.6 1.4 %copy-start = (bf16[96,8192]{1,0:T(8,128)(2,1)S(1)}, bf16[96,8192]{1,0:T(8,128)(2,1)}, u32[]{:S(2)}) copy-start(bf16[96,8192]{1,0:T(8,128)(2,1)} %q_ref) | copy-start | bytes 4718596
  7.0 12.4 %copy-start.1 = (bf16[384,2048]{1,0:T(8,128)(2,1)S(1)}, bf16[384,2048]{1,0:T(8,128)(2,1)}, u32[]{:S(2)}) copy-start(bf16[384,2048]{1,0:T(8,128)(2,1)} %out_ref.1) | copy-start | bytes 4718596
  7.8 3.3 %copy-start.7 = (bf16[96,512]{1,0:T(8,128)(2,1)}, bf16[96,512]{1,0:T(8,128)(2,1)S(1)}, u32[]{:S(2)}) copy-start(bf16[96,512]{1,0:T(8,128)(2,1)S(1)} %collective-permute-done.refs_1_) | copy-start | bytes 294916
  9.3 1.7 %copy-start.8 = (bf16[96,512]{1,0:T(8,128)(2,1)}, bf16[96,512]{1,0:T(8,128)(2,1)S(1)}, u32[]{:S(2)}) copy-start(bf16[96,512]{1,0:T(8,128)(2,1)S(1)} %collective-permute-done.1.refs_2_) | copy-start | bytes 294916
  11.1 0.6 copy-start.9
  11.7 7.5 %collective-permute-start.4 = (bf16[96,1024]{1,0:T(8,128)(2,1)}, bf16[96,1024]{1,0:T(8,128)(2,1)S(1)}, u32[]{:S(2)}, u32[]{:S(2)}) collective-permute-start(bf16[96,1024]{1,0:T(8,128)(2,1)} %get-tuple-element.97), channel_id=1, source_target_pairs={{0,2},{1,3},{2,0},{3,1},{4,6},{5,7},{6,4},{7,5},{8,10},{9,11},{10,... | collective-permute-start | bytes 589832 | tf_op jit(solution)/shard_map/ppermute | solution.py:388
  13.2 17.5 %collective-permute-start.3 = (bf16[96,2048]{1,0:T(8,128)(2,1)S(1)}, bf16[96,2048]{1,0:T(8,128)(2,1)S(1)}, u32[]{:S(2)}, u32[]{:S(2)}) collective-permute-start(bf16[96,2048]{1,0:T(8,128)(2,1)S(1)} %get-tuple-element.96), channel_id=1, source_target_pairs={{0,1},{1,0},{2,3},{3,2},{4,5},{5,4},{6,7},{7,6},{8,9},{9,8},{10,11... | collective-permute-start | bytes 1179656 | tf_op jit(solution)/shard_map/ppermute | solution.py:388
  15.7 13.1 %collective-permute-start.8 = (bf16[400,256]{1,0:T(8,128)(2,1)}, bf16[400,256]{1,0:T(8,128)(2,1)S(1)}, u32[]{:S(2)}, u32[]{:S(2)}) collective-permute-start(bf16[400,256]{1,0:T(8,128)(2,1)} %get-tuple-element.103.refs_7_), channel_id=1, source_target_pairs={{0,12},{4,8},{8,4},{12,0},{16,28},{20,24},{24,20},{28,16},{1,13},{... | collective-permute-start | bytes 614408 | tf_op jit(solution)/shard_map/ppermute | solution.py:392
  18.2 11.0 %collective-permute-start.7 = (bf16[400,256]{1,0:T(8,128)(2,1)}, bf16[400,256]{1,0:T(8,128)(2,1)S(1)}, u32[]{:S(2)}, u32[]{:S(2)}) collective-permute-start(bf16[400,256]{1,0:T(8,128)(2,1)} %get-tuple-element.103.refs_7_), channel_id=1, source_target_pairs={{0,8},{4,12},{8,0},{12,4},{16,24},{20,28},{24,16},{28,20},{1,9},{5... | collective-permute-start | bytes 614408 | tf_op jit(solution)/shard_map/ppermute | solution.py:392
  18.6 11.1 %collective-permute-start.6 = (bf16[400,256]{1,0:T(8,128)(2,1)}, bf16[400,256]{1,0:T(8,128)(2,1)S(1)}, u32[]{:S(2)}, u32[]{:S(2)}) collective-permute-start(bf16[400,256]{1,0:T(8,128)(2,1)} %get-tuple-element.103.refs_7_), channel_id=1, source_target_pairs={{0,4},{4,0},{8,12},{12,8},{16,20},{20,16},{24,28},{28,24},{1,5},{5... | collective-permute-start | bytes 614408 | tf_op jit(solution)/shard_map/ppermute | solution.py:392
  19.2 7.1 %collective-permute-start.5 = (bf16[96,1024]{1,0:T(8,128)(2,1)S(1)}, bf16[96,1024]{1,0:T(8,128)(2,1)S(1)}, u32[]{:S(2)}, u32[]{:S(2)}) collective-permute-start(bf16[96,1024]{1,0:T(8,128)(2,1)S(1)} %get-tuple-element.98), channel_id=1, source_target_pairs={{0,3},{1,2},{2,1},{3,0},{4,7},{5,6},{6,5},{7,4},{8,11},{9,10},{10,... | collective-permute-start | bytes 589832 | tf_op jit(solution)/shard_map/ppermute | solution.py:388
  19.5 1.4 %copy-start.2 = (bf16[384,2048]{1,0:T(8,128)(2,1)S(1)}, bf16[384,2048]{1,0:T(8,128)(2,1)}, u32[]{:S(2)}) copy-start(bf16[384,2048]{1,0:T(8,128)(2,1)} %refs_2_.3) | copy-start | bytes 4718596
  20.9 5.3 %copy-start.4 = (bf16[400,256]{1,0:T(8,128)(2,1)S(1)}, bf16[400,256]{1,0:T(8,128)(2,1)}, u32[]{:S(2)}) copy-start(bf16[400,256]{1,0:T(8,128)(2,1)} %get-tuple-element.121.refs_7_) | copy-start | bytes 614404
  20.9 9.9 %copy-start.3 = (bf16[384,2048]{1,0:T(8,128)(2,1)S(1)}, bf16[384,2048]{1,0:T(8,128)(2,1)}, u32[]{:S(2)}) copy-start(bf16[384,2048]{1,0:T(8,128)(2,1)} %refs_2_.3) | copy-start | bytes 4718596
  20.9 9.9 %copy-start.5 = (bf16[400,256]{1,0:T(8,128)(2,1)S(1)}, bf16[400,256]{1,0:T(8,128)(2,1)}, u32[]{:S(2)}) copy-start(bf16[400,256]{1,0:T(8,128)(2,1)} %get-tuple-element.103.refs_7_) | copy-start | bytes 614404
  20.9 9.9 %copy-start.6 = (f32[16,384]{1,0:T(8,128)S(1)}, f32[16,384]{1,0:T(8,128)}, u32[]{:S(2)}) copy-start(f32[16,384]{1,0:T(8,128)} %refs_0_.3) | copy-start | bytes 73732
  26.2 12.0 %collective-permute-start.13 = (bf16[400,256]{1,0:T(8,128)(2,1)S(1)}, bf16[400,256]{1,0:T(8,128)(2,1)S(1)}, u32[]{:S(2)}, u32[]{:S(2)}) collective-permute-start(bf16[400,256]{1,0:T(8,128)(2,1)S(1)} %copy-done.4), channel_id=1, source_target_pairs={{0,12},{4,8},{8,4},{12,0},{16,28},{20,24},{24,20},{28,16},{1,13},{... | collective-permute-start | bytes 614408 | tf_op jit(solution)/shard_map/ppermute | solution.py:392
  28.7 9.8 %collective-permute-start.12 = (bf16[400,256]{1,0:T(8,128)(2,1)S(1)}, bf16[400,256]{1,0:T(8,128)(2,1)S(1)}, u32[]{:S(2)}, u32[]{:S(2)}) collective-permute-start(bf16[400,256]{1,0:T(8,128)(2,1)S(1)} %copy-done.4), channel_id=1, source_target_pairs={{0,8},{4,12},{8,0},{12,4},{16,24},{20,28},{24,16},{28,20},{1,9},{5... | collective-permute-start | bytes 614408 | tf_op jit(solution)/shard_map/ppermute | solution.py:392
  29.2 9.4 %collective-permute-start.11 = (bf16[400,256]{1,0:T(8,128)(2,1)S(1)}, bf16[400,256]{1,0:T(8,128)(2,1)S(1)}, u32[]{:S(2)}, u32[]{:S(2)}) collective-permute-start(bf16[400,256]{1,0:T(8,128)(2,1)S(1)} %copy-done.4), channel_id=1, source_target_pairs={{0,4},{4,0},{8,12},{12,8},{16,20},{20,16},{24,28},{28,24},{1,5},{5... | collective-permute-start | bytes 614408 | tf_op jit(solution)/shard_map/ppermute | solution.py:392
  29.7 7.8 %collective-permute-start.9 = (bf16[96,1024]{1,0:T(8,128)(2,1)S(1)}, bf16[96,1024]{1,0:T(8,128)(2,1)S(1)}, u32[]{:S(2)}, u32[]{:S(2)}) collective-permute-start(bf16[96,1024]{1,0:T(8,128)(2,1)S(1)} %get-tuple-element.112), channel_id=1, source_target_pairs={{0,2},{1,3},{2,0},{3,1},{4,6},{5,7},{6,4},{7,5},{8,10},{9,11},{10,... | collective-permute-start | bytes 589832 | tf_op jit(solution)/shard_map/ppermute | solution.py:388
  30.8 7.5 %collective-permute-start.10 = (bf16[96,1024]{1,0:T(8,128)(2,1)S(1)}, bf16[96,1024]{1,0:T(8,128)(2,1)S(1)}, u32[]{:S(2)}, u32[]{:S(2)}) collective-permute-start(bf16[96,1024]{1,0:T(8,128)(2,1)S(1)} %get-tuple-element.113), channel_id=1, source_target_pairs={{0,3},{1,2},{2,1},{3,0},{4,7},{5,6},{6,5},{7,4},{8,11},{9,10},{10,... | collective-permute-start | bytes 589832 | tf_op jit(solution)/shard_map/ppermute | solution.py:388
  38.6 20.9 %collective-permute-start.15 = (bf16[384,256]{1,0:T(8,128)(2,1)S(1)}, bf16[384,256]{1,0:T(8,128)(2,1)S(1)}, u32[]{:S(2)}, u32[]{:S(2)}) collective-permute-start(bf16[384,256]{1,0:T(8,128)(2,1)S(1)} %get-tuple-element.134), channel_id=1, source_target_pairs={{0,4},{4,0},{8,12},{12,8},{16,20},{20,16},{24,28},{28,24},{1,5},{5... | collective-permute-start | bytes 589832 | tf_op jit(solution)/shard_map/ppermute | solution.py:392
  42.3 17.2 %collective-permute-start.16 = (bf16[384,256]{1,0:T(8,128)(2,1)S(1)}, bf16[384,256]{1,0:T(8,128)(2,1)S(1)}, u32[]{:S(2)}, u32[]{:S(2)}) collective-permute-start(bf16[384,256]{1,0:T(8,128)(2,1)S(1)} %get-tuple-element.135), channel_id=1, source_target_pairs={{0,8},{4,12},{8,0},{12,4},{16,24},{20,28},{24,16},{28,20},{1,9},{5... | collective-permute-start | bytes 589832 | tf_op jit(solution)/shard_map/ppermute | solution.py:392
  51.3 9.4 %collective-permute-start.17 = (bf16[384,256]{1,0:T(8,128)(2,1)S(1)}, bf16[384,256]{1,0:T(8,128)(2,1)S(1)}, u32[]{:S(2)}, u32[]{:S(2)}) collective-permute-start(bf16[384,256]{1,0:T(8,128)(2,1)S(1)} %get-tuple-element.136), channel_id=1, source_target_pairs={{0,12},{4,8},{8,4},{12,0},{16,28},{20,24},{24,20},{28,16},{1,13},{... | collective-permute-start | bytes 589832 | tf_op jit(solution)/shard_map/ppermute | solution.py:392
  51.3 9.4 %collective-permute-start.18 = (bf16[96,1024]{1,0:T(8,128)(2,1)S(1)}, bf16[96,1024]{1,0:T(8,128)(2,1)S(1)}, u32[]{:S(2)}, u32[]{:S(2)}) collective-permute-start(bf16[96,1024]{1,0:T(8,128)(2,1)S(1)} %get-tuple-element.137), channel_id=1, source_target_pairs={{0,2},{1,3},{2,0},{3,1},{4,6},{5,7},{6,4},{7,5},{8,10},{9,11},{10,... | collective-permute-start | bytes 589832 | tf_op jit(solution)/shard_map/ppermute | solution.py:388
  52.3 10.2 %collective-permute-start.19 = (bf16[96,1024]{1,0:T(8,128)(2,1)S(1)}, bf16[96,1024]{1,0:T(8,128)(2,1)S(1)}, u32[]{:S(2)}, u32[]{:S(2)}) collective-permute-start(bf16[96,1024]{1,0:T(8,128)(2,1)S(1)} %get-tuple-element.138), channel_id=1, source_target_pairs={{0,3},{1,2},{2,1},{3,0},{4,7},{5,6},{6,5},{7,4},{8,11},{9,10},{10,... | collective-permute-start | bytes 589832 | tf_op jit(solution)/shard_map/ppermute | solution.py:388
  62.5 12.0 %collective-permute-start.23 = (bf16[384,256]{1,0:T(8,128)(2,1)S(1)}, bf16[384,256]{1,0:T(8,128)(2,1)S(1)}, u32[]{:S(2)}, u32[]{:S(2)}) collective-permute-start(bf16[384,256]{1,0:T(8,128)(2,1)S(1)} %get-tuple-element.150), channel_id=1, source_target_pairs={{0,4},{4,0},{8,12},{12,8},{16,20},{20,16},{24,28},{28,24},{1,5},{5... | collective-permute-start | bytes 589832 | tf_op jit(solution)/shard_map/ppermute | solution.py:392
  64.8 14.9 %collective-permute-start.24 = (bf16[384,256]{1,0:T(8,128)(2,1)S(1)}, bf16[384,256]{1,0:T(8,128)(2,1)S(1)}, u32[]{:S(2)}, u32[]{:S(2)}) collective-permute-start(bf16[384,256]{1,0:T(8,128)(2,1)S(1)} %get-tuple-element.151), channel_id=1, source_target_pairs={{0,8},{4,12},{8,0},{12,4},{16,24},{20,28},{24,16},{28,20},{1,9},{5... | collective-permute-start | bytes 589832 | tf_op jit(solution)/shard_map/ppermute | solution.py:392
  74.0 9.3 %collective-permute-start.25 = (bf16[384,256]{1,0:T(8,128)(2,1)S(1)}, bf16[384,256]{1,0:T(8,128)(2,1)S(1)}, u32[]{:S(2)}, u32[]{:S(2)}) collective-permute-start(bf16[384,256]{1,0:T(8,128)(2,1)S(1)} %get-tuple-element.152), channel_id=1, source_target_pairs={{0,12},{4,8},{8,4},{12,0},{16,28},{20,24},{24,20},{28,16},{1,13},{... | collective-permute-start | bytes 589832 | tf_op jit(solution)/shard_map/ppermute | solution.py:392
  74.0 9.8 %collective-permute-start.14 = (bf16[96,1024]{1,0:T(8,128)(2,1)S(1)}, bf16[96,1024]{1,0:T(8,128)(2,1)S(1)}, u32[]{:S(2)}, u32[]{:S(2)}) collective-permute-start(bf16[96,1024]{1,0:T(8,128)(2,1)S(1)} %get-tuple-element.116), channel_id=1, source_target_pairs={{0,1},{1,0},{2,3},{3,2},{4,5},{5,4},{6,7},{7,6},{8,9},{9,8},{10,11... | collective-permute-start | bytes 589832 | tf_op jit(solution)/shard_map/ppermute | solution.py:388
  74.0 10.9 %collective-permute-start.20 = (bf16[96,1024]{1,0:T(8,128)(2,1)S(1)}, bf16[96,1024]{1,0:T(8,128)(2,1)S(1)}, u32[]{:S(2)}, u32[]{:S(2)}) collective-permute-start(bf16[96,1024]{1,0:T(8,128)(2,1)S(1)} %get-tuple-element.142), channel_id=1, source_target_pairs={{0,1},{1,0},{2,3},{3,2},{4,5},{5,4},{6,7},{7,6},{8,9},{9,8},{10,11... | collective-permute-start | bytes 589832 | tf_op jit(solution)/shard_map/ppermute | solution.py:388
  74.5 11.2 %collective-permute-start.21 = (bf16[96,1024]{1,0:T(8,128)(2,1)S(1)}, bf16[96,1024]{1,0:T(8,128)(2,1)S(1)}, u32[]{:S(2)}, u32[]{:S(2)}) collective-permute-start(bf16[96,1024]{1,0:T(8,128)(2,1)S(1)} %get-tuple-element.143), channel_id=1, source_target_pairs={{0,2},{1,3},{2,0},{3,1},{4,6},{5,7},{6,4},{7,5},{8,10},{9,11},{10,... | collective-permute-start | bytes 589832 | tf_op jit(solution)/shard_map/ppermute | solution.py:388
  79.7 6.8 %collective-permute-start.22 = (bf16[96,1024]{1,0:T(8,128)(2,1)S(1)}, bf16[96,1024]{1,0:T(8,128)(2,1)S(1)}, u32[]{:S(2)}, u32[]{:S(2)}) collective-permute-start(bf16[96,1024]{1,0:T(8,128)(2,1)S(1)} %get-tuple-element.144), channel_id=1, source_target_pairs={{0,3},{1,2},{2,1},{3,0},{4,7},{5,6},{6,5},{7,4},{8,11},{9,10},{10,... | collective-permute-start | bytes 589832 | tf_op jit(solution)/shard_map/ppermute | solution.py:388
  83.8 2.7 %collective-permute-start.26 = (bf16[96,512]{1,0:T(8,128)(2,1)S(1)}, bf16[96,512]{1,0:T(8,128)(2,1)S(1)}, u32[]{:S(2)}, u32[]{:S(2)}) collective-permute-start(bf16[96,512]{1,0:T(8,128)(2,1)S(1)} %get-tuple-element.154), channel_id=1, source_target_pairs={{0,1},{1,0},{2,3},{3,2},{4,5},{5,4},{6,7},{7,6},{8,9},{9,8},{10,11... | collective-permute-start | bytes 294920 | tf_op jit(solution)/shard_map/ppermute | solution.py:388
  83.8 5.7 %collective-permute-start.27 = (bf16[96,512]{1,0:T(8,128)(2,1)S(1)}, bf16[96,512]{1,0:T(8,128)(2,1)S(1)}, u32[]{:S(2)}, u32[]{:S(2)}) collective-permute-start(bf16[96,512]{1,0:T(8,128)(2,1)S(1)} %get-tuple-element.155), channel_id=1, source_target_pairs={{0,2},{1,3},{2,0},{3,1},{4,6},{5,7},{6,4},{7,5},{8,10},{9,11},{10,... | collective-permute-start | bytes 294920 | tf_op jit(solution)/shard_map/ppermute | solution.py:388
  84.9 5.8 %collective-permute-start.28 = (bf16[96,512]{1,0:T(8,128)(2,1)S(1)}, bf16[96,512]{1,0:T(8,128)(2,1)S(1)}, u32[]{:S(2)}, u32[]{:S(2)}) collective-permute-start(bf16[96,512]{1,0:T(8,128)(2,1)S(1)} %get-tuple-element.156), channel_id=1, source_target_pairs={{0,3},{1,2},{2,1},{3,0},{4,7},{5,6},{6,5},{7,4},{8,11},{9,10},{10,... | collective-permute-start | bytes 294920 | tf_op jit(solution)/shard_map/ppermute | solution.py:388

commit v4 on v3

v4 whole, which is shorter than its diff:
```python
import math

import jax
import jax.numpy as jnp
from jax import lax
from jax.experimental import pallas as pl
from jax.experimental.pallas import tpu as pltpu
from jax.sharding import PartitionSpec as P

DH = 128
TAG_ROWS = 16
SCORE_SCALE = 1.0 / math.sqrt(DH)
LOG2E = math.log2(math.e)
NT = (((1,), (1,)), ((), ()))
NN = (((1,), (0,)), ((), ()))
TN = (((0,), (0,)), ((), ()))


ANY = pl.BlockSpec(memory_space=pl.ANY)
VMEM = pl.BlockSpec(memory_space=pltpu.VMEM)


def dot(a, b, dims):
    return lax.dot_general(a, b, dims, preferred_element_type=jnp.float32)


def aligned(index, size):
    return pl.ds(pl.multiple_of(index * size, size), size)


def cost(flops, moved):
    return pl.CostEstimate(flops=flops, bytes_accessed=moved, transcendentals=0)


def row_deltas(out_grad, attn_out, heads):
    rows = out_grad.shape[0]

    def kernel(grad_ref, out_ref, delta_ref):
        for head in range(heads):
            cols = slice(head * DH, (head + 1) * DH)
            prod = grad_ref[:, cols].astype(jnp.float32) * out_ref[:, cols].astype(jnp.float32)
            delta_ref[head : head + 1, :] = jnp.sum(jnp.transpose(prod), axis=0, keepdims=True)

    return pl.pallas_call(
        kernel,
        out_shape=jax.ShapeDtypeStruct((heads, rows), jnp.float32),
        compiler_params=pltpu.CompilerParams(vmem_limit_bytes=32 << 20),
        cost_estimate=cost(4 * rows * heads * DH, 4 * rows * heads * DH),
        name="row_deltas",
    )(out_grad, attn_out)


def run_copies(pairs, sems):
    copies = [pltpu.make_async_copy(src, dst, sems.at[i]) for i, (src, dst) in enumerate(pairs)]
    for copy in copies:
        copy.start()
    for copy in copies:
        copy.wait()


def pack_heads(queries, keys, values, file_ids, head_count, chunks, whole):
    part, rows = queries.shape[0], file_ids.shape[1]
    width = queries.shape[1] // (head_count * chunks)
    layout = []
    for step in range(head_count):
        layout += [(step, 0, chunks)] if step in whole else [(step, c, 1) for c in range(chunks)]

    def kernel(q_ref, k_ref, v_ref, id_ref, *refs):
        kv_outs, q_outs = refs[:head_count], refs[head_count : head_count + len(layout)]
        tag_out, sems = refs[-2:]
        own = lax.axis_index("head")
        pairs = []
        for step in range(head_count):
            for chunk in range(chunks):
                cols = aligned((own ^ step) * chunks + chunk, DH)
                at = 2 * DH * chunk
                pairs.append((k_ref.at[:, cols], kv_outs[step].at[:, at : at + DH]))
                pairs.append((v_ref.at[:, cols], kv_outs[step].at[:, at + DH : at + 2 * DH]))
        for out, (step, chunk, count) in zip(q_outs, layout):
            first = pl.multiple_of(((own ^ step) * chunks + chunk) * width, width)
            pairs.append((q_ref.at[:, pl.ds(first, count * width)], out))
        line = lax.broadcasted_iota(jnp.int32, (TAG_ROWS, DH), 0)
        tags = id_ref[...].astype(jnp.float32)
        for column in range(0, 2 * DH, DH):
            value = jnp.zeros((TAG_ROWS, DH), jnp.float32)
            for first in range(column, rows, 2 * DH):
                value = jnp.where(line == first // (2 * DH), tags[:, first : first + DH], value)
            tag_out[:, column : column + DH] = value.astype(jnp.bfloat16)
        run_copies(pairs, sems)

    outs = pl.pallas_call(
        kernel,
        out_shape=[jax.ShapeDtypeStruct((part, 2 * chunks * DH), keys.dtype)] * head_count
        + [jax.ShapeDtypeStruct((part, count * width), queries.dtype) for _, _, count in layout]
        + [jax.ShapeDtypeStruct((TAG_ROWS, 2 * DH), jnp.bfloat16)],
        in_specs=[ANY] * 3 + [VMEM],
        scratch_shapes=[pltpu.SemaphoreType.DMA((2 * head_count * chunks + len(layout),))],
        cost_estimate=cost(0, 4 * (queries.size + 2 * keys.size)),
        name="pack_heads",
    )(queries, keys, values, file_ids)
    q_outs = outs[head_count:-1]
    return outs[:head_count], {(k[0], k[1]): out for out, k in zip(q_outs, layout)}, outs[-1]


def join_kv(parts, tags, chunks):
    head_count = len(parts)
    part, width = parts[0].shape[0], 2 * DH
    rows = part * head_count

    def kernel(tag_ref, *refs):
        ins, outs, sems = refs[:head_count], refs[head_count:-1], refs[-1]
        own = lax.axis_index("head")
        pairs = []
        for chunk, out in enumerate(outs):
            cols = slice(chunk * width, (chunk + 1) * width)
            for step in range(head_count):
                pairs.append((ins[step].at[:, cols], out.at[aligned(own ^ step, part)]))
            pairs.append((tag_ref, out.at[rows:]))
        run_copies(pairs, sems)

    shape = jax.ShapeDtypeStruct((rows + TAG_ROWS, width), parts[0].dtype)
    return pl.pallas_call(
        kernel,
        out_shape=[shape] * chunks,
        in_specs=[ANY] * (1 + head_count),
        scratch_shapes=[pltpu.SemaphoreType.DMA((chunks * (head_count + 1),))],
        cost_estimate=cost(0, 4 * rows * width * chunks),
        name="join_kv",
    )(tags, *parts)


def tile_grads(chunk, half, own_tile, q_parts, out_grad, log_sum, delta, kv_blocks, dq_in, final):
    head_count = len(q_parts)
    part, rows = q_parts[0].shape[0], out_grad.shape[0]
    width = min(x.shape[1] for x in q_parts)
    group = width // DH
    pair = 2 if group % 2 == 0 else 1
    slots = 1 if own_tile else half
    sum_in = [] if dq_in is None else [dq_in]
    dq_count = head_count if final else 1
    dkv_count = 1 if own_tile else half - 1

    def kernel(*refs):
        refs = list(refs)
        lse_ref, delta_ref, g_ref = refs[:3]
        q_in = refs[3 : 3 + head_count]
        kv_refs = refs[3 + head_count : 3 + head_count + slots]
        refs = refs[3 + head_count + slots :]
        start_ref = refs.pop(0) if sum_in else None
        dq_out, dkv_out = refs[:dq_count], refs[dq_count : dq_count + dkv_count]
        q_buf, kv_buf, dkv_buf, dq_acc, dq_low, dk_acc, dv_acc, bias = refs[dq_count + dkv_count :]
        head_index = lax.axis_index("head")
        own = lax.rem(lax.axis_index("ctx"), half)
        for step, ref in enumerate(q_in):
            first = 0 if ref.shape[1] == width else chunk * width
            q_buf[aligned(head_index ^ step, part), :] = ref[:, first : first + width]
        for slot, ref in enumerate(kv_refs):
            kv_buf[slot] = ref[...]
        if sum_in:
            dq_acc[...] = start_ref[...]
        elif not own_tile:
            dq_acc[...] = jnp.zeros_like(dq_acc)

        def load_tags(slot):
            lines = kv_buf[slot, rows:, :].astype(jnp.float32)
            pieces = [
                lines[first // (2 * DH) : first // (2 * DH) + 1, : min(rows - first, 2 * DH)]
                for first in range(0, rows, 2 * DH)
            ]
            return jnp.concatenate(pieces, axis=1)

        own_tags = load_tags(0)

        def set_bias(tags, block):
            key_tags = jnp.transpose(jnp.broadcast_to(tags, (8, rows)))[:, :1]
            key_pos = block * rows + lax.broadcasted_iota(jnp.int32, (rows, rows), 0)
            query_pos = own * rows + lax.broadcasted_iota(jnp.int32, (rows, rows), 1)
            allowed = (key_tags == own_tags) & (key_pos <= query_pos)
            bias[...] = jnp.where(allowed, 0.0, -1e30)

        def tile(slot, masked, strips):
            for first in range(0, group, pair):
                heads_here = [chunk * group + first + i for i in range(pair)]
                columns = [slice((first + i) * DH, (first + i + 1) * DH) for i in range(pair)]
                for top, bottom, left in strips:
                    count = rows - left
                    key = kv_buf[slot, top:bottom, :DH]
                    value = kv_buf[slot, top:bottom, DH:]

                    def side(pieces, axis):
                        return jnp.concatenate(pieces, axis=axis)

                    query = side([q_buf[left:, cols] for cols in columns], 0)
                    grad = side([g_ref[left:, h * DH : (h + 1) * DH] for h in heads_here], 0)
                    lse = side([lse_ref[h : h + 1, left:] for h in heads_here], 1) * LOG2E
                    shift = side([delta_ref[h : h + 1, left:] for h in heads_here], 1)
                    scores = dot(key, query, NT) * (SCORE_SCALE * LOG2E) - lse
                    if masked:
                        scores = scores + side([bias[top:bottom, left:]] * pair, 1)
                    probs = jnp.exp2(scores)
                    dprobs = dot(value, grad, NT)
                    dscores = (probs * (dprobs - shift)).astype(jnp.bfloat16)
                    dv_part = dot(probs.astype(jnp.bfloat16), grad, NN)
                    dk_part = dot(dscores, query, NN)
                    dq_part = dot(key, dscores, TN)
                    if first == 0:
                        dv_acc[top:bottom, :] = dv_part
                        dk_acc[top:bottom, :] = dk_part
                    else:
                        dv_acc[top:bottom, :] += dv_part
                        dk_acc[top:bottom, :] += dk_part
                    for i, cols in enumerate(columns):
                        piece = dq_part[:, i * count : (i + 1) * count]
                        if own_tile and not sum_in and left == 0:
                            dq_acc[cols, :] = piece
                        else:
                            dq_acc[cols, left:] += piece

        if own_tile:
            set_bias(own_tags, own)
            tile(0, True, [(top, top + DH, top) for top in range(0, rows, DH)])
            dkv_out[0][:, :DH] = dk_acc[...] * SCORE_SCALE
            dkv_out[0][:, DH:] = dv_acc[...]
        else:
            own_low, own_high = jnp.min(own_tags), jnp.max(own_tags)
            whole_tile = [(0, rows, 0)]

            def store(slot):
                dkv_buf[slot, :, :DH] = (dk_acc[...] * SCORE_SCALE).astype(jnp.bfloat16)
                dkv_buf[slot, :, DH:] = dv_acc[...].astype(jnp.bfloat16)

            def visit(slot, _):
                block = own ^ slot

                @pl.when(block < own)
                def _():
                    tags = load_tags(slot)
                    needed = jnp.max(tags) == own_low
                    full = jnp.min(tags) == own_high

                    @pl.when(full)
                    def _():
                        tile(slot, False, whole_tile)
                        store(slot)

                    @pl.when(jnp.logical_not(full) & needed)
                    def _():
                        set_bias(tags, block)
                        tile(slot, True, whole_tile)
                        store(slot)

                    @pl.when(jnp.logical_not(full | needed))
                    def _():
                        dkv_buf[slot] = jnp.zeros(dkv_buf.shape[1:], dkv_buf.dtype)

                return 0

            lax.fori_loop(1, slots, visit, 0)
            for slot in range(1, slots):
                @pl.when((own ^ slot) < own)
                def _():
                    dkv_out[slot - 1][...] = dkv_buf[slot]

        if final:
            for member in range(group):
                cols = slice(member * DH, (member + 1) * DH)
                low = (dq_acc[cols, :] * SCORE_SCALE).astype(dq_low.dtype)
                dq_low[:, cols] = jnp.transpose(low)
            for step in range(head_count):
                dq_out[step][...] = dq_low[aligned(head_index ^ step, part), :]
        else:
            dq_out[0][...] = dq_acc[...]

    bf16, f32 = jnp.bfloat16, jnp.float32
    dq_shape = jax.ShapeDtypeStruct((part, width), bf16)
    if not final:
        dq_shape = jax.ShapeDtypeStruct((width, rows), f32)
    dkv_shape = jax.ShapeDtypeStruct((rows, 2 * DH), f32 if own_tile else bf16)
    outs = pl.pallas_call(
        kernel,
        out_shape=[dq_shape] * dq_count + [dkv_shape] * dkv_count,
        scratch_shapes=[
            pltpu.VMEM((rows, width), bf16),
            pltpu.VMEM((slots,) + kv_blocks[0].shape, bf16),
            pltpu.VMEM((slots, rows, 2 * DH), bf16),
            pltpu.VMEM((width, rows), f32),
            pltpu.VMEM((rows, width), bf16),
            pltpu.VMEM((rows, DH), f32),
            pltpu.VMEM((rows, DH), f32),
            pltpu.VMEM((rows, rows), f32),
        ],
        compiler_params=pltpu.CompilerParams(vmem_limit_bytes=32 << 20),
        cost_estimate=pl.CostEstimate(
            flops=10 * rows * rows * width * dkv_count,
            bytes_accessed=8 * rows * width + 8 * slots * rows * 2 * DH,
            transcendentals=rows * rows * group * dkv_count,
        ),
        name="own_tile" if own_tile else "earlier_tiles",
    )(log_sum, delta, out_grad, *q_parts, *kv_blocks[:slots], *sum_in)
    return outs[:dq_count], outs[dq_count:]


def sum_kv(parts, head_count, half):
    chunks, count = len(parts), len(parts[0])
    rows, width = parts[0][0].shape
    part = rows // head_count

    def kernel(*refs):
        ins, outs, total = refs[: chunks * count], refs[chunks * count : -1], refs[-1]
        block = lax.rem(lax.axis_index("ctx"), half)
        for chunk in range(chunks):
            value = ins[chunk * count][...]
            for step in range(1, count):
                later = jnp.full((1, width), block ^ step, jnp.int32) > block
                sent = ins[chunk * count + step][...].astype(jnp.float32)
                value = value + jnp.where(later, sent, 0.0)
            total[:, chunk * width : (chunk + 1) * width] = value.astype(jnp.bfloat16)
        index = lax.axis_index("head")
        for step in range(head_count):
            outs[step][...] = total[aligned(index ^ step, part), :]

    return pl.pallas_call(
        kernel,
        out_shape=[jax.ShapeDtypeStruct((part, chunks * width), jnp.bfloat16)] * head_count,
        scratch_shapes=[pltpu.VMEM((rows, chunks * width), jnp.bfloat16)],
        compiler_params=pltpu.CompilerParams(vmem_limit_bytes=32 << 20),
        cost_estimate=cost(4 * chunks * rows * width, 12 * chunks * rows * width),
        name="sum_kv",
    )(*[x for group in parts for x in group])


def join_grads(dq_parts, dkv_parts):
    chunks, head_count = len(dq_parts), len(dkv_parts)
    part, width = dq_parts[0][0].shape
    count = chunks * head_count

    def kernel(*refs):
        q_ins, kv_ins = refs[:count], refs[count : count + head_count]
        q_out, k_out, v_out = refs[count + head_count :]
        own = lax.axis_index("head")
        for chunk in range(chunks):
            for step in range(head_count):
                slot = (own ^ step) * chunks + chunk
                q_out[:, aligned(slot, width)] = q_ins[chunk * head_count + step][...]
                at = 2 * DH * chunk
                k_out[:, aligned(slot, DH)] = kv_ins[step][:, at : at + DH]
                v_out[:, aligned(slot, DH)] = kv_ins[step][:, at + DH : at + 2 * DH]

    kv_shape = jax.ShapeDtypeStruct((part, count * DH), jnp.bfloat16)
    return pl.pallas_call(
        kernel,
        out_shape=[jax.ShapeDtypeStruct((part, count * width), jnp.bfloat16), kv_shape, kv_shape],
        compiler_params=pltpu.CompilerParams(vmem_limit_bytes=32 << 20),
        cost_estimate=cost(0, 5 * part * count * width),
        name="join_grads",
    )(*[x for group in dq_parts for x in group], *dkv_parts)


def per_device(queries, keys, values, attn_out, out_grad, log_sum, file_ids):
    ctx_count = lax.axis_size("ctx")
    head_count = lax.axis_size("head")
    half = ctx_count // 2
    heads = log_sum.shape[0]
    chunks = keys.shape[1] // head_count // DH
    whole = (0, 1)

    def over_head(block, step):
        if step == 0:
            return block
        return lax.ppermute(block, "head", [(i, i ^ step) for i in range(head_count)])

    def over_ctx(block, step):
        pairs = [(i, i - i % half + (i % half ^ step)) for i in range(ctx_count)]
        return lax.ppermute(block, "ctx", pairs)

    steps = range(head_count)
    kv_packed, packed, tags = pack_heads(
        queries, keys, values, file_ids[None, :], head_count, chunks, whole
    )
    kv_parts = [over_head(kv_packed[step], step) for step in steps]
    q_sent = {(step, 0): over_head(packed.pop((step, 0)), step) for step in whole}
    packed, kv_parts, tags, q_sent = lax.optimization_barrier((packed, kv_parts, tags, q_sent))
    kv_joined = join_kv(kv_parts, tags, chunks)
    q_sent.update({key: over_head(packed[key], key[0]) for key in packed})
    delta = row_deltas(out_grad, attn_out, heads)
    inputs = []
    for chunk in range(chunks):
        q_parts = [q_sent[step, 0 if step in whole else chunk] for step in steps]
        own = kv_joined[chunk]
        inputs.append((q_parts, [own] + [over_ctx(own, step) for step in range(1, half)]))

    dq_parts, dq_kept, dkv_parts = [], [], []
    for chunk in range(chunks):
        q_parts, kv_blocks = inputs[chunk]
        args = (q_parts, out_grad, log_sum, delta, kv_blocks)
        if chunk == 0:
            partial, (own_dkv,) = tile_grads(chunk, half, True, *args, None, False)
            dq, dkv = tile_grads(chunk, half, False, *args, partial[0], True)
            if chunks > 1:
                dq, dkv, inputs[1] = lax.optimization_barrier((dq, dkv, inputs[1]))
        else:
            partial, dkv = tile_grads(chunk, half, False, *args, None, False)
            partial, dkv, dkv_parts, dq_parts = lax.optimization_barrier(
                (partial, dkv, dkv_parts, dq_parts)
            )
            dq, (own_dkv,) = tile_grads(chunk, half, True, *args, partial[0], True)
            if chunk + 1 < chunks:
                dq, inputs[chunk + 1] = lax.optimization_barrier((dq, inputs[chunk + 1]))
        back = [over_ctx(x, step) for step, x in enumerate(dkv, 1)]
        dkv_parts.append([own_dkv] + back)
        dq_parts.append({step: over_head(dq[step], step) for step in steps if step not in whole})
        dq_kept.append([dq[step] for step in steps if step in whole])
    dq_kept, dkv_parts[-1] = lax.optimization_barrier((dq_kept, dkv_parts[-1]))
    dq_parts = [
        [over_head(kept[step], step) if step in whole else sent[step] for step in steps]
        for kept, sent in zip(dq_kept, dq_parts)
    ]
    pieces = sum_kv(dkv_parts, head_count, half)
    return tuple(join_grads(dq_parts, [over_head(pieces[step], step) for step in steps]))


def solution(mesh):
    return jax.shard_map(
        per_device,
        mesh=mesh,
        in_specs=(
            P(("ctx", "head"), None),
            P(("ctx", "head"), None),
            P(("ctx", "head"), None),
            P("ctx", "head"),
            P("ctx", "head"),
            P("head", "ctx"),
            P("ctx"),
        ),
        out_specs=(P(("ctx", "head"), None), P(("ctx", "head"), None), P(("ctx", "head"), None)),
        check_vma=False,
    )
```

time: 93.5 us -> 82 us (0.88)
  starting transfers between devices: 42.6 us -> 29.5 us
  waiting for transfers between devices: 25.2 us -> 31.7 us
  Pallas kernels: 19.6 us -> 16.2 us
  local copies, waits for them, and re-layouts: 4.07 us -> 2.85 us
    ppermute x12, starting transfers between devices: 31.2 us -> 15.7 us  [over_ctx(): return lax.ppermute(block, 'ctx', pairs)]
    ppermute x17, waiting for transfers between devices: 15.8 us -> 20.1 us  [over_head(): lax.ppermute(block, 'head', [(i, i ^ step) for i in range(head_count)])]
    pallas_call x5 -> x6, Pallas kernels: 16.8 us -> 13.5 us  [the longest x4 7.87 us: tile_grads(): pl.pallas_call(kernel, out_shape=[dq_shape] * dq_count + [dkv_shape] * dk...]
    ppermute x17, starting transfers between devices: 11.3 us -> 13.8 us  [over_head(): lax.ppermute(block, 'head', [(i, i ^ step) for i in range(head_count)])]
    ppermute x12, waiting for transfers between devices: 9.32 us -> 11.6 us  [over_ctx(): return lax.ppermute(block, 'ctx', pairs)]
    unnamed x22, local copies, waits for them, and re-layouts: 3.48 us -> 1.47 us
  transfers between devices with their start and end apart: 29 -> 29, of which waited for: 13 -> 14; matrix products, arithmetic and copies ran while one was open for 1% -> 0% of each run, Pallas kernels for 18% -> 14%
where the time goes in v4:
time: 82 us; the launch traced here: 81.1 us
  waiting for transfers between devices  31.7 us (39%)
  starting transfers between devices  29.5 us (36%)
  Pallas kernels  16.2 us (20%)
  local copies, waits for them, and re-layouts  2.85 us (3%)
    ppermute x17, waiting for transfers between devices, over_head(): lax.ppermute(block, 'head', [(i, i ^ step) for i in range(head_count)])  20.1 us
    ppermute x12, starting transfers between devices, over_ctx(): return lax.ppermute(block, 'ctx', pairs)  15.7 us
    ppermute x17, starting transfers between devices, over_head(): lax.ppermute(block, 'head', [(i, i ^ step) for i in range(head_count)])  13.8 us
    ppermute x12, waiting for transfers between devices, over_ctx(): return lax.ppermute(block, 'ctx', pairs)  11.6 us
    pallas_call x4, Pallas kernels, tile_grads(): pl.pallas_call(kernel, out_shape=[dq_shape] * dq_count + [dkv_shape] * dk...  7.87 us
    pallas_call x1, Pallas kernels, pack_heads(): pl.pallas_call(kernel, out_shape=[jax.ShapeDtypeStruct((part, 2 * chunks...  3.71 us
    pallas_call x1, Pallas kernels, join_kv(): pl.pallas_call(kernel, out_shape=[shape] * chunks, in_specs=[ANY] * (1 +...  1.88 us
  transfers between devices with their start and end apart: 29, of which 14 were waited for; matrix products, arithmetic and copies ran while one was open for 0% of the time, Pallas kernels for 14%

profile of v4, /device:TPU:0, one launch (start us, length us, event | category | flops | bytes accessed | tf_op | source)
XLA Modules:
  0.0 81.1 jit_solution(17806955733899990717)
XLA Ops:
  0.6 1.4 %broadcast_in_dim.3.id_ref = s32[1,384]{1,0:T(1,128)} reshape(s32[384]{0:T(512)} %param.13) | data formatting | bytes 3072 | tf_op jit(solution)/shard_map/broadcast_in_dim | solution.py:378
  2.0 3.7 %pack_heads.1 = (bf16[96,512]{1,0:T(8,128)(2,1)}, bf16[96,512]{1,0:T(8,128)(2,1)}, bf16[96,512]{1,0:T(8,128)(2,1)}, bf16[96,512]{1,0:T(8,128)(2,1)}, bf16[96,204...) custom-call(bf16[96,8192]{1,0:T(8,128)(2,1)} %q_ref.1, ...), custom_call_target="tpu_custom_call" | custom-call | bytes 3932160 | tf_op jit(solution)/shard_map/pack_heads/pallas_call | solution.py:91
  5.7 0.5 collective-permute-start.3
  6.3 0.1 collective-permute-start
  6.3 2.9 %collective-permute-start.1 = (bf16[96,512]{1,0:T(8,128)(2,1)}, bf16[96,512]{1,0:T(8,128)(2,1)S(1)}, u32[]{:S(2)}, u32[]{:S(2)}) collective-permute-start(bf16[96,512]{1,0:T(8,128)(2,1)} %get-tuple-element.88), channel_id=1, source_target_pairs={{0,2},{1,3},{2,0},{3,1},{4,6},{5,7},{6,4},{7,5},{8,10},{9,11},{10,... | collective-permute-start | bytes 294920 | tf_op jit(solution)/shard_map/ppermute | solution.py:370
  9.3 0.0 collective-permute-start.2
  9.3 0.0 collective-permute-done.refs_1_
  9.3 3.5 %collective-permute-done.1.refs_2_ = bf16[96,512]{1,0:T(8,128)(2,1)S(1)} collective-permute-done((bf16[96,512]{1,0:T(8,128)(2,1)}, bf16[96,512]{1,0:T(8,128)(2,1)S(1)}, u32[]{:S(2)}, u32[]{:S(2)}) %collective-permute-start.1) | collective-permute-done | bytes 98336 | tf_op jit(solution)/shard_map/ppermute | solution.py:370
  12.8 1.9 %collective-permute-done.2.refs_3_ = bf16[96,512]{1,0:T(8,128)(2,1)S(1)} collective-permute-done((bf16[96,512]{1,0:T(8,128)(2,1)}, bf16[96,512]{1,0:T(8,128)(2,1)S(1)}, u32[]{:S(2)}, u32[]{:S(2)}) %collective-permute-start.2) | collective-permute-done | bytes 98336 | tf_op jit(solution)/shard_map/ppermute | solution.py:370
  14.6 0.0 collective-permute-done.3.refs_4_
  14.6 0.9 %collective-permute-start.4 = (bf16[96,1024]{1,0:T(8,128)(2,1)}, bf16[96,1024]{1,0:T(8,128)(2,1)S(1)}, u32[]{:S(2)}, u32[]{:S(2)}) collective-permute-start(bf16[96,1024]{1,0:T(8,128)(2,1)} %get-tuple-element.95), channel_id=1, source_target_pairs={{0,2},{1,3},{2,0},{3,1},{4,6},{5,7},{6,4},{7,5},{8,10},{9,11},{10,... | collective-permute-start | bytes 589832 | tf_op jit(solution)/shard_map/ppermute | solution.py:370
  15.5 0.6 collective-permute-start.5
  16.1 1.9 %join_kv.1 = (bf16[400,256]{1,0:T(8,128)(2,1)}, bf16[400,256]{1,0:T(8,128)(2,1)}) custom-call(bf16[16,256]{1,0:T(8,128)(2,1)} %get-tuple-element.97.tag_ref, bf16[96,512]{1,0:T(8,128)(2,1)} %get-tuple-element.98.refs_0_, bf16[96,512]{1,0:T(8,128)(2,1)} %copy-done.6, bf16[96,512]{1,0:T(8,128)(2,1)} %copy-done.7, bf16[96,512]{1,0:T(8,128)(2,1)} %copy-done.8), custom_call_target="tpu_custom_call" | custom-call | bytes 786432 | tf_op jit(solution)/shard_map/join_kv/pallas_call | solution.py:122
  18.0 1.5 %collective-permute-start.6 = (bf16[400,256]{1,0:T(8,128)(2,1)}, bf16[400,256]{1,0:T(8,128)(2,1)S(1)}, u32[]{:S(2)}, u32[]{:S(2)}) collective-permute-start(bf16[400,256]{1,0:T(8,128)(2,1)} %get-tuple-element.102.refs_7_), channel_id=1, source_target_pairs={{0,4},{4,0},{8,12},{12,8},{16,20},{20,16},{24,28},{28,24},{1,5},{5... | collective-permute-start | bytes 614408 | tf_op jit(solution)/shard_map/ppermute | solution.py:374
  19.5 1.6 %collective-permute-start.7 = (bf16[400,256]{1,0:T(8,128)(2,1)}, bf16[400,256]{1,0:T(8,128)(2,1)S(1)}, u32[]{:S(2)}, u32[]{:S(2)}) collective-permute-start(bf16[400,256]{1,0:T(8,128)(2,1)} %get-tuple-element.102.refs_7_), channel_id=1, source_target_pairs={{0,8},{4,12},{8,0},{12,4},{16,24},{20,28},{24,16},{28,20},{1,9},{5... | collective-permute-start | bytes 614408 | tf_op jit(solution)/shard_map/ppermute | solution.py:374
  21.1 0.5 collective-permute-start.8
  21.6 1.4 %copy-done.1 = bf16[384,2048]{1,0:T(8,128)(2,1)S(1)} copy-done((bf16[384,2048]{1,0:T(8,128)(2,1)S(1)}, bf16[384,2048]{1,0:T(8,128)(2,1)}, u32[]{:S(2)}) %copy-start.1) | copy-done | bytes 1572888
  23.0 0.9 %row_deltas.1.refs_1_ = f32[16,384]{1,0:T(8,128)S(1)} custom-call(bf16[384,2048]{1,0:T(8,128)(2,1)S(1)} %copy-done.1, bf16[384,2048]{1,0:T(8,128)(2,1)S(1)} %copy-done), custom_call_target="tpu_custom_call" | custom-call | flops 3145728 | bytes 3145728 | tf_op jit(solution)/shard_map/row_deltas/pallas_call | solution.py:44
  23.9 0.0 collective-permute-done.4.refs_5_
  23.9 0.0 copy-done.3
  23.9 1.5 %collective-permute-start.11 = (bf16[400,256]{1,0:T(8,128)(2,1)S(1)}, bf16[400,256]{1,0:T(8,128)(2,1)S(1)}, u32[]{:S(2)}, u32[]{:S(2)}) collective-permute-start(bf16[400,256]{1,0:T(8,128)(2,1)S(1)} %copy-done.3), channel_id=1, source_target_pairs={{0,4},{4,0},{8,12},{12,8},{16,20},{20,16},{24,28},{28,24},{1,5},{5... | collective-permute-start | bytes 614408 | tf_op jit(solution)/shard_map/ppermute | solution.py:374
  25.4 0.0 collective-permute-done.5.refs_6_
  25.4 1.6 %collective-permute-start.12 = (bf16[400,256]{1,0:T(8,128)(2,1)S(1)}, bf16[400,256]{1,0:T(8,128)(2,1)S(1)}, u32[]{:S(2)}, u32[]{:S(2)}) collective-permute-start(bf16[400,256]{1,0:T(8,128)(2,1)S(1)} %copy-done.3), channel_id=1, source_target_pairs={{0,8},{4,12},{8,0},{12,4},{16,24},{20,28},{24,16},{28,20},{1,9},{5... | collective-permute-start | bytes 614408 | tf_op jit(solution)/shard_map/ppermute | solution.py:374
  27.0 3.3 %own_tile.2 = (f32[1024,384]{1,0:T(8,128)S(1)}, f32[384,256]{1,0:T(8,128)S(1)}) custom-call(f32[16,384]{1,0:T(8,128)S(1)} %copy-done.5, f32[16,384]{1,0:T(8,128)S(1)} %row_deltas.1.refs_1_, bf16[384,2048]{1,0:T(8,128)(2,1)S(1)} %copy-done.1, bf16[96,2048]{1,0:T(8,128)(2,1)S(1)} %copy-done.2, bf16[96,2048]{1,0:T(8,128)(2,1)S(1)} %collective-permute-done.3.refs_4_, ...), custom_call_target="tpu_custom_call" | custom-call | flops 1509949440 | bytes 3932160 | tf_op jit(solution)/shard_map/own_tile/pallas_call | solution.py:279
  30.3 0.0 collective-permute-done.6.refs_8_
  30.3 1.1 %collective-permute-start.13 = (bf16[400,256]{1,0:T(8,128)(2,1)S(1)}, bf16[400,256]{1,0:T(8,128)(2,1)S(1)}, u32[]{:S(2)}, u32[]{:S(2)}) collective-permute-start(bf16[400,256]{1,0:T(8,128)(2,1)S(1)} %copy-done.3), channel_id=1, source_target_pairs={{0,12},{4,8},{8,4},{12,0},{16,28},{20,24},{24,20},{28,16},{1,13},{... | collective-permute-start | bytes 614408 | tf_op jit(solution)/shard_map/ppermute | solution.py:374
  31.4 0.0 collective-permute-done.7.refs_9_
  31.4 2.1 %collective-permute-start.9 = (bf16[96,1024]{1,0:T(8,128)(2,1)S(1)}, bf16[96,1024]{1,0:T(8,128)(2,1)S(1)}, u32[]{:S(2)}, u32[]{:S(2)}) collective-permute-start(bf16[96,1024]{1,0:T(8,128)(2,1)S(1)} %copy-done.10), channel_id=1, source_target_pairs={{0,2},{1,3},{2,0},{3,1},{4,6},{5,7},{6,4},{7,5},{8,10},{9,11},{10,... | collective-permute-start | bytes 589832 | tf_op jit(solution)/shard_map/ppermute | solution.py:370
  33.5 0.0 collective-permute-done.8.refs_10_
  33.5 0.0 collective-permute-start.10
  33.5 0.8 earlier_tiles.2
  34.3 4.9 %collective-permute-done.9.refs_5_ = bf16[96,1024]{1,0:T(8,128)(2,1)S(1)} collective-permute-done((bf16[96,1024]{1,0:T(8,128)(2,1)S(1)}, bf16[96,1024]{1,0:T(8,128)(2,1)S(1)}, u32[]{:S(2)}, u32[]{:S(2)}) %collective-permute-start.9) | collective-permute-done | bytes 196640 | tf_op jit(solution)/shard_map/ppermute | solution.py:370
  39.2 3.0 %collective-permute-done.10.refs_6_ = bf16[96,1024]{1,0:T(8,128)(2,1)S(1)} collective-permute-done((bf16[96,1024]{1,0:T(8,128)(2,1)S(1)}, bf16[96,1024]{1,0:T(8,128)(2,1)S(1)}, u32[]{:S(2)}, u32[]{:S(2)}) %collective-permute-start.10) | collective-permute-done | bytes 196640 | tf_op jit(solution)/shard_map/ppermute | solution.py:370
  42.2 0.4 collective-permute-start.14
  42.6 3.6 %collective-permute-start.15 = (bf16[384,256]{1,0:T(8,128)(2,1)S(1)}, bf16[384,256]{1,0:T(8,128)(2,1)S(1)}, u32[]{:S(2)}, u32[]{:S(2)}) collective-permute-start(bf16[384,256]{1,0:T(8,128)(2,1)S(1)} %get-tuple-element.130), channel_id=1, source_target_pairs={{0,8},{4,12},{8,0},{12,4},{16,24},{20,28},{24,16},{28,20},{1,9},{5... | collective-permute-start | bytes 589832 | tf_op jit(solution)/shard_map/ppermute | solution.py:374
  46.2 0.0 collective-permute-start.16
  46.2 1.1 %collective-permute-start.17 = (bf16[96,1024]{1,0:T(8,128)(2,1)S(1)}, bf16[96,1024]{1,0:T(8,128)(2,1)S(1)}, u32[]{:S(2)}, u32[]{:S(2)}) collective-permute-start(bf16[96,1024]{1,0:T(8,128)(2,1)S(1)} %get-tuple-element.132), channel_id=1, source_target_pairs={{0,2},{1,3},{2,0},{3,1},{4,6},{5,7},{6,4},{7,5},{8,10},{9,11},{10,... | collective-permute-start | bytes 589832 | tf_op jit(solution)/shard_map/ppermute | solution.py:370
  47.3 0.8 collective-permute-start.18
  48.1 0.4 earlier_tiles.3
  48.5 1.0 %collective-permute-done.14.refs_1_ = bf16[384,256]{1,0:T(8,128)(2,1)S(1)} collective-permute-done((bf16[384,256]{1,0:T(8,128)(2,1)S(1)}, bf16[384,256]{1,0:T(8,128)(2,1)S(1)}, u32[]{:S(2)}, u32[]{:S(2)}) %collective-permute-start.14) | collective-permute-done | bytes 196640 | tf_op jit(solution)/shard_map/ppermute | solution.py:374
  49.5 2.2 %collective-permute-done.15.refs_2_ = bf16[384,256]{1,0:T(8,128)(2,1)S(1)} collective-permute-done((bf16[384,256]{1,0:T(8,128)(2,1)S(1)}, bf16[384,256]{1,0:T(8,128)(2,1)S(1)}, u32[]{:S(2)}, u32[]{:S(2)}) %collective-permute-start.15) | collective-permute-done | bytes 196640 | tf_op jit(solution)/shard_map/ppermute | solution.py:374
  51.8 3.8 %collective-permute-done.16.refs_3_ = bf16[384,256]{1,0:T(8,128)(2,1)S(1)} collective-permute-done((bf16[384,256]{1,0:T(8,128)(2,1)S(1)}, bf16[384,256]{1,0:T(8,128)(2,1)S(1)}, u32[]{:S(2)}, u32[]{:S(2)}) %collective-permute-start.16) | collective-permute-done | bytes 196640 | tf_op jit(solution)/shard_map/ppermute | solution.py:374
  55.6 0.0 collective-permute-done.17.refs_2_
  55.6 1.9 %collective-permute-done.18.refs_3_ = bf16[96,1024]{1,0:T(8,128)(2,1)S(1)} collective-permute-done((bf16[96,1024]{1,0:T(8,128)(2,1)S(1)}, bf16[96,1024]{1,0:T(8,128)(2,1)S(1)}, u32[]{:S(2)}, u32[]{:S(2)}) %collective-permute-start.18) | collective-permute-done | bytes 196640 | tf_op jit(solution)/shard_map/ppermute | solution.py:370
  57.5 1.5 %collective-permute-start.19 = (bf16[384,256]{1,0:T(8,128)(2,1)S(1)}, bf16[384,256]{1,0:T(8,128)(2,1)S(1)}, u32[]{:S(2)}, u32[]{:S(2)}) collective-permute-start(bf16[384,256]{1,0:T(8,128)(2,1)S(1)} %get-tuple-element.138), channel_id=1, source_target_pairs={{0,4},{4,0},{8,12},{12,8},{16,20},{20,16},{24,28},{28,24},{1,5},{5... | collective-permute-start | bytes 589832 | tf_op jit(solution)/shard_map/ppermute | solution.py:374
  59.0 2.5 %collective-permute-start.20 = (bf16[384,256]{1,0:T(8,128)(2,1)S(1)}, bf16[384,256]{1,0:T(8,128)(2,1)S(1)}, u32[]{:S(2)}, u32[]{:S(2)}) collective-permute-start(bf16[384,256]{1,0:T(8,128)(2,1)S(1)} %get-tuple-element.139), channel_id=1, source_target_pairs={{0,8},{4,12},{8,0},{12,4},{16,24},{20,28},{24,16},{28,20},{1,9},{5... | collective-permute-start | bytes 589832 | tf_op jit(solution)/shard_map/ppermute | solution.py:374
  61.5 3.4 %own_tile.3 = (bf16[96,1024]{1,0:T(8,128)(2,1)S(1)}, bf16[96,1024]{1,0:T(8,128)(2,1)S(1)}, bf16[96,1024]{1,0:T(8,128)(2,1)S(1)}, bf16[96,1024]{1,0:T(8,128)(2,1)S(1)}, f32[384,256]{1,0:T(8,128)S(1)}) custom-call(f32[16,384]{1,0:T(8,128)S(1)} %copy-done.5, f32[16,384]{1,0:T(8,128)S(1)} %row_deltas.1.refs_1_, bf16[384,2048]{1,0:T(8,128)(2,1)S(1)} %copy-done.1, ...), custom_call_target="tpu_custom_call" | custom-call | flops 1509949440 | bytes 3932160 | tf_op jit(solution)/shard_map/own_tile/pallas_call | solution.py:279
  64.9 1.1 %collective-permute-start.24 = (bf16[96,1024]{1,0:T(8,128)(2,1)S(1)}, bf16[96,1024]{1,0:T(8,128)(2,1)S(1)}, u32[]{:S(2)}, u32[]{:S(2)}) collective-permute-start(bf16[96,1024]{1,0:T(8,128)(2,1)S(1)} %get-tuple-element.147), channel_id=1, source_target_pairs={{0,2},{1,3},{2,0},{3,1},{4,6},{5,7},{6,4},{7,5},{8,10},{9,11},{10,... | collective-permute-start | bytes 589832 | tf_op jit(solution)/shard_map/ppermute | solution.py:370
  65.9 0.3 collective-permute-start.25
  66.2 0.0 collective-permute-done.19.refs_5_
  66.2 0.9 %collective-permute-done.20.refs_6_ = bf16[384,256]{1,0:T(8,128)(2,1)S(1)} collective-permute-done((bf16[384,256]{1,0:T(8,128)(2,1)S(1)}, bf16[384,256]{1,0:T(8,128)(2,1)S(1)}, u32[]{:S(2)}, u32[]{:S(2)}) %collective-permute-start.20) | collective-permute-done | bytes 196640 | tf_op jit(solution)/shard_map/ppermute | solution.py:374
  67.1 3.6 %collective-permute-done.21.refs_7_ = bf16[384,256]{1,0:T(8,128)(2,1)S(1)} collective-permute-done((bf16[384,256]{1,0:T(8,128)(2,1)S(1)}, bf16[384,256]{1,0:T(8,128)(2,1)S(1)}, u32[]{:S(2)}, u32[]{:S(2)}) %collective-permute-start.21) | collective-permute-done | bytes 196640 | tf_op jit(solution)/shard_map/ppermute | solution.py:374
  70.7 0.0 collective-permute-start.22
  70.7 0.5 collective-permute-start.23
  71.3 0.4 sum_kv.1
  71.7 0.1 collective-permute-start.26
  71.8 1.0 %collective-permute-done.24.refs_6_ = bf16[96,1024]{1,0:T(8,128)(2,1)S(1)} collective-permute-done((bf16[96,1024]{1,0:T(8,128)(2,1)S(1)}, bf16[96,1024]{1,0:T(8,128)(2,1)S(1)}, u32[]{:S(2)}, u32[]{:S(2)}) %collective-permute-start.24) | collective-permute-done | bytes 196640 | tf_op jit(solution)/shard_map/ppermute | solution.py:370
  72.7 1.0 %collective-permute-start.27 = (bf16[96,512]{1,0:T(8,128)(2,1)S(1)}, bf16[96,512]{1,0:T(8,128)(2,1)S(1)}, u32[]{:S(2)}, u32[]{:S(2)}) collective-permute-start(bf16[96,512]{1,0:T(8,128)(2,1)S(1)} %get-tuple-element.159), channel_id=1, source_target_pairs={{0,2},{1,3},{2,0},{3,1},{4,6},{5,7},{6,4},{7,5},{8,10},{9,11},{10,... | collective-permute-start | bytes 294920 | tf_op jit(solution)/shard_map/ppermute | solution.py:370
  73.7 1.7 %collective-permute-done.25.refs_7_ = bf16[96,1024]{1,0:T(8,128)(2,1)S(1)} collective-permute-done((bf16[96,1024]{1,0:T(8,128)(2,1)S(1)}, bf16[96,1024]{1,0:T(8,128)(2,1)S(1)}, u32[]{:S(2)}, u32[]{:S(2)}) %collective-permute-start.25) | collective-permute-done | bytes 196640 | tf_op jit(solution)/shard_map/ppermute | solution.py:370
  75.4 1.9 %collective-permute-start.28 = (bf16[96,512]{1,0:T(8,128)(2,1)S(1)}, bf16[96,512]{1,0:T(8,128)(2,1)S(1)}, u32[]{:S(2)}, u32[]{:S(2)}) collective-permute-start(bf16[96,512]{1,0:T(8,128)(2,1)S(1)} %get-tuple-element.160), channel_id=1, source_target_pairs={{0,3},{1,2},{2,1},{3,0},{4,7},{5,6},{6,5},{7,4},{8,11},{9,10},{10,... | collective-permute-start | bytes 294920 | tf_op jit(solution)/shard_map/ppermute | solution.py:370
  77.3 0.0 collective-permute-done.26.refs_9_
  77.3 0.7 collective-permute-done.27.refs_10_
  78.0 1.6 %collective-permute-done.28.refs_11_ = bf16[96,512]{1,0:T(8,128)(2,1)S(1)} collective-permute-done((bf16[96,512]{1,0:T(8,128)(2,1)S(1)}, bf16[96,512]{1,0:T(8,128)(2,1)S(1)}, u32[]{:S(2)}, u32[]{:S(2)}) %collective-permute-start.28) | collective-permute-done | bytes 98336 | tf_op jit(solution)/shard_map/ppermute | solution.py:370
  79.6 1.4 %join_grads.1 = (bf16[96,8192]{1,0:T(8,128)(2,1)}, bf16[96,1024]{1,0:T(8,128)(2,1)}, bf16[96,1024]{1,0:T(8,128)(2,1)}) custom-call(bf16[96,1024]{1,0:T(8,128)(2,1)S(1)} %get-tuple-element.141.refs_0_, bf16[96,1024]{1,0:T(8,128)(2,1)S(1)} %collective-permute-done.22.refs_1_, bf16[96,1024]{1,0:T(8,128)(2,1)S(1)} %collective-permute-done.17.refs_2_, ...), custom_call_target="tpu_custom_call" | custom-call | bytes 3932160 | tf_op jit(solution)/shard_map/join_grads/pallas_call | solution.py:350
  (26 shorter events, 0.1 us)
Async XLA Ops:
  0.6 20.9 %copy-start = (bf16[384,2048]{1,0:T(8,128)(2,1)S(1)}, bf16[384,2048]{1,0:T(8,128)(2,1)}, u32[]{:S(2)}) copy-start(bf16[384,2048]{1,0:T(8,128)(2,1)} %out_ref.1) | copy-start | bytes 4718596
  5.7 8.9 %collective-permute-start.3 = (bf16[96,2048]{1,0:T(8,128)(2,1)}, bf16[96,2048]{1,0:T(8,128)(2,1)S(1)}, u32[]{:S(2)}, u32[]{:S(2)}) collective-permute-start(bf16[96,2048]{1,0:T(8,128)(2,1)} %get-tuple-element.92), channel_id=1, source_target_pairs={{0,1},{1,0},{2,3},{3,2},{4,5},{5,4},{6,7},{7,6},{8,9},{9,8},{10,11... | collective-permute-start | bytes 1179656 | tf_op jit(solution)/shard_map/ppermute | solution.py:370
  6.3 3.0 %collective-permute-start = (bf16[96,512]{1,0:T(8,128)(2,1)}, bf16[96,512]{1,0:T(8,128)(2,1)S(1)}, u32[]{:S(2)}, u32[]{:S(2)}) collective-permute-start(bf16[96,512]{1,0:T(8,128)(2,1)} %get-tuple-element.87), channel_id=1, source_target_pairs={{0,1},{1,0},{2,3},{3,2},{4,5},{5,4},{6,7},{7,6},{8,9},{9,8},{10,11... | collective-permute-start | bytes 294920 | tf_op jit(solution)/shard_map/ppermute | solution.py:370
  6.3 6.4 %collective-permute-start.1 = (bf16[96,512]{1,0:T(8,128)(2,1)}, bf16[96,512]{1,0:T(8,128)(2,1)S(1)}, u32[]{:S(2)}, u32[]{:S(2)}) collective-permute-start(bf16[96,512]{1,0:T(8,128)(2,1)} %get-tuple-element.88), channel_id=1, source_target_pairs={{0,2},{1,3},{2,0},{3,1},{4,6},{5,7},{6,4},{7,5},{8,10},{9,11},{10,... | collective-permute-start | bytes 294920 | tf_op jit(solution)/shard_map/ppermute | solution.py:370
  9.3 5.4 %collective-permute-start.2 = (bf16[96,512]{1,0:T(8,128)(2,1)}, bf16[96,512]{1,0:T(8,128)(2,1)S(1)}, u32[]{:S(2)}, u32[]{:S(2)}) collective-permute-start(bf16[96,512]{1,0:T(8,128)(2,1)} %get-tuple-element.89), channel_id=1, source_target_pairs={{0,3},{1,2},{2,1},{3,0},{4,7},{5,6},{6,5},{7,4},{8,11},{9,10},{10,... | collective-permute-start | bytes 294920 | tf_op jit(solution)/shard_map/ppermute | solution.py:370
  9.3 6.8 %copy-start.6 = (bf16[96,512]{1,0:T(8,128)(2,1)}, bf16[96,512]{1,0:T(8,128)(2,1)S(1)}, u32[]{:S(2)}) copy-start(bf16[96,512]{1,0:T(8,128)(2,1)S(1)} %collective-permute-done.refs_1_) | copy-start | bytes 294916
  12.8 3.3 %copy-start.7 = (bf16[96,512]{1,0:T(8,128)(2,1)}, bf16[96,512]{1,0:T(8,128)(2,1)S(1)}, u32[]{:S(2)}) copy-start(bf16[96,512]{1,0:T(8,128)(2,1)S(1)} %collective-permute-done.1.refs_2_) | copy-start | bytes 294916
  14.6 1.5 %copy-start.8 = (bf16[96,512]{1,0:T(8,128)(2,1)}, bf16[96,512]{1,0:T(8,128)(2,1)S(1)}, u32[]{:S(2)}) copy-start(bf16[96,512]{1,0:T(8,128)(2,1)S(1)} %collective-permute-done.2.refs_3_) | copy-start | bytes 294916
  14.6 9.2 %collective-permute-start.4 = (bf16[96,1024]{1,0:T(8,128)(2,1)}, bf16[96,1024]{1,0:T(8,128)(2,1)S(1)}, u32[]{:S(2)}, u32[]{:S(2)}) collective-permute-start(bf16[96,1024]{1,0:T(8,128)(2,1)} %get-tuple-element.95), channel_id=1, source_target_pairs={{0,2},{1,3},{2,0},{3,1},{4,6},{5,7},{6,4},{7,5},{8,10},{9,11},{10,... | collective-permute-start | bytes 589832 | tf_op jit(solution)/shard_map/ppermute | solution.py:370
  15.5 9.9 %collective-permute-start.5 = (bf16[96,1024]{1,0:T(8,128)(2,1)}, bf16[96,1024]{1,0:T(8,128)(2,1)S(1)}, u32[]{:S(2)}, u32[]{:S(2)}) collective-permute-start(bf16[96,1024]{1,0:T(8,128)(2,1)} %get-tuple-element.96), channel_id=1, source_target_pairs={{0,3},{1,2},{2,1},{3,0},{4,7},{5,6},{6,5},{7,4},{8,11},{9,10},{10,... | collective-permute-start | bytes 589832 | tf_op jit(solution)/shard_map/ppermute | solution.py:370
  16.1 10.9 %copy-start.2 = (bf16[96,2048]{1,0:T(8,128)(2,1)S(1)}, bf16[96,2048]{1,0:T(8,128)(2,1)}, u32[]{:S(2)}) copy-start(bf16[96,2048]{1,0:T(8,128)(2,1)} %get-tuple-element.116.refs_3_) | copy-start | bytes 1179652
  18.0 12.3 %collective-permute-start.6 = (bf16[400,256]{1,0:T(8,128)(2,1)}, bf16[400,256]{1,0:T(8,128)(2,1)S(1)}, u32[]{:S(2)}, u32[]{:S(2)}) collective-permute-start(bf16[400,256]{1,0:T(8,128)(2,1)} %get-tuple-element.102.refs_7_), channel_id=1, source_target_pairs={{0,4},{4,0},{8,12},{12,8},{16,20},{20,16},{24,28},{28,24},{1,5},{5... | collective-permute-start | bytes 614408 | tf_op jit(solution)/shard_map/ppermute | solution.py:374
  19.5 11.9 %collective-permute-start.7 = (bf16[400,256]{1,0:T(8,128)(2,1)}, bf16[400,256]{1,0:T(8,128)(2,1)S(1)}, u32[]{:S(2)}, u32[]{:S(2)}) collective-permute-start(bf16[400,256]{1,0:T(8,128)(2,1)} %get-tuple-element.102.refs_7_), channel_id=1, source_target_pairs={{0,8},{4,12},{8,0},{12,4},{16,24},{20,28},{24,16},{28,20},{1,9},{5... | collective-permute-start | bytes 614408 | tf_op jit(solution)/shard_map/ppermute | solution.py:374
  21.1 12.4 %collective-permute-start.8 = (bf16[400,256]{1,0:T(8,128)(2,1)}, bf16[400,256]{1,0:T(8,128)(2,1)S(1)}, u32[]{:S(2)}, u32[]{:S(2)}) collective-permute-start(bf16[400,256]{1,0:T(8,128)(2,1)} %get-tuple-element.102.refs_7_), channel_id=1, source_target_pairs={{0,12},{4,8},{8,4},{12,0},{16,28},{20,24},{24,20},{28,16},{1,13},{... | collective-permute-start | bytes 614408 | tf_op jit(solution)/shard_map/ppermute | solution.py:374
  21.5 1.4 %copy-start.1 = (bf16[384,2048]{1,0:T(8,128)(2,1)S(1)}, bf16[384,2048]{1,0:T(8,128)(2,1)}, u32[]{:S(2)}) copy-start(bf16[384,2048]{1,0:T(8,128)(2,1)} %refs_2_.7) | copy-start | bytes 4718596
  23.0 0.9 %copy-start.3 = (bf16[400,256]{1,0:T(8,128)(2,1)S(1)}, bf16[400,256]{1,0:T(8,128)(2,1)}, u32[]{:S(2)}) copy-start(bf16[400,256]{1,0:T(8,128)(2,1)} %get-tuple-element.120.refs_7_) | copy-start | bytes 614404
  23.0 4.0 %copy-start.4 = (bf16[400,256]{1,0:T(8,128)(2,1)S(1)}, bf16[400,256]{1,0:T(8,128)(2,1)}, u32[]{:S(2)}) copy-start(bf16[400,256]{1,0:T(8,128)(2,1)} %get-tuple-element.102.refs_7_) | copy-start | bytes 614404
  23.0 4.0 %copy-start.5 = (f32[16,384]{1,0:T(8,128)S(1)}, f32[16,384]{1,0:T(8,128)}, u32[]{:S(2)}) copy-start(f32[16,384]{1,0:T(8,128)} %refs_0_.7) | copy-start | bytes 73732
  23.9 7.5 %copy-start.10 = (bf16[96,1024]{1,0:T(8,128)(2,1)S(1)}, bf16[96,1024]{1,0:T(8,128)(2,1)}, u32[]{:S(2)}) copy-start(bf16[96,1024]{1,0:T(8,128)(2,1)} %get-tuple-element.111) | copy-start | bytes 589828
  23.9 9.6 %copy-start.9 = (bf16[96,1024]{1,0:T(8,128)(2,1)S(1)}, bf16[96,1024]{1,0:T(8,128)(2,1)}, u32[]{:S(2)}) copy-start(bf16[96,1024]{1,0:T(8,128)(2,1)} %get-tuple-element.112) | copy-start | bytes 589828
  23.9 18.3 %collective-permute-start.11 = (bf16[400,256]{1,0:T(8,128)(2,1)S(1)}, bf16[400,256]{1,0:T(8,128)(2,1)S(1)}, u32[]{:S(2)}, u32[]{:S(2)}) collective-permute-start(bf16[400,256]{1,0:T(8,128)(2,1)S(1)} %copy-done.3), channel_id=1, source_target_pairs={{0,4},{4,0},{8,12},{12,8},{16,20},{20,16},{24,28},{28,24},{1,5},{5... | collective-permute-start | bytes 614408 | tf_op jit(solution)/shard_map/ppermute | solution.py:374
  25.4 16.8 %collective-permute-start.12 = (bf16[400,256]{1,0:T(8,128)(2,1)S(1)}, bf16[400,256]{1,0:T(8,128)(2,1)S(1)}, u32[]{:S(2)}, u32[]{:S(2)}) collective-permute-start(bf16[400,256]{1,0:T(8,128)(2,1)S(1)} %copy-done.3), channel_id=1, source_target_pairs={{0,8},{4,12},{8,0},{12,4},{16,24},{20,28},{24,16},{28,20},{1,9},{5... | collective-permute-start | bytes 614408 | tf_op jit(solution)/shard_map/ppermute | solution.py:374
  30.3 11.9 %collective-permute-start.13 = (bf16[400,256]{1,0:T(8,128)(2,1)S(1)}, bf16[400,256]{1,0:T(8,128)(2,1)S(1)}, u32[]{:S(2)}, u32[]{:S(2)}) collective-permute-start(bf16[400,256]{1,0:T(8,128)(2,1)S(1)} %copy-done.3), channel_id=1, source_target_pairs={{0,12},{4,8},{8,4},{12,0},{16,28},{20,24},{24,20},{28,16},{1,13},{... | collective-permute-start | bytes 614408 | tf_op jit(solution)/shard_map/ppermute | solution.py:374
  31.4 7.8 %collective-permute-start.9 = (bf16[96,1024]{1,0:T(8,128)(2,1)S(1)}, bf16[96,1024]{1,0:T(8,128)(2,1)S(1)}, u32[]{:S(2)}, u32[]{:S(2)}) collective-permute-start(bf16[96,1024]{1,0:T(8,128)(2,1)S(1)} %copy-done.10), channel_id=1, source_target_pairs={{0,2},{1,3},{2,0},{3,1},{4,6},{5,7},{6,4},{7,5},{8,10},{9,11},{10,... | collective-permute-start | bytes 589832 | tf_op jit(solution)/shard_map/ppermute | solution.py:370
  33.5 8.7 %collective-permute-start.10 = (bf16[96,1024]{1,0:T(8,128)(2,1)S(1)}, bf16[96,1024]{1,0:T(8,128)(2,1)S(1)}, u32[]{:S(2)}, u32[]{:S(2)}) collective-permute-start(bf16[96,1024]{1,0:T(8,128)(2,1)S(1)} %copy-done.9), channel_id=1, source_target_pairs={{0,3},{1,2},{2,1},{3,0},{4,7},{5,6},{6,5},{7,4},{8,11},{9,10},{10,... | collective-permute-start | bytes 589832 | tf_op jit(solution)/shard_map/ppermute | solution.py:370
  42.2 7.3 %collective-permute-start.14 = (bf16[384,256]{1,0:T(8,128)(2,1)S(1)}, bf16[384,256]{1,0:T(8,128)(2,1)S(1)}, u32[]{:S(2)}, u32[]{:S(2)}) collective-permute-start(bf16[384,256]{1,0:T(8,128)(2,1)S(1)} %get-tuple-element.129), channel_id=1, source_target_pairs={{0,4},{4,0},{8,12},{12,8},{16,20},{20,16},{24,28},{28,24},{1,5},{5... | collective-permute-start | bytes 589832 | tf_op jit(solution)/shard_map/ppermute | solution.py:374
  42.6 9.1 %collective-permute-start.15 = (bf16[384,256]{1,0:T(8,128)(2,1)S(1)}, bf16[384,256]{1,0:T(8,128)(2,1)S(1)}, u32[]{:S(2)}, u32[]{:S(2)}) collective-permute-start(bf16[384,256]{1,0:T(8,128)(2,1)S(1)} %get-tuple-element.130), channel_id=1, source_target_pairs={{0,8},{4,12},{8,0},{12,4},{16,24},{20,28},{24,16},{28,20},{1,9},{5... | collective-permute-start | bytes 589832 | tf_op jit(solution)/shard_map/ppermute | solution.py:374
  46.2 9.4 %collective-permute-start.16 = (bf16[384,256]{1,0:T(8,128)(2,1)S(1)}, bf16[384,256]{1,0:T(8,128)(2,1)S(1)}, u32[]{:S(2)}, u32[]{:S(2)}) collective-permute-start(bf16[384,256]{1,0:T(8,128)(2,1)S(1)} %get-tuple-element.131), channel_id=1, source_target_pairs={{0,12},{4,8},{8,4},{12,0},{16,28},{20,24},{24,20},{28,16},{1,13},{... | collective-permute-start | bytes 589832 | tf_op jit(solution)/shard_map/ppermute | solution.py:374
  46.2 9.4 %collective-permute-start.17 = (bf16[96,1024]{1,0:T(8,128)(2,1)S(1)}, bf16[96,1024]{1,0:T(8,128)(2,1)S(1)}, u32[]{:S(2)}, u32[]{:S(2)}) collective-permute-start(bf16[96,1024]{1,0:T(8,128)(2,1)S(1)} %get-tuple-element.132), channel_id=1, source_target_pairs={{0,2},{1,3},{2,0},{3,1},{4,6},{5,7},{6,4},{7,5},{8,10},{9,11},{10,... | collective-permute-start | bytes 589832 | tf_op jit(solution)/shard_map/ppermute | solution.py:370
  47.3 10.2 %collective-permute-start.18 = (bf16[96,1024]{1,0:T(8,128)(2,1)S(1)}, bf16[96,1024]{1,0:T(8,128)(2,1)S(1)}, u32[]{:S(2)}, u32[]{:S(2)}) collective-permute-start(bf16[96,1024]{1,0:T(8,128)(2,1)S(1)} %get-tuple-element.133), channel_id=1, source_target_pairs={{0,3},{1,2},{2,1},{3,0},{4,7},{5,6},{6,5},{7,4},{8,11},{9,10},{10,... | collective-permute-start | bytes 589832 | tf_op jit(solution)/shard_map/ppermute | solution.py:370
  57.5 8.7 %collective-permute-start.19 = (bf16[384,256]{1,0:T(8,128)(2,1)S(1)}, bf16[384,256]{1,0:T(8,128)(2,1)S(1)}, u32[]{:S(2)}, u32[]{:S(2)}) collective-permute-start(bf16[384,256]{1,0:T(8,128)(2,1)S(1)} %get-tuple-element.138), channel_id=1, source_target_pairs={{0,4},{4,0},{8,12},{12,8},{16,20},{20,16},{24,28},{28,24},{1,5},{5... | collective-permute-start | bytes 589832 | tf_op jit(solution)/shard_map/ppermute | solution.py:374
  59.0 8.2 %collective-permute-start.20 = (bf16[384,256]{1,0:T(8,128)(2,1)S(1)}, bf16[384,256]{1,0:T(8,128)(2,1)S(1)}, u32[]{:S(2)}, u32[]{:S(2)}) collective-permute-start(bf16[384,256]{1,0:T(8,128)(2,1)S(1)} %get-tuple-element.139), channel_id=1, source_target_pairs={{0,8},{4,12},{8,0},{12,4},{16,24},{20,28},{24,16},{28,20},{1,9},{5... | collective-permute-start | bytes 589832 | tf_op jit(solution)/shard_map/ppermute | solution.py:374
  61.5 9.3 %collective-permute-start.21 = (bf16[384,256]{1,0:T(8,128)(2,1)S(1)}, bf16[384,256]{1,0:T(8,128)(2,1)S(1)}, u32[]{:S(2)}, u32[]{:S(2)}) collective-permute-start(bf16[384,256]{1,0:T(8,128)(2,1)S(1)} %get-tuple-element.140), channel_id=1, source_target_pairs={{0,12},{4,8},{8,4},{12,0},{16,28},{20,24},{24,20},{28,16},{1,13},{... | collective-permute-start | bytes 589832 | tf_op jit(solution)/shard_map/ppermute | solution.py:374
  64.9 7.8 %collective-permute-start.24 = (bf16[96,1024]{1,0:T(8,128)(2,1)S(1)}, bf16[96,1024]{1,0:T(8,128)(2,1)S(1)}, u32[]{:S(2)}, u32[]{:S(2)}) collective-permute-start(bf16[96,1024]{1,0:T(8,128)(2,1)S(1)} %get-tuple-element.147), channel_id=1, source_target_pairs={{0,2},{1,3},{2,0},{3,1},{4,6},{5,7},{6,4},{7,5},{8,10},{9,11},{10,... | collective-permute-start | bytes 589832 | tf_op jit(solution)/shard_map/ppermute | solution.py:370
  65.9 9.5 %collective-permute-start.25 = (bf16[96,1024]{1,0:T(8,128)(2,1)S(1)}, bf16[96,1024]{1,0:T(8,128)(2,1)S(1)}, u32[]{:S(2)}, u32[]{:S(2)}) collective-permute-start(bf16[96,1024]{1,0:T(8,128)(2,1)S(1)} %get-tuple-element.148), channel_id=1, source_target_pairs={{0,3},{1,2},{2,1},{3,0},{4,7},{5,6},{6,5},{7,4},{8,11},{9,10},{10,... | collective-permute-start | bytes 589832 | tf_op jit(solution)/shard_map/ppermute | solution.py:370
  70.7 8.9 %collective-permute-start.22 = (bf16[96,1024]{1,0:T(8,128)(2,1)S(1)}, bf16[96,1024]{1,0:T(8,128)(2,1)S(1)}, u32[]{:S(2)}, u32[]{:S(2)}) collective-permute-start(bf16[96,1024]{1,0:T(8,128)(2,1)S(1)} %get-tuple-element.142), channel_id=1, source_target_pairs={{0,1},{1,0},{2,3},{3,2},{4,5},{5,4},{6,7},{7,6},{8,9},{9,8},{10,11... | collective-permute-start | bytes 589832 | tf_op jit(solution)/shard_map/ppermute | solution.py:370
  70.7 8.9 %collective-permute-start.23 = (bf16[96,1024]{1,0:T(8,128)(2,1)S(1)}, bf16[96,1024]{1,0:T(8,128)(2,1)S(1)}, u32[]{:S(2)}, u32[]{:S(2)}) collective-permute-start(bf16[96,1024]{1,0:T(8,128)(2,1)S(1)} %get-tuple-element.146), channel_id=1, source_target_pairs={{0,1},{1,0},{2,3},{3,2},{4,5},{5,4},{6,7},{7,6},{8,9},{9,8},{10,11... | collective-permute-start | bytes 589832 | tf_op jit(solution)/shard_map/ppermute | solution.py:370
  71.7 5.7 %collective-permute-start.26 = (bf16[96,512]{1,0:T(8,128)(2,1)S(1)}, bf16[96,512]{1,0:T(8,128)(2,1)S(1)}, u32[]{:S(2)}, u32[]{:S(2)}) collective-permute-start(bf16[96,512]{1,0:T(8,128)(2,1)S(1)} %get-tuple-element.158), channel_id=1, source_target_pairs={{0,1},{1,0},{2,3},{3,2},{4,5},{5,4},{6,7},{7,6},{8,9},{9,8},{10,11... | collective-permute-start | bytes 294920 | tf_op jit(solution)/shard_map/ppermute | solution.py:370
  72.7 5.3 %collective-permute-start.27 = (bf16[96,512]{1,0:T(8,128)(2,1)S(1)}, bf16[96,512]{1,0:T(8,128)(2,1)S(1)}, u32[]{:S(2)}, u32[]{:S(2)}) collective-permute-start(bf16[96,512]{1,0:T(8,128)(2,1)S(1)} %get-tuple-element.159), channel_id=1, source_target_pairs={{0,2},{1,3},{2,0},{3,1},{4,6},{5,7},{6,4},{7,5},{8,10},{9,11},{10,... | collective-permute-start | bytes 294920 | tf_op jit(solution)/shard_map/ppermute | solution.py:370
  75.4 4.2 %collective-permute-start.28 = (bf16[96,512]{1,0:T(8,128)(2,1)S(1)}, bf16[96,512]{1,0:T(8,128)(2,1)S(1)}, u32[]{:S(2)}, u32[]{:S(2)}) collective-permute-start(bf16[96,512]{1,0:T(8,128)(2,1)S(1)} %get-tuple-element.160), channel_id=1, source_target_pairs={{0,3},{1,2},{2,1},{3,0},{4,7},{5,6},{6,5},{7,4},{8,11},{9,10},{10,... | collective-permute-start | bytes 294920 | tf_op jit(solution)/shard_map/ppermute | solution.py:370

commit v5 on v4

--- a/solution.py
+++ b/solution.py
@@ -58,48 +58,55 @@
         copy.wait()
 
 
-def pack_heads(queries, keys, values, file_ids, head_count, chunks, whole):
-    part, rows = queries.shape[0], file_ids.shape[1]
-    width = queries.shape[1] // (head_count * chunks)
-    layout = []
-    for step in range(head_count):
-        layout += [(step, 0, chunks)] if step in whole else [(step, c, 1) for c in range(chunks)]
-
-    def kernel(q_ref, k_ref, v_ref, id_ref, *refs):
-        kv_outs, q_outs = refs[:head_count], refs[head_count : head_count + len(layout)]
-        tag_out, sems = refs[-2:]
+def pack_kv(keys, values, head_count, chunks):
+    def kernel(k_ref, v_ref, *refs):
+        outs, sems = refs[:-1], refs[-1]
         own = lax.axis_index("head")
         pairs = []
         for step in range(head_count):
             for chunk in range(chunks):
                 cols = aligned((own ^ step) * chunks + chunk, DH)
                 at = 2 * DH * chunk
-                pairs.append((k_ref.at[:, cols], kv_outs[step].at[:, at : at + DH]))
-                pairs.append((v_ref.at[:, cols], kv_outs[step].at[:, at + DH : at + 2 * DH]))
-        for out, (step, chunk, count) in zip(q_outs, layout):
+                pairs.append((k_ref.at[:, cols], outs[step].at[:, at : at + DH]))
+                pairs.append((v_ref.at[:, cols], outs[step].at[:, at + DH : at + 2 * DH]))
+        run_copies(pairs, sems)
+
+    return pl.pallas_call(
+        kernel,
+        out_shape=[jax.ShapeDtypeStruct((keys.shape[0], 2 * chunks * DH), keys.dtype)] * head_count,
+        in_specs=[ANY] * 2,
+        scratch_shapes=[pltpu.SemaphoreType.DMA((2 * head_count * chunks,))],
+        cost_estimate=cost(0, 8 * keys.size),
+        name="pack_kv",
+    )(keys, values)
+
+
+def pack_q(queries, head_count, chunks, whole):
+    part, width = queries.shape[0], queries.shape[1] // (head_count * chunks)
+    layout = []
+    for step in range(head_count):
+        layout += [(step, 0, chunks)] if step in whole else [(step, c, 1) for c in range(chunks)]
+
+    def kernel(q_ref, *refs):
+        outs, sems = refs[:-1], refs[-1]
+        own = lax.axis_index("head")
+        pairs = []
+        for out, (step, chunk, count) in zip(outs, layout):
             first = pl.multiple_of(((own ^ step) * chunks + chunk) * width, width)
             pairs.append((q_ref.at[:, pl.ds(first, count * width)], out))
-        line = lax.broadcasted_iota(jnp.int32, (TAG_ROWS, DH), 0)
-        tags = id_ref[...].astype(jnp.float32)
-        for column in range(0, 2 * DH, DH):
-            value = jnp.zeros((TAG_ROWS, DH), jnp.float32)
-            for first in range(column, rows, 2 * DH):
-                value = jnp.where(line == first // (2 * DH), tags[:, first : first + DH], value)
-            tag_out[:, column : column + DH] = value.astype(jnp.bfloat16)
         run_copies(pairs, sems)
 
     outs = pl.pallas_call(
         kernel,
-        out_shape=[jax.ShapeDtypeStruct((part, 2 * chunks * DH), keys.dtype)] * head_count
-        + [jax.ShapeDtypeStruct((part, count * width), queries.dtype) for _, _, count in layout]
-        + [jax.ShapeDtypeStruct((TAG_ROWS, 2 * DH), jnp.bfloat16)],
-        in_specs=[ANY] * 3 + [VMEM],
-        scratch_shapes=[pltpu.SemaphoreType.DMA((2 * head_count * chunks + len(layout),))],
-        cost_estimate=cost(0, 4 * (queries.size + 2 * keys.size)),
-        name="pack_heads",
-    )(queries, keys, values, file_ids)
-    q_outs = outs[head_count:-1]
-    return outs[:head_count], {(k[0], k[1]): out for out, k in zip(q_outs, layout)}, outs[-1]
+        out_shape=[
+            jax.ShapeDtypeStruct((part, count * width), queries.dtype) for _, _, count in layout
+        ],
+        in_specs=[ANY],
+        scratch_shapes=[pltpu.SemaphoreType.DMA((len(layout),))],
+        cost_estimate=cost(0, 4 * queries.size),
+        name="pack_q",
+    )(queries)
+    return {(step, chunk): out for out, (step, chunk, _) in zip(outs, layout)}
 
 
 def join_kv(parts, tags, chunks):
@@ -374,14 +381,19 @@
         return lax.ppermute(block, "ctx", pairs)
 
     steps = range(head_count)
-    kv_packed, packed, tags = pack_heads(
-        queries, keys, values, file_ids[None, :], head_count, chunks, whole
-    )
+    kv_packed = pack_kv(keys, values, head_count, chunks)
+    queries, kv_packed, file_ids = lax.optimization_barrier((queries, kv_packed, file_ids))
     kv_parts = [over_head(kv_packed[step], step) for step in steps]
-    q_sent = {(step, 0): over_head(packed.pop((step, 0)), step) for step in whole}
-    packed, kv_parts, tags, q_sent = lax.optimization_barrier((packed, kv_parts, tags, q_sent))
+    packed = pack_q(queries, head_count, chunks, whole)
+    rows = file_ids.shape[0]
+    tags = jnp.pad(file_ids.astype(jnp.bfloat16), (0, TAG_ROWS * 2 * DH - rows))
+    tags = tags.reshape(TAG_ROWS, 2 * DH)
+    packed, kv_parts, tags = lax.optimization_barrier((packed, kv_parts, tags))
     kv_joined = join_kv(kv_parts, tags, chunks)
-    q_sent.update({key: over_head(packed[key], key[0]) for key in packed})
+    q_sent = {key: over_head(packed[key], key[0]) for key in packed}
+    near = {(step, 0): q_sent.pop((step, 0)) for step in whole}
+    kv_joined, near = lax.optimization_barrier((kv_joined, near))
+    q_sent.update(near)
     delta = row_deltas(out_grad, attn_out, heads)
     inputs = []
     for chunk in range(chunks):
@@ -411,11 +423,12 @@
         dq_parts.append({step: over_head(dq[step], step) for step in steps if step not in whole})
         dq_kept.append([dq[step] for step in steps if step in whole])
     dq_kept, dkv_parts[-1] = lax.optimization_barrier((dq_kept, dkv_parts[-1]))
+    dq_kept = [[over_head(x, step) for step, x in zip(whole, kept)] for kept in dq_kept]
+    pieces = sum_kv(dkv_parts, head_count, half)
     dq_parts = [
-        [over_head(kept[step], step) if step in whole else sent[step] for step in steps]
+        [kept[step] if step in whole else sent[step] for step in steps]
         for kept, sent in zip(dq_kept, dq_parts)
     ]
-    pieces = sum_kv(dkv_parts, head_count, half)
     return tuple(join_grads(dq_parts, [over_head(pieces[step], step) for step in steps]))
 
 

time: 82 us -> 81.1 us (0.989)
  waiting for transfers between devices: 31.7 us -> 28 us
  starting transfers between devices: 29.5 us -> 33 us
    ppermute x17, waiting for transfers between devices: 20.1 us -> 10 us  [over_head(): lax.ppermute(block, 'head', [(i, i ^ step) for i in range(head_count)])]
    ppermute x12, waiting for transfers between devices: 11.6 us -> 18 us  [over_ctx(): return lax.ppermute(block, 'ctx', pairs)]
    ppermute x12, starting transfers between devices: 15.7 us -> 18.2 us  [over_ctx(): return lax.ppermute(block, 'ctx', pairs)]
    broadcast_in_dim x1 -> x0, local copies, waits for them, and re-layouts: 1.38 us -> none  [per_device(): file_ids[None, :]]
    ppermute x17, starting transfers between devices: 13.8 us -> 14.9 us  [over_head(): lax.ppermute(block, 'head', [(i, i ^ step) for i in range(head_count)])]
    pallas_call x1 -> x2, Pallas kernels: 3.71 us -> 4.49 us  [the longest x1 2.53 us: pack_q(): pl.pallas_call(kernel, out_shape=[jax.ShapeDtypeStruct((part, count * wid...]
  transfers between devices with their start and end apart: 29 -> 29, of which waited for: 14 -> 14; matrix products, arithmetic and copies ran while one was open for 0% -> 1% of each run, Pallas kernels for 14% -> 17%
where the time goes in v5:
time: 81.1 us; the launch traced here: 80.8 us
  starting transfers between devices  33 us (41%)
  waiting for transfers between devices  28 us (35%)
  Pallas kernels  17 us (21%)
  local copies, waits for them, and re-layouts  2.05 us (3%)
  between operations  0.85 us (1%)
    ppermute x12, starting transfers between devices, over_ctx(): return lax.ppermute(block, 'ctx', pairs)  18.2 us
    ppermute x12, waiting for transfers between devices, over_ctx(): return lax.ppermute(block, 'ctx', pairs)  18 us
    ppermute x17, starting transfers between devices, over_head(): lax.ppermute(block, 'head', [(i, i ^ step) for i in range(head_count)])  14.9 us
    ppermute x17, waiting for transfers between devices, over_head(): lax.ppermute(block, 'head', [(i, i ^ step) for i in range(head_count)])  10 us
    pallas_call x4, Pallas kernels, tile_grads(): pl.pallas_call(kernel, out_shape=[dq_shape] * dq_count + [dkv_shape] * dk...  7.87 us
    pallas_call x1, Pallas kernels, pack_q(): pl.pallas_call(kernel, out_shape=[jax.ShapeDtypeStruct((part, count * wid...  2.53 us
    pallas_call x1, Pallas kernels, pack_kv(): pl.pallas_call(kernel, out_shape=[jax.ShapeDtypeStruct((keys.shape[0], 2...  1.96 us
    pallas_call x1, Pallas kernels, join_kv(): pl.pallas_call(kernel, out_shape=[shape] * chunks, in_specs=[ANY] * (1 +...  1.84 us
  transfers between devices with their start and end apart: 29, of which 14 were waited for; matrix products, arithmetic and copies ran while one was open for 1% of the time, Pallas kernels for 17%

profile of v5, /device:TPU:0, one launch (start us, length us, event | category | flops | bytes accessed | tf_op | source)
XLA Modules:
  0.0 80.8 jit_solution(11628226237809554117)
XLA Ops:
  0.7 2.0 %pack_kv.1 = (bf16[96,512]{1,0:T(8,128)(2,1)}, bf16[96,512]{1,0:T(8,128)(2,1)}, bf16[96,512]{1,0:T(8,128)(2,1)}, bf16[96,512]{1,0:T(8,128)(2,1)}) custom-call(bf16[96,1024]{1,0:T(8,128)(2,1)} %k_ref.1, bf16[96,1024]{1,0:T(8,128)(2,1)} %v_ref.1), custom_call_target="tpu_custom_call" | custom-call | bytes 786432 | tf_op jit(solution)/shard_map/pack_kv/pallas_call | solution.py:74
  2.6 0.5 collective-permute-start
  3.1 2.6 %collective-permute-start.1 = (bf16[96,512]{1,0:T(8,128)(2,1)}, bf16[96,512]{1,0:T(8,128)(2,1)S(1)}, u32[]{:S(2)}, u32[]{:S(2)}) collective-permute-start(bf16[96,512]{1,0:T(8,128)(2,1)} %get-tuple-element.104), channel_id=1, source_target_pairs={{0,2},{1,3},{2,0},{3,1},{4,6},{5,7},{6,4},{7,5},{8,10},{9,11},{10,... | collective-permute-start | bytes 294920 | tf_op jit(solution)/shard_map/ppermute | solution.py:377
  5.7 0.1 collective-permute-start.2
  5.8 2.5 %pack_q.1 = (bf16[96,2048]{1,0:T(8,128)(2,1)}, bf16[96,2048]{1,0:T(8,128)(2,1)}, bf16[96,1024]{1,0:T(8,128)(2,1)}, bf16[96,1024]{1,0:T(8,128)(2,1)}, bf16[96,1024]{1,0:T(8,128)(2,1)}, /*index=5*/bf16[96,1024]{1,0:T(8,128)(2,1)}) custom-call(bf16[96,8192]{1,0:T(8,128)(2,1)} %q_ref), custom_call_target="tpu_custom_call" | custom-call | bytes 3145728 | tf_op jit(solution)/shard_map/pack_q/pallas_call | solution.py:99
  8.4 0.6 reshape.9.tag_ref
  9.0 0.0 collective-permute-done.refs_1_
  9.0 0.6 collective-permute-done.1.refs_2_
  9.6 1.6 %collective-permute-done.2.refs_3_ = bf16[96,512]{1,0:T(8,128)(2,1)S(1)} collective-permute-done((bf16[96,512]{1,0:T(8,128)(2,1)}, bf16[96,512]{1,0:T(8,128)(2,1)S(1)}, u32[]{:S(2)}, u32[]{:S(2)}) %collective-permute-start.2) | collective-permute-done | bytes 98336 | tf_op jit(solution)/shard_map/ppermute | solution.py:377
  11.2 0.1 collective-permute-start.3
  11.3 1.7 %collective-permute-start.4 = (bf16[96,1024]{1,0:T(8,128)(2,1)}, bf16[96,1024]{1,0:T(8,128)(2,1)S(1)}, u32[]{:S(2)}, u32[]{:S(2)}) collective-permute-start(bf16[96,1024]{1,0:T(8,128)(2,1)} %get-tuple-element.118), channel_id=1, source_target_pairs={{0,2},{1,3},{2,0},{3,1},{4,6},{5,7},{6,4},{7,5},{8,10},{9,11},{10,... | collective-permute-start | bytes 589832 | tf_op jit(solution)/shard_map/ppermute | solution.py:377
  13.0 0.0 collective-permute-start.5
  13.1 1.8 %join_kv.1 = (bf16[400,256]{1,0:T(8,128)(2,1)}, bf16[400,256]{1,0:T(8,128)(2,1)}) custom-call(bf16[16,256]{1,0:T(8,128)(2,1)} %reshape.9.tag_ref, bf16[96,512]{1,0:T(8,128)(2,1)} %get-tuple-element.108.refs_0_, bf16[96,512]{1,0:T(8,128)(2,1)} %copy-done.6, bf16[96,512]{1,0:T(8,128)(2,1)} %copy-done.7, bf16[96,512]{1,0:T(8,128)(2,1)} %copy-done.8), custom_call_target="tpu_custom_call" | custom-call | bytes 786432 | tf_op jit(solution)/shard_map/join_kv/pallas_call | solution.py:129
  14.9 1.6 %collective-permute-start.6 = (bf16[400,256]{1,0:T(8,128)(2,1)}, bf16[400,256]{1,0:T(8,128)(2,1)S(1)}, u32[]{:S(2)}, u32[]{:S(2)}) collective-permute-start(bf16[400,256]{1,0:T(8,128)(2,1)} %get-tuple-element.120.refs_7_), channel_id=1, source_target_pairs={{0,4},{4,0},{8,12},{12,8},{16,20},{20,16},{24,28},{28,24},{1,5},{5... | collective-permute-start | bytes 614408 | tf_op jit(solution)/shard_map/ppermute | solution.py:381
  16.5 1.6 %collective-permute-start.7 = (bf16[400,256]{1,0:T(8,128)(2,1)}, bf16[400,256]{1,0:T(8,128)(2,1)S(1)}, u32[]{:S(2)}, u32[]{:S(2)}) collective-permute-start(bf16[400,256]{1,0:T(8,128)(2,1)} %get-tuple-element.120.refs_7_), channel_id=1, source_target_pairs={{0,8},{4,12},{8,0},{12,4},{16,24},{20,28},{24,16},{28,20},{1,9},{5... | collective-permute-start | bytes 614408 | tf_op jit(solution)/shard_map/ppermute | solution.py:381
  18.1 0.4 collective-permute-start.8
  18.5 1.4 %copy-done.1 = bf16[384,2048]{1,0:T(8,128)(2,1)S(1)} copy-done((bf16[384,2048]{1,0:T(8,128)(2,1)S(1)}, bf16[384,2048]{1,0:T(8,128)(2,1)}, u32[]{:S(2)}) %copy-start.1) | copy-done | bytes 1572888
  19.9 0.0 copy-start.5
  19.9 0.9 %row_deltas.1.refs_1_ = f32[16,384]{1,0:T(8,128)S(1)} custom-call(bf16[384,2048]{1,0:T(8,128)(2,1)S(1)} %copy-done.1, bf16[384,2048]{1,0:T(8,128)(2,1)S(1)} %copy-done), custom_call_target="tpu_custom_call" | custom-call | flops 3145728 | bytes 3145728 | tf_op jit(solution)/shard_map/row_deltas/pallas_call | solution.py:44
  20.8 0.0 collective-permute-done.4.refs_5_
  20.8 1.6 %collective-permute-start.9 = (bf16[96,1024]{1,0:T(8,128)(2,1)S(1)}, bf16[96,1024]{1,0:T(8,128)(2,1)S(1)}, u32[]{:S(2)}, u32[]{:S(2)}) collective-permute-start(bf16[96,1024]{1,0:T(8,128)(2,1)S(1)} %copy-done.11), channel_id=1, source_target_pairs={{0,2},{1,3},{2,0},{3,1},{4,6},{5,7},{6,4},{7,5},{8,10},{9,11},{10,... | collective-permute-start | bytes 589832 | tf_op jit(solution)/shard_map/ppermute | solution.py:377
  22.5 1.8 %collective-permute-start.10 = (bf16[96,1024]{1,0:T(8,128)(2,1)S(1)}, bf16[96,1024]{1,0:T(8,128)(2,1)S(1)}, u32[]{:S(2)}, u32[]{:S(2)}) collective-permute-start(bf16[96,1024]{1,0:T(8,128)(2,1)S(1)} %copy-done.10), channel_id=1, source_target_pairs={{0,3},{1,2},{2,1},{3,0},{4,7},{5,6},{6,5},{7,4},{8,11},{9,10},{10,... | collective-permute-start | bytes 589832 | tf_op jit(solution)/shard_map/ppermute | solution.py:377
  24.2 3.3 %own_tile.2 = (f32[1024,384]{1,0:T(8,128)S(1)}, f32[384,256]{1,0:T(8,128)S(1)}) custom-call(f32[16,384]{1,0:T(8,128)S(1)} %copy-done.5, f32[16,384]{1,0:T(8,128)S(1)} %row_deltas.1.refs_1_, bf16[384,2048]{1,0:T(8,128)(2,1)S(1)} %copy-done.1, bf16[96,2048]{1,0:T(8,128)(2,1)S(1)} %copy-done.2, bf16[96,2048]{1,0:T(8,128)(2,1)S(1)} %collective-permute-done.3.refs_4_, ...), custom_call_target="tpu_custom_call" | custom-call | flops 1509949440 | bytes 3932160 | tf_op jit(solution)/shard_map/own_tile/pallas_call | solution.py:286
  27.5 0.0 collective-permute-done.6.refs_8_
  27.5 1.6 %collective-permute-start.11 = (bf16[400,256]{1,0:T(8,128)(2,1)S(1)}, bf16[400,256]{1,0:T(8,128)(2,1)S(1)}, u32[]{:S(2)}, u32[]{:S(2)}) collective-permute-start(bf16[400,256]{1,0:T(8,128)(2,1)S(1)} %copy-done.3), channel_id=1, source_target_pairs={{0,4},{4,0},{8,12},{12,8},{16,20},{20,16},{24,28},{28,24},{1,5},{5... | collective-permute-start | bytes 614408 | tf_op jit(solution)/shard_map/ppermute | solution.py:381
  29.1 1.6 %collective-permute-start.12 = (bf16[400,256]{1,0:T(8,128)(2,1)S(1)}, bf16[400,256]{1,0:T(8,128)(2,1)S(1)}, u32[]{:S(2)}, u32[]{:S(2)}) collective-permute-start(bf16[400,256]{1,0:T(8,128)(2,1)S(1)} %copy-done.3), channel_id=1, source_target_pairs={{0,8},{4,12},{8,0},{12,4},{16,24},{20,28},{24,16},{28,20},{1,9},{5... | collective-permute-start | bytes 614408 | tf_op jit(solution)/shard_map/ppermute | solution.py:381
  30.7 0.0 collective-permute-done.8.refs_10_
  30.7 0.4 collective-permute-start.13
  31.1 0.8 earlier_tiles.2
  31.9 0.0 collective-permute-done.10.refs_6_
  31.9 2.8 %collective-permute-done.11.refs_8_ = bf16[400,256]{1,0:T(8,128)(2,1)S(1)} collective-permute-done((bf16[400,256]{1,0:T(8,128)(2,1)S(1)}, bf16[400,256]{1,0:T(8,128)(2,1)S(1)}, u32[]{:S(2)}, u32[]{:S(2)}) %collective-permute-start.11) | collective-permute-done | bytes 204832 | tf_op jit(solution)/shard_map/ppermute | solution.py:381
  34.7 2.4 %collective-permute-done.12.refs_9_ = bf16[400,256]{1,0:T(8,128)(2,1)S(1)} collective-permute-done((bf16[400,256]{1,0:T(8,128)(2,1)S(1)}, bf16[400,256]{1,0:T(8,128)(2,1)S(1)}, u32[]{:S(2)}, u32[]{:S(2)}) %collective-permute-start.12) | collective-permute-done | bytes 204832 | tf_op jit(solution)/shard_map/ppermute | solution.py:381
  37.1 2.7 %collective-permute-done.13.refs_10_ = bf16[400,256]{1,0:T(8,128)(2,1)S(1)} collective-permute-done((bf16[400,256]{1,0:T(8,128)(2,1)S(1)}, bf16[400,256]{1,0:T(8,128)(2,1)S(1)}, u32[]{:S(2)}, u32[]{:S(2)}) %collective-permute-start.13) | collective-permute-done | bytes 204832 | tf_op jit(solution)/shard_map/ppermute | solution.py:381
  39.8 1.5 %collective-permute-start.14 = (bf16[384,256]{1,0:T(8,128)(2,1)S(1)}, bf16[384,256]{1,0:T(8,128)(2,1)S(1)}, u32[]{:S(2)}, u32[]{:S(2)}) collective-permute-start(bf16[384,256]{1,0:T(8,128)(2,1)S(1)} %get-tuple-element.147), channel_id=1, source_target_pairs={{0,4},{4,0},{8,12},{12,8},{16,20},{20,16},{24,28},{28,24},{1,5},{5... | collective-permute-start | bytes 589832 | tf_op jit(solution)/shard_map/ppermute | solution.py:381
  41.3 3.4 %collective-permute-start.15 = (bf16[384,256]{1,0:T(8,128)(2,1)S(1)}, bf16[384,256]{1,0:T(8,128)(2,1)S(1)}, u32[]{:S(2)}, u32[]{:S(2)}) collective-permute-start(bf16[384,256]{1,0:T(8,128)(2,1)S(1)} %get-tuple-element.148), channel_id=1, source_target_pairs={{0,8},{4,12},{8,0},{12,4},{16,24},{20,28},{24,16},{28,20},{1,9},{5... | collective-permute-start | bytes 589832 | tf_op jit(solution)/shard_map/ppermute | solution.py:381
  44.7 0.5 collective-permute-start.17
  45.2 0.0 collective-permute-start.18
  45.2 0.4 earlier_tiles.3
  45.6 0.0 collective-permute-done.14.refs_1_
  45.6 4.8 %collective-permute-done.15.refs_2_ = bf16[384,256]{1,0:T(8,128)(2,1)S(1)} collective-permute-done((bf16[384,256]{1,0:T(8,128)(2,1)S(1)}, bf16[384,256]{1,0:T(8,128)(2,1)S(1)}, u32[]{:S(2)}, u32[]{:S(2)}) %collective-permute-start.15) | collective-permute-done | bytes 196640 | tf_op jit(solution)/shard_map/ppermute | solution.py:381
  50.4 1.9 %collective-permute-done.16.refs_3_ = bf16[384,256]{1,0:T(8,128)(2,1)S(1)} collective-permute-done((bf16[384,256]{1,0:T(8,128)(2,1)S(1)}, bf16[384,256]{1,0:T(8,128)(2,1)S(1)}, u32[]{:S(2)}, u32[]{:S(2)}) %collective-permute-start.16) | collective-permute-done | bytes 196640 | tf_op jit(solution)/shard_map/ppermute | solution.py:381
  52.3 0.1 collective-permute-done.17.refs_2_
  52.4 0.2 collective-permute-done.18.refs_3_
  52.6 1.5 %collective-permute-start.19 = (bf16[384,256]{1,0:T(8,128)(2,1)S(1)}, bf16[384,256]{1,0:T(8,128)(2,1)S(1)}, u32[]{:S(2)}, u32[]{:S(2)}) collective-permute-start(bf16[384,256]{1,0:T(8,128)(2,1)S(1)} %get-tuple-element.156), channel_id=1, source_target_pairs={{0,4},{4,0},{8,12},{12,8},{16,20},{20,16},{24,28},{28,24},{1,5},{5... | collective-permute-start | bytes 589832 | tf_op jit(solution)/shard_map/ppermute | solution.py:381
  54.1 4.8 %collective-permute-start.20 = (bf16[384,256]{1,0:T(8,128)(2,1)S(1)}, bf16[384,256]{1,0:T(8,128)(2,1)S(1)}, u32[]{:S(2)}, u32[]{:S(2)}) collective-permute-start(bf16[384,256]{1,0:T(8,128)(2,1)S(1)} %get-tuple-element.157), channel_id=1, source_target_pairs={{0,8},{4,12},{8,0},{12,4},{16,24},{20,28},{24,16},{28,20},{1,9},{5... | collective-permute-start | bytes 589832 | tf_op jit(solution)/shard_map/ppermute | solution.py:381
  58.8 3.4 %own_tile.3 = (bf16[96,1024]{1,0:T(8,128)(2,1)S(1)}, bf16[96,1024]{1,0:T(8,128)(2,1)S(1)}, bf16[96,1024]{1,0:T(8,128)(2,1)S(1)}, bf16[96,1024]{1,0:T(8,128)(2,1)S(1)}, f32[384,256]{1,0:T(8,128)S(1)}) custom-call(f32[16,384]{1,0:T(8,128)S(1)} %copy-done.5, f32[16,384]{1,0:T(8,128)S(1)} %row_deltas.1.refs_1_, bf16[384,2048]{1,0:T(8,128)(2,1)S(1)} %copy-done.1, ...), custom_call_target="tpu_custom_call" | custom-call | flops 1509949440 | bytes 3932160 | tf_op jit(solution)/shard_map/own_tile/pallas_call | solution.py:286
  62.2 1.6 %collective-permute-start.24 = (bf16[96,1024]{1,0:T(8,128)(2,1)S(1)}, bf16[96,1024]{1,0:T(8,128)(2,1)S(1)}, u32[]{:S(2)}, u32[]{:S(2)}) collective-permute-start(bf16[96,1024]{1,0:T(8,128)(2,1)S(1)} %get-tuple-element.165), channel_id=1, source_target_pairs={{0,2},{1,3},{2,0},{3,1},{4,6},{5,7},{6,4},{7,5},{8,10},{9,11},{10,... | collective-permute-start | bytes 589832 | tf_op jit(solution)/shard_map/ppermute | solution.py:377
  63.8 0.9 %collective-permute-start.25 = (bf16[96,1024]{1,0:T(8,128)(2,1)S(1)}, bf16[96,1024]{1,0:T(8,128)(2,1)S(1)}, u32[]{:S(2)}, u32[]{:S(2)}) collective-permute-start(bf16[96,1024]{1,0:T(8,128)(2,1)S(1)} %get-tuple-element.166), channel_id=1, source_target_pairs={{0,3},{1,2},{2,1},{3,0},{4,7},{5,6},{6,5},{7,4},{8,11},{9,10},{10,... | collective-permute-start | bytes 589832 | tf_op jit(solution)/shard_map/ppermute | solution.py:377
  64.7 0.0 collective-permute-done.19.refs_5_
  64.7 0.0 collective-permute-done.20.refs_6_
  64.7 3.3 %collective-permute-done.21.refs_7_ = bf16[384,256]{1,0:T(8,128)(2,1)S(1)} collective-permute-done((bf16[384,256]{1,0:T(8,128)(2,1)S(1)}, bf16[384,256]{1,0:T(8,128)(2,1)S(1)}, u32[]{:S(2)}, u32[]{:S(2)}) %collective-permute-start.21) | collective-permute-done | bytes 196640 | tf_op jit(solution)/shard_map/ppermute | solution.py:381
  68.0 0.4 collective-permute-start.22
  68.4 0.1 collective-permute-start.23
  68.5 0.4 sum_kv.1
  69.0 0.5 collective-permute-start.26
  69.4 0.5 collective-permute-done.24.refs_6_
  70.0 1.6 %collective-permute-start.27 = (bf16[96,512]{1,0:T(8,128)(2,1)S(1)}, bf16[96,512]{1,0:T(8,128)(2,1)S(1)}, u32[]{:S(2)}, u32[]{:S(2)}) collective-permute-start(bf16[96,512]{1,0:T(8,128)(2,1)S(1)} %get-tuple-element.177), channel_id=1, source_target_pairs={{0,2},{1,3},{2,0},{3,1},{4,6},{5,7},{6,4},{7,5},{8,10},{9,11},{10,... | collective-permute-start | bytes 294920 | tf_op jit(solution)/shard_map/ppermute | solution.py:377
  71.6 2.8 %collective-permute-done.25.refs_7_ = bf16[96,1024]{1,0:T(8,128)(2,1)S(1)} collective-permute-done((bf16[96,1024]{1,0:T(8,128)(2,1)S(1)}, bf16[96,1024]{1,0:T(8,128)(2,1)S(1)}, u32[]{:S(2)}, u32[]{:S(2)}) %collective-permute-start.25) | collective-permute-done | bytes 196640 | tf_op jit(solution)/shard_map/ppermute | solution.py:377
  74.4 0.8 %collective-permute-start.28 = (bf16[96,512]{1,0:T(8,128)(2,1)S(1)}, bf16[96,512]{1,0:T(8,128)(2,1)S(1)}, u32[]{:S(2)}, u32[]{:S(2)}) collective-permute-start(bf16[96,512]{1,0:T(8,128)(2,1)S(1)} %get-tuple-element.178), channel_id=1, source_target_pairs={{0,3},{1,2},{2,1},{3,0},{4,7},{5,6},{6,5},{7,4},{8,11},{9,10},{10,... | collective-permute-start | bytes 294920 | tf_op jit(solution)/shard_map/ppermute | solution.py:377
  75.2 0.0 collective-permute-done.26.refs_9_
  75.2 1.1 %collective-permute-done.27.refs_10_ = bf16[96,512]{1,0:T(8,128)(2,1)S(1)} collective-permute-done((bf16[96,512]{1,0:T(8,128)(2,1)S(1)}, bf16[96,512]{1,0:T(8,128)(2,1)S(1)}, u32[]{:S(2)}, u32[]{:S(2)}) %collective-permute-start.27) | collective-permute-done | bytes 98336 | tf_op jit(solution)/shard_map/ppermute | solution.py:377
  76.3 3.1 %collective-permute-done.28.refs_11_ = bf16[96,512]{1,0:T(8,128)(2,1)S(1)} collective-permute-done((bf16[96,512]{1,0:T(8,128)(2,1)S(1)}, bf16[96,512]{1,0:T(8,128)(2,1)S(1)}, u32[]{:S(2)}, u32[]{:S(2)}) %collective-permute-start.28) | collective-permute-done | bytes 98336 | tf_op jit(solution)/shard_map/ppermute | solution.py:377
  79.4 0.0 collective-permute-done.22.refs_1_
  79.4 1.4 %join_grads.1 = (bf16[96,8192]{1,0:T(8,128)(2,1)}, bf16[96,1024]{1,0:T(8,128)(2,1)}, bf16[96,1024]{1,0:T(8,128)(2,1)}) custom-call(bf16[96,1024]{1,0:T(8,128)(2,1)S(1)} %get-tuple-element.159.refs_0_, bf16[96,1024]{1,0:T(8,128)(2,1)S(1)} %collective-permute-done.22.refs_1_, bf16[96,1024]{1,0:T(8,128)(2,1)S(1)} %collective-permute-done.17.refs_2_, ...), custom_call_target="tpu_custom_call" | custom-call | bytes 3932160 | tf_op jit(solution)/shard_map/join_grads/pallas_call | solution.py:357
  (31 shorter events, 0.1 us)
Async XLA Ops:
  0.6 7.7 %copy-start.9 = (s32[384]{0:T(512)S(1)}, s32[384]{0:T(512)}, u32[]{:S(2)}) copy-start(s32[384]{0:T(512)} %param.13) | copy-start | bytes 4612
  0.6 17.8 %copy-start = (bf16[384,2048]{1,0:T(8,128)(2,1)S(1)}, bf16[384,2048]{1,0:T(8,128)(2,1)}, u32[]{:S(2)}) copy-start(bf16[384,2048]{1,0:T(8,128)(2,1)} %out_ref.1) | copy-start | bytes 4718596
  2.6 6.3 %collective-permute-start = (bf16[96,512]{1,0:T(8,128)(2,1)}, bf16[96,512]{1,0:T(8,128)(2,1)S(1)}, u32[]{:S(2)}, u32[]{:S(2)}) collective-permute-start(bf16[96,512]{1,0:T(8,128)(2,1)} %get-tuple-element.103), channel_id=1, source_target_pairs={{0,1},{1,0},{2,3},{3,2},{4,5},{5,4},{6,7},{7,6},{8,9},{9,8},{10,11... | collective-permute-start | bytes 294920 | tf_op jit(solution)/shard_map/ppermute | solution.py:377
  3.1 6.4 %collective-permute-start.1 = (bf16[96,512]{1,0:T(8,128)(2,1)}, bf16[96,512]{1,0:T(8,128)(2,1)S(1)}, u32[]{:S(2)}, u32[]{:S(2)}) collective-permute-start(bf16[96,512]{1,0:T(8,128)(2,1)} %get-tuple-element.104), channel_id=1, source_target_pairs={{0,2},{1,3},{2,0},{3,1},{4,6},{5,7},{6,4},{7,5},{8,10},{9,11},{10,... | collective-permute-start | bytes 294920 | tf_op jit(solution)/shard_map/ppermute | solution.py:377
  5.7 5.4 %collective-permute-start.2 = (bf16[96,512]{1,0:T(8,128)(2,1)}, bf16[96,512]{1,0:T(8,128)(2,1)S(1)}, u32[]{:S(2)}, u32[]{:S(2)}) collective-permute-start(bf16[96,512]{1,0:T(8,128)(2,1)} %get-tuple-element.105), channel_id=1, source_target_pairs={{0,3},{1,2},{2,1},{3,0},{4,7},{5,6},{6,5},{7,4},{8,11},{9,10},{10,... | collective-permute-start | bytes 294920 | tf_op jit(solution)/shard_map/ppermute | solution.py:377
  9.0 4.1 %copy-start.6 = (bf16[96,512]{1,0:T(8,128)(2,1)}, bf16[96,512]{1,0:T(8,128)(2,1)S(1)}, u32[]{:S(2)}) copy-start(bf16[96,512]{1,0:T(8,128)(2,1)S(1)} %collective-permute-done.refs_1_) | copy-start | bytes 294916
  9.6 3.5 %copy-start.7 = (bf16[96,512]{1,0:T(8,128)(2,1)}, bf16[96,512]{1,0:T(8,128)(2,1)S(1)}, u32[]{:S(2)}) copy-start(bf16[96,512]{1,0:T(8,128)(2,1)S(1)} %collective-permute-done.1.refs_2_) | copy-start | bytes 294916
  11.2 1.9 %copy-start.8 = (bf16[96,512]{1,0:T(8,128)(2,1)}, bf16[96,512]{1,0:T(8,128)(2,1)S(1)}, u32[]{:S(2)}) copy-start(bf16[96,512]{1,0:T(8,128)(2,1)S(1)} %collective-permute-done.2.refs_3_) | copy-start | bytes 294916
  11.2 3.7 %collective-permute-start.3 = (bf16[96,2048]{1,0:T(8,128)(2,1)}, bf16[96,2048]{1,0:T(8,128)(2,1)S(1)}, u32[]{:S(2)}, u32[]{:S(2)}) collective-permute-start(bf16[96,2048]{1,0:T(8,128)(2,1)} %get-tuple-element.115), channel_id=1, source_target_pairs={{0,1},{1,0},{2,3},{3,2},{4,5},{5,4},{6,7},{7,6},{8,9},{9,8},{10,11... | collective-permute-start | bytes 1179656 | tf_op jit(solution)/shard_map/ppermute | solution.py:377
  11.3 9.5 %collective-permute-start.4 = (bf16[96,1024]{1,0:T(8,128)(2,1)}, bf16[96,1024]{1,0:T(8,128)(2,1)S(1)}, u32[]{:S(2)}, u32[]{:S(2)}) collective-permute-start(bf16[96,1024]{1,0:T(8,128)(2,1)} %get-tuple-element.118), channel_id=1, source_target_pairs={{0,2},{1,3},{2,0},{3,1},{4,6},{5,7},{6,4},{7,5},{8,10},{9,11},{10,... | collective-permute-start | bytes 589832 | tf_op jit(solution)/shard_map/ppermute | solution.py:377
  13.0 9.4 %collective-permute-start.5 = (bf16[96,1024]{1,0:T(8,128)(2,1)}, bf16[96,1024]{1,0:T(8,128)(2,1)S(1)}, u32[]{:S(2)}, u32[]{:S(2)}) collective-permute-start(bf16[96,1024]{1,0:T(8,128)(2,1)} %get-tuple-element.119), channel_id=1, source_target_pairs={{0,3},{1,2},{2,1},{3,0},{4,7},{5,6},{6,5},{7,4},{8,11},{9,10},{10,... | collective-permute-start | bytes 589832 | tf_op jit(solution)/shard_map/ppermute | solution.py:377
  14.9 12.6 %collective-permute-start.6 = (bf16[400,256]{1,0:T(8,128)(2,1)}, bf16[400,256]{1,0:T(8,128)(2,1)S(1)}, u32[]{:S(2)}, u32[]{:S(2)}) collective-permute-start(bf16[400,256]{1,0:T(8,128)(2,1)} %get-tuple-element.120.refs_7_), channel_id=1, source_target_pairs={{0,4},{4,0},{8,12},{12,8},{16,20},{20,16},{24,28},{28,24},{1,5},{5... | collective-permute-start | bytes 614408 | tf_op jit(solution)/shard_map/ppermute | solution.py:381
  16.5 12.6 %collective-permute-start.7 = (bf16[400,256]{1,0:T(8,128)(2,1)}, bf16[400,256]{1,0:T(8,128)(2,1)S(1)}, u32[]{:S(2)}, u32[]{:S(2)}) collective-permute-start(bf16[400,256]{1,0:T(8,128)(2,1)} %get-tuple-element.120.refs_7_), channel_id=1, source_target_pairs={{0,8},{4,12},{8,0},{12,4},{16,24},{20,28},{24,16},{28,20},{1,9},{5... | collective-permute-start | bytes 614408 | tf_op jit(solution)/shard_map/ppermute | solution.py:381
  18.1 12.6 %collective-permute-start.8 = (bf16[400,256]{1,0:T(8,128)(2,1)}, bf16[400,256]{1,0:T(8,128)(2,1)S(1)}, u32[]{:S(2)}, u32[]{:S(2)}) collective-permute-start(bf16[400,256]{1,0:T(8,128)(2,1)} %get-tuple-element.120.refs_7_), channel_id=1, source_target_pairs={{0,12},{4,8},{8,4},{12,0},{16,28},{20,24},{24,20},{28,16},{1,13},{... | collective-permute-start | bytes 614408 | tf_op jit(solution)/shard_map/ppermute | solution.py:381
  18.5 1.4 %copy-start.1 = (bf16[384,2048]{1,0:T(8,128)(2,1)S(1)}, bf16[384,2048]{1,0:T(8,128)(2,1)}, u32[]{:S(2)}) copy-start(bf16[384,2048]{1,0:T(8,128)(2,1)} %refs_2_.7) | copy-start | bytes 4718596
  19.9 0.9 %copy-start.11 = (bf16[96,1024]{1,0:T(8,128)(2,1)S(1)}, bf16[96,1024]{1,0:T(8,128)(2,1)}, u32[]{:S(2)}) copy-start(bf16[96,1024]{1,0:T(8,128)(2,1)} %get-tuple-element.129) | copy-start | bytes 589828
  19.9 2.6 %copy-start.10 = (bf16[96,1024]{1,0:T(8,128)(2,1)S(1)}, bf16[96,1024]{1,0:T(8,128)(2,1)}, u32[]{:S(2)}) copy-start(bf16[96,1024]{1,0:T(8,128)(2,1)} %get-tuple-element.130) | copy-start | bytes 589828
  19.9 4.3 %copy-start.2 = (bf16[96,2048]{1,0:T(8,128)(2,1)S(1)}, bf16[96,2048]{1,0:T(8,128)(2,1)}, u32[]{:S(2)}) copy-start(bf16[96,2048]{1,0:T(8,128)(2,1)} %get-tuple-element.134.refs_3_) | copy-start | bytes 1179652
  19.9 4.3 %copy-start.4 = (bf16[400,256]{1,0:T(8,128)(2,1)S(1)}, bf16[400,256]{1,0:T(8,128)(2,1)}, u32[]{:S(2)}) copy-start(bf16[400,256]{1,0:T(8,128)(2,1)} %get-tuple-element.120.refs_7_) | copy-start | bytes 614404
  19.9 4.3 %copy-start.5 = (f32[16,384]{1,0:T(8,128)S(1)}, f32[16,384]{1,0:T(8,128)}, u32[]{:S(2)}) copy-start(f32[16,384]{1,0:T(8,128)} %refs_0_.7) | copy-start | bytes 73732
  20.8 6.7 %copy-start.3 = (bf16[400,256]{1,0:T(8,128)(2,1)S(1)}, bf16[400,256]{1,0:T(8,128)(2,1)}, u32[]{:S(2)}) copy-start(bf16[400,256]{1,0:T(8,128)(2,1)} %get-tuple-element.138.refs_7_) | copy-start | bytes 614404
  20.8 11.0 %collective-permute-start.9 = (bf16[96,1024]{1,0:T(8,128)(2,1)S(1)}, bf16[96,1024]{1,0:T(8,128)(2,1)S(1)}, u32[]{:S(2)}, u32[]{:S(2)}) collective-permute-start(bf16[96,1024]{1,0:T(8,128)(2,1)S(1)} %copy-done.11), channel_id=1, source_target_pairs={{0,2},{1,3},{2,0},{3,1},{4,6},{5,7},{6,4},{7,5},{8,10},{9,11},{10,... | collective-permute-start | bytes 589832 | tf_op jit(solution)/shard_map/ppermute | solution.py:377
  22.5 9.4 %collective-permute-start.10 = (bf16[96,1024]{1,0:T(8,128)(2,1)S(1)}, bf16[96,1024]{1,0:T(8,128)(2,1)S(1)}, u32[]{:S(2)}, u32[]{:S(2)}) collective-permute-start(bf16[96,1024]{1,0:T(8,128)(2,1)S(1)} %copy-done.10), channel_id=1, source_target_pairs={{0,3},{1,2},{2,1},{3,0},{4,7},{5,6},{6,5},{7,4},{8,11},{9,10},{10,... | collective-permute-start | bytes 589832 | tf_op jit(solution)/shard_map/ppermute | solution.py:377
  27.5 7.2 %collective-permute-start.11 = (bf16[400,256]{1,0:T(8,128)(2,1)S(1)}, bf16[400,256]{1,0:T(8,128)(2,1)S(1)}, u32[]{:S(2)}, u32[]{:S(2)}) collective-permute-start(bf16[400,256]{1,0:T(8,128)(2,1)S(1)} %copy-done.3), channel_id=1, source_target_pairs={{0,4},{4,0},{8,12},{12,8},{16,20},{20,16},{24,28},{28,24},{1,5},{5... | collective-permute-start | bytes 614408 | tf_op jit(solution)/shard_map/ppermute | solution.py:381
  29.1 8.0 %collective-permute-start.12 = (bf16[400,256]{1,0:T(8,128)(2,1)S(1)}, bf16[400,256]{1,0:T(8,128)(2,1)S(1)}, u32[]{:S(2)}, u32[]{:S(2)}) collective-permute-start(bf16[400,256]{1,0:T(8,128)(2,1)S(1)} %copy-done.3), channel_id=1, source_target_pairs={{0,8},{4,12},{8,0},{12,4},{16,24},{20,28},{24,16},{28,20},{1,9},{5... | collective-permute-start | bytes 614408 | tf_op jit(solution)/shard_map/ppermute | solution.py:381
  30.7 9.2 %collective-permute-start.13 = (bf16[400,256]{1,0:T(8,128)(2,1)S(1)}, bf16[400,256]{1,0:T(8,128)(2,1)S(1)}, u32[]{:S(2)}, u32[]{:S(2)}) collective-permute-start(bf16[400,256]{1,0:T(8,128)(2,1)S(1)} %copy-done.3), channel_id=1, source_target_pairs={{0,12},{4,8},{8,4},{12,0},{16,28},{20,24},{24,20},{28,16},{1,13},{... | collective-permute-start | bytes 614408 | tf_op jit(solution)/shard_map/ppermute | solution.py:381
  39.8 5.8 %collective-permute-start.14 = (bf16[384,256]{1,0:T(8,128)(2,1)S(1)}, bf16[384,256]{1,0:T(8,128)(2,1)S(1)}, u32[]{:S(2)}, u32[]{:S(2)}) collective-permute-start(bf16[384,256]{1,0:T(8,128)(2,1)S(1)} %get-tuple-element.147), channel_id=1, source_target_pairs={{0,4},{4,0},{8,12},{12,8},{16,20},{20,16},{24,28},{28,24},{1,5},{5... | collective-permute-start | bytes 589832 | tf_op jit(solution)/shard_map/ppermute | solution.py:381
  41.3 9.1 %collective-permute-start.15 = (bf16[384,256]{1,0:T(8,128)(2,1)S(1)}, bf16[384,256]{1,0:T(8,128)(2,1)S(1)}, u32[]{:S(2)}, u32[]{:S(2)}) collective-permute-start(bf16[384,256]{1,0:T(8,128)(2,1)S(1)} %get-tuple-element.148), channel_id=1, source_target_pairs={{0,8},{4,12},{8,0},{12,4},{16,24},{20,28},{24,16},{28,20},{1,9},{5... | collective-permute-start | bytes 589832 | tf_op jit(solution)/shard_map/ppermute | solution.py:381
  44.7 7.6 %collective-permute-start.16 = (bf16[384,256]{1,0:T(8,128)(2,1)S(1)}, bf16[384,256]{1,0:T(8,128)(2,1)S(1)}, u32[]{:S(2)}, u32[]{:S(2)}) collective-permute-start(bf16[384,256]{1,0:T(8,128)(2,1)S(1)} %get-tuple-element.149), channel_id=1, source_target_pairs={{0,12},{4,8},{8,4},{12,0},{16,28},{20,24},{24,20},{28,16},{1,13},{... | collective-permute-start | bytes 589832 | tf_op jit(solution)/shard_map/ppermute | solution.py:381
  44.7 7.7 %collective-permute-start.17 = (bf16[96,1024]{1,0:T(8,128)(2,1)S(1)}, bf16[96,1024]{1,0:T(8,128)(2,1)S(1)}, u32[]{:S(2)}, u32[]{:S(2)}) collective-permute-start(bf16[96,1024]{1,0:T(8,128)(2,1)S(1)} %get-tuple-element.150), channel_id=1, source_target_pairs={{0,2},{1,3},{2,0},{3,1},{4,6},{5,7},{6,4},{7,5},{8,10},{9,11},{10,... | collective-permute-start | bytes 589832 | tf_op jit(solution)/shard_map/ppermute | solution.py:377
  45.2 7.4 %collective-permute-start.18 = (bf16[96,1024]{1,0:T(8,128)(2,1)S(1)}, bf16[96,1024]{1,0:T(8,128)(2,1)S(1)}, u32[]{:S(2)}, u32[]{:S(2)}) collective-permute-start(bf16[96,1024]{1,0:T(8,128)(2,1)S(1)} %get-tuple-element.151), channel_id=1, source_target_pairs={{0,3},{1,2},{2,1},{3,0},{4,7},{5,6},{6,5},{7,4},{8,11},{9,10},{10,... | collective-permute-start | bytes 589832 | tf_op jit(solution)/shard_map/ppermute | solution.py:377
  52.6 12.1 %collective-permute-start.19 = (bf16[384,256]{1,0:T(8,128)(2,1)S(1)}, bf16[384,256]{1,0:T(8,128)(2,1)S(1)}, u32[]{:S(2)}, u32[]{:S(2)}) collective-permute-start(bf16[384,256]{1,0:T(8,128)(2,1)S(1)} %get-tuple-element.156), channel_id=1, source_target_pairs={{0,4},{4,0},{8,12},{12,8},{16,20},{20,16},{24,28},{28,24},{1,5},{5... | collective-permute-start | bytes 589832 | tf_op jit(solution)/shard_map/ppermute | solution.py:381
  54.1 10.7 %collective-permute-start.20 = (bf16[384,256]{1,0:T(8,128)(2,1)S(1)}, bf16[384,256]{1,0:T(8,128)(2,1)S(1)}, u32[]{:S(2)}, u32[]{:S(2)}) collective-permute-start(bf16[384,256]{1,0:T(8,128)(2,1)S(1)} %get-tuple-element.157), channel_id=1, source_target_pairs={{0,8},{4,12},{8,0},{12,4},{16,24},{20,28},{24,16},{28,20},{1,9},{5... | collective-permute-start | bytes 589832 | tf_op jit(solution)/shard_map/ppermute | solution.py:381
  58.8 9.2 %collective-permute-start.21 = (bf16[384,256]{1,0:T(8,128)(2,1)S(1)}, bf16[384,256]{1,0:T(8,128)(2,1)S(1)}, u32[]{:S(2)}, u32[]{:S(2)}) collective-permute-start(bf16[384,256]{1,0:T(8,128)(2,1)S(1)} %get-tuple-element.158), channel_id=1, source_target_pairs={{0,12},{4,8},{8,4},{12,0},{16,28},{20,24},{24,20},{28,16},{1,13},{... | collective-permute-start | bytes 589832 | tf_op jit(solution)/shard_map/ppermute | solution.py:381
  62.2 7.7 %collective-permute-start.24 = (bf16[96,1024]{1,0:T(8,128)(2,1)S(1)}, bf16[96,1024]{1,0:T(8,128)(2,1)S(1)}, u32[]{:S(2)}, u32[]{:S(2)}) collective-permute-start(bf16[96,1024]{1,0:T(8,128)(2,1)S(1)} %get-tuple-element.165), channel_id=1, source_target_pairs={{0,2},{1,3},{2,0},{3,1},{4,6},{5,7},{6,4},{7,5},{8,10},{9,11},{10,... | collective-permute-start | bytes 589832 | tf_op jit(solution)/shard_map/ppermute | solution.py:377
  63.8 10.6 %collective-permute-start.25 = (bf16[96,1024]{1,0:T(8,128)(2,1)S(1)}, bf16[96,1024]{1,0:T(8,128)(2,1)S(1)}, u32[]{:S(2)}, u32[]{:S(2)}) collective-permute-start(bf16[96,1024]{1,0:T(8,128)(2,1)S(1)} %get-tuple-element.166), channel_id=1, source_target_pairs={{0,3},{1,2},{2,1},{3,0},{4,7},{5,6},{6,5},{7,4},{8,11},{9,10},{10,... | collective-permute-start | bytes 589832 | tf_op jit(solution)/shard_map/ppermute | solution.py:377
  68.0 11.4 %collective-permute-start.22 = (bf16[96,1024]{1,0:T(8,128)(2,1)S(1)}, bf16[96,1024]{1,0:T(8,128)(2,1)S(1)}, u32[]{:S(2)}, u32[]{:S(2)}) collective-permute-start(bf16[96,1024]{1,0:T(8,128)(2,1)S(1)} %get-tuple-element.160), channel_id=1, source_target_pairs={{0,1},{1,0},{2,3},{3,2},{4,5},{5,4},{6,7},{7,6},{8,9},{9,8},{10,11... | collective-permute-start | bytes 589832 | tf_op jit(solution)/shard_map/ppermute | solution.py:377
  68.4 11.0 %collective-permute-start.23 = (bf16[96,1024]{1,0:T(8,128)(2,1)S(1)}, bf16[96,1024]{1,0:T(8,128)(2,1)S(1)}, u32[]{:S(2)}, u32[]{:S(2)}) collective-permute-start(bf16[96,1024]{1,0:T(8,128)(2,1)S(1)} %get-tuple-element.164), channel_id=1, source_target_pairs={{0,1},{1,0},{2,3},{3,2},{4,5},{5,4},{6,7},{7,6},{8,9},{9,8},{10,11... | collective-permute-start | bytes 589832 | tf_op jit(solution)/shard_map/ppermute | solution.py:377
  69.0 6.3 %collective-permute-start.26 = (bf16[96,512]{1,0:T(8,128)(2,1)S(1)}, bf16[96,512]{1,0:T(8,128)(2,1)S(1)}, u32[]{:S(2)}, u32[]{:S(2)}) collective-permute-start(bf16[96,512]{1,0:T(8,128)(2,1)S(1)} %get-tuple-element.176), channel_id=1, source_target_pairs={{0,1},{1,0},{2,3},{3,2},{4,5},{5,4},{6,7},{7,6},{8,9},{9,8},{10,11... | collective-permute-start | bytes 294920 | tf_op jit(solution)/shard_map/ppermute | solution.py:377
  70.0 6.3 %collective-permute-start.27 = (bf16[96,512]{1,0:T(8,128)(2,1)S(1)}, bf16[96,512]{1,0:T(8,128)(2,1)S(1)}, u32[]{:S(2)}, u32[]{:S(2)}) collective-permute-start(bf16[96,512]{1,0:T(8,128)(2,1)S(1)} %get-tuple-element.177), channel_id=1, source_target_pairs={{0,2},{1,3},{2,0},{3,1},{4,6},{5,7},{6,4},{7,5},{8,10},{9,11},{10,... | collective-permute-start | bytes 294920 | tf_op jit(solution)/shard_map/ppermute | solution.py:377
  74.4 5.0 %collective-permute-start.28 = (bf16[96,512]{1,0:T(8,128)(2,1)S(1)}, bf16[96,512]{1,0:T(8,128)(2,1)S(1)}, u32[]{:S(2)}, u32[]{:S(2)}) collective-permute-start(bf16[96,512]{1,0:T(8,128)(2,1)S(1)} %get-tuple-element.178), channel_id=1, source_target_pairs={{0,3},{1,2},{2,1},{3,0},{4,7},{5,6},{6,5},{7,4},{8,11},{9,10},{10,... | collective-permute-start | bytes 294920 | tf_op jit(solution)/shard_map/ppermute | solution.py:377

commit v6 on v5

--- a/solution.py
+++ b/solution.py
@@ -103,6 +103,7 @@
         ],
         in_specs=[ANY],
         scratch_shapes=[pltpu.SemaphoreType.DMA((len(layout),))],
+        compiler_params=pltpu.CompilerParams(vmem_limit_bytes=16 << 20),
         cost_estimate=cost(0, 4 * queries.size),
         name="pack_q",
     )(queries)
@@ -115,22 +116,18 @@
     rows = part * head_count
 
     def kernel(tag_ref, *refs):
-        ins, outs, sems = refs[:head_count], refs[head_count:-1], refs[-1]
+        ins, outs = refs[:head_count], refs[head_count:]
         own = lax.axis_index("head")
-        pairs = []
         for chunk, out in enumerate(outs):
-            cols = slice(chunk * width, (chunk + 1) * width)
             for step in range(head_count):
-                pairs.append((ins[step].at[:, cols], out.at[aligned(own ^ step, part)]))
-            pairs.append((tag_ref, out.at[rows:]))
-        run_copies(pairs, sems)
+                out[aligned(own ^ step, part), :] = ins[step][:, chunk * width : (chunk + 1) * width]
+            out[rows:, :] = tag_ref[...]
 
     shape = jax.ShapeDtypeStruct((rows + TAG_ROWS, width), parts[0].dtype)
     return pl.pallas_call(
         kernel,
         out_shape=[shape] * chunks,
-        in_specs=[ANY] * (1 + head_count),
-        scratch_shapes=[pltpu.SemaphoreType.DMA((chunks * (head_count + 1),))],
+        compiler_params=pltpu.CompilerParams(vmem_limit_bytes=16 << 20),
         cost_estimate=cost(0, 4 * rows * width * chunks),
         name="join_kv",
     )(tags, *parts)
@@ -156,6 +153,7 @@
         start_ref = refs.pop(0) if sum_in else None
         dq_out, dkv_out = refs[:dq_count], refs[dq_count : dq_count + dkv_count]
         q_buf, kv_buf, dkv_buf, dq_acc, dq_low, dk_acc, dv_acc, bias = refs[dq_count + dkv_count :]
+        dq_acc = dq_acc if final else dq_out[0]
         head_index = lax.axis_index("head")
         own = lax.rem(lax.axis_index("ctx"), half)
         for step, ref in enumerate(q_in):
@@ -275,8 +273,6 @@
                 dq_low[:, cols] = jnp.transpose(low)
             for step in range(head_count):
                 dq_out[step][...] = dq_low[aligned(head_index ^ step, part), :]
-        else:
-            dq_out[0][...] = dq_acc[...]
 
     bf16, f32 = jnp.bfloat16, jnp.float32
     dq_shape = jax.ShapeDtypeStruct((part, width), bf16)

time: 81.1 us -> 80.8 us (level)
  Pallas kernels: 17 us -> 12.6 us
  waiting for transfers between devices: 28 us -> 29.8 us
  local copies, waits for them, and re-layouts: 2.05 us -> 3.73 us
    pallas_call x1, Pallas kernels: 2.53 us -> 0.23 us  [pack_q(): pl.pallas_call(kernel, out_shape=[jax.ShapeDtypeStruct((part, count * wid...]
    ppermute x17, waiting for transfers between devices: 10 us -> 12.3 us  [over_head(): lax.ppermute(block, 'head', [(i, i ^ step) for i in range(head_count)])]
    unnamed x24 -> x12, local copies, waits for them, and re-layouts: 1.45 us -> 3.72 us
    pallas_call x1, Pallas kernels: 1.84 us -> 0.04 us  [join_kv(): pl.pallas_call(kernel, out_shape=[shape] * chunks, compiler_params=pltpu....]
  transfers between devices with their start and end apart: 29 -> 29, of which waited for: 14 -> 15; matrix products, arithmetic and copies ran while one was open for 1% -> 0% of each run, Pallas kernels for 17% -> 12%
where the time goes in v6:
time: 80.8 us; the launch traced here: 80.5 us
  starting transfers between devices  33.5 us (41%)
  waiting for transfers between devices  29.8 us (37%)
  Pallas kernels  12.6 us (16%)
  local copies, waits for them, and re-layouts  3.73 us (5%)
  between operations  0.81 us (1%)
    ppermute x12, starting transfers between devices, over_ctx(): return lax.ppermute(block, 'ctx', pairs)  18.2 us
    ppermute x12, waiting for transfers between devices, over_ctx(): return lax.ppermute(block, 'ctx', pairs)  17.5 us
    ppermute x17, starting transfers between devices, over_head(): lax.ppermute(block, 'head', [(i, i ^ step) for i in range(head_count)])  15.3 us
    ppermute x17, waiting for transfers between devices, over_head(): lax.ppermute(block, 'head', [(i, i ^ step) for i in range(head_count)])  12.3 us
    pallas_call x4, Pallas kernels, tile_grads(): pl.pallas_call(kernel, out_shape=[dq_shape] * dq_count + [dkv_shape] * dk...  7.76 us
    unnamed x12, local copies, waits for them, and re-layouts  3.72 us
    pallas_call x1, Pallas kernels, pack_kv(): pl.pallas_call(kernel, out_shape=[jax.ShapeDtypeStruct((keys.shape[0], 2...  1.84 us
  transfers between devices with their start and end apart: 29, of which 15 were waited for; matrix products, arithmetic and copies ran while one was open for 0% of the time, Pallas kernels for 12%

profile of v6, /device:TPU:0, one launch (start us, length us, event | category | flops | bytes accessed | tf_op | source)
XLA Modules:
  0.0 80.5 jit_solution(12789338203741460170)
XLA Ops:
  0.6 1.8 %pack_kv.1 = (bf16[96,512]{1,0:T(8,128)(2,1)}, bf16[96,512]{1,0:T(8,128)(2,1)}, bf16[96,512]{1,0:T(8,128)(2,1)}, bf16[96,512]{1,0:T(8,128)(2,1)}) custom-call(bf16[96,1024]{1,0:T(8,128)(2,1)} %k_ref.1, bf16[96,1024]{1,0:T(8,128)(2,1)} %v_ref.1), custom_call_target="tpu_custom_call" | custom-call | bytes 786432 | tf_op jit(solution)/shard_map/pack_kv/pallas_call | solution.py:74
  2.5 0.5 collective-permute-start
  3.0 2.6 %collective-permute-start.1 = (bf16[96,512]{1,0:T(8,128)(2,1)}, bf16[96,512]{1,0:T(8,128)(2,1)S(1)}, u32[]{:S(2)}, u32[]{:S(2)}) collective-permute-start(bf16[96,512]{1,0:T(8,128)(2,1)} %get-tuple-element.104), channel_id=1, source_target_pairs={{0,2},{1,3},{2,0},{3,1},{4,6},{5,7},{6,4},{7,5},{8,10},{9,11},{10,... | collective-permute-start | bytes 294920 | tf_op jit(solution)/shard_map/ppermute | solution.py:373
  5.6 0.1 collective-permute-start.2
  5.7 1.4 %copy-done = bf16[96,8192]{1,0:T(8,128)(2,1)S(1)} copy-done((bf16[96,8192]{1,0:T(8,128)(2,1)S(1)}, bf16[96,8192]{1,0:T(8,128)(2,1)}, u32[]{:S(2)}) %copy-start) | copy-done | bytes 1572888
  7.1 0.2 pack_q.1
  7.4 0.0 collective-permute-done.refs_1_
  7.4 2.1 %collective-permute-done.1.refs_2_ = bf16[96,512]{1,0:T(8,128)(2,1)S(1)} collective-permute-done((bf16[96,512]{1,0:T(8,128)(2,1)}, bf16[96,512]{1,0:T(8,128)(2,1)S(1)}, u32[]{:S(2)}, u32[]{:S(2)}) %collective-permute-start.1) | collective-permute-done | bytes 98336 | tf_op jit(solution)/shard_map/ppermute | solution.py:373
  9.5 1.6 %collective-permute-done.2.refs_3_ = bf16[96,512]{1,0:T(8,128)(2,1)S(1)} collective-permute-done((bf16[96,512]{1,0:T(8,128)(2,1)}, bf16[96,512]{1,0:T(8,128)(2,1)S(1)}, u32[]{:S(2)}, u32[]{:S(2)}) %collective-permute-start.2) | collective-permute-done | bytes 98336 | tf_op jit(solution)/shard_map/ppermute | solution.py:373
  11.0 0.1 collective-permute-start.3
  11.2 1.7 %collective-permute-start.4 = (bf16[96,1024]{1,0:T(8,128)(2,1)S(1)}, bf16[96,1024]{1,0:T(8,128)(2,1)S(1)}, u32[]{:S(2)}, u32[]{:S(2)}) collective-permute-start(bf16[96,1024]{1,0:T(8,128)(2,1)S(1)} %get-tuple-element.118), channel_id=1, source_target_pairs={{0,2},{1,3},{2,0},{3,1},{4,6},{5,7},{6,4},{7,5},{8,10},{9,11},{10,... | collective-permute-start | bytes 589832 | tf_op jit(solution)/shard_map/ppermute | solution.py:373
  12.9 0.0 collective-permute-start.5
  12.9 0.9 %copy-done.3 = bf16[96,512]{1,0:T(8,128)(2,1)S(1)} copy-done((bf16[96,512]{1,0:T(8,128)(2,1)S(1)}, bf16[96,512]{1,0:T(8,128)(2,1)}, u32[]{:S(2)}) %copy-start.3) | copy-done | bytes 98328
  13.8 0.0 collective-permute-done.3.refs_4_
  13.9 1.6 %collective-permute-start.6 = (bf16[400,256]{1,0:T(8,128)(2,1)S(1)}, bf16[400,256]{1,0:T(8,128)(2,1)S(1)}, u32[]{:S(2)}, u32[]{:S(2)}) collective-permute-start(bf16[400,256]{1,0:T(8,128)(2,1)S(1)} %get-tuple-element.120.refs_7_), channel_id=1, source_target_pairs={{0,4},{4,0},{8,12},{12,8},{16,20},{20,16},{24,28},{28,24},{1,5},{5... | collective-permute-start | bytes 614408 | tf_op jit(solution)/shard_map/ppermute | solution.py:377
  15.4 1.6 %collective-permute-start.7 = (bf16[400,256]{1,0:T(8,128)(2,1)S(1)}, bf16[400,256]{1,0:T(8,128)(2,1)S(1)}, u32[]{:S(2)}, u32[]{:S(2)}) collective-permute-start(bf16[400,256]{1,0:T(8,128)(2,1)S(1)} %get-tuple-element.120.refs_7_), channel_id=1, source_target_pairs={{0,8},{4,12},{8,0},{12,4},{16,24},{20,28},{24,16},{28,20},{1,9},{5... | collective-permute-start | bytes 614408 | tf_op jit(solution)/shard_map/ppermute | solution.py:377
  17.0 0.4 collective-permute-start.8
  17.4 1.4 %copy-done.2 = bf16[384,2048]{1,0:T(8,128)(2,1)S(1)} copy-done((bf16[384,2048]{1,0:T(8,128)(2,1)S(1)}, bf16[384,2048]{1,0:T(8,128)(2,1)}, u32[]{:S(2)}) %copy-start.2) | copy-done | bytes 1572888
  18.8 0.9 %row_deltas.1.refs_1_ = f32[16,384]{1,0:T(8,128)S(1)} custom-call(bf16[384,2048]{1,0:T(8,128)(2,1)S(1)} %copy-done.2, bf16[384,2048]{1,0:T(8,128)(2,1)S(1)} %copy-done.1), custom_call_target="tpu_custom_call" | custom-call | flops 3145728 | bytes 3145728 | tf_op jit(solution)/shard_map/row_deltas/pallas_call | solution.py:44
  19.7 0.0 collective-permute-done.4.refs_5_
  19.7 1.6 %collective-permute-start.9 = (bf16[96,1024]{1,0:T(8,128)(2,1)S(1)}, bf16[96,1024]{1,0:T(8,128)(2,1)S(1)}, u32[]{:S(2)}, u32[]{:S(2)}) collective-permute-start(bf16[96,1024]{1,0:T(8,128)(2,1)S(1)} %get-tuple-element.129), channel_id=1, source_target_pairs={{0,2},{1,3},{2,0},{3,1},{4,6},{5,7},{6,4},{7,5},{8,10},{9,11},{10,... | collective-permute-start | bytes 589832 | tf_op jit(solution)/shard_map/ppermute | solution.py:373
  21.3 0.7 collective-permute-done.5.refs_6_
  22.1 2.2 %collective-permute-start.10 = (bf16[96,1024]{1,0:T(8,128)(2,1)S(1)}, bf16[96,1024]{1,0:T(8,128)(2,1)S(1)}, u32[]{:S(2)}, u32[]{:S(2)}) collective-permute-start(bf16[96,1024]{1,0:T(8,128)(2,1)S(1)} %get-tuple-element.130), channel_id=1, source_target_pairs={{0,3},{1,2},{2,1},{3,0},{4,7},{5,6},{6,5},{7,4},{8,11},{9,10},{10,... | collective-permute-start | bytes 589832 | tf_op jit(solution)/shard_map/ppermute | solution.py:373
  24.3 3.3 %own_tile.2 = (f32[1024,384]{1,0:T(8,128)S(1)}, f32[384,256]{1,0:T(8,128)S(1)}) custom-call(f32[16,384]{1,0:T(8,128)S(1)} %copy-done.4, f32[16,384]{1,0:T(8,128)S(1)} %row_deltas.1.refs_1_, bf16[384,2048]{1,0:T(8,128)(2,1)S(1)} %copy-done.2, bf16[96,2048]{1,0:T(8,128)(2,1)S(1)} %get-tuple-element.134.refs_3_, ...), custom_call_target="tpu_custom_call" | custom-call | flops 1509949440 | bytes 3932160 | tf_op jit(solution)/shard_map/own_tile/pallas_call | solution.py:282
  27.6 0.0 collective-permute-done.6.refs_8_
  27.6 1.3 %collective-permute-start.11 = (bf16[400,256]{1,0:T(8,128)(2,1)S(1)}, bf16[400,256]{1,0:T(8,128)(2,1)S(1)}, u32[]{:S(2)}, u32[]{:S(2)}) collective-permute-start(bf16[400,256]{1,0:T(8,128)(2,1)S(1)} %get-tuple-element.138.refs_7_), channel_id=1, source_target_pairs={{0,4},{4,0},{8,12},{12,8},{16,20},{20,16},{24,28},{28,24},{1,5},{5... | collective-permute-start | bytes 614408 | tf_op jit(solution)/shard_map/ppermute | solution.py:377
  28.8 0.0 collective-permute-done.7.refs_9_
  28.8 1.6 %collective-permute-start.12 = (bf16[400,256]{1,0:T(8,128)(2,1)S(1)}, bf16[400,256]{1,0:T(8,128)(2,1)S(1)}, u32[]{:S(2)}, u32[]{:S(2)}) collective-permute-start(bf16[400,256]{1,0:T(8,128)(2,1)S(1)} %get-tuple-element.138.refs_7_), channel_id=1, source_target_pairs={{0,8},{4,12},{8,0},{12,4},{16,24},{20,28},{24,16},{28,20},{1,9},{5... | collective-permute-start | bytes 614408 | tf_op jit(solution)/shard_map/ppermute | solution.py:377
  30.4 0.0 collective-permute-done.8.refs_10_
  30.4 0.7 collective-permute-start.13
  31.1 0.8 earlier_tiles.2
  31.9 0.0 collective-permute-done.10.refs_6_
  32.0 2.8 %collective-permute-done.11.refs_8_ = bf16[400,256]{1,0:T(8,128)(2,1)S(1)} collective-permute-done((bf16[400,256]{1,0:T(8,128)(2,1)S(1)}, bf16[400,256]{1,0:T(8,128)(2,1)S(1)}, u32[]{:S(2)}, u32[]{:S(2)}) %collective-permute-start.11) | collective-permute-done | bytes 204832 | tf_op jit(solution)/shard_map/ppermute | solution.py:377
  34.7 2.1 %collective-permute-done.12.refs_9_ = bf16[400,256]{1,0:T(8,128)(2,1)S(1)} collective-permute-done((bf16[400,256]{1,0:T(8,128)(2,1)S(1)}, bf16[400,256]{1,0:T(8,128)(2,1)S(1)}, u32[]{:S(2)}, u32[]{:S(2)}) %collective-permute-start.12) | collective-permute-done | bytes 204832 | tf_op jit(solution)/shard_map/ppermute | solution.py:377
  36.9 2.6 %collective-permute-done.13.refs_10_ = bf16[400,256]{1,0:T(8,128)(2,1)S(1)} collective-permute-done((bf16[400,256]{1,0:T(8,128)(2,1)S(1)}, bf16[400,256]{1,0:T(8,128)(2,1)S(1)}, u32[]{:S(2)}, u32[]{:S(2)}) %collective-permute-start.13) | collective-permute-done | bytes 204832 | tf_op jit(solution)/shard_map/ppermute | solution.py:377
  39.5 1.5 %collective-permute-start.14 = (bf16[384,256]{1,0:T(8,128)(2,1)S(1)}, bf16[384,256]{1,0:T(8,128)(2,1)S(1)}, u32[]{:S(2)}, u32[]{:S(2)}) collective-permute-start(bf16[384,256]{1,0:T(8,128)(2,1)S(1)} %get-tuple-element.147), channel_id=1, source_target_pairs={{0,4},{4,0},{8,12},{12,8},{16,20},{20,16},{24,28},{28,24},{1,5},{5... | collective-permute-start | bytes 589832 | tf_op jit(solution)/shard_map/ppermute | solution.py:377
  41.0 3.5 %collective-permute-start.15 = (bf16[384,256]{1,0:T(8,128)(2,1)S(1)}, bf16[384,256]{1,0:T(8,128)(2,1)S(1)}, u32[]{:S(2)}, u32[]{:S(2)}) collective-permute-start(bf16[384,256]{1,0:T(8,128)(2,1)S(1)} %get-tuple-element.148), channel_id=1, source_target_pairs={{0,8},{4,12},{8,0},{12,4},{16,24},{20,28},{24,16},{28,20},{1,9},{5... | collective-permute-start | bytes 589832 | tf_op jit(solution)/shard_map/ppermute | solution.py:377
  44.5 0.5 collective-permute-start.17
  45.0 0.3 earlier_tiles.3
  45.3 0.0 collective-permute-done.14.refs_1_
  45.3 4.8 %collective-permute-done.15.refs_2_ = bf16[384,256]{1,0:T(8,128)(2,1)S(1)} collective-permute-done((bf16[384,256]{1,0:T(8,128)(2,1)S(1)}, bf16[384,256]{1,0:T(8,128)(2,1)S(1)}, u32[]{:S(2)}, u32[]{:S(2)}) %collective-permute-start.15) | collective-permute-done | bytes 196640 | tf_op jit(solution)/shard_map/ppermute | solution.py:377
  50.1 1.9 %collective-permute-done.16.refs_3_ = bf16[384,256]{1,0:T(8,128)(2,1)S(1)} collective-permute-done((bf16[384,256]{1,0:T(8,128)(2,1)S(1)}, bf16[384,256]{1,0:T(8,128)(2,1)S(1)}, u32[]{:S(2)}, u32[]{:S(2)}) %collective-permute-start.16) | collective-permute-done | bytes 196640 | tf_op jit(solution)/shard_map/ppermute | solution.py:377
  52.0 0.2 collective-permute-done.17.refs_2_
  52.2 0.2 collective-permute-done.18.refs_3_
  52.4 1.5 %collective-permute-start.19 = (bf16[384,256]{1,0:T(8,128)(2,1)S(1)}, bf16[384,256]{1,0:T(8,128)(2,1)S(1)}, u32[]{:S(2)}, u32[]{:S(2)}) collective-permute-start(bf16[384,256]{1,0:T(8,128)(2,1)S(1)} %get-tuple-element.156), channel_id=1, source_target_pairs={{0,4},{4,0},{8,12},{12,8},{16,20},{20,16},{24,28},{28,24},{1,5},{5... | collective-permute-start | bytes 589832 | tf_op jit(solution)/shard_map/ppermute | solution.py:377
  53.8 4.6 %collective-permute-start.20 = (bf16[384,256]{1,0:T(8,128)(2,1)S(1)}, bf16[384,256]{1,0:T(8,128)(2,1)S(1)}, u32[]{:S(2)}, u32[]{:S(2)}) collective-permute-start(bf16[384,256]{1,0:T(8,128)(2,1)S(1)} %get-tuple-element.157), channel_id=1, source_target_pairs={{0,8},{4,12},{8,0},{12,4},{16,24},{20,28},{24,16},{28,20},{1,9},{5... | collective-permute-start | bytes 589832 | tf_op jit(solution)/shard_map/ppermute | solution.py:377
  58.5 3.4 %own_tile.3 = (bf16[96,1024]{1,0:T(8,128)(2,1)S(1)}, bf16[96,1024]{1,0:T(8,128)(2,1)S(1)}, bf16[96,1024]{1,0:T(8,128)(2,1)S(1)}, bf16[96,1024]{1,0:T(8,128)(2,1)S(1)}, f32[384,256]{1,0:T(8,128)S(1)}) custom-call(f32[16,384]{1,0:T(8,128)S(1)} %copy-done.4, f32[16,384]{1,0:T(8,128)S(1)} %row_deltas.1.refs_1_, bf16[384,2048]{1,0:T(8,128)(2,1)S(1)} %copy-done.2, ...), custom_call_target="tpu_custom_call" | custom-call | flops 1509949440 | bytes 3932160 | tf_op jit(solution)/shard_map/own_tile/pallas_call | solution.py:282
  61.9 1.6 %collective-permute-start.24 = (bf16[96,1024]{1,0:T(8,128)(2,1)S(1)}, bf16[96,1024]{1,0:T(8,128)(2,1)S(1)}, u32[]{:S(2)}, u32[]{:S(2)}) collective-permute-start(bf16[96,1024]{1,0:T(8,128)(2,1)S(1)} %get-tuple-element.165), channel_id=1, source_target_pairs={{0,2},{1,3},{2,0},{3,1},{4,6},{5,7},{6,4},{7,5},{8,10},{9,11},{10,... | collective-permute-start | bytes 589832 | tf_op jit(solution)/shard_map/ppermute | solution.py:373
  63.5 0.9 %collective-permute-start.25 = (bf16[96,1024]{1,0:T(8,128)(2,1)S(1)}, bf16[96,1024]{1,0:T(8,128)(2,1)S(1)}, u32[]{:S(2)}, u32[]{:S(2)}) collective-permute-start(bf16[96,1024]{1,0:T(8,128)(2,1)S(1)} %get-tuple-element.166), channel_id=1, source_target_pairs={{0,3},{1,2},{2,1},{3,0},{4,7},{5,6},{6,5},{7,4},{8,11},{9,10},{10,... | collective-permute-start | bytes 589832 | tf_op jit(solution)/shard_map/ppermute | solution.py:373
  64.4 0.0 collective-permute-done.19.refs_5_
  64.4 0.0 collective-permute-done.20.refs_6_
  64.4 3.3 %collective-permute-done.21.refs_7_ = bf16[384,256]{1,0:T(8,128)(2,1)S(1)} collective-permute-done((bf16[384,256]{1,0:T(8,128)(2,1)S(1)}, bf16[384,256]{1,0:T(8,128)(2,1)S(1)}, u32[]{:S(2)}, u32[]{:S(2)}) %collective-permute-start.21) | collective-permute-done | bytes 196640 | tf_op jit(solution)/shard_map/ppermute | solution.py:377
  67.7 0.4 collective-permute-start.22
  68.1 0.1 collective-permute-start.23
  68.2 0.4 sum_kv.1
  68.6 0.5 collective-permute-start.26
  69.1 0.5 collective-permute-done.24.refs_6_
  69.6 1.6 %collective-permute-start.27 = (bf16[96,512]{1,0:T(8,128)(2,1)S(1)}, bf16[96,512]{1,0:T(8,128)(2,1)S(1)}, u32[]{:S(2)}, u32[]{:S(2)}) collective-permute-start(bf16[96,512]{1,0:T(8,128)(2,1)S(1)} %get-tuple-element.177), channel_id=1, source_target_pairs={{0,2},{1,3},{2,0},{3,1},{4,6},{5,7},{6,4},{7,5},{8,10},{9,11},{10,... | collective-permute-start | bytes 294920 | tf_op jit(solution)/shard_map/ppermute | solution.py:373
  71.2 2.8 %collective-permute-done.25.refs_7_ = bf16[96,1024]{1,0:T(8,128)(2,1)S(1)} collective-permute-done((bf16[96,1024]{1,0:T(8,128)(2,1)S(1)}, bf16[96,1024]{1,0:T(8,128)(2,1)S(1)}, u32[]{:S(2)}, u32[]{:S(2)}) %collective-permute-start.25) | collective-permute-done | bytes 196640 | tf_op jit(solution)/shard_map/ppermute | solution.py:373
  74.0 0.8 %collective-permute-start.28 = (bf16[96,512]{1,0:T(8,128)(2,1)S(1)}, bf16[96,512]{1,0:T(8,128)(2,1)S(1)}, u32[]{:S(2)}, u32[]{:S(2)}) collective-permute-start(bf16[96,512]{1,0:T(8,128)(2,1)S(1)} %get-tuple-element.178), channel_id=1, source_target_pairs={{0,3},{1,2},{2,1},{3,0},{4,7},{5,6},{6,5},{7,4},{8,11},{9,10},{10,... | collective-permute-start | bytes 294920 | tf_op jit(solution)/shard_map/ppermute | solution.py:373
  74.9 0.0 collective-permute-done.26.refs_9_
  74.9 1.1 %collective-permute-done.27.refs_10_ = bf16[96,512]{1,0:T(8,128)(2,1)S(1)} collective-permute-done((bf16[96,512]{1,0:T(8,128)(2,1)S(1)}, bf16[96,512]{1,0:T(8,128)(2,1)S(1)}, u32[]{:S(2)}, u32[]{:S(2)}) %collective-permute-start.27) | collective-permute-done | bytes 98336 | tf_op jit(solution)/shard_map/ppermute | solution.py:373
  75.9 3.1 %collective-permute-done.28.refs_11_ = bf16[96,512]{1,0:T(8,128)(2,1)S(1)} collective-permute-done((bf16[96,512]{1,0:T(8,128)(2,1)S(1)}, bf16[96,512]{1,0:T(8,128)(2,1)S(1)}, u32[]{:S(2)}, u32[]{:S(2)}) %collective-permute-start.28) | collective-permute-done | bytes 98336 | tf_op jit(solution)/shard_map/ppermute | solution.py:373
  79.0 1.4 %join_grads.1 = (bf16[96,8192]{1,0:T(8,128)(2,1)}, bf16[96,1024]{1,0:T(8,128)(2,1)}, bf16[96,1024]{1,0:T(8,128)(2,1)}) custom-call(bf16[96,1024]{1,0:T(8,128)(2,1)S(1)} %get-tuple-element.159.refs_0_, bf16[96,1024]{1,0:T(8,128)(2,1)S(1)} %collective-permute-done.22.refs_1_, bf16[96,1024]{1,0:T(8,128)(2,1)S(1)} %collective-permute-done.17.refs_2_, ...), custom_call_target="tpu_custom_call" | custom-call | bytes 3932160 | tf_op jit(solution)/shard_map/join_grads/pallas_call | solution.py:353
  (19 shorter events, 0.1 us)
Async XLA Ops:
  0.6 6.7 %copy-start.5 = (s32[384]{0:T(512)S(1)}, s32[384]{0:T(512)}, u32[]{:S(2)}) copy-start(s32[384]{0:T(512)} %param.13) | copy-start | bytes 4612
  2.5 4.9 %collective-permute-start = (bf16[96,512]{1,0:T(8,128)(2,1)}, bf16[96,512]{1,0:T(8,128)(2,1)S(1)}, u32[]{:S(2)}, u32[]{:S(2)}) collective-permute-start(bf16[96,512]{1,0:T(8,128)(2,1)} %get-tuple-element.103), channel_id=1, source_target_pairs={{0,1},{1,0},{2,3},{3,2},{4,5},{5,4},{6,7},{7,6},{8,9},{9,8},{10,11... | collective-permute-start | bytes 294920 | tf_op jit(solution)/shard_map/ppermute | solution.py:373
  3.0 6.4 %collective-permute-start.1 = (bf16[96,512]{1,0:T(8,128)(2,1)}, bf16[96,512]{1,0:T(8,128)(2,1)S(1)}, u32[]{:S(2)}, u32[]{:S(2)}) collective-permute-start(bf16[96,512]{1,0:T(8,128)(2,1)} %get-tuple-element.104), channel_id=1, source_target_pairs={{0,2},{1,3},{2,0},{3,1},{4,6},{5,7},{6,4},{7,5},{8,10},{9,11},{10,... | collective-permute-start | bytes 294920 | tf_op jit(solution)/shard_map/ppermute | solution.py:373
  5.6 5.4 %collective-permute-start.2 = (bf16[96,512]{1,0:T(8,128)(2,1)}, bf16[96,512]{1,0:T(8,128)(2,1)S(1)}, u32[]{:S(2)}, u32[]{:S(2)}) collective-permute-start(bf16[96,512]{1,0:T(8,128)(2,1)} %get-tuple-element.105), channel_id=1, source_target_pairs={{0,3},{1,2},{2,1},{3,0},{4,7},{5,6},{6,5},{7,4},{8,11},{9,10},{10,... | collective-permute-start | bytes 294920 | tf_op jit(solution)/shard_map/ppermute | solution.py:373
  5.7 1.4 %copy-start = (bf16[96,8192]{1,0:T(8,128)(2,1)S(1)}, bf16[96,8192]{1,0:T(8,128)(2,1)}, u32[]{:S(2)}) copy-start(bf16[96,8192]{1,0:T(8,128)(2,1)} %q_ref) | copy-start | bytes 4718596
  7.1 10.3 %copy-start.1 = (bf16[384,2048]{1,0:T(8,128)(2,1)S(1)}, bf16[384,2048]{1,0:T(8,128)(2,1)}, u32[]{:S(2)}) copy-start(bf16[384,2048]{1,0:T(8,128)(2,1)} %out_ref.1) | copy-start | bytes 4718596
  11.0 2.8 %collective-permute-start.3 = (bf16[96,2048]{1,0:T(8,128)(2,1)S(1)}, bf16[96,2048]{1,0:T(8,128)(2,1)S(1)}, u32[]{:S(2)}, u32[]{:S(2)}) collective-permute-start(bf16[96,2048]{1,0:T(8,128)(2,1)S(1)} %get-tuple-element.115), channel_id=1, source_target_pairs={{0,1},{1,0},{2,3},{3,2},{4,5},{5,4},{6,7},{7,6},{8,9},{9,8},{10,11... | collective-permute-start | bytes 1179656 | tf_op jit(solution)/shard_map/ppermute | solution.py:373
  11.2 8.6 %collective-permute-start.4 = (bf16[96,1024]{1,0:T(8,128)(2,1)S(1)}, bf16[96,1024]{1,0:T(8,128)(2,1)S(1)}, u32[]{:S(2)}, u32[]{:S(2)}) collective-permute-start(bf16[96,1024]{1,0:T(8,128)(2,1)S(1)} %get-tuple-element.118), channel_id=1, source_target_pairs={{0,2},{1,3},{2,0},{3,1},{4,6},{5,7},{6,4},{7,5},{8,10},{9,11},{10,... | collective-permute-start | bytes 589832 | tf_op jit(solution)/shard_map/ppermute | solution.py:373
  12.9 9.2 %collective-permute-start.5 = (bf16[96,1024]{1,0:T(8,128)(2,1)S(1)}, bf16[96,1024]{1,0:T(8,128)(2,1)S(1)}, u32[]{:S(2)}, u32[]{:S(2)}) collective-permute-start(bf16[96,1024]{1,0:T(8,128)(2,1)S(1)} %get-tuple-element.119), channel_id=1, source_target_pairs={{0,3},{1,2},{2,1},{3,0},{4,7},{5,6},{6,5},{7,4},{8,11},{9,10},{10,... | collective-permute-start | bytes 589832 | tf_op jit(solution)/shard_map/ppermute | solution.py:373
  12.9 0.9 %copy-start.3 = (bf16[96,512]{1,0:T(8,128)(2,1)S(1)}, bf16[96,512]{1,0:T(8,128)(2,1)}, u32[]{:S(2)}) copy-start(bf16[96,512]{1,0:T(8,128)(2,1)} %get-tuple-element.108.refs_0_) | copy-start | bytes 294916
  13.9 13.7 %collective-permute-start.6 = (bf16[400,256]{1,0:T(8,128)(2,1)S(1)}, bf16[400,256]{1,0:T(8,128)(2,1)S(1)}, u32[]{:S(2)}, u32[]{:S(2)}) collective-permute-start(bf16[400,256]{1,0:T(8,128)(2,1)S(1)} %get-tuple-element.120.refs_7_), channel_id=1, source_target_pairs={{0,4},{4,0},{8,12},{12,8},{16,20},{20,16},{24,28},{28,24},{1,5},{5... | collective-permute-start | bytes 614408 | tf_op jit(solution)/shard_map/ppermute | solution.py:377
  15.4 13.4 %collective-permute-start.7 = (bf16[400,256]{1,0:T(8,128)(2,1)S(1)}, bf16[400,256]{1,0:T(8,128)(2,1)S(1)}, u32[]{:S(2)}, u32[]{:S(2)}) collective-permute-start(bf16[400,256]{1,0:T(8,128)(2,1)S(1)} %get-tuple-element.120.refs_7_), channel_id=1, source_target_pairs={{0,8},{4,12},{8,0},{12,4},{16,24},{20,28},{24,16},{28,20},{1,9},{5... | collective-permute-start | bytes 614408 | tf_op jit(solution)/shard_map/ppermute | solution.py:377
  17.0 13.4 %collective-permute-start.8 = (bf16[400,256]{1,0:T(8,128)(2,1)S(1)}, bf16[400,256]{1,0:T(8,128)(2,1)S(1)}, u32[]{:S(2)}, u32[]{:S(2)}) collective-permute-start(bf16[400,256]{1,0:T(8,128)(2,1)S(1)} %get-tuple-element.120.refs_7_), channel_id=1, source_target_pairs={{0,12},{4,8},{8,4},{12,0},{16,28},{20,24},{24,20},{28,16},{1,13},{... | collective-permute-start | bytes 614408 | tf_op jit(solution)/shard_map/ppermute | solution.py:377
  17.4 1.4 %copy-start.2 = (bf16[384,2048]{1,0:T(8,128)(2,1)S(1)}, bf16[384,2048]{1,0:T(8,128)(2,1)}, u32[]{:S(2)}) copy-start(bf16[384,2048]{1,0:T(8,128)(2,1)} %refs_2_.7) | copy-start | bytes 4718596
  18.8 5.5 %copy-start.4 = (f32[16,384]{1,0:T(8,128)S(1)}, f32[16,384]{1,0:T(8,128)}, u32[]{:S(2)}) copy-start(f32[16,384]{1,0:T(8,128)} %refs_0_.7) | copy-start | bytes 73732
  19.7 12.2 %collective-permute-start.9 = (bf16[96,1024]{1,0:T(8,128)(2,1)S(1)}, bf16[96,1024]{1,0:T(8,128)(2,1)S(1)}, u32[]{:S(2)}, u32[]{:S(2)}) collective-permute-start(bf16[96,1024]{1,0:T(8,128)(2,1)S(1)} %get-tuple-element.129), channel_id=1, source_target_pairs={{0,2},{1,3},{2,0},{3,1},{4,6},{5,7},{6,4},{7,5},{8,10},{9,11},{10,... | collective-permute-start | bytes 589832 | tf_op jit(solution)/shard_map/ppermute | solution.py:373
  22.1 9.9 %collective-permute-start.10 = (bf16[96,1024]{1,0:T(8,128)(2,1)S(1)}, bf16[96,1024]{1,0:T(8,128)(2,1)S(1)}, u32[]{:S(2)}, u32[]{:S(2)}) collective-permute-start(bf16[96,1024]{1,0:T(8,128)(2,1)S(1)} %get-tuple-element.130), channel_id=1, source_target_pairs={{0,3},{1,2},{2,1},{3,0},{4,7},{5,6},{6,5},{7,4},{8,11},{9,10},{10,... | collective-permute-start | bytes 589832 | tf_op jit(solution)/shard_map/ppermute | solution.py:373
  27.6 7.2 %collective-permute-start.11 = (bf16[400,256]{1,0:T(8,128)(2,1)S(1)}, bf16[400,256]{1,0:T(8,128)(2,1)S(1)}, u32[]{:S(2)}, u32[]{:S(2)}) collective-permute-start(bf16[400,256]{1,0:T(8,128)(2,1)S(1)} %get-tuple-element.138.refs_7_), channel_id=1, source_target_pairs={{0,4},{4,0},{8,12},{12,8},{16,20},{20,16},{24,28},{28,24},{1,5},{5... | collective-permute-start | bytes 614408 | tf_op jit(solution)/shard_map/ppermute | solution.py:377
  28.8 8.0 %collective-permute-start.12 = (bf16[400,256]{1,0:T(8,128)(2,1)S(1)}, bf16[400,256]{1,0:T(8,128)(2,1)S(1)}, u32[]{:S(2)}, u32[]{:S(2)}) collective-permute-start(bf16[400,256]{1,0:T(8,128)(2,1)S(1)} %get-tuple-element.138.refs_7_), channel_id=1, source_target_pairs={{0,8},{4,12},{8,0},{12,4},{16,24},{20,28},{24,16},{28,20},{1,9},{5... | collective-permute-start | bytes 614408 | tf_op jit(solution)/shard_map/ppermute | solution.py:377
  30.4 9.1 %collective-permute-start.13 = (bf16[400,256]{1,0:T(8,128)(2,1)S(1)}, bf16[400,256]{1,0:T(8,128)(2,1)S(1)}, u32[]{:S(2)}, u32[]{:S(2)}) collective-permute-start(bf16[400,256]{1,0:T(8,128)(2,1)S(1)} %get-tuple-element.138.refs_7_), channel_id=1, source_target_pairs={{0,12},{4,8},{8,4},{12,0},{16,28},{20,24},{24,20},{28,16},{1,13},{... | collective-permute-start | bytes 614408 | tf_op jit(solution)/shard_map/ppermute | solution.py:377
  39.5 5.8 %collective-permute-start.14 = (bf16[384,256]{1,0:T(8,128)(2,1)S(1)}, bf16[384,256]{1,0:T(8,128)(2,1)S(1)}, u32[]{:S(2)}, u32[]{:S(2)}) collective-permute-start(bf16[384,256]{1,0:T(8,128)(2,1)S(1)} %get-tuple-element.147), channel_id=1, source_target_pairs={{0,4},{4,0},{8,12},{12,8},{16,20},{20,16},{24,28},{28,24},{1,5},{5... | collective-permute-start | bytes 589832 | tf_op jit(solution)/shard_map/ppermute | solution.py:377
  41.0 9.1 %collective-permute-start.15 = (bf16[384,256]{1,0:T(8,128)(2,1)S(1)}, bf16[384,256]{1,0:T(8,128)(2,1)S(1)}, u32[]{:S(2)}, u32[]{:S(2)}) collective-permute-start(bf16[384,256]{1,0:T(8,128)(2,1)S(1)} %get-tuple-element.148), channel_id=1, source_target_pairs={{0,8},{4,12},{8,0},{12,4},{16,24},{20,28},{24,16},{28,20},{1,9},{5... | collective-permute-start | bytes 589832 | tf_op jit(solution)/shard_map/ppermute | solution.py:377
  44.5 7.5 %collective-permute-start.16 = (bf16[384,256]{1,0:T(8,128)(2,1)S(1)}, bf16[384,256]{1,0:T(8,128)(2,1)S(1)}, u32[]{:S(2)}, u32[]{:S(2)}) collective-permute-start(bf16[384,256]{1,0:T(8,128)(2,1)S(1)} %get-tuple-element.149), channel_id=1, source_target_pairs={{0,12},{4,8},{8,4},{12,0},{16,28},{20,24},{24,20},{28,16},{1,13},{... | collective-permute-start | bytes 589832 | tf_op jit(solution)/shard_map/ppermute | solution.py:377
  44.5 7.7 %collective-permute-start.17 = (bf16[96,1024]{1,0:T(8,128)(2,1)S(1)}, bf16[96,1024]{1,0:T(8,128)(2,1)S(1)}, u32[]{:S(2)}, u32[]{:S(2)}) collective-permute-start(bf16[96,1024]{1,0:T(8,128)(2,1)S(1)} %get-tuple-element.150), channel_id=1, source_target_pairs={{0,2},{1,3},{2,0},{3,1},{4,6},{5,7},{6,4},{7,5},{8,10},{9,11},{10,... | collective-permute-start | bytes 589832 | tf_op jit(solution)/shard_map/ppermute | solution.py:373
  45.0 7.4 %collective-permute-start.18 = (bf16[96,1024]{1,0:T(8,128)(2,1)S(1)}, bf16[96,1024]{1,0:T(8,128)(2,1)S(1)}, u32[]{:S(2)}, u32[]{:S(2)}) collective-permute-start(bf16[96,1024]{1,0:T(8,128)(2,1)S(1)} %get-tuple-element.151), channel_id=1, source_target_pairs={{0,3},{1,2},{2,1},{3,0},{4,7},{5,6},{6,5},{7,4},{8,11},{9,10},{10,... | collective-permute-start | bytes 589832 | tf_op jit(solution)/shard_map/ppermute | solution.py:373
  52.4 12.0 %collective-permute-start.19 = (bf16[384,256]{1,0:T(8,128)(2,1)S(1)}, bf16[384,256]{1,0:T(8,128)(2,1)S(1)}, u32[]{:S(2)}, u32[]{:S(2)}) collective-permute-start(bf16[384,256]{1,0:T(8,128)(2,1)S(1)} %get-tuple-element.156), channel_id=1, source_target_pairs={{0,4},{4,0},{8,12},{12,8},{16,20},{20,16},{24,28},{28,24},{1,5},{5... | collective-permute-start | bytes 589832 | tf_op jit(solution)/shard_map/ppermute | solution.py:377
  53.8 10.5 %collective-permute-start.20 = (bf16[384,256]{1,0:T(8,128)(2,1)S(1)}, bf16[384,256]{1,0:T(8,128)(2,1)S(1)}, u32[]{:S(2)}, u32[]{:S(2)}) collective-permute-start(bf16[384,256]{1,0:T(8,128)(2,1)S(1)} %get-tuple-element.157), channel_id=1, source_target_pairs={{0,8},{4,12},{8,0},{12,4},{16,24},{20,28},{24,16},{28,20},{1,9},{5... | collective-permute-start | bytes 589832 | tf_op jit(solution)/shard_map/ppermute | solution.py:377
  58.5 9.2 %collective-permute-start.21 = (bf16[384,256]{1,0:T(8,128)(2,1)S(1)}, bf16[384,256]{1,0:T(8,128)(2,1)S(1)}, u32[]{:S(2)}, u32[]{:S(2)}) collective-permute-start(bf16[384,256]{1,0:T(8,128)(2,1)S(1)} %get-tuple-element.158), channel_id=1, source_target_pairs={{0,12},{4,8},{8,4},{12,0},{16,28},{20,24},{24,20},{28,16},{1,13},{... | collective-permute-start | bytes 589832 | tf_op jit(solution)/shard_map/ppermute | solution.py:377
  61.9 7.7 %collective-permute-start.24 = (bf16[96,1024]{1,0:T(8,128)(2,1)S(1)}, bf16[96,1024]{1,0:T(8,128)(2,1)S(1)}, u32[]{:S(2)}, u32[]{:S(2)}) collective-permute-start(bf16[96,1024]{1,0:T(8,128)(2,1)S(1)} %get-tuple-element.165), channel_id=1, source_target_pairs={{0,2},{1,3},{2,0},{3,1},{4,6},{5,7},{6,4},{7,5},{8,10},{9,11},{10,... | collective-permute-start | bytes 589832 | tf_op jit(solution)/shard_map/ppermute | solution.py:373
  63.5 10.6 %collective-permute-start.25 = (bf16[96,1024]{1,0:T(8,128)(2,1)S(1)}, bf16[96,1024]{1,0:T(8,128)(2,1)S(1)}, u32[]{:S(2)}, u32[]{:S(2)}) collective-permute-start(bf16[96,1024]{1,0:T(8,128)(2,1)S(1)} %get-tuple-element.166), channel_id=1, source_target_pairs={{0,3},{1,2},{2,1},{3,0},{4,7},{5,6},{6,5},{7,4},{8,11},{9,10},{10,... | collective-permute-start | bytes 589832 | tf_op jit(solution)/shard_map/ppermute | solution.py:373
  67.7 11.4 %collective-permute-start.22 = (bf16[96,1024]{1,0:T(8,128)(2,1)S(1)}, bf16[96,1024]{1,0:T(8,128)(2,1)S(1)}, u32[]{:S(2)}, u32[]{:S(2)}) collective-permute-start(bf16[96,1024]{1,0:T(8,128)(2,1)S(1)} %get-tuple-element.160), channel_id=1, source_target_pairs={{0,1},{1,0},{2,3},{3,2},{4,5},{5,4},{6,7},{7,6},{8,9},{9,8},{10,11... | collective-permute-start | bytes 589832 | tf_op jit(solution)/shard_map/ppermute | solution.py:373
  68.1 11.0 %collective-permute-start.23 = (bf16[96,1024]{1,0:T(8,128)(2,1)S(1)}, bf16[96,1024]{1,0:T(8,128)(2,1)S(1)}, u32[]{:S(2)}, u32[]{:S(2)}) collective-permute-start(bf16[96,1024]{1,0:T(8,128)(2,1)S(1)} %get-tuple-element.164), channel_id=1, source_target_pairs={{0,1},{1,0},{2,3},{3,2},{4,5},{5,4},{6,7},{7,6},{8,9},{9,8},{10,11... | collective-permute-start | bytes 589832 | tf_op jit(solution)/shard_map/ppermute | solution.py:373
  68.6 6.3 %collective-permute-start.26 = (bf16[96,512]{1,0:T(8,128)(2,1)S(1)}, bf16[96,512]{1,0:T(8,128)(2,1)S(1)}, u32[]{:S(2)}, u32[]{:S(2)}) collective-permute-start(bf16[96,512]{1,0:T(8,128)(2,1)S(1)} %get-tuple-element.176), channel_id=1, source_target_pairs={{0,1},{1,0},{2,3},{3,2},{4,5},{5,4},{6,7},{7,6},{8,9},{9,8},{10,11... | collective-permute-start | bytes 294920 | tf_op jit(solution)/shard_map/ppermute | solution.py:373
  69.6 6.3 %collective-permute-start.27 = (bf16[96,512]{1,0:T(8,128)(2,1)S(1)}, bf16[96,512]{1,0:T(8,128)(2,1)S(1)}, u32[]{:S(2)}, u32[]{:S(2)}) collective-permute-start(bf16[96,512]{1,0:T(8,128)(2,1)S(1)} %get-tuple-element.177), channel_id=1, source_target_pairs={{0,2},{1,3},{2,0},{3,1},{4,6},{5,7},{6,4},{7,5},{8,10},{9,11},{10,... | collective-permute-start | bytes 294920 | tf_op jit(solution)/shard_map/ppermute | solution.py:373
  74.0 5.0 %collective-permute-start.28 = (bf16[96,512]{1,0:T(8,128)(2,1)S(1)}, bf16[96,512]{1,0:T(8,128)(2,1)S(1)}, u32[]{:S(2)}, u32[]{:S(2)}) collective-permute-start(bf16[96,512]{1,0:T(8,128)(2,1)S(1)} %get-tuple-element.178), channel_id=1, source_target_pairs={{0,3},{1,2},{2,1},{3,0},{4,7},{5,6},{6,5},{7,4},{8,11},{9,10},{10,... | collective-permute-start | bytes 294920 | tf_op jit(solution)/shard_map/ppermute | solution.py:373

commit v7 on v6

--- a/solution.py
+++ b/solution.py
@@ -63,51 +63,58 @@
         outs, sems = refs[:-1], refs[-1]
         own = lax.axis_index("head")
         pairs = []
-        for step in range(head_count):
+        for step in range(1, head_count):
             for chunk in range(chunks):
                 cols = aligned((own ^ step) * chunks + chunk, DH)
                 at = 2 * DH * chunk
-                pairs.append((k_ref.at[:, cols], outs[step].at[:, at : at + DH]))
-                pairs.append((v_ref.at[:, cols], outs[step].at[:, at + DH : at + 2 * DH]))
+                pairs.append((k_ref.at[:, cols], outs[step - 1].at[:, at : at + DH]))
+                pairs.append((v_ref.at[:, cols], outs[step - 1].at[:, at + DH : at + 2 * DH]))
         run_copies(pairs, sems)
 
     return pl.pallas_call(
         kernel,
-        out_shape=[jax.ShapeDtypeStruct((keys.shape[0], 2 * chunks * DH), keys.dtype)] * head_count,
+        out_shape=[jax.ShapeDtypeStruct((keys.shape[0], 2 * chunks * DH), keys.dtype)]
+        * (head_count - 1),
         in_specs=[ANY] * 2,
-        scratch_shapes=[pltpu.SemaphoreType.DMA((2 * head_count * chunks,))],
+        scratch_shapes=[pltpu.SemaphoreType.DMA((2 * (head_count - 1) * chunks,))],
         cost_estimate=cost(0, 8 * keys.size),
         name="pack_kv",
     )(keys, values)
 
 
-def pack_q(queries, head_count, chunks, whole):
+def pack_q(queries, keys, values, head_count, chunks, whole):
     part, width = queries.shape[0], queries.shape[1] // (head_count * chunks)
     layout = []
     for step in range(head_count):
         layout += [(step, 0, chunks)] if step in whole else [(step, c, 1) for c in range(chunks)]
 
-    def kernel(q_ref, *refs):
-        outs, sems = refs[:-1], refs[-1]
+    def kernel(q_ref, k_ref, v_ref, *refs):
+        outs, kv_out, sems = refs[:-2], refs[-2], refs[-1]
         own = lax.axis_index("head")
         pairs = []
         for out, (step, chunk, count) in zip(outs, layout):
             first = pl.multiple_of(((own ^ step) * chunks + chunk) * width, width)
             pairs.append((q_ref.at[:, pl.ds(first, count * width)], out))
+        for chunk in range(chunks):
+            cols = aligned(own * chunks + chunk, DH)
+            at = 2 * DH * chunk
+            pairs.append((k_ref.at[:, cols], kv_out.at[:, at : at + DH]))
+            pairs.append((v_ref.at[:, cols], kv_out.at[:, at + DH : at + 2 * DH]))
         run_copies(pairs, sems)
 
     outs = pl.pallas_call(
         kernel,
         out_shape=[
             jax.ShapeDtypeStruct((part, count * width), queries.dtype) for _, _, count in layout
-        ],
-        in_specs=[ANY],
-        scratch_shapes=[pltpu.SemaphoreType.DMA((len(layout),))],
+        ]
+        + [jax.ShapeDtypeStruct((part, 2 * chunks * DH), keys.dtype)],
+        in_specs=[ANY] * 3,
+        scratch_shapes=[pltpu.SemaphoreType.DMA((len(layout) + 2 * chunks,))],
         compiler_params=pltpu.CompilerParams(vmem_limit_bytes=16 << 20),
         cost_estimate=cost(0, 4 * queries.size),
         name="pack_q",
-    )(queries)
-    return {(step, chunk): out for out, (step, chunk, _) in zip(outs, layout)}
+    )(queries, keys, values)
+    return {(step, chunk): out for out, (step, chunk, _) in zip(outs, layout)}, outs[-1]
 
 
 def join_kv(parts, tags, chunks):
@@ -379,8 +386,8 @@
     steps = range(head_count)
     kv_packed = pack_kv(keys, values, head_count, chunks)
     queries, kv_packed, file_ids = lax.optimization_barrier((queries, kv_packed, file_ids))
-    kv_parts = [over_head(kv_packed[step], step) for step in steps]
-    packed = pack_q(queries, head_count, chunks, whole)
+    packed, kv_near = pack_q(queries, keys, values, head_count, chunks, whole)
+    kv_parts = [kv_near] + [over_head(kv_packed[step - 1], step) for step in steps[1:]]
     rows = file_ids.shape[0]
     tags = jnp.pad(file_ids.astype(jnp.bfloat16), (0, TAG_ROWS * 2 * DH - rows))
     tags = tags.reshape(TAG_ROWS, 2 * DH)

time: 80.8 us -> 81.3 us (level)
  waiting for transfers between devices: 29.8 us -> 28.4 us
  local copies, waits for them, and re-layouts: 3.73 us -> 5.06 us
    unnamed x12 -> x14, local copies, waits for them, and re-layouts: 3.72 us -> 5.04 us
    ppermute x17, waiting for transfers between devices: 12.3 us -> 11.2 us  [over_head(): lax.ppermute(block, 'head', [(i, i ^ step) for i in range(head_count)])]
where the time goes in v7:
time: 81.3 us; the launch traced here: 81.1 us
  starting transfers between devices  34.1 us (42%)
  waiting for transfers between devices  28.4 us (35%)
  Pallas kernels  12.7 us (16%)
  local copies, waits for them, and re-layouts  5.06 us (6%)
    ppermute x12, starting transfers between devices, over_ctx(): return lax.ppermute(block, 'ctx', pairs)  18.7 us
    ppermute x12, waiting for transfers between devices, over_ctx(): return lax.ppermute(block, 'ctx', pairs)  17.1 us
    ppermute x17, starting transfers between devices, over_head(): lax.ppermute(block, 'head', [(i, i ^ step) for i in range(head_count)])  15.4 us
    ppermute x17, waiting for transfers between devices, over_head(): lax.ppermute(block, 'head', [(i, i ^ step) for i in range(head_count)])  11.2 us
    pallas_call x4, Pallas kernels, tile_grads(): pl.pallas_call(kernel, out_shape=[dq_shape] * dq_count + [dkv_shape] * dk...  7.75 us
    unnamed x14, local copies, waits for them, and re-layouts  5.04 us
    pallas_call x1, Pallas kernels, pack_kv(): pl.pallas_call(kernel, out_shape=[jax.ShapeDtypeStruct((keys.shape[0], 2...  1.82 us
  transfers between devices with their start and end apart: 29, of which 15 were waited for; matrix products, arithmetic and copies ran while one was open for 0% of the time, Pallas kernels for 12%

profile of v7, /device:TPU:0, one launch (start us, length us, event | category | flops | bytes accessed | tf_op | source)
XLA Modules:
  0.0 81.1 jit_solution(9405451590311638456)
XLA Ops:
  0.6 1.8 %pack_kv.1 = (bf16[96,512]{1,0:T(8,128)(2,1)}, bf16[96,512]{1,0:T(8,128)(2,1)}, bf16[96,512]{1,0:T(8,128)(2,1)}) custom-call(bf16[96,1024]{1,0:T(8,128)(2,1)} %k_ref.3, bf16[96,1024]{1,0:T(8,128)(2,1)} %v_ref.3), custom_call_target="tpu_custom_call" | custom-call | bytes 786432 | tf_op jit(solution)/shard_map/pack_kv/pallas_call | solution.py:74
  2.5 0.5 collective-permute-start
  3.0 2.6 %collective-permute-start.1 = (bf16[96,512]{1,0:T(8,128)(2,1)}, bf16[96,512]{1,0:T(8,128)(2,1)S(1)}, u32[]{:S(2)}, u32[]{:S(2)}) collective-permute-start(bf16[96,512]{1,0:T(8,128)(2,1)} %get-tuple-element.102), channel_id=1, source_target_pairs={{0,2},{1,3},{2,0},{3,1},{4,6},{5,7},{6,4},{7,5},{8,10},{9,11},{10,... | collective-permute-start | bytes 294920 | tf_op jit(solution)/shard_map/ppermute | solution.py:380
  5.6 0.1 collective-permute-start.2
  5.7 1.4 %copy-done.2 = bf16[96,8192]{1,0:T(8,128)(2,1)S(1)} copy-done((bf16[96,8192]{1,0:T(8,128)(2,1)S(1)}, bf16[96,8192]{1,0:T(8,128)(2,1)}, u32[]{:S(2)}) %copy-start.2) | copy-done | bytes 1572888
  7.1 0.9 %copy-done.3 = bf16[96,1024]{1,0:T(8,128)(2,1)S(1)} copy-done((bf16[96,1024]{1,0:T(8,128)(2,1)S(1)}, bf16[96,1024]{1,0:T(8,128)(2,1)}, u32[]{:S(2)}) %copy-start.3) | copy-done | bytes 196632
  8.0 0.9 %copy-done.4 = bf16[96,1024]{1,0:T(8,128)(2,1)S(1)} copy-done((bf16[96,1024]{1,0:T(8,128)(2,1)S(1)}, bf16[96,1024]{1,0:T(8,128)(2,1)}, u32[]{:S(2)}) %copy-start.4) | copy-done | bytes 196632
  8.9 0.3 pack_q.1
  9.2 0.4 copy-done.6
  9.6 0.0 collective-permute-done.refs_1_
  9.6 0.0 collective-permute-done.1.refs_2_
  9.6 1.4 %collective-permute-done.2.refs_3_ = bf16[96,512]{1,0:T(8,128)(2,1)S(1)} collective-permute-done((bf16[96,512]{1,0:T(8,128)(2,1)}, bf16[96,512]{1,0:T(8,128)(2,1)S(1)}, u32[]{:S(2)}, u32[]{:S(2)}) %collective-permute-start.2) | collective-permute-done | bytes 98336 | tf_op jit(solution)/shard_map/ppermute | solution.py:380
  11.0 0.1 collective-permute-start.3
  11.1 1.7 %collective-permute-start.4 = (bf16[96,1024]{1,0:T(8,128)(2,1)S(1)}, bf16[96,1024]{1,0:T(8,128)(2,1)S(1)}, u32[]{:S(2)}, u32[]{:S(2)}) collective-permute-start(bf16[96,1024]{1,0:T(8,128)(2,1)S(1)} %get-tuple-element.116), channel_id=1, source_target_pairs={{0,2},{1,3},{2,0},{3,1},{4,6},{5,7},{6,4},{7,5},{8,10},{9,11},{10,... | collective-permute-start | bytes 589832 | tf_op jit(solution)/shard_map/ppermute | solution.py:380
  12.9 0.0 collective-permute-start.5
  12.9 0.0 collective-permute-done.3.refs_4_
  13.0 1.6 %collective-permute-start.6 = (bf16[400,256]{1,0:T(8,128)(2,1)S(1)}, bf16[400,256]{1,0:T(8,128)(2,1)S(1)}, u32[]{:S(2)}, u32[]{:S(2)}) collective-permute-start(bf16[400,256]{1,0:T(8,128)(2,1)S(1)} %get-tuple-element.118.refs_7_), channel_id=1, source_target_pairs={{0,4},{4,0},{8,12},{12,8},{16,20},{20,16},{24,28},{28,24},{1,5},{5... | collective-permute-start | bytes 614408 | tf_op jit(solution)/shard_map/ppermute | solution.py:384
  14.5 1.6 %collective-permute-start.7 = (bf16[400,256]{1,0:T(8,128)(2,1)S(1)}, bf16[400,256]{1,0:T(8,128)(2,1)S(1)}, u32[]{:S(2)}, u32[]{:S(2)}) collective-permute-start(bf16[400,256]{1,0:T(8,128)(2,1)S(1)} %get-tuple-element.118.refs_7_), channel_id=1, source_target_pairs={{0,8},{4,12},{8,0},{12,4},{16,24},{20,28},{24,16},{28,20},{1,9},{5... | collective-permute-start | bytes 614408 | tf_op jit(solution)/shard_map/ppermute | solution.py:384
  16.1 0.4 collective-permute-start.8
  16.5 1.4 %copy-done.1 = bf16[384,2048]{1,0:T(8,128)(2,1)S(1)} copy-done((bf16[384,2048]{1,0:T(8,128)(2,1)S(1)}, bf16[384,2048]{1,0:T(8,128)(2,1)}, u32[]{:S(2)}) %copy-start.1) | copy-done | bytes 1572888
  17.9 0.9 %row_deltas.1.refs_1_ = f32[16,384]{1,0:T(8,128)S(1)} custom-call(bf16[384,2048]{1,0:T(8,128)(2,1)S(1)} %copy-done.1, bf16[384,2048]{1,0:T(8,128)(2,1)S(1)} %copy-done), custom_call_target="tpu_custom_call" | custom-call | flops 3145728 | bytes 3145728 | tf_op jit(solution)/shard_map/row_deltas/pallas_call | solution.py:44
  18.8 0.1 collective-permute-done.4.refs_5_
  18.9 1.7 %collective-permute-start.9 = (bf16[96,1024]{1,0:T(8,128)(2,1)S(1)}, bf16[96,1024]{1,0:T(8,128)(2,1)S(1)}, u32[]{:S(2)}, u32[]{:S(2)}) collective-permute-start(bf16[96,1024]{1,0:T(8,128)(2,1)S(1)} %get-tuple-element.127), channel_id=1, source_target_pairs={{0,2},{1,3},{2,0},{3,1},{4,6},{5,7},{6,4},{7,5},{8,10},{9,11},{10,... | collective-permute-start | bytes 589832 | tf_op jit(solution)/shard_map/ppermute | solution.py:380
  20.6 1.7 %collective-permute-done.5.refs_6_ = bf16[96,1024]{1,0:T(8,128)(2,1)S(1)} collective-permute-done((bf16[96,1024]{1,0:T(8,128)(2,1)S(1)}, bf16[96,1024]{1,0:T(8,128)(2,1)S(1)}, u32[]{:S(2)}, u32[]{:S(2)}) %collective-permute-start.5) | collective-permute-done | bytes 196640 | tf_op jit(solution)/shard_map/ppermute | solution.py:380
  22.3 2.2 %collective-permute-start.10 = (bf16[96,1024]{1,0:T(8,128)(2,1)S(1)}, bf16[96,1024]{1,0:T(8,128)(2,1)S(1)}, u32[]{:S(2)}, u32[]{:S(2)}) collective-permute-start(bf16[96,1024]{1,0:T(8,128)(2,1)S(1)} %get-tuple-element.128), channel_id=1, source_target_pairs={{0,3},{1,2},{2,1},{3,0},{4,7},{5,6},{6,5},{7,4},{8,11},{9,10},{10,... | collective-permute-start | bytes 589832 | tf_op jit(solution)/shard_map/ppermute | solution.py:380
  24.5 3.3 %own_tile.2 = (f32[1024,384]{1,0:T(8,128)S(1)}, f32[384,256]{1,0:T(8,128)S(1)}) custom-call(f32[16,384]{1,0:T(8,128)S(1)} %copy-done.5, f32[16,384]{1,0:T(8,128)S(1)} %row_deltas.1.refs_1_, bf16[384,2048]{1,0:T(8,128)(2,1)S(1)} %copy-done.1, bf16[96,2048]{1,0:T(8,128)(2,1)S(1)} %get-tuple-element.132.refs_3_, ...), custom_call_target="tpu_custom_call" | custom-call | flops 1509949440 | bytes 3932160 | tf_op jit(solution)/shard_map/own_tile/pallas_call | solution.py:289
  27.8 0.0 collective-permute-done.6.refs_8_
  27.8 1.6 %collective-permute-start.11 = (bf16[400,256]{1,0:T(8,128)(2,1)S(1)}, bf16[400,256]{1,0:T(8,128)(2,1)S(1)}, u32[]{:S(2)}, u32[]{:S(2)}) collective-permute-start(bf16[400,256]{1,0:T(8,128)(2,1)S(1)} %get-tuple-element.136.refs_7_), channel_id=1, source_target_pairs={{0,4},{4,0},{8,12},{12,8},{16,20},{20,16},{24,28},{28,24},{1,5},{5... | collective-permute-start | bytes 614408 | tf_op jit(solution)/shard_map/ppermute | solution.py:384
  29.4 0.0 collective-permute-done.7.refs_9_
  29.4 1.6 %collective-permute-start.12 = (bf16[400,256]{1,0:T(8,128)(2,1)S(1)}, bf16[400,256]{1,0:T(8,128)(2,1)S(1)}, u32[]{:S(2)}, u32[]{:S(2)}) collective-permute-start(bf16[400,256]{1,0:T(8,128)(2,1)S(1)} %get-tuple-element.136.refs_7_), channel_id=1, source_target_pairs={{0,8},{4,12},{8,0},{12,4},{16,24},{20,28},{24,16},{28,20},{1,9},{5... | collective-permute-start | bytes 614408 | tf_op jit(solution)/shard_map/ppermute | solution.py:384
  31.0 0.0 collective-permute-done.8.refs_10_
  31.0 0.4 collective-permute-start.13
  31.4 0.8 earlier_tiles.2
  32.2 0.0 collective-permute-done.9.refs_5_
  32.2 0.0 collective-permute-done.10.refs_6_
  32.2 2.7 %collective-permute-done.11.refs_8_ = bf16[400,256]{1,0:T(8,128)(2,1)S(1)} collective-permute-done((bf16[400,256]{1,0:T(8,128)(2,1)S(1)}, bf16[400,256]{1,0:T(8,128)(2,1)S(1)}, u32[]{:S(2)}, u32[]{:S(2)}) %collective-permute-start.11) | collective-permute-done | bytes 204832 | tf_op jit(solution)/shard_map/ppermute | solution.py:384
  34.9 2.4 %collective-permute-done.12.refs_9_ = bf16[400,256]{1,0:T(8,128)(2,1)S(1)} collective-permute-done((bf16[400,256]{1,0:T(8,128)(2,1)S(1)}, bf16[400,256]{1,0:T(8,128)(2,1)S(1)}, u32[]{:S(2)}, u32[]{:S(2)}) %collective-permute-start.12) | collective-permute-done | bytes 204832 | tf_op jit(solution)/shard_map/ppermute | solution.py:384
  37.3 2.2 %collective-permute-done.13.refs_10_ = bf16[400,256]{1,0:T(8,128)(2,1)S(1)} collective-permute-done((bf16[400,256]{1,0:T(8,128)(2,1)S(1)}, bf16[400,256]{1,0:T(8,128)(2,1)S(1)}, u32[]{:S(2)}, u32[]{:S(2)}) %collective-permute-start.13) | collective-permute-done | bytes 204832 | tf_op jit(solution)/shard_map/ppermute | solution.py:384
  39.5 1.5 %collective-permute-start.14 = (bf16[384,256]{1,0:T(8,128)(2,1)S(1)}, bf16[384,256]{1,0:T(8,128)(2,1)S(1)}, u32[]{:S(2)}, u32[]{:S(2)}) collective-permute-start(bf16[384,256]{1,0:T(8,128)(2,1)S(1)} %get-tuple-element.145), channel_id=1, source_target_pairs={{0,4},{4,0},{8,12},{12,8},{16,20},{20,16},{24,28},{28,24},{1,5},{5... | collective-permute-start | bytes 589832 | tf_op jit(solution)/shard_map/ppermute | solution.py:384
  41.0 4.1 %collective-permute-start.15 = (bf16[384,256]{1,0:T(8,128)(2,1)S(1)}, bf16[384,256]{1,0:T(8,128)(2,1)S(1)}, u32[]{:S(2)}, u32[]{:S(2)}) collective-permute-start(bf16[384,256]{1,0:T(8,128)(2,1)S(1)} %get-tuple-element.146), channel_id=1, source_target_pairs={{0,8},{4,12},{8,0},{12,4},{16,24},{20,28},{24,16},{28,20},{1,9},{5... | collective-permute-start | bytes 589832 | tf_op jit(solution)/shard_map/ppermute | solution.py:384
  45.0 0.0 collective-permute-start.16
  45.0 0.5 collective-permute-start.17
  45.5 0.3 earlier_tiles.3
  45.8 4.2 %collective-permute-done.15.refs_2_ = bf16[384,256]{1,0:T(8,128)(2,1)S(1)} collective-permute-done((bf16[384,256]{1,0:T(8,128)(2,1)S(1)}, bf16[384,256]{1,0:T(8,128)(2,1)S(1)}, u32[]{:S(2)}, u32[]{:S(2)}) %collective-permute-start.15) | collective-permute-done | bytes 196640 | tf_op jit(solution)/shard_map/ppermute | solution.py:384
  50.1 2.3 %collective-permute-done.16.refs_3_ = bf16[384,256]{1,0:T(8,128)(2,1)S(1)} collective-permute-done((bf16[384,256]{1,0:T(8,128)(2,1)S(1)}, bf16[384,256]{1,0:T(8,128)(2,1)S(1)}, u32[]{:S(2)}, u32[]{:S(2)}) %collective-permute-start.16) | collective-permute-done | bytes 196640 | tf_op jit(solution)/shard_map/ppermute | solution.py:384
  52.4 0.3 collective-permute-done.17.refs_2_
  52.7 0.2 collective-permute-done.18.refs_3_
  52.9 1.5 %collective-permute-start.19 = (bf16[384,256]{1,0:T(8,128)(2,1)S(1)}, bf16[384,256]{1,0:T(8,128)(2,1)S(1)}, u32[]{:S(2)}, u32[]{:S(2)}) collective-permute-start(bf16[384,256]{1,0:T(8,128)(2,1)S(1)} %get-tuple-element.154), channel_id=1, source_target_pairs={{0,4},{4,0},{8,12},{12,8},{16,20},{20,16},{24,28},{28,24},{1,5},{5... | collective-permute-start | bytes 589832 | tf_op jit(solution)/shard_map/ppermute | solution.py:384
  54.4 4.6 %collective-permute-start.20 = (bf16[384,256]{1,0:T(8,128)(2,1)S(1)}, bf16[384,256]{1,0:T(8,128)(2,1)S(1)}, u32[]{:S(2)}, u32[]{:S(2)}) collective-permute-start(bf16[384,256]{1,0:T(8,128)(2,1)S(1)} %get-tuple-element.155), channel_id=1, source_target_pairs={{0,8},{4,12},{8,0},{12,4},{16,24},{20,28},{24,16},{28,20},{1,9},{5... | collective-permute-start | bytes 589832 | tf_op jit(solution)/shard_map/ppermute | solution.py:384
  59.0 3.4 %own_tile.3 = (bf16[96,1024]{1,0:T(8,128)(2,1)S(1)}, bf16[96,1024]{1,0:T(8,128)(2,1)S(1)}, bf16[96,1024]{1,0:T(8,128)(2,1)S(1)}, bf16[96,1024]{1,0:T(8,128)(2,1)S(1)}, f32[384,256]{1,0:T(8,128)S(1)}) custom-call(f32[16,384]{1,0:T(8,128)S(1)} %copy-done.5, f32[16,384]{1,0:T(8,128)S(1)} %row_deltas.1.refs_1_, bf16[384,2048]{1,0:T(8,128)(2,1)S(1)} %copy-done.1, ...), custom_call_target="tpu_custom_call" | custom-call | flops 1509949440 | bytes 3932160 | tf_op jit(solution)/shard_map/own_tile/pallas_call | solution.py:289
  62.4 1.6 %collective-permute-start.24 = (bf16[96,1024]{1,0:T(8,128)(2,1)S(1)}, bf16[96,1024]{1,0:T(8,128)(2,1)S(1)}, u32[]{:S(2)}, u32[]{:S(2)}) collective-permute-start(bf16[96,1024]{1,0:T(8,128)(2,1)S(1)} %get-tuple-element.163), channel_id=1, source_target_pairs={{0,2},{1,3},{2,0},{3,1},{4,6},{5,7},{6,4},{7,5},{8,10},{9,11},{10,... | collective-permute-start | bytes 589832 | tf_op jit(solution)/shard_map/ppermute | solution.py:380
  64.0 0.9 %collective-permute-start.25 = (bf16[96,1024]{1,0:T(8,128)(2,1)S(1)}, bf16[96,1024]{1,0:T(8,128)(2,1)S(1)}, u32[]{:S(2)}, u32[]{:S(2)}) collective-permute-start(bf16[96,1024]{1,0:T(8,128)(2,1)S(1)} %get-tuple-element.164), channel_id=1, source_target_pairs={{0,3},{1,2},{2,1},{3,0},{4,7},{5,6},{6,5},{7,4},{8,11},{9,10},{10,... | collective-permute-start | bytes 589832 | tf_op jit(solution)/shard_map/ppermute | solution.py:380
  64.9 3.3 %collective-permute-done.21.refs_7_ = bf16[384,256]{1,0:T(8,128)(2,1)S(1)} collective-permute-done((bf16[384,256]{1,0:T(8,128)(2,1)S(1)}, bf16[384,256]{1,0:T(8,128)(2,1)S(1)}, u32[]{:S(2)}, u32[]{:S(2)}) %collective-permute-start.21) | collective-permute-done | bytes 196640 | tf_op jit(solution)/shard_map/ppermute | solution.py:384
  68.2 0.4 collective-permute-start.22
  68.7 0.1 collective-permute-start.23
  68.8 0.4 sum_kv.1
  69.2 0.5 collective-permute-start.26
  69.7 0.5 collective-permute-done.24.refs_6_
  70.2 1.6 %collective-permute-start.27 = (bf16[96,512]{1,0:T(8,128)(2,1)S(1)}, bf16[96,512]{1,0:T(8,128)(2,1)S(1)}, u32[]{:S(2)}, u32[]{:S(2)}) collective-permute-start(bf16[96,512]{1,0:T(8,128)(2,1)S(1)} %get-tuple-element.175), channel_id=1, source_target_pairs={{0,2},{1,3},{2,0},{3,1},{4,6},{5,7},{6,4},{7,5},{8,10},{9,11},{10,... | collective-permute-start | bytes 294920 | tf_op jit(solution)/shard_map/ppermute | solution.py:380
  71.8 2.8 %collective-permute-done.25.refs_7_ = bf16[96,1024]{1,0:T(8,128)(2,1)S(1)} collective-permute-done((bf16[96,1024]{1,0:T(8,128)(2,1)S(1)}, bf16[96,1024]{1,0:T(8,128)(2,1)S(1)}, u32[]{:S(2)}, u32[]{:S(2)}) %collective-permute-start.25) | collective-permute-done | bytes 196640 | tf_op jit(solution)/shard_map/ppermute | solution.py:380
  74.6 0.8 %collective-permute-start.28 = (bf16[96,512]{1,0:T(8,128)(2,1)S(1)}, bf16[96,512]{1,0:T(8,128)(2,1)S(1)}, u32[]{:S(2)}, u32[]{:S(2)}) collective-permute-start(bf16[96,512]{1,0:T(8,128)(2,1)S(1)} %get-tuple-element.176), channel_id=1, source_target_pairs={{0,3},{1,2},{2,1},{3,0},{4,7},{5,6},{6,5},{7,4},{8,11},{9,10},{10,... | collective-permute-start | bytes 294920 | tf_op jit(solution)/shard_map/ppermute | solution.py:380
  75.4 1.1 %collective-permute-done.27.refs_10_ = bf16[96,512]{1,0:T(8,128)(2,1)S(1)} collective-permute-done((bf16[96,512]{1,0:T(8,128)(2,1)S(1)}, bf16[96,512]{1,0:T(8,128)(2,1)S(1)}, u32[]{:S(2)}, u32[]{:S(2)}) %collective-permute-start.27) | collective-permute-done | bytes 98336 | tf_op jit(solution)/shard_map/ppermute | solution.py:380
  76.5 3.1 %collective-permute-done.28.refs_11_ = bf16[96,512]{1,0:T(8,128)(2,1)S(1)} collective-permute-done((bf16[96,512]{1,0:T(8,128)(2,1)S(1)}, bf16[96,512]{1,0:T(8,128)(2,1)S(1)}, u32[]{:S(2)}, u32[]{:S(2)}) %collective-permute-start.28) | collective-permute-done | bytes 98336 | tf_op jit(solution)/shard_map/ppermute | solution.py:380
  79.6 1.4 %join_grads.1 = (bf16[96,8192]{1,0:T(8,128)(2,1)}, bf16[96,1024]{1,0:T(8,128)(2,1)}, bf16[96,1024]{1,0:T(8,128)(2,1)}) custom-call(bf16[96,1024]{1,0:T(8,128)(2,1)S(1)} %get-tuple-element.157.refs_0_, bf16[96,1024]{1,0:T(8,128)(2,1)S(1)} %collective-permute-done.22.refs_1_, bf16[96,1024]{1,0:T(8,128)(2,1)S(1)} %collective-permute-done.17.refs_2_, ...), custom_call_target="tpu_custom_call" | custom-call | bytes 3932160 | tf_op jit(solution)/shard_map/join_grads/pallas_call | solution.py:360
  (21 shorter events, 0.1 us)
Async XLA Ops:
  0.6 15.9 %copy-start = (bf16[384,2048]{1,0:T(8,128)(2,1)S(1)}, bf16[384,2048]{1,0:T(8,128)(2,1)}, u32[]{:S(2)}) copy-start(bf16[384,2048]{1,0:T(8,128)(2,1)} %out_ref.1) | copy-start | bytes 4718596
  2.5 7.2 %collective-permute-start = (bf16[96,512]{1,0:T(8,128)(2,1)}, bf16[96,512]{1,0:T(8,128)(2,1)S(1)}, u32[]{:S(2)}, u32[]{:S(2)}) collective-permute-start(bf16[96,512]{1,0:T(8,128)(2,1)} %get-tuple-element.101), channel_id=1, source_target_pairs={{0,1},{1,0},{2,3},{3,2},{4,5},{5,4},{6,7},{7,6},{8,9},{9,8},{10,11... | collective-permute-start | bytes 294920 | tf_op jit(solution)/shard_map/ppermute | solution.py:380
  3.0 6.6 %collective-permute-start.1 = (bf16[96,512]{1,0:T(8,128)(2,1)}, bf16[96,512]{1,0:T(8,128)(2,1)S(1)}, u32[]{:S(2)}, u32[]{:S(2)}) collective-permute-start(bf16[96,512]{1,0:T(8,128)(2,1)} %get-tuple-element.102), channel_id=1, source_target_pairs={{0,2},{1,3},{2,0},{3,1},{4,6},{5,7},{6,4},{7,5},{8,10},{9,11},{10,... | collective-permute-start | bytes 294920 | tf_op jit(solution)/shard_map/ppermute | solution.py:380
  5.6 5.4 %collective-permute-start.2 = (bf16[96,512]{1,0:T(8,128)(2,1)}, bf16[96,512]{1,0:T(8,128)(2,1)S(1)}, u32[]{:S(2)}, u32[]{:S(2)}) collective-permute-start(bf16[96,512]{1,0:T(8,128)(2,1)} %get-tuple-element.103), channel_id=1, source_target_pairs={{0,3},{1,2},{2,1},{3,0},{4,7},{5,6},{6,5},{7,4},{8,11},{9,10},{10,... | collective-permute-start | bytes 294920 | tf_op jit(solution)/shard_map/ppermute | solution.py:380
  5.7 1.4 %copy-start.2 = (bf16[96,8192]{1,0:T(8,128)(2,1)S(1)}, bf16[96,8192]{1,0:T(8,128)(2,1)}, u32[]{:S(2)}) copy-start(bf16[96,8192]{1,0:T(8,128)(2,1)} %q_ref) | copy-start | bytes 4718596
  7.1 0.9 %copy-start.3 = (bf16[96,1024]{1,0:T(8,128)(2,1)S(1)}, bf16[96,1024]{1,0:T(8,128)(2,1)}, u32[]{:S(2)}) copy-start(bf16[96,1024]{1,0:T(8,128)(2,1)} %k_ref.3) | copy-start | bytes 589828
  8.0 0.9 %copy-start.4 = (bf16[96,1024]{1,0:T(8,128)(2,1)S(1)}, bf16[96,1024]{1,0:T(8,128)(2,1)}, u32[]{:S(2)}) copy-start(bf16[96,1024]{1,0:T(8,128)(2,1)} %v_ref.3) | copy-start | bytes 589828
  8.9 0.7 copy-start.6
  11.0 1.9 %collective-permute-start.3 = (bf16[96,2048]{1,0:T(8,128)(2,1)S(1)}, bf16[96,2048]{1,0:T(8,128)(2,1)S(1)}, u32[]{:S(2)}, u32[]{:S(2)}) collective-permute-start(bf16[96,2048]{1,0:T(8,128)(2,1)S(1)} %get-tuple-element.113), channel_id=1, source_target_pairs={{0,1},{1,0},{2,3},{3,2},{4,5},{5,4},{6,7},{7,6},{8,9},{9,8},{10,11... | collective-permute-start | bytes 1179656 | tf_op jit(solution)/shard_map/ppermute | solution.py:380
  11.1 7.8 %collective-permute-start.4 = (bf16[96,1024]{1,0:T(8,128)(2,1)S(1)}, bf16[96,1024]{1,0:T(8,128)(2,1)S(1)}, u32[]{:S(2)}, u32[]{:S(2)}) collective-permute-start(bf16[96,1024]{1,0:T(8,128)(2,1)S(1)} %get-tuple-element.116), channel_id=1, source_target_pairs={{0,2},{1,3},{2,0},{3,1},{4,6},{5,7},{6,4},{7,5},{8,10},{9,11},{10,... | collective-permute-start | bytes 589832 | tf_op jit(solution)/shard_map/ppermute | solution.py:380
  12.9 9.5 %collective-permute-start.5 = (bf16[96,1024]{1,0:T(8,128)(2,1)S(1)}, bf16[96,1024]{1,0:T(8,128)(2,1)S(1)}, u32[]{:S(2)}, u32[]{:S(2)}) collective-permute-start(bf16[96,1024]{1,0:T(8,128)(2,1)S(1)} %get-tuple-element.117), channel_id=1, source_target_pairs={{0,3},{1,2},{2,1},{3,0},{4,7},{5,6},{6,5},{7,4},{8,11},{9,10},{10,... | collective-permute-start | bytes 589832 | tf_op jit(solution)/shard_map/ppermute | solution.py:380
  13.0 14.9 %collective-permute-start.6 = (bf16[400,256]{1,0:T(8,128)(2,1)S(1)}, bf16[400,256]{1,0:T(8,128)(2,1)S(1)}, u32[]{:S(2)}, u32[]{:S(2)}) collective-permute-start(bf16[400,256]{1,0:T(8,128)(2,1)S(1)} %get-tuple-element.118.refs_7_), channel_id=1, source_target_pairs={{0,4},{4,0},{8,12},{12,8},{16,20},{20,16},{24,28},{28,24},{1,5},{5... | collective-permute-start | bytes 614408 | tf_op jit(solution)/shard_map/ppermute | solution.py:384
  14.5 14.9 %collective-permute-start.7 = (bf16[400,256]{1,0:T(8,128)(2,1)S(1)}, bf16[400,256]{1,0:T(8,128)(2,1)S(1)}, u32[]{:S(2)}, u32[]{:S(2)}) collective-permute-start(bf16[400,256]{1,0:T(8,128)(2,1)S(1)} %get-tuple-element.118.refs_7_), channel_id=1, source_target_pairs={{0,8},{4,12},{8,0},{12,4},{16,24},{20,28},{24,16},{28,20},{1,9},{5... | collective-permute-start | bytes 614408 | tf_op jit(solution)/shard_map/ppermute | solution.py:384
  16.1 14.9 %collective-permute-start.8 = (bf16[400,256]{1,0:T(8,128)(2,1)S(1)}, bf16[400,256]{1,0:T(8,128)(2,1)S(1)}, u32[]{:S(2)}, u32[]{:S(2)}) collective-permute-start(bf16[400,256]{1,0:T(8,128)(2,1)S(1)} %get-tuple-element.118.refs_7_), channel_id=1, source_target_pairs={{0,12},{4,8},{8,4},{12,0},{16,28},{20,24},{24,20},{28,16},{1,13},{... | collective-permute-start | bytes 614408 | tf_op jit(solution)/shard_map/ppermute | solution.py:384
  16.5 1.4 %copy-start.1 = (bf16[384,2048]{1,0:T(8,128)(2,1)S(1)}, bf16[384,2048]{1,0:T(8,128)(2,1)}, u32[]{:S(2)}) copy-start(bf16[384,2048]{1,0:T(8,128)(2,1)} %refs_2_.7) | copy-start | bytes 4718596
  17.9 6.6 %copy-start.5 = (f32[16,384]{1,0:T(8,128)S(1)}, f32[16,384]{1,0:T(8,128)}, u32[]{:S(2)}) copy-start(f32[16,384]{1,0:T(8,128)} %refs_0_.7) | copy-start | bytes 73732
  18.9 13.3 %collective-permute-start.9 = (bf16[96,1024]{1,0:T(8,128)(2,1)S(1)}, bf16[96,1024]{1,0:T(8,128)(2,1)S(1)}, u32[]{:S(2)}, u32[]{:S(2)}) collective-permute-start(bf16[96,1024]{1,0:T(8,128)(2,1)S(1)} %get-tuple-element.127), channel_id=1, source_target_pairs={{0,2},{1,3},{2,0},{3,1},{4,6},{5,7},{6,4},{7,5},{8,10},{9,11},{10,... | collective-permute-start | bytes 589832 | tf_op jit(solution)/shard_map/ppermute | solution.py:380
  22.3 9.9 %collective-permute-start.10 = (bf16[96,1024]{1,0:T(8,128)(2,1)S(1)}, bf16[96,1024]{1,0:T(8,128)(2,1)S(1)}, u32[]{:S(2)}, u32[]{:S(2)}) collective-permute-start(bf16[96,1024]{1,0:T(8,128)(2,1)S(1)} %get-tuple-element.128), channel_id=1, source_target_pairs={{0,3},{1,2},{2,1},{3,0},{4,7},{5,6},{6,5},{7,4},{8,11},{9,10},{10,... | collective-permute-start | bytes 589832 | tf_op jit(solution)/shard_map/ppermute | solution.py:380
  27.8 7.0 %collective-permute-start.11 = (bf16[400,256]{1,0:T(8,128)(2,1)S(1)}, bf16[400,256]{1,0:T(8,128)(2,1)S(1)}, u32[]{:S(2)}, u32[]{:S(2)}) collective-permute-start(bf16[400,256]{1,0:T(8,128)(2,1)S(1)} %get-tuple-element.136.refs_7_), channel_id=1, source_target_pairs={{0,4},{4,0},{8,12},{12,8},{16,20},{20,16},{24,28},{28,24},{1,5},{5... | collective-permute-start | bytes 614408 | tf_op jit(solution)/shard_map/ppermute | solution.py:384
  29.4 7.9 %collective-permute-start.12 = (bf16[400,256]{1,0:T(8,128)(2,1)S(1)}, bf16[400,256]{1,0:T(8,128)(2,1)S(1)}, u32[]{:S(2)}, u32[]{:S(2)}) collective-permute-start(bf16[400,256]{1,0:T(8,128)(2,1)S(1)} %get-tuple-element.136.refs_7_), channel_id=1, source_target_pairs={{0,8},{4,12},{8,0},{12,4},{16,24},{20,28},{24,16},{28,20},{1,9},{5... | collective-permute-start | bytes 614408 | tf_op jit(solution)/shard_map/ppermute | solution.py:384
  31.0 8.5 %collective-permute-start.13 = (bf16[400,256]{1,0:T(8,128)(2,1)S(1)}, bf16[400,256]{1,0:T(8,128)(2,1)S(1)}, u32[]{:S(2)}, u32[]{:S(2)}) collective-permute-start(bf16[400,256]{1,0:T(8,128)(2,1)S(1)} %get-tuple-element.136.refs_7_), channel_id=1, source_target_pairs={{0,12},{4,8},{8,4},{12,0},{16,28},{20,24},{24,20},{28,16},{1,13},{... | collective-permute-start | bytes 614408 | tf_op jit(solution)/shard_map/ppermute | solution.py:384
  39.5 6.3 %collective-permute-start.14 = (bf16[384,256]{1,0:T(8,128)(2,1)S(1)}, bf16[384,256]{1,0:T(8,128)(2,1)S(1)}, u32[]{:S(2)}, u32[]{:S(2)}) collective-permute-start(bf16[384,256]{1,0:T(8,128)(2,1)S(1)} %get-tuple-element.145), channel_id=1, source_target_pairs={{0,4},{4,0},{8,12},{12,8},{16,20},{20,16},{24,28},{28,24},{1,5},{5... | collective-permute-start | bytes 589832 | tf_op jit(solution)/shard_map/ppermute | solution.py:384
  41.0 9.1 %collective-permute-start.15 = (bf16[384,256]{1,0:T(8,128)(2,1)S(1)}, bf16[384,256]{1,0:T(8,128)(2,1)S(1)}, u32[]{:S(2)}, u32[]{:S(2)}) collective-permute-start(bf16[384,256]{1,0:T(8,128)(2,1)S(1)} %get-tuple-element.146), channel_id=1, source_target_pairs={{0,8},{4,12},{8,0},{12,4},{16,24},{20,28},{24,16},{28,20},{1,9},{5... | collective-permute-start | bytes 589832 | tf_op jit(solution)/shard_map/ppermute | solution.py:384
  45.0 7.4 %collective-permute-start.16 = (bf16[384,256]{1,0:T(8,128)(2,1)S(1)}, bf16[384,256]{1,0:T(8,128)(2,1)S(1)}, u32[]{:S(2)}, u32[]{:S(2)}) collective-permute-start(bf16[384,256]{1,0:T(8,128)(2,1)S(1)} %get-tuple-element.147), channel_id=1, source_target_pairs={{0,12},{4,8},{8,4},{12,0},{16,28},{20,24},{24,20},{28,16},{1,13},{... | collective-permute-start | bytes 589832 | tf_op jit(solution)/shard_map/ppermute | solution.py:384
  45.0 7.7 %collective-permute-start.17 = (bf16[96,1024]{1,0:T(8,128)(2,1)S(1)}, bf16[96,1024]{1,0:T(8,128)(2,1)S(1)}, u32[]{:S(2)}, u32[]{:S(2)}) collective-permute-start(bf16[96,1024]{1,0:T(8,128)(2,1)S(1)} %get-tuple-element.148), channel_id=1, source_target_pairs={{0,2},{1,3},{2,0},{3,1},{4,6},{5,7},{6,4},{7,5},{8,10},{9,11},{10,... | collective-permute-start | bytes 589832 | tf_op jit(solution)/shard_map/ppermute | solution.py:380
  45.5 7.4 %collective-permute-start.18 = (bf16[96,1024]{1,0:T(8,128)(2,1)S(1)}, bf16[96,1024]{1,0:T(8,128)(2,1)S(1)}, u32[]{:S(2)}, u32[]{:S(2)}) collective-permute-start(bf16[96,1024]{1,0:T(8,128)(2,1)S(1)} %get-tuple-element.149), channel_id=1, source_target_pairs={{0,3},{1,2},{2,1},{3,0},{4,7},{5,6},{6,5},{7,4},{8,11},{9,10},{10,... | collective-permute-start | bytes 589832 | tf_op jit(solution)/shard_map/ppermute | solution.py:380
  52.9 12.0 %collective-permute-start.19 = (bf16[384,256]{1,0:T(8,128)(2,1)S(1)}, bf16[384,256]{1,0:T(8,128)(2,1)S(1)}, u32[]{:S(2)}, u32[]{:S(2)}) collective-permute-start(bf16[384,256]{1,0:T(8,128)(2,1)S(1)} %get-tuple-element.154), channel_id=1, source_target_pairs={{0,4},{4,0},{8,12},{12,8},{16,20},{20,16},{24,28},{28,24},{1,5},{5... | collective-permute-start | bytes 589832 | tf_op jit(solution)/shard_map/ppermute | solution.py:384
  54.4 10.6 %collective-permute-start.20 = (bf16[384,256]{1,0:T(8,128)(2,1)S(1)}, bf16[384,256]{1,0:T(8,128)(2,1)S(1)}, u32[]{:S(2)}, u32[]{:S(2)}) collective-permute-start(bf16[384,256]{1,0:T(8,128)(2,1)S(1)} %get-tuple-element.155), channel_id=1, source_target_pairs={{0,8},{4,12},{8,0},{12,4},{16,24},{20,28},{24,16},{28,20},{1,9},{5... | collective-permute-start | bytes 589832 | tf_op jit(solution)/shard_map/ppermute | solution.py:384
  59.0 9.2 %collective-permute-start.21 = (bf16[384,256]{1,0:T(8,128)(2,1)S(1)}, bf16[384,256]{1,0:T(8,128)(2,1)S(1)}, u32[]{:S(2)}, u32[]{:S(2)}) collective-permute-start(bf16[384,256]{1,0:T(8,128)(2,1)S(1)} %get-tuple-element.156), channel_id=1, source_target_pairs={{0,12},{4,8},{8,4},{12,0},{16,28},{20,24},{24,20},{28,16},{1,13},{... | collective-permute-start | bytes 589832 | tf_op jit(solution)/shard_map/ppermute | solution.py:384
  62.4 7.7 %collective-permute-start.24 = (bf16[96,1024]{1,0:T(8,128)(2,1)S(1)}, bf16[96,1024]{1,0:T(8,128)(2,1)S(1)}, u32[]{:S(2)}, u32[]{:S(2)}) collective-permute-start(bf16[96,1024]{1,0:T(8,128)(2,1)S(1)} %get-tuple-element.163), channel_id=1, source_target_pairs={{0,2},{1,3},{2,0},{3,1},{4,6},{5,7},{6,4},{7,5},{8,10},{9,11},{10,... | collective-permute-start | bytes 589832 | tf_op jit(solution)/shard_map/ppermute | solution.py:380
  64.0 10.6 %collective-permute-start.25 = (bf16[96,1024]{1,0:T(8,128)(2,1)S(1)}, bf16[96,1024]{1,0:T(8,128)(2,1)S(1)}, u32[]{:S(2)}, u32[]{:S(2)}) collective-permute-start(bf16[96,1024]{1,0:T(8,128)(2,1)S(1)} %get-tuple-element.164), channel_id=1, source_target_pairs={{0,3},{1,2},{2,1},{3,0},{4,7},{5,6},{6,5},{7,4},{8,11},{9,10},{10,... | collective-permute-start | bytes 589832 | tf_op jit(solution)/shard_map/ppermute | solution.py:380
  68.2 11.4 %collective-permute-start.22 = (bf16[96,1024]{1,0:T(8,128)(2,1)S(1)}, bf16[96,1024]{1,0:T(8,128)(2,1)S(1)}, u32[]{:S(2)}, u32[]{:S(2)}) collective-permute-start(bf16[96,1024]{1,0:T(8,128)(2,1)S(1)} %get-tuple-element.158), channel_id=1, source_target_pairs={{0,1},{1,0},{2,3},{3,2},{4,5},{5,4},{6,7},{7,6},{8,9},{9,8},{10,11... | collective-permute-start | bytes 589832 | tf_op jit(solution)/shard_map/ppermute | solution.py:380
  68.7 11.0 %collective-permute-start.23 = (bf16[96,1024]{1,0:T(8,128)(2,1)S(1)}, bf16[96,1024]{1,0:T(8,128)(2,1)S(1)}, u32[]{:S(2)}, u32[]{:S(2)}) collective-permute-start(bf16[96,1024]{1,0:T(8,128)(2,1)S(1)} %get-tuple-element.162), channel_id=1, source_target_pairs={{0,1},{1,0},{2,3},{3,2},{4,5},{5,4},{6,7},{7,6},{8,9},{9,8},{10,11... | collective-permute-start | bytes 589832 | tf_op jit(solution)/shard_map/ppermute | solution.py:380
  69.2 6.3 %collective-permute-start.26 = (bf16[96,512]{1,0:T(8,128)(2,1)S(1)}, bf16[96,512]{1,0:T(8,128)(2,1)S(1)}, u32[]{:S(2)}, u32[]{:S(2)}) collective-permute-start(bf16[96,512]{1,0:T(8,128)(2,1)S(1)} %get-tuple-element.174), channel_id=1, source_target_pairs={{0,1},{1,0},{2,3},{3,2},{4,5},{5,4},{6,7},{7,6},{8,9},{9,8},{10,11... | collective-permute-start | bytes 294920 | tf_op jit(solution)/shard_map/ppermute | solution.py:380
  70.2 6.3 %collective-permute-start.27 = (bf16[96,512]{1,0:T(8,128)(2,1)S(1)}, bf16[96,512]{1,0:T(8,128)(2,1)S(1)}, u32[]{:S(2)}, u32[]{:S(2)}) collective-permute-start(bf16[96,512]{1,0:T(8,128)(2,1)S(1)} %get-tuple-element.175), channel_id=1, source_target_pairs={{0,2},{1,3},{2,0},{3,1},{4,6},{5,7},{6,4},{7,5},{8,10},{9,11},{10,... | collective-permute-start | bytes 294920 | tf_op jit(solution)/shard_map/ppermute | solution.py:380
  74.6 5.0 %collective-permute-start.28 = (bf16[96,512]{1,0:T(8,128)(2,1)S(1)}, bf16[96,512]{1,0:T(8,128)(2,1)S(1)}, u32[]{:S(2)}, u32[]{:S(2)}) collective-permute-start(bf16[96,512]{1,0:T(8,128)(2,1)S(1)} %get-tuple-element.176), channel_id=1, source_target_pairs={{0,3},{1,2},{2,1},{3,0},{4,7},{5,6},{6,5},{7,4},{8,11},{9,10},{10,... | collective-permute-start | bytes 294920 | tf_op jit(solution)/shard_map/ppermute | solution.py:380
